TPU v7x, 32 devices: a whole 2x2x4 slice. The times are simulated.
32 devices in a mesh: dp: 16 (over z, x, core), seq: 2 (over y).
Axes of the slice: x: 2, y: 2, z: 4, core: 2. Of those that a mesh axis runs over, the one named last changes fastest.
Arguments:
- gene_ids: int32 [16, 2048], P('dp', 'seq'), may hold values from 0 to 9215, as said below
- homolog_ids: int32 [16, 2048], P('dp', 'seq'), may hold values from 0 to 9215, as said below
- knowledge_ids: int32 [16, 2048], P('dp', 'seq'), may hold values from 0 to 9215, as said below
- expr_bins: int32 [16, 2048], P('dp', 'seq'), may hold values from 0 to 127
- species: int32 [16], P('dp'), may hold values from 0 to 1, as said below
- cell_lengths: int32 [16], P('dp'), may hold values from 1025 to 2048, as said below
- gene_table: bfloat16 [9216, 768], P(('dp', 'seq')), may hold values from -4.1875 to 4.1875
- knowledge_tables: bfloat16 [4, 9216, 768], P(None, ('dp', 'seq')), may hold values from -2.09375 to 2.09375
- expr_table: bfloat16 [128, 768], replicated, may hold values from -4.1875 to 4.1875
- w_query: bfloat16 [768, 768], replicated, may hold values from -0.21875 to 0.21875
- b_query: float32 [768], replicated, may hold values from -1.8 to 1.8
- w_key: bfloat16 [768, 768], replicated, may hold values from -0.21875 to 0.21875
- w_value: bfloat16 [768, 768], replicated, may hold values from -0.21875 to 0.21875
- b_value: float32 [768], replicated, may hold values from -1.8 to 1.8
- w_out: bfloat16 [768, 768], replicated, may hold values from -2.5 to 2.5
- b_out: float32 [768], replicated, may hold values from -1.8 to 1.8
- gain_one: float32 [768], replicated, may hold values from 0.1 to 1.9
- shift_one: float32 [768], replicated, may hold values from -1.8 to 1.8
- w_up: bfloat16 [768, 3072], replicated, may hold values from -0.21875 to 0.21875
- b_up: float32 [3072], replicated, may hold values from -1.8 to 1.8
- w_down: bfloat16 [3072, 768], replicated, may hold values from -0.109375 to 0.109375
- b_down: float32 [768], replicated, may hold values from -1.8 to 1.8
- gain_two: float32 [768], replicated, may hold values from 0.1 to 1.9
- shift_two: float32 [768], replicated, may hold values from -1.8 to 1.8
- cotangent: bfloat16 [16, 2048, 768], P('dp', 'seq'), may hold values from -6 to 6
Outputs:
- layer_output: bfloat16 [16, 2048, 768], P('dp', 'seq')
- gene_table_grad: float32 [9216, 768], P(('dp', 'seq'))
- knowledge_grad: float32 [9216, 768], P(('dp', 'seq'))
- expr_table_grad: float32 [128, 768], replicated
- w_query_grad: float32 [768, 768], replicated
- b_query_grad: float32 [768], replicated
- w_key_grad: float32 [768, 768], replicated
- w_value_grad: float32 [768, 768], replicated
- b_value_grad: float32 [768], replicated
- w_out_grad: float32 [768, 768], replicated
- b_out_grad: float32 [768], replicated
- gain_one_grad: float32 [768], replicated
- shift_one_grad: float32 [768], replicated
- w_up_grad: float32 [768, 3072], replicated
- b_up_grad: float32 [3072], replicated
- w_down_grad: float32 [3072, 768], replicated
- b_down_grad: float32 [768], replicated
- gain_two_grad: float32 [768], replicated
- shift_two_grad: float32 [768], replicated
- row_counts: int32 [2, 9216], P(None, ('dp', 'seq'))
Inputs may be any that keep to these rules, and one draw needn't show every extreme that they name: Of the 1024 genes that one device holds (the cells of its dp index, the positions of its seq index), at most 64 have an id in one block of 288 rows (ids r * 288 to (r + 1) * 288 - 1); in every draw one block has exactly 64 from every device. A gene's gene_ids and homolog_ids lie in the same block. `homolog_ids`: as gene_ids: at most 64 of one device's genes in one block of 288 rows, one block reaching 64 from every device, and the same block as gene_ids for every gene. `knowledge_ids`: at most 64 of one device's genes in one block of 288 rows; in every draw one block has exactly 64 from every device. `species`: exactly a quarter of the cells, rounded down and at least one, have 1. `cell_lengths`: one cell has 2048 and one has 1025.
All inputs are finite; a program needn't handle non-finite values.
Results may differ from a plain program's by a relative error of at most 0.015.
The roundings to bfloat16 on the way count: a program that leaves them out, or rounds other values in their place, can miss the bound.
Values may be sent and summed in bfloat16 or wider, within the bound.
No kernel may reach another device: no remote copies, remote signals or barrier semaphores. Data moves between devices by JAX's collectives and lax.ppermute only.
A program may use at most 192 MiB of HBM per device.

v0:
```python
import jax
import jax.numpy as jnp
from jax import lax
from jax.sharding import PartitionSpec as P

HEADS = 12
HEAD_DIM = 64


def layer_norm(value, gain_vec, shift_vec):
    centre = jnp.mean(value, axis=-1, keepdims=True)
    centred = value - centre
    variance = jnp.mean(centred * centred, axis=-1, keepdims=True)
    return centred * lax.rsqrt(variance + 1e-05) * gain_vec + shift_vec


def gelu_exact(value):
    return jax.nn.gelu(value, approximate=False)


def head_split(array):
    return array.reshape(array.shape[0], HEADS, HEAD_DIM).transpose(1, 0, 2)


def head_merge(array):
    return array.transpose(1, 0, 2).reshape(array.shape[1], HEADS * HEAD_DIM)


def head_scores(query_head, key_head, valid_keys):
    scores = jnp.dot(query_head, key_head.T, preferred_element_type=jnp.float32) * HEAD_DIM ** (
        -0.5
    )
    return jnp.where(valid_keys[None, :], scores, -1e30)


def attend_forward(query_cell, key_cell, value_cell, valid_keys):

    def one_head(head_parts):
        query_head, key_head, value_head = head_parts
        scores = head_scores(query_head, key_head, valid_keys)
        log_total = jax.nn.logsumexp(scores, axis=-1, keepdims=True)
        probs_low = jnp.exp(scores - log_total).astype(jnp.bfloat16)
        context = jnp.dot(probs_low, value_head, preferred_element_type=jnp.float32)
        return (context, log_total[:, 0])

    context, log_total = lax.map(
        one_head, (head_split(query_cell), head_split(key_cell), head_split(value_cell))
    )
    return (head_merge(context), log_total)


def attend_backward(query_cell, key_cell, value_cell, valid_keys, log_total, grad_context):

    def one_head(head_parts):
        query_head, key_head, value_head, total_head, grad_head = head_parts
        scores = head_scores(query_head, key_head, valid_keys)
        attn_probs = jnp.exp(scores - total_head[:, None])
        probs_low = attn_probs.astype(jnp.bfloat16)
        grad_probs = jnp.dot(grad_head, value_head.T, preferred_element_type=jnp.float32)
        inner = jnp.sum(attn_probs * grad_probs, axis=-1, keepdims=True)
        grad_scores = (attn_probs * (grad_probs - inner) * HEAD_DIM ** (-0.5)).astype(jnp.bfloat16)
        grad_query = jnp.dot(grad_scores, key_head, preferred_element_type=jnp.float32)
        grad_key = jnp.dot(grad_scores.T, query_head, preferred_element_type=jnp.float32)
        grad_value = jnp.dot(probs_low.T, grad_head, preferred_element_type=jnp.float32)
        return (grad_query, grad_key, grad_value)

    grad_query, grad_key, grad_value = lax.map(
        one_head,
        (
            head_split(query_cell),
            head_split(key_cell),
            head_split(value_cell),
            log_total,
            head_split(grad_context),
        ),
    )
    return (head_merge(grad_query), head_merge(grad_key), head_merge(grad_value))


def place(identity, rows_dev, devices):
    owner_dev = identity // rows_dev
    owner_hits = (owner_dev[:, None] == jnp.arange(devices)[None, :]).astype(jnp.int32)
    before = jnp.cumsum(owner_hits, axis=0) - owner_hits
    slot_rank = jnp.sum(before * owner_hits, axis=1)
    return (owner_dev, slot_rank, identity - owner_dev * rows_dev)


def local(
    gene_ids,
    homolog_ids,
    knowledge_ids,
    expr_bins,
    species,
    cell_lengths,
    gene_table,
    knowledge_tables,
    expr_table,
    w_query,
    b_query,
    w_key,
    w_value,
    b_value,
    w_out,
    b_out,
    gain_one,
    shift_one,
    w_up,
    b_up,
    w_down,
    b_down,
    gain_two,
    shift_two,
    cotangent,
):
    cells_here, half_len = gene_ids.shape
    width = gene_table.shape[1]
    rows_dev = gene_table.shape[0]
    devices = lax.axis_size(("dp", "seq"))
    looked = cells_here * half_len
    capacity = 2 * looked // devices
    slots_all = 2 * capacity
    chosen = jnp.where(species[:, None] == 1, homolog_ids, gene_ids).reshape(-1)
    gene_owner, gene_rank, gene_local = place(chosen, rows_dev, devices)
    know_owner, know_rank, know_local = place(knowledge_ids.reshape(-1), rows_dev, devices)
    gene_slot = gene_owner * slots_all + gene_rank
    know_slot = know_owner * slots_all + capacity + know_rank
    requests = jnp.full((devices * slots_all,), -1, jnp.int32)
    requests = requests.at[gene_slot].set(gene_local).at[know_slot].set(know_local + rows_dev)
    requests = requests.reshape(devices, slots_all)
    know_sum = jnp.sum(knowledge_tables.astype(jnp.float32), axis=0).astype(jnp.bfloat16)
    combined = jnp.concatenate([gene_table, know_sum], axis=0)
    received = lax.all_to_all(requests, ("dp", "seq"), split_axis=0, concat_axis=0, tiled=True)
    found = jnp.take(combined, jnp.clip(received, 0, 2 * rows_dev - 1), axis=0)
    fetched = lax.all_to_all(found, ("dp", "seq"), split_axis=0, concat_axis=0, tiled=True)
    fetched_flat = fetched.reshape(devices * slots_all, width)
    bin_hot = expr_bins.reshape(-1)[:, None] == jnp.arange(expr_table.shape[0])[None, :]
    expr_rows = jnp.dot(
        bin_hot.astype(jnp.bfloat16), expr_table, preferred_element_type=jnp.float32
    )
    embedded = (
        fetched_flat[gene_slot].astype(jnp.float32)
        + fetched_flat[know_slot].astype(jnp.float32)
        + expr_rows
    )
    x_low = embedded.astype(jnp.bfloat16)
    query_all = (jnp.dot(x_low, w_query, preferred_element_type=jnp.float32) + b_query).astype(
        jnp.bfloat16
    )
    key_local = jnp.dot(x_low, w_key, preferred_element_type=jnp.float32).astype(jnp.bfloat16)
    value_local = (jnp.dot(x_low, w_value, preferred_element_type=jnp.float32) + b_value).astype(
        jnp.bfloat16
    )
    query_cells = query_all.reshape(cells_here, half_len, width)
    key_cells = key_local.reshape(cells_here, half_len, width)
    value_cells = value_local.reshape(cells_here, half_len, width)
    key_whole, value_whole = (
        lax.all_gather(key_cells, "seq", axis=1, tiled=True),
        lax.all_gather(value_cells, "seq", axis=1, tiled=True),
    )
    positions = jnp.arange(key_whole.shape[1])
    valid_keys = positions[None, :] < cell_lengths[:, None]
    context_cells, log_totals = lax.map(
        lambda cell_parts: attend_forward(*cell_parts),
        (query_cells, key_whole, value_whole, valid_keys),
    )
    context_low = context_cells.reshape(looked, width).astype(jnp.bfloat16)
    attn_out = jnp.dot(context_low, w_out, preferred_element_type=jnp.float32) + b_out
    normed_one, norm_one_back = jax.vjp(layer_norm, embedded + attn_out, gain_one, shift_one)
    normed_low = normed_one.astype(jnp.bfloat16)
    pre_ffn = jnp.dot(normed_low, w_up, preferred_element_type=jnp.float32) + b_up
    gelu_value, gelu_back = jax.vjp(gelu_exact, pre_ffn)
    activated = gelu_value.astype(jnp.bfloat16)
    ffn_out = jnp.dot(activated, w_down, preferred_element_type=jnp.float32) + b_down
    final, norm_two_back = jax.vjp(layer_norm, normed_one + ffn_out, gain_two, shift_two)
    layer_output = final.astype(jnp.bfloat16).reshape(cells_here, half_len, width)
    grad_final = cotangent.reshape(looked, width).astype(jnp.float32)
    grad_two, gain_two_grad, shift_two_grad = norm_two_back(grad_final)
    grad_ffn_low = grad_two.astype(jnp.bfloat16)
    w_down_grad = jnp.einsum(
        "tf,td->fd", activated, grad_ffn_low, preferred_element_type=jnp.float32
    )
    b_down_grad = jnp.sum(grad_ffn_low.astype(jnp.float32), axis=0)
    grad_act = jnp.einsum("td,fd->tf", grad_ffn_low, w_down, preferred_element_type=jnp.float32)
    grad_pre_low = gelu_back(grad_act)[0].astype(jnp.bfloat16)
    w_up_grad = jnp.einsum(
        "td,tf->df", normed_low, grad_pre_low, preferred_element_type=jnp.float32
    )
    b_up_grad = jnp.sum(grad_pre_low.astype(jnp.float32), axis=0)
    grad_normed = grad_two + jnp.einsum(
        "tf,df->td", grad_pre_low, w_up, preferred_element_type=jnp.float32
    )
    grad_one, gain_one_grad, shift_one_grad = norm_one_back(grad_normed)
    grad_attn_low = grad_one.astype(jnp.bfloat16)
    w_out_grad = jnp.einsum(
        "te,td->ed", context_low, grad_attn_low, preferred_element_type=jnp.float32
    )
    b_out_grad = jnp.sum(grad_attn_low.astype(jnp.float32), axis=0)
    grad_context = jnp.einsum(
        "td,ed->te", grad_attn_low, w_out, preferred_element_type=jnp.float32
    ).astype(jnp.bfloat16)
    key_back, value_back = (key_whole, value_whole)
    grad_q_cells, grad_k_whole, grad_v_whole = lax.map(
        lambda cell_parts: attend_backward(*cell_parts),
        (
            query_cells,
            key_back,
            value_back,
            valid_keys,
            log_totals,
            grad_context.reshape(cells_here, half_len, width),
        ),
    )
    grad_key_part, grad_value_part = (
        lax.psum_scatter(grad_k_whole, "seq", scatter_dimension=1, tiled=True),
        lax.psum_scatter(grad_v_whole, "seq", scatter_dimension=1, tiled=True),
    )
    grad_query_low = grad_q_cells.reshape(looked, width).astype(jnp.bfloat16)
    grad_key_low = grad_key_part.reshape(looked, width).astype(jnp.bfloat16)
    grad_value_low = grad_value_part.reshape(looked, width).astype(jnp.bfloat16)
    w_query_grad = jnp.einsum(
        "td,te->de", x_low, grad_query_low, preferred_element_type=jnp.float32
    )
    b_query_grad = jnp.sum(grad_query_low.astype(jnp.float32), axis=0)
    w_key_grad = jnp.einsum("td,te->de", x_low, grad_key_low, preferred_element_type=jnp.float32)
    w_value_grad = jnp.einsum(
        "td,te->de", x_low, grad_value_low, preferred_element_type=jnp.float32
    )
    b_value_grad = jnp.sum(grad_value_low.astype(jnp.float32), axis=0)
    grad_embedded = (
        grad_one
        + jnp.einsum("te,de->td", grad_query_low, w_query, preferred_element_type=jnp.float32)
        + jnp.einsum("te,de->td", grad_key_low, w_key, preferred_element_type=jnp.float32)
        + jnp.einsum("te,de->td", grad_value_low, w_value, preferred_element_type=jnp.float32)
    )
    expr_grad_local = jnp.dot(
        bin_hot.astype(jnp.float32).T, grad_embedded, precision=lax.Precision.HIGHEST
    )
    outgoing = jnp.zeros((devices * slots_all, width), jnp.float32)
    outgoing = outgoing.at[gene_slot].set(grad_embedded).at[know_slot].set(grad_embedded)
    outgoing = outgoing.reshape(devices, slots_all, width)
    returned = lax.all_to_all(
        outgoing.astype(jnp.bfloat16), ("dp", "seq"), split_axis=0, concat_axis=0, tiled=True
    ).astype(outgoing.dtype)
    owned = jnp.arange(2 * rows_dev)[:, None] == received.reshape(1, -1)
    table_grads = jnp.dot(
        owned.astype(jnp.float32),
        returned.reshape(devices * slots_all, width),
        precision=lax.Precision.HIGHEST,
    )
    row_counts = jnp.sum(owned.astype(jnp.int32), axis=1).reshape(2, rows_dev)
    whole_summed = lax.psum(
        (
            expr_grad_local,
            w_query_grad,
            b_query_grad,
            w_key_grad,
            w_value_grad,
            b_value_grad,
            w_out_grad,
            b_out_grad,
            gain_one_grad,
            shift_one_grad,
            w_down_grad,
            b_down_grad,
            gain_two_grad,
            shift_two_grad,
            w_up_grad,
            b_up_grad,
        ),
        ("dp", "seq"),
    )
    rest_summed = whole_summed[:10]
    ffn_summed = whole_summed[10:]
    return (
        layer_output,
        table_grads[:rows_dev],
        table_grads[rows_dev:],
        rest_summed[0],
        rest_summed[1],
        rest_summed[2],
        rest_summed[3],
        rest_summed[4],
        rest_summed[5],
        rest_summed[6],
        rest_summed[7],
        rest_summed[8],
        rest_summed[9],
        ffn_summed[4],
        ffn_summed[5],
        ffn_summed[0],
        ffn_summed[1],
        ffn_summed[2],
        ffn_summed[3],
        row_counts,
    )


def solution(mesh):
    placed = (
        P("dp", "seq"),
        P("dp", "seq"),
        P("dp", "seq"),
        P("dp", "seq"),
        P("dp"),
        P("dp"),
        P(("dp", "seq"), None),
        P(None, ("dp", "seq"), None),
        P(),
        P(),
        P(),
        P(),
        P(),
        P(),
        P(),
        P(),
        P(),
        P(),
        P(),
        P(),
        P(),
        P(),
        P(),
        P(),
        P("dp", "seq", None),
    )
    return jax.shard_map(
        local,
        mesh=mesh,
        in_specs=placed,
        out_specs=(
            P("dp", "seq", None),
            P(("dp", "seq"), None),
            P(("dp", "seq"), None),
            P(),
            P(),
            P(),
            P(),
            P(),
            P(),
            P(),
            P(),
            P(),
            P(),
            P(),
            P(),
            P(),
            P(),
            P(),
            P(),
            P(None, ("dp", "seq")),
        ),
        check_vma=False,
    )
```

profile of v0, /device:TPU:0, one launch (start us, length us, event | category | flops | bytes accessed | tf_op | source)
XLA Modules:
  0.0 1586.1 jit_solution(10476663562340610577)
XLA Ops:
  10.3 9.0 reduce-window.14
  19.3 9.0 reduce-window.16
  40.6 7.3 all-to-all-start
  55.1 17.7 %gather_fusion = bf16[4096,768]{1,0:T(8,128)(2,1)} fusion(bf16[576,768]{1,0:T(8,128)(2,1)S(1)} %pad_maximum_fusion, s32[4096]{0:T(1024)S(1)} %fusion.98), kind=kCustom, calls=%fused_computation | custom fusion | bytes 12599296 | tf_op jit(solution)/shard_map/jit(_take)/gather | solution.py:133
  83.1 140.1 %all-to-all-done.1 = bf16[32,128,768]{2,1,0:T(8,128)(2,1)} async-done(((bf16[32,128,768]{2,1,0:T(8,128)(2,1)}), bf16[32,128,768]{2,1,0:T(8,128)(2,1)}, u32[]{:S(2)}, u32[]{:S(2)}) %all-to-all-start.1) | async-done | bytes 6291488 | tf_op jit(solution)/shard_map/all_to_all | solution.py:134
  223.3 9.2 gather_fusion.2
  232.4 9.2 gather_fusion.1
  269.0 28.5 %all-gather.5.cloned.1.call-done = bf16[2048,768]{1,0:T(8,128)(2,1)} async-done(((bf16[1024,768]{1,0:T(8,128)(2,1)}), bf16[2048,768]{1,0:T(8,128)(2,1)}) %all-gather.5.cloned.1.call-update) | async-done | bytes 3145744 | tf_op jit(solution)/shard_map/all_gather | solution.py:157
  308.9 35.7 %all-gather.7.cloned.1.call-done = bf16[2048,768]{1,0:T(8,128)(2,1)} async-done(((bf16[1024,768]{1,0:T(8,128)(2,1)}), bf16[2048,768]{1,0:T(8,128)(2,1)}) %all-gather.7.cloned.1.call-update) | async-done | bytes 3145744 | tf_op jit(solution)/shard_map/all_gather | solution.py:158
  356.0 117.5 %while.48 = (s32[]{:T(128)}, bf16[12,1024,64]{1,2,0:T(8,128)(2,1)S(1)}, f32[12,1024]{1,0:T(8,128)}, bf16[12,1024,64]{2,1,0:T(8,128)(2,1)}, bf16[12,2048,64]{2,1,...) while((s32[]{:T(128)}, ...), condition=%wide.region_12.13_spmd.clone, body=%wide.region_9.12_spmd.clone.sunk | while | flops 559948800 | bytes 26810476 | solution.py:46
  478.6 48.7 %multiply_convert_fusion.1 = (bf16[1024,3072]{1,0:T(8,128)(2,1)S(1)}, f32[1024,3072]{1,0:T(8,128)}, f32[1024,3072]{1,0:T(8,128)}) fusion(f32[3072]{0:T(1024)S(1)} %copy-done.50, bf16[768,3072]{1,0:T(8,128)(2,1)S(1)} %bitcast.320, f32[1024,768]{0,1:T(8,128)S(1)} %get-tuple-element.424, f32[768]{0:T(1024)S(1)} %copy-done.55, f32[768]{0:T(1024)S(1)} %copy-done.43, ...), kind=kOutput, calls=%fused_computation.75 | convolution fusion | flops 5043388416 | bytes 39348224 | tf_op jit(solution)/shard_map/dot_general | solution.py:170
  540.0 19.4 %convert_reduce_fusion = (f32[3072]{0:T(1024)}, bf16[1024,3072]{1,0:T(8,128)(2,1)}) fusion(f32[1024,3072]{1,0:T(8,128)} %get-tuple-element.403, bf16[1024,768]{0,1:T(8,128)(2,1)} %get-tuple-element.397, bf16[3072,768]{1,0:T(8,128)(2,1)} %param.49, f32[1024,3072]{1,0:T(8,128)} %get-tuple-element.425, f32[3072]{0:T(1024)S(1)} %copy-done.50), kind=kOutput, calls=%fused_computation.73 | convolution fusion | flops 4885312512 | bytes 37773312 | tf_op jit(solution)/shard_map/td,fd->tf/dot_general | solution.py:183
  559.4 11.4 multiply_reduce_fusion.1
  577.2 225.5 %while.49 = (s32[]{:T(128)}, bf16[12,1024,64]{1,2,0:T(8,128)(2,1)S(1)}, f32[12,2048,64]{1,2,0:T(8,128)}, f32[12,2048,64]{1,2,0:T(8,128)}, bf16[12,1024,64]{2,1,0...) while((s32[]{:T(128)}, ...), condition=%wide.region_23.24_spmd.clone, body=%wide.region_21.23_spmd.clone.sunk | while | flops 1375732736 | bytes 66888828 | solution.py:67
  813.5 8.1 fusion.112
  821.6 7.7 fusion.125
  829.3 50.7 %reduce-scatter.3.cloned.1.call-done = f32[1,1024,768]{1,2,0:T(8,128)} async-done(((f32[1,2048,768]{1,2,0:T(8,128)}), f32[1,1024,768]{1,2,0:T(8,128)}) %reduce-scatter.3.cloned.1.call-update) | async-done | bytes 3145744 | tf_op jit(solution)/shard_map/reduce_scatter | solution.py:214
  884.9 74.4 %reduce-scatter.5.cloned.1.call-done = f32[1,1024,768]{1,2,0:T(8,128)} async-done(((f32[1,2048,768]{1,2,0:T(8,128)}), f32[1,1024,768]{1,2,0:T(8,128)}) %reduce-scatter.5.cloned.1.call-update) | async-done | bytes 3145744 | tf_op jit(solution)/shard_map/reduce_scatter | solution.py:215
  978.0 11.5 scatter_custom_fusion.2
  989.5 14.9 scatter_fusion.1
  1004.4 8.0 convert_element_type.161
  1024.2 220.7 %all-reduce = (f32[768]{0:T(1024)}, f32[768]{0:T(1024)}, f32[768]{0:T(1024)}, f32[768]{0:T(1024)}, f32[768]{0:T(1024)}, /*index=5*/f32[3072]{0:T(1024)}, f32[768]{0:T(1024)}, f32[768]{0:T(1024)}, f32[768]{0:T(1024)}) all-reduce(f32[768]{0:T(1024)S(1)} %reduce_sum.262, ...), channel_id=1, replica_groups=mesh['dp'=16,'seq'=2] {'dp','seq'}, use_global_device_ids=true, to_apply=%region_31.32 | all-reduce | flops 9216 | bytes 73728 | tf_op jit(solution)/shard_map/psum | solution.py:251
  1252.6 301.8 %all-reduce.4.cloned.1.call-done = (f32[128,768]{1,0:T(8,128)}, f32[768,768]{1,0:T(8,128)}, f32[768,768]{1,0:T(8,128)}, f32[768,768]{1,0:T(8,128)}, f32[768,768]...) async-done(((f32[128,768]{1,0:T(8,128)}, f32[768,768]{1,0:T(8,128)}, f32[768,768]{1,0:T(8,128)}, f32[768,768]{1,0:T(8,128)}, f32[768,768]{1,0:T(8,128)}, ...) | async-done | bytes 28704784 | tf_op jit(solution)/shard_map/psum | solution.py:251
  1566.0 9.3 copy.175
  (442 shorter events, 516.9 us)
Async XLA Ops:
  7.2 466.4 %copy-start = (bf16[768,768]{1,0:T(8,128)(2,1)S(1)}, bf16[768,768]{1,0:T(8,128)(2,1)}, u32[]{:S(2)}) copy-start(bf16[768,768]{1,0:T(8,128)(2,1)} %param.43) | copy-start | bytes 3538948
  29.5 53.6 %copy-start.30 = (s32[1024,1]{0,1:T(1,128)}, s32[1024,1]{0,1:T(1,128)S(1)}, u32[]{:S(2)}) copy-start(s32[1024,1]{0,1:T(1,128)S(1)} %compare_select_fusion.2) | copy-start | bytes 12292
  30.0 53.1 %copy-start.40 = (s32[1024,1]{0,1:T(1,128)}, s32[1024,1]{0,1:T(1,128)S(1)}, u32[]{:S(2)}) copy-start(s32[1024,1]{0,1:T(1,128)S(1)} %compare_select_fusion.3) | copy-start | bytes 12292
  34.9 14.9 copy-start.26
  40.6 14.4 all-to-all-start
  55.0 17.8 %copy-start.28 = (s32[32,1,128]{2,1,0:T(1,128)}, s32[32,1,128]{2,1,0:T(1,128)S(1)}, u32[]{:S(2)}) copy-start(s32[32,1,128]{2,1,0:T(1,128)S(1)} %all-to-all-done) | copy-start | bytes 49156
  79.4 143.9 %all-to-all-start.1 = ((bf16[32,128,768]{2,1,0:T(8,128)(2,1)}), bf16[32,128,768]{2,1,0:T(8,128)(2,1)}, u32[]{:S(2)}, u32[]{:S(2)}) async-start(bf16[32,128,768]{2,1,0:T(8,128)(2,1)} %broadcast_select_fusion), calls=%async_computation.1 | async-start | bytes 12582912 | tf_op jit(solution)/shard_map/all_to_all | solution.py:134
  83.0 214.4 %all-gather.5.cloned.1.call-start = ((), (), s32[]{:S(2)}) async-start(), calls=%async_computation.7 | async-start | bytes 4718592 | tf_op jit(solution)/shard_map/all_gather | solution.py:157
  253.5 91.0 %all-gather.7.cloned.1.call-start = ((), (), s32[]{:S(2)}) async-start(), calls=%async_computation.8 | async-start | bytes 4718592 | tf_op jit(solution)/shard_map/all_gather | solution.py:158
  257.6 622.4 %reduce-scatter.3.cloned.1.call-start = ((), (), s32[]{:S(2)}) async-start(), calls=%async_computation.5 | async-start | bytes 9437184 | tf_op jit(solution)/shard_map/reduce_scatter | solution.py:214
  356.0 117.6 %copy-start.53 = (f32[768]{0:T(1024)S(1)}, f32[768]{0:T(1024)}, u32[]{:S(2)}) copy-start(f32[768]{0:T(1024)} %param.44) | copy-start | bytes 9220
  473.6 53.7 %slice-start.3 = ((s8[4718592]{0:T(1024)(128)(4,1)}), s8[4194304]{0:T(1024)(128)(4,1)S(1)}, s32[]{:S(2)}) async-start(s8[4718592]{0:T(1024)(128)(4,1)} %bitcast.317), calls=%async_computation.13 | async-start | bytes 8388608
  477.7 49.6 %copy-start.7 = (f32[1024,768]{0,1:T(8,128)}, f32[1024,768]{0,1:T(8,128)S(1)}, u32[]{:S(2)}) copy-start(f32[1024,768]{0,1:T(8,128)S(1)} %get-tuple-element.424) | copy-start | bytes 9437188
  478.6 48.8 %slice-start.4 = ((s8[4718592]{0:T(1024)(128)(4,1)}), s8[524288]{0:T(1024)(128)(4,1)S(1)}, s32[]{:S(2)}) async-start(s8[4718592]{0:T(1024)(128)(4,1)} %bitcast.317), calls=%async_computation.14 | async-start | bytes 1048576
  478.6 48.8 %copy-start.54 = (f32[768]{0:T(1024)S(1)}, f32[768]{0:T(1024)}, u32[]{:S(2)}) copy-start(f32[768]{0:T(1024)} %param.50) | copy-start | bytes 9220
  559.4 11.4 copy-start.8
  802.8 156.6 %reduce-scatter.5.cloned.1.call-start = ((), (), s32[]{:S(2)}) async-start(), calls=%async_computation.6 | async-start | bytes 9437184 | tf_op jit(solution)/shard_map/reduce_scatter | solution.py:215
  803.4 751.0 %all-reduce.4.cloned.1.call-start = ((), (), s32[]{:S(2)}) async-start(), calls=%async_computation.9 | async-start | bytes 57409536 | tf_op jit(solution)/shard_map/psum | solution.py:251
  821.6 58.4 %copy-start.49 = (bf16[768,768]{1,0:T(8,128)(2,1)S(1)}, bf16[768,768]{1,0:T(8,128)(2,1)}, u32[]{:S(2)}) copy-start(bf16[768,768]{1,0:T(8,128)(2,1)} %param.40) | copy-start | bytes 3538948
  829.3 130.1 %copy-start.25 = (bf16[768,768]{1,0:T(8,128)(2,1)S(1)}, bf16[768,768]{1,0:T(8,128)(2,1)}, u32[]{:S(2)}) copy-start(bf16[768,768]{1,0:T(8,128)(2,1)} %param.41) | copy-start | bytes 3538948
  829.3 130.1 %copy-start.34 = (f32[1024]{0:T(1024)S(1)}, f32[1024]{0:T(1024)}, u32[]{:S(2)}) copy-start(f32[1024]{0:T(1024)} %copy-done.33) | copy-start | bytes 12292
  884.9 80.7 %copy-start.36 = (s32[1,1024]{1,0:T(1,128)S(1)}, s32[1,1024]{1,0:T(1,128)}, u32[]{:S(2)}) copy-start(s32[1,1024]{1,0:T(1,128)} %param.32) | copy-start | bytes 12292
  978.0 11.5 copy-start.31
  1012.5 232.4 %all-to-all-start.2 = ((bf16[32,128,768]{2,1,0:T(8,128)(2,1)}), bf16[32,128,768]{2,1,0:T(8,128)(2,1)}, u32[]{:S(2)}, u32[]{:S(2)}) async-start(bf16[32,128,768]{2,1,0:T(8,128)(2,1)} %bitcast.274), calls=%async_computation.4 | async-start | bytes 12582912 | tf_op jit(solution)/shard_map/all_to_all | solution.py:241
  (53 other events, 229.0 us)
Sparse Core Ops, SparseCore 0:
  253.7 43.7 all-gather.4
  299.6 44.9 all-gather.6
  802.9 77.0 reduce-scatter.2
  882.2 77.0 reduce-scatter.4
  974.6 579.7 all-reduce.3
where the time goes:
time: 1600 us; the launch traced here: 1590 us
  waiting for transfers between devices  637 us (40%)
  matrix products  397 us (25%)
  blocking collectives  221 us (14%)
  local copies, waits for them, and re-layouts  173 us (11%)
  other arithmetic  126 us (8%)
    psum x1, waiting for transfers between devices, local(): lax.psum((expr_grad_local, w_query_grad, b_query_grad, w_key_grad, w_valu...  302 us
    psum x1, blocking collectives, local(): lax.psum((expr_grad_local, w_query_grad, b_query_grad, w_key_grad, w_valu...  221 us
    all_to_all x1, waiting for transfers between devices, local(): lax.all_to_all(found, ('dp', 'seq'), split_axis=0, concat_axis=0, tiled=T...  140 us
    reduce_scatter x1, waiting for transfers between devices, local(): lax.psum_scatter(grad_v_whole, 'seq', scatter_dimension=1, tiled=True)  74.4 us
    dot_general x24, matrix products, head_scores(): jnp.dot(query_head, key_head.T, preferred_element_type=jnp.float32)  59.4 us
    reduce_scatter x1, waiting for transfers between devices, local(): lax.psum_scatter(grad_k_whole, 'seq', scatter_dimension=1, tiled=True)  50.7 us
    dot_general x1, matrix products, local(): jnp.dot(normed_low, w_up, preferred_element_type=jnp.float32) + b_up  48.7 us
    unnamed x149, local copies, waits for them, and re-layouts  47.2 us
  transfers between devices with their start and end apart: 8, of which 7 were waited for; matrix products, arithmetic and copies ran while one was open for 7% of the time, Pallas kernels for 0%

commit v1 on v0

v1 whole, which is shorter than its diff:
```python
import functools

import jax
import jax.numpy as jnp
from jax import lax
from jax.experimental import pallas as pl
from jax.experimental.pallas import tpu as pltpu
from jax.sharding import PartitionSpec as P

HEADS = 12
HEAD_DIM = 64
PAIR = 2 * HEAD_DIM
CHUNK = 256
EVERY = ("dp", "seq")
F32 = jnp.float32
BF16 = jnp.bfloat16
NN = (((1,), (0,)), ((), ()))
NT = (((1,), (1,)), ((), ()))
TN = (((0,), (0,)), ((), ()))


def mm(left, right, dims=NN):
    return lax.dot_general(left, right, dims, preferred_element_type=F32)


def params(mib):
    return pltpu.CompilerParams(vmem_limit_bytes=mib * 2**20)


def route_kernel(rows_dev, capacity, gene_ref, know_ref, req_ref, gene_slot_ref, know_slot_ref):
    tokens = gene_ref.shape[0]
    devices, slots_all = req_ref.shape
    lane = lax.broadcasted_iota(jnp.int32, (tokens, devices), 1)
    earlier = (
        lax.broadcasted_iota(jnp.int32, (tokens, tokens), 0)
        > lax.broadcasted_iota(jnp.int32, (tokens, tokens), 1)
    ).astype(F32).astype(BF16)
    rank_lane = lax.broadcasted_iota(jnp.int32, (tokens, capacity), 1)
    asked = []
    for which, (ids_ref, slot_ref) in enumerate(((gene_ref, gene_slot_ref), (know_ref, know_slot_ref))):
        row = ids_ref[...] - lane * rows_dev
        hit = (row >= 0) & (row < rows_dev)
        before = mm(earlier, hit.astype(F32).astype(BF16))
        rank = jnp.sum(jnp.where(hit, before, 0.0), axis=1, keepdims=True)
        owner = jnp.sum(jnp.where(hit, lane, 0).astype(F32), axis=1, keepdims=True)
        slot_ref[...] = (owner * slots_all + rank).astype(jnp.int32) + which * capacity
        rank_hit = (rank_lane == rank.astype(jnp.int32)).astype(F32).astype(BF16)
        coded = jnp.where(hit, row + 1, 0)
        high = (coded >> 4).astype(F32).astype(BF16)
        low = (coded & 15).astype(F32).astype(BF16)
        wanted = (mm(high, rank_hit, TN) * 16.0 + mm(low, rank_hit, TN)).astype(jnp.int32)
        asked.append(jnp.where(wanted > 0, wanted - 1 + which * rows_dev, -1))
    req_ref[:, :capacity] = asked[0]
    req_ref[:, capacity:] = asked[1]


def route(gene_ids, know_ids, rows_dev, capacity, devices):
    tokens = gene_ids.shape[0]
    return pl.pallas_call(
        functools.partial(route_kernel, rows_dev, capacity),
        out_shape=(
            jax.ShapeDtypeStruct((devices, 2 * capacity), jnp.int32),
            jax.ShapeDtypeStruct((tokens, 1), jnp.int32),
            jax.ShapeDtypeStruct((tokens, 1), jnp.int32),
        ),
        compiler_params=params(32),
        name="route",
    )(gene_ids[:, None], know_ids[:, None])


def head_mask(rows, head):
    lanes = lax.broadcasted_iota(jnp.int32, (rows, PAIR), 1)
    return (lanes >= head * HEAD_DIM) & (lanes < (head + 1) * HEAD_DIM)


def masked_scores(scores, first_key, count):
    at = lax.broadcasted_iota(jnp.int32, scores.shape, 0) + first_key
    return jnp.where(at < count, scores, -1e30)


def fold_rows(value, how):
    return how(value.reshape(value.shape[0] // 8, 8, value.shape[1]), axis=0)


def attend_kernel(
    where_ref, q_ref, ka_ref, kb_ref, va_ref, vb_ref, out_ref, lse_ref, vt_ref, score_ref
):
    half = ka_ref.shape[0]
    chunks = half // CHUNK
    vt_ref[:, :half] = va_ref[...].T
    vt_ref[:, half:] = vb_ref[...].T

    def block(at, carry):
        rows = pl.ds(pl.multiple_of(at * CHUNK, CHUNK), CHUNK)
        query = q_ref[rows, :]
        outs = []
        for head in range(2):
            q_head = jnp.where(head_mask(CHUNK, head), query, jnp.zeros_like(query))
            top = None
            for c in range(2 * chunks):
                part, inner = divmod(c, chunks)
                key = (ka_ref, kb_ref)[part][inner * CHUNK : (inner + 1) * CHUNK, :]
                scores = masked_scores(
                    mm(key, q_head, NT), where_ref[part] + inner * CHUNK, where_ref[2]
                )
                score_ref[head, c * CHUNK : (c + 1) * CHUNK, :] = scores
                high = fold_rows(scores, jnp.max)
                top = high if top is None else jnp.maximum(top, high)
            top = jnp.max(top, axis=0, keepdims=True)
            total = None
            acc = None
            for c in range(2 * chunks):
                probs = jnp.exp(score_ref[head, c * CHUNK : (c + 1) * CHUNK, :] - top)
                part_sum = fold_rows(probs, jnp.sum)
                total = part_sum if total is None else total + part_sum
                part_out = mm(
                    vt_ref[head * HEAD_DIM : (head + 1) * HEAD_DIM, c * CHUNK : (c + 1) * CHUNK],
                    probs.astype(BF16),
                )
                acc = part_out if acc is None else acc + part_out
            total = jnp.sum(total, axis=0, keepdims=True)
            outs.append(acc / total)
            lse_ref[0, head : head + 1, rows] = top + jnp.log(total)
        out_ref[rows, :] = jnp.concatenate(outs, axis=0).T
        return carry

    lax.fori_loop(0, q_ref.shape[0] // CHUNK, block, 0)


def attend(where, query, key_a, key_b, value_a, value_b):
    tokens, width = query.shape
    half = key_a.shape[0]
    pairs = width // PAIR
    column = lambda rows: pl.BlockSpec((rows, PAIR), lambda p, w: (0, p))
    return pl.pallas_call(
        attend_kernel,
        grid_spec=pltpu.PrefetchScalarGridSpec(
            num_scalar_prefetch=1,
            grid=(pairs,),
            in_specs=[column(tokens)] + [column(half)] * 4,
            out_specs=[column(tokens), pl.BlockSpec((1, 2, tokens), lambda p, w: (p, 0, 0))],
            scratch_shapes=[
                pltpu.VMEM((PAIR, 2 * half), BF16),
                pltpu.VMEM((2, 2 * half, CHUNK), F32),
            ],
        ),
        out_shape=(
            jax.ShapeDtypeStruct((tokens, width), F32),
            jax.ShapeDtypeStruct((pairs, 2, tokens), F32),
        ),
        compiler_params=params(48),
        name="attend",
    )(where, query, key_a, key_b, value_a, value_b)


def attend_back_kernel(
    where_ref, q_ref, g_ref, o_ref, lse_ref, k_ref, v_ref, *rest
):
    if len(rest) == 7:
        dq_in_ref, dq_ref, dk_ref, dv_ref, kt_ref, dk_acc, dv_acc = rest
    else:
        dq_in_ref = None
        dq_ref, dk_ref, dv_ref, kt_ref, dk_acc, dv_acc = rest
    keys = k_ref.shape[0]
    kt_ref[...] = k_ref[...].T
    dk_acc[...] = jnp.zeros_like(dk_acc)
    dv_acc[...] = jnp.zeros_like(dv_acc)
    picks = (
        lax.broadcasted_iota(jnp.int32, (8, PAIR), 1) // HEAD_DIM
        == lax.broadcasted_iota(jnp.int32, (8, PAIR), 0)
    ).astype(F32)

    def block(at, carry):
        rows = pl.ds(pl.multiple_of(at * CHUNK, CHUNK), CHUNK)
        query = q_ref[rows, :]
        grad = g_ref[rows, :]
        inner = lax.dot_general(
            picks,
            grad.astype(F32) * o_ref[rows, :],
            NT,
            precision=lax.Precision.HIGHEST,
            preferred_element_type=F32,
        )
        masks = [head_mask(CHUNK, head) for head in range(2)]
        q_heads = [jnp.where(m, query, jnp.zeros_like(query)) for m in masks]
        g_heads = [jnp.where(m, grad, jnp.zeros_like(grad)) for m in masks]
        dqs = [None, None]
        for c in range(keys // CHUNK):
            span = slice(c * CHUNK, (c + 1) * CHUNK)
            key = k_ref[span, :]
            value = v_ref[span, :]
            dk = None
            dv = None
            for head in range(2):
                scores = masked_scores(
                    mm(key, q_heads[head], NT), where_ref[0] + c * CHUNK, where_ref[1]
                )
                probs = jnp.exp(scores - lse_ref[0, head : head + 1, rows])
                grad_probs = mm(value, g_heads[head], NT)
                grad_scores = (probs * (grad_probs - inner[head : head + 1, :])).astype(BF16)
                dv_head = mm(probs.astype(BF16), g_heads[head])
                dk_head = mm(grad_scores, q_heads[head])
                dv = dv_head if dv is None else dv + dv_head
                dk = dk_head if dk is None else dk + dk_head
                dq = mm(kt_ref[head * HEAD_DIM : (head + 1) * HEAD_DIM, span], grad_scores)
                dqs[head] = dq if dqs[head] is None else dqs[head] + dq
            dk_acc[span, :] += dk
            dv_acc[span, :] += dv
        dq = jnp.concatenate(dqs, axis=0).T * HEAD_DIM ** (-0.5)
        if dq_in_ref is not None:
            dq = dq + dq_in_ref[rows, :]
        dq_ref[rows, :] = dq.astype(dq_ref.dtype)
        return carry

    lax.fori_loop(0, q_ref.shape[0] // CHUNK, block, 0)
    dk_ref[...] = dk_acc[...].astype(BF16)
    dv_ref[...] = dv_acc[...].astype(BF16)


def attend_back(where, query, grad, out, lse, key, value, dq_in=None):
    tokens, width = query.shape
    keys = key.shape[0]
    pairs = width // PAIR
    column = lambda rows: pl.BlockSpec((rows, PAIR), lambda p, w: (0, p))
    more = [] if dq_in is None else [dq_in]
    return pl.pallas_call(
        attend_back_kernel,
        grid_spec=pltpu.PrefetchScalarGridSpec(
            num_scalar_prefetch=1,
            grid=(pairs,),
            in_specs=[column(tokens)] * 3
            + [pl.BlockSpec((1, 2, tokens), lambda p, w: (p, 0, 0))]
            + [column(keys)] * 2
            + [column(tokens)] * len(more),
            out_specs=[column(tokens), column(keys), column(keys)],
            scratch_shapes=[
                pltpu.VMEM((PAIR, keys), BF16),
                pltpu.VMEM((keys, PAIR), F32),
                pltpu.VMEM((keys, PAIR), F32),
            ],
        ),
        out_shape=(
            jax.ShapeDtypeStruct((tokens, width), F32 if dq_in is None else BF16),
            jax.ShapeDtypeStruct((keys, width), BF16),
            jax.ShapeDtypeStruct((keys, width), BF16),
        ),
        compiler_params=params(48),
        name="attend_back" if dq_in is None else "attend_back_last",
    )(where, query, grad, out, lse, key, value, *more)


def norm_parts(value):
    centre = jnp.mean(value, axis=-1, keepdims=True)
    centred = value - centre
    variance = jnp.mean(centred * centred, axis=-1, keepdims=True)
    inverse = lax.rsqrt(variance + 1e-05)
    return centred * inverse, inverse


def norm_back(grad, unit, inverse, gain):
    grad_unit = grad * gain
    return inverse * (
        grad_unit
        - jnp.mean(grad_unit, axis=-1, keepdims=True)
        - unit * jnp.mean(grad_unit * unit, axis=-1, keepdims=True)
    )


def middle_kernel(
    ctx_ref,
    emb_ref,
    cot_ref,
    w_out_ref,
    w_up_ref,
    w_down_ref,
    small_ref,
    b_up_ref,
    out_ref,
    ctx_low_ref,
    normed_ref,
    act_ref,
    gffn_ref,
    gpre_ref,
    gattn_ref,
    gone_ref,
    gctx_ref,
    sums_ref,
    up_sums_ref,
    slope_ref,
):
    step = pl.program_id(0)
    width = emb_ref.shape[1]
    wide = w_up_ref.shape[1]

    @pl.when(step == 0)
    def _():
        sums_ref[...] = jnp.zeros_like(sums_ref)
        up_sums_ref[...] = jnp.zeros_like(up_sums_ref)

    b_out, gain_one, shift_one, b_down, gain_two, shift_two = (
        small_ref[i : i + 1, :] for i in range(6)
    )
    ctx_low = ctx_ref[...].astype(BF16)
    ctx_low_ref[...] = ctx_low
    unit_one, inv_one = norm_parts(emb_ref[...] + mm(ctx_low, w_out_ref[...]) + b_out)
    normed = unit_one * gain_one + shift_one
    normed_low = normed.astype(BF16)
    normed_ref[...] = normed_low
    ffn = None
    for c in range(wide // width):
        span = slice(c * width, (c + 1) * width)
        pre = mm(normed_low, w_up_ref[:, span]) + b_up_ref[:, span]
        below = 0.5 * (1.0 + lax.erf(pre * 0.7071067811865476))
        act = (pre * below).astype(BF16)
        act_ref[:, span] = act
        slope_ref[:, span] = below + pre * (0.3989422804014327 * jnp.exp(-0.5 * pre * pre))
        part = mm(act, w_down_ref[span, :])
        ffn = part if ffn is None else ffn + part
    unit_two, inv_two = norm_parts(normed + ffn + b_down)
    out_ref[...] = (unit_two * gain_two + shift_two).astype(BF16)
    grad = cot_ref[...].astype(F32)
    sums_ref[0:8, :] += fold_rows(grad * unit_two, jnp.sum)
    sums_ref[8:16, :] += fold_rows(grad, jnp.sum)
    grad_two = norm_back(grad, unit_two, inv_two, gain_two)
    gffn = grad_two.astype(BF16)
    gffn_ref[...] = gffn
    sums_ref[16:24, :] += fold_rows(gffn.astype(F32), jnp.sum)
    grad_normed = grad_two
    for c in range(wide // width):
        span = slice(c * width, (c + 1) * width)
        gpre = (mm(gffn, w_down_ref[span, :], NT) * slope_ref[:, span]).astype(BF16)
        gpre_ref[:, span] = gpre
        up_sums_ref[:, span] += fold_rows(gpre.astype(F32), jnp.sum)
        grad_normed = grad_normed + mm(gpre, w_up_ref[:, span], NT)
    sums_ref[24:32, :] += fold_rows(grad_normed * unit_one, jnp.sum)
    sums_ref[32:40, :] += fold_rows(grad_normed, jnp.sum)
    grad_one = norm_back(grad_normed, unit_one, inv_one, gain_one)
    gone_ref[...] = grad_one
    gattn = grad_one.astype(BF16)
    gattn_ref[...] = gattn
    sums_ref[40:48, :] += fold_rows(gattn.astype(F32), jnp.sum)
    gctx_ref[...] = mm(gattn, w_out_ref[...], NT).astype(BF16)


def middle(ctx, embedded, cotangent, w_out, w_up, w_down, small, b_up, block=256):
    tokens, width = embedded.shape
    wide = w_up.shape[1]
    whole = lambda a: pl.BlockSpec(a.shape, lambda i: (0, 0), pipeline_mode=pl.Buffered(1))
    rows = lambda n: pl.BlockSpec((block, n), lambda i: (i, 0))
    fixed = lambda r, n: pl.BlockSpec((r, n), lambda i: (0, 0))
    shape = lambda n, dtype: jax.ShapeDtypeStruct((tokens, n), dtype)
    return pl.pallas_call(
        middle_kernel,
        grid=(tokens // block,),
        in_specs=[rows(width)] * 3 + [whole(w_out), whole(w_up), whole(w_down), whole(small), whole(b_up)],
        out_specs=[
            rows(width),
            rows(width),
            rows(width),
            rows(wide),
            rows(width),
            rows(wide),
            rows(width),
            rows(width),
            rows(width),
            fixed(48, width),
            fixed(8, wide),
        ],
        out_shape=[
            shape(width, BF16),
            shape(width, BF16),
            shape(width, BF16),
            shape(wide, BF16),
            shape(width, BF16),
            shape(wide, BF16),
            shape(width, BF16),
            shape(width, F32),
            shape(width, BF16),
            jax.ShapeDtypeStruct((48, width), F32),
            jax.ShapeDtypeStruct((8, wide), F32),
        ],
        scratch_shapes=[pltpu.VMEM((block, wide), F32)],
        compiler_params=params(60),
        name="middle",
    )(ctx, embedded, cotangent, w_out, w_up, w_down, small, b_up)


def local(
    gene_ids,
    homolog_ids,
    knowledge_ids,
    expr_bins,
    species,
    cell_lengths,
    gene_table,
    knowledge_tables,
    expr_table,
    w_query,
    b_query,
    w_key,
    w_value,
    b_value,
    w_out,
    b_out,
    gain_one,
    shift_one,
    w_up,
    b_up,
    w_down,
    b_down,
    gain_two,
    shift_two,
    cotangent,
):
    tokens = gene_ids.shape[1]
    rows_dev, width = gene_table.shape
    devices = lax.axis_size(EVERY)
    capacity = 2 * tokens // devices
    slots_all = 2 * capacity
    slots = devices * slots_all
    bins = expr_table.shape[0]
    me = lax.axis_index("seq")

    chosen = jnp.where(species[0] == 1, homolog_ids, gene_ids).reshape(-1)
    requests, gene_slot, know_slot = route(
        chosen, knowledge_ids.reshape(-1), rows_dev, capacity, devices
    )
    received = lax.all_to_all(requests, EVERY, split_axis=0, concat_axis=0, tiled=True)
    know_sum = jnp.sum(knowledge_tables.astype(F32), axis=0).astype(BF16)
    combined = jnp.concatenate([gene_table, know_sum], axis=0)
    asked = received.reshape(-1)
    asked_hot = (asked[:, None] == jnp.arange(2 * rows_dev)[None, :]).astype(BF16)
    found = mm(asked_hot, combined).astype(BF16).reshape(devices, slots_all, width)
    fetched = lax.all_to_all(found, EVERY, split_axis=0, concat_axis=0, tiled=True)
    slot_at = jnp.arange(slots)[None, :]
    slot_hot = ((slot_at == gene_slot) | (slot_at == know_slot)).astype(BF16)
    bin_hot = (expr_bins.reshape(-1)[:, None] == jnp.arange(bins)[None, :]).astype(BF16)
    embedded = mm(slot_hot, fetched.reshape(slots, width)) + mm(bin_hot, expr_table)
    x_low = embedded.astype(BF16)

    x_other = lax.ppermute(x_low, "seq", [(0, 1), (1, 0)])
    query = ((mm(x_low, w_query) + b_query).astype(BF16) * HEAD_DIM ** (-0.5)).astype(BF16)
    key, key_other = (mm(x, w_key).astype(BF16) for x in (x_low, x_other))
    value, value_other = ((mm(x, w_value) + b_value).astype(BF16) for x in (x_low, x_other))
    where = jnp.stack([me * tokens, (1 - me) * tokens, cell_lengths[0]]).astype(jnp.int32)
    context, lse = attend(where, query, key, key_other, value, value_other)

    small = jnp.stack([b_out, gain_one, shift_one, b_down, gain_two, shift_two])
    (
        layer_output,
        ctx_low,
        normed_low,
        activated,
        grad_ffn,
        grad_pre,
        grad_attn,
        grad_one,
        grad_ctx,
        sums,
        up_sums,
    ) = middle(
        context, embedded, cotangent.reshape(tokens, width), w_out, w_up, w_down, small, b_up[None, :]
    )
    w_down_grad = mm(activated, grad_ffn, TN)
    w_up_grad = mm(normed_low, grad_pre, TN)
    w_out_grad = mm(ctx_low, grad_attn, TN)
    early = lax.psum(
        (
            w_down_grad.astype(BF16),
            w_up_grad.astype(BF16),
            w_out_grad.astype(BF16),
        ),
        EVERY,
    )
    w_down_grad, w_up_grad, w_out_grad = (g.astype(F32) for g in early)

    dq_part, dk_other, dv_other = attend_back(
        where[1:], query, grad_ctx, context, lse, key_other, value_other
    )
    dx_other = (mm(dk_other, w_key, NT) + mm(dv_other, w_value, NT)).astype(BF16)
    dx_from_other = lax.ppermute(dx_other, "seq", [(0, 1), (1, 0)])
    dq, dk, dv = attend_back(
        where[0::2], query, grad_ctx, context, lse, key, value, dq_part
    )
    grad_embedded = (
        grad_one
        + mm(dq, w_query, NT)
        + mm(dk, w_key, NT)
        + mm(dv, w_value, NT)
        + dx_from_other.astype(F32)
    )
    w_query_grad = mm(x_low, dq, TN)
    w_key_grad = mm(x_low, dk, TN) + mm(x_other, dk_other, TN)
    w_value_grad = mm(x_low, dv, TN) + mm(x_other, dv_other, TN)
    b_query_grad = jnp.sum(dq.astype(F32), axis=0)
    b_value_grad = jnp.sum(dv.astype(F32), axis=0) + jnp.sum(dv_other.astype(F32), axis=0)

    grad_low = grad_embedded.astype(BF16)
    grad_rest = (grad_embedded - grad_low.astype(F32)).astype(BF16)
    expr_grad = mm(bin_hot, grad_low, TN) + mm(bin_hot, grad_rest, TN)
    outgoing = mm(slot_hot, grad_low, TN).astype(BF16).reshape(devices, slots_all, width)
    returned = lax.all_to_all(outgoing, EVERY, split_axis=0, concat_axis=0, tiled=True)
    owned = jnp.arange(2 * rows_dev)[:, None] == asked[None, :]
    table_grads = mm(owned.astype(BF16), returned.reshape(slots, width))
    row_counts = jnp.sum(owned.astype(jnp.int32), axis=1).reshape(2, rows_dev)

    late = lax.psum(
        (
            expr_grad,
            w_query_grad,
            w_key_grad,
            w_value_grad,
            b_query_grad,
            b_value_grad,
            jnp.sum(sums.reshape(6, 8, width), axis=1),
            jnp.sum(up_sums, axis=0),
        ),
        EVERY,
    )
    expr_grad, w_query_grad, w_key_grad, w_value_grad, b_query_grad, b_value_grad, sums, b_up_grad = late
    gain_two_grad, shift_two_grad, b_down_grad, gain_one_grad, shift_one_grad, b_out_grad = (
        sums[i] for i in range(6)
    )
    return (
        layer_output.reshape(1, tokens, width),
        table_grads[:rows_dev],
        table_grads[rows_dev:],
        expr_grad,
        w_query_grad,
        b_query_grad,
        w_key_grad,
        w_value_grad,
        b_value_grad,
        w_out_grad,
        b_out_grad,
        gain_one_grad,
        shift_one_grad,
        w_up_grad,
        b_up_grad,
        w_down_grad,
        b_down_grad,
        gain_two_grad,
        shift_two_grad,
        row_counts,
    )


def solution(mesh):
    whole = P()
    placed = (
        (P("dp", "seq"),) * 4
        + (P("dp"),) * 2
        + (P(EVERY, None), P(None, EVERY, None))
        + (whole,) * 16
        + (P("dp", "seq", None),)
    )
    given = (
        (P("dp", "seq", None),)
        + (P(EVERY, None),) * 2
        + (whole,) * 16
        + (P(None, EVERY),)
    )
    return jax.shard_map(local, mesh=mesh, in_specs=placed, out_specs=given, check_vma=False)
```

time: 1600 us -> 1020 us (0.64)
  matrix products: 397 us -> 110 us
  Pallas kernels: 0 us -> 222 us
  waiting for transfers between devices: 637 us -> 445 us
  local copies, waits for them, and re-layouts: 173 us -> 15.9 us
  other arithmetic: 126 us -> 23.3 us
  blocking collectives: 221 us -> 162 us
    dot_general x105 -> x25, matrix products: 397 us -> 110 us  [mm(): return lax.dot_general(left, right, dims, preferred_element_type=F32)]
    pallas_call x0 -> x5, Pallas kernels: none -> 222 us  [the longest x2 122 us: attend_back(): pl.pallas_call(attend_back_kernel, grid_spec=pltpu.PrefetchScalarGridSpec...]
    reduce_scatter x2 -> x0, waiting for transfers between devices: 125 us -> none  [the longest x1 74.4 us: local(): lax.psum_scatter(grad_v_whole, 'seq', scatter_dimension=1, tiled=True)]
    all_gather x2 -> x0, waiting for transfers between devices: 64.2 us -> none  [the longest x1 35.7 us: local(): lax.all_gather(value_cells, 'seq', axis=1, tiled=True)]
    psum x1, blocking collectives: 221 us -> 162 us  [local(): lax.psum((expr_grad, w_query_grad, w_key_grad, w_value_grad, b_query_grad...]
    gather x5 -> x0, local copies, waits for them, and re-layouts: 40.4 us -> none  [the longest x1 17.7 us: local(): found = jnp.take(combined, jnp.clip(received, 0, 2 * rows_dev - 1), axis=0)]
    scatter x4 -> x0, local copies, waits for them, and re-layouts: 37 us -> none  [the longest x2 26.4 us: local(): outgoing.at[gene_slot].set(grad_embedded).at[know_slot].set(grad_embedded)]
    unnamed x149 -> x86, local copies, waits for them, and re-layouts: 47.2 us -> 11.4 us
  transfers between devices with their start and end apart: 8 -> 7, of which waited for: 7 -> 5; matrix products, arithmetic and copies ran while one was open for 7% -> 9% of each run, Pallas kernels for 0% -> 6%
where the time goes in v1:
time: 1020 us; the launch traced here: 1010 us
  waiting for transfers between devices  445 us (44%)
  Pallas kernels  222 us (22%)
  blocking collectives  162 us (16%)
  matrix products  110 us (11%)
  other arithmetic  23.3 us (2%)
  between operations  16.5 us (2%)
  local copies, waits for them, and re-layouts  15.9 us (2%)
  starting transfers between devices  15.8 us (2%)
    psum x1, blocking collectives, local(): lax.psum((expr_grad, w_query_grad, w_key_grad, w_value_grad, b_query_grad...  162 us
    psum x1, waiting for transfers between devices, local(): lax.psum((expr_grad, w_query_grad, w_key_grad, w_value_grad, b_query_grad...  154 us
    all_to_all x1, waiting for transfers between devices, local(): lax.all_to_all(found, EVERY, split_axis=0, concat_axis=0, tiled=True)  140 us
    psum x1, waiting for transfers between devices, local(): lax.psum((w_down_grad.astype(BF16), w_up_grad.astype(BF16), w_out_grad.as...  123 us
    pallas_call x2, Pallas kernels, attend_back(): pl.pallas_call(attend_back_kernel, grid_spec=pltpu.PrefetchScalarGridSpec...  122 us
    dot_general x25, matrix products, mm(): return lax.dot_general(left, right, dims, preferred_element_type=F32)  110 us
    pallas_call x1, Pallas kernels, attend(): pl.pallas_call(attend_kernel, grid_spec=pltpu.PrefetchScalarGridSpec(num_...  59 us
    pallas_call x1, Pallas kernels, middle(): pl.pallas_call(middle_kernel, grid=(tokens // block,), in_specs=[rows(wid...  37.1 us
  transfers between devices with their start and end apart: 7, of which 5 were waited for; matrix products, arithmetic and copies ran while one was open for 9% of the time, Pallas kernels for 6%

profile of v1, /device:TPU:0, one launch (start us, length us, event | category | flops | bytes accessed | tf_op | source)
XLA Modules:
  0.0 1010.6 jit_solution(16074750729443885733)
XLA Ops:
  13.6 7.3 all-to-all-start
  22.8 5.2 all-to-all-done
  28.0 7.4 fusion.11
  39.6 139.6 %all-to-all-done.1 = bf16[32,128,768]{2,1,0:T(8,128)(2,1)} async-done(((bf16[32,128,768]{2,1,0:T(8,128)(2,1)}), bf16[32,128,768]{2,1,0:T(8,128)(2,1)}, u32[]{:S(2)}, u32[]{:S(2)}) %all-to-all-start.1) | async-done | bytes 6291488 | tf_op jit(solution)/shard_map/all_to_all | solution.py:434
  179.2 11.3 %fusion.3 = f32[1024,768]{1,0:T(8,128)S(1)} fusion(bf16[4096,768]{1,0:T(8,128)(2,1)} %bitcast.9, s32[1024]{0:T(1024)S(1)} %reduce.2, s32[1024]{0:T(1024)S(1)} %reduce.1), kind=kOutput, calls=%fused_computation.4 | convolution fusion | flops 6455033856 | bytes 9445376 | tf_op jit(solution)/shard_map/dot_general | solution.py:23
  201.8 4.5 add_convert_fusion.2.va_ref.v_ref
  206.3 23.3 %collective-permute-done = bf16[1024,768]{1,0:T(8,128)(2,1)} collective-permute-done((bf16[1024,768]{1,0:T(8,128)(2,1)}, bf16[1024,768]{1,0:T(8,128)(2,1)}, u32[]{:S(2)}, u32[]{:S(2)}) %collective-permute-start) | collective-permute-done | bytes 1572896 | tf_op jit(solution)/shard_map/ppermute | solution.py:441
  236.4 59.0 %attend.1 = (f32[1024,768]{1,0:T(8,128)}, f32[6,2,1024]{2,1,0:T(2,128)S(1)}) custom-call(s32[3]{0:T(128)S(1)} %pad_add_fusion.where_ref, bf16[1024,768]{1,0:T(8,128)(2,1)S(1)} %fusion.18.q_ref, bf16[1024,768]{1,0:T(8,128)(2,1)S(1)} %convolution_convert_fusion.3.ka_ref.k_ref, bf16[1024,768]{1,0:T(8,128)(2,1)S(1)} %convolution_convert_fusion.2.kb_ref.k_ref, ...), custom_call_target="tpu_custom_call" | custom-call | tf_op jit(solution)/shard_map/attend/pallas_call | solution.py:135
  295.4 37.1 %middle.1 = (bf16[1024,768]{1,0:T(8,128)(2,1)}, bf16[1024,768]{1,0:T(8,128)(2,1)}, bf16[1024,768]{1,0:T(8,128)(2,1)}, bf16[1024,3072]{1,0:T(8,128)(2,1)}, bf16[1...) custom-call(f32[1024,768]{1,0:T(8,128)} %get-tuple-element.45.ctx_re, ...), custom_call_target="tpu_custom_call" | custom-call | tf_op jit(solution)/shard_map/middle/pallas_call | solution.py:352
  332.5 61.3 %attend_back.1 = (f32[1024,768]{1,0:T(8,128)}, bf16[1024,768]{1,0:T(8,128)(2,1)S(1)}, bf16[1024,768]{1,0:T(8,128)(2,1)S(1)}) custom-call(s32[2]{0:T(128)S(1)} %pad_add_fusion.1.where_ref, bf16[1024,768]{1,0:T(8,128)(2,1)S(1)} %fusion.18.q_ref, bf16[1024,768]{1,0:T(8,128)(2,1)} %get-tuple-element.48.g_ref, f32[1024,768]{1,0:T(8,128)} %get-tuple-element.45.ctx_ref.o_ref, ...), custom_call_target="tpu_custom_call" | custom-call | tf_op jit(solution)/shard_map/attend_back/pallas_call | solution.py:226
  398.8 61.2 %attend_back_last.1 = (bf16[1024,768]{1,0:T(8,128)(2,1)S(1)}, bf16[1024,768]{1,0:T(8,128)(2,1)S(1)}, bf16[1024,768]{1,0:T(8,128)(2,1)S(1)}) custom-call(s32[2]{0:T(128)S(1)} %slice.29.where_ref, bf16[1024,768]{1,0:T(8,128)(2,1)} %copy-done.2, bf16[1024,768]{1,0:T(8,128)(2,1)} %get-tuple-element.48.g_ref, f32[1024,768]{1,0:T(8,128)} %get-tuple-element.45.ctx_ref.o_ref, ...), custom_call_target="tpu_custom_call" | custom-call | tf_op jit(solution)/shard_map/attend_back_last/pallas_call | solution.py:226
  467.7 11.0 %fusion.12 = bf16[4096,768]{1,0:T(8,128)(2,1)} fusion(s32[1024]{0:T(1024)S(1)} %reduce.2, s32[1024]{0:T(1024)S(1)} %reduce.1, f32[1024,768]{1,0:T(8,128)S(1)} %convert_add_fusion), kind=kOutput, calls=%fused_computation.15 | convolution fusion | flops 6458966016 | bytes 9445376 | tf_op jit(solution)/shard_map/dot_general | solution.py:23
  478.7 4.3 all-to-all-start.2
  483.1 4.5 convolution_convert_fusion.4
  487.5 9.9 convolution_convert_fusion.1
  497.4 6.9 convolution_convert_fusion
  515.2 4.5 convolution_add_fusion.2
  519.6 4.5 convolution_add_fusion.1
  531.5 162.1 %all-reduce = (f32[768]{0:T(1024)}, f32[768]{0:T(1024)}, f32[6,768]{1,0:T(8,128)S(1)}, f32[3072]{0:T(1024)}) all-reduce(f32[768]{0:T(1024)S(1)} %get-tuple-element.86, f32[768]{0:T(1024)S(1)} %add.88, f32[6,768]{1,0:T(8,128)S(1)} %bitcast_reduce_fusion, f32[3072]{0:T(1024)S(1)} %reduce_sum.71), channel_id=1, replica_groups=mesh['dp'=16,'seq'=2] {'dp','seq'}, use_global_device_ids=true, to_apply=%region_4.5 | all-reduce | flops 9216 | bytes 73728 | tf_op jit(solution)/shard_map/psum | solution.py:507
  694.3 123.2 %all-reduce.8.cloned.1.call-done = (bf16[768,768]{1,0:T(8,128)(2,1)}, bf16[768,3072]{1,0:T(8,128)(2,1)}, bf16[3072,768]{1,0:T(8,128)(2,1)}) async-done(((bf16[768,768]{1,0:T(8,128)(2,1)}, bf16[768,3072]{1,0:T(8,128)(2,1)}, bf16[3072,768]{1,0:T(8,128)(2,1)}), (bf16[768,768]{1,0:T(8,128)(2,1)}, bf16[768,3072]{1,0:T(8,128)(2,1)}, bf16[3072,768]{1,0:T(8,128)(2,1)})) %all-reduce.8.cloned.1.call-update) | async-done | bytes 10616848 | tf_op jit(solution)/shard_map/psum | solution.py:467
  820.5 7.4 convert_element_type.94
  827.9 4.9 convert_element_type.96
  832.9 6.2 fusion.6
  840.4 153.9 %all-reduce.6.cloned.1.call-done = (f32[128,768]{1,0:T(8,128)}, f32[768,768]{1,0:T(8,128)}, f32[768,768]{1,0:T(8,128)}, f32[768,768]{1,0:T(8,128)}) async-done(((f32[128,768]{1,0:T(8,128)}, f32[768,768]{1,0:T(8,128)}, f32[768,768]{1,0:T(8,128)}, f32[768,768]{1,0:T(8,128)}), (f32[128,768]{1,0:T(8,128)}, f32[768,768]{1,0:T(8,128)}, f32[768,768]{1,0:T(8,128)}, ...) | async-done | bytes 7471120 | tf_op jit(solution)/shard_map/psum | solution.py:507
  (139 shorter events, 73.8 us)
Async XLA Ops:
  7.2 187.8 %copy-start = (bf16[768,768]{1,0:T(8,128)(2,1)S(1)}, bf16[768,768]{1,0:T(8,128)(2,1)}, u32[]{:S(2)}) copy-start(bf16[768,768]{1,0:T(8,128)(2,1)} %param.36) | copy-start | bytes 3538948
  13.6 14.4 %copy-start.34 = (bf16[288,768]{1,0:T(8,128)(2,1)S(1)}, bf16[288,768]{1,0:T(8,128)(2,1)}, u32[]{:S(2)}) copy-start(bf16[288,768]{1,0:T(8,128)(2,1)} %param.31) | copy-start | bytes 1327108
  13.6 14.4 %all-to-all-start = ((s32[32,1,128]{2,1,0:T(1,128)}), s32[32,1,128]{2,1,0:T(1,128)S(1)}, u32[]{:S(2)}, u32[]{:S(2)}) async-start(s32[32,1,128]{2,1,0:T(1,128)} %bitcast.6), calls=%async_computation | async-start | bytes 32768 | tf_op jit(solution)/shard_map/all_to_all | solution.py:428
  35.4 143.8 %all-to-all-start.1 = ((bf16[32,128,768]{2,1,0:T(8,128)(2,1)}), bf16[32,128,768]{2,1,0:T(8,128)(2,1)}, u32[]{:S(2)}, u32[]{:S(2)}) async-start(bf16[32,128,768]{2,1,0:T(8,128)(2,1)} %bitcast.60), calls=%async_computation.1 | async-start | bytes 12582912 | tf_op jit(solution)/shard_map/all_to_all | solution.py:434
  179.2 11.3 %copy-start.20 = (bf16[128,768]{1,0:T(8,128)(2,1)S(1)}, bf16[128,768]{1,0:T(8,128)(2,1)}, u32[]{:S(2)}) copy-start(bf16[128,768]{1,0:T(8,128)(2,1)} %param.33) | copy-start | bytes 589828
  179.2 11.3 %copy-start.23 = (s32[1,1024]{1,0:T(1,128)S(1)}, s32[1,1024]{1,0:T(1,128)}, u32[]{:S(2)}) copy-start(s32[1,1024]{1,0:T(1,128)} %param.28) | copy-start | bytes 12292
  193.4 36.3 %collective-permute-start = (bf16[1024,768]{1,0:T(8,128)(2,1)}, bf16[1024,768]{1,0:T(8,128)(2,1)}, u32[]{:S(2)}, u32[]{:S(2)}) collective-permute-start(bf16[1024,768]{1,0:T(8,128)(2,1)} %get-tuple-element.83), channel_id=1, source_target_pairs={{0,1},{1,0},{2,3},{3,2},{4,5},{5,4},{6,7},{7,6},{8,9},{9,8},{10,11... | collective-permute-start | bytes 4718600 | tf_op jit(solution)/shard_map/ppermute | solution.py:441
  197.9 38.5 %copy-start.3 = (bf16[1024,768]{1,0:T(8,128)(2,1)}, bf16[1024,768]{1,0:T(8,128)(2,1)S(1)}, u32[]{:S(2)}) copy-start(bf16[1024,768]{1,0:T(8,128)(2,1)S(1)} %convolution_convert_fusion.3.ka_ref.k_ref) | copy-start | bytes 4718596
  201.8 130.7 %copy-start.2 = (bf16[1024,768]{1,0:T(8,128)(2,1)}, bf16[1024,768]{1,0:T(8,128)(2,1)S(1)}, u32[]{:S(2)}) copy-start(bf16[1024,768]{1,0:T(8,128)(2,1)S(1)} %fusion.18.q_ref) | copy-start | bytes 4718596
  236.4 59.0 %copy-start.4 = (bf16[1024,768]{1,0:T(8,128)(2,1)}, bf16[1024,768]{1,0:T(8,128)(2,1)S(1)}, u32[]{:S(2)}) copy-start(bf16[1024,768]{1,0:T(8,128)(2,1)S(1)} %convolution_convert_fusion.2.kb_ref.k_ref) | copy-start | bytes 4718596
  398.5 65.2 %collective-permute-start.1 = (bf16[1024,768]{1,0:T(8,128)(2,1)}, bf16[1024,768]{1,0:T(8,128)(2,1)}, u32[]{:S(2)}, u32[]{:S(2)}) collective-permute-start(bf16[1024,768]{1,0:T(8,128)(2,1)} %add_convert_fusion), channel_id=1, source_target_pairs={{0,1},{1,0},{2,3},{3,2},{4,5},{5,4},{6,7},{7,6},{8,9},{9,8},{10,11... | collective-permute-start | bytes 4718600 | tf_op jit(solution)/shard_map/ppermute | solution.py:481
  467.7 11.1 %copy-start.12 = (f32[1024,768]{1,0:T(8,128)}, f32[1024,768]{1,0:T(8,128)S(1)}, u32[]{:S(2)}) copy-start(f32[1024,768]{1,0:T(8,128)S(1)} %convert_add_fusion) | copy-start | bytes 9437188
  478.7 354.1 %all-to-all-start.2 = ((bf16[32,128,768]{2,1,0:T(8,128)(2,1)}), bf16[32,128,768]{2,1,0:T(8,128)(2,1)}, u32[]{:S(2)}, u32[]{:S(2)}) async-start(bf16[32,128,768]{2,1,0:T(8,128)(2,1)} %bitcast.59), calls=%async_computation.2 | async-start | bytes 12582912 | tf_op jit(solution)/shard_map/all_to_all | solution.py:502
  483.0 334.5 %all-reduce.8.cloned.1.call-start = ((), (), s32[]{:S(2)}) async-start(), calls=%async_computation.4 | async-start | bytes 21233664 | tf_op jit(solution)/shard_map/psum | solution.py:467
  483.0 4.5 copy-start.31
  483.1 14.4 %slice-start.2 = ((s8[6291456]{0:T(1024)(128)(4,1)}), s8[4194304]{0:T(1024)(128)(4,1)S(1)}, s32[]{:S(2)}) async-start(s8[6291456]{0:T(1024)(128)(4,1)} %bitcast.72), calls=%async_computation.7 | async-start | bytes 8388608
  487.5 9.9 slice-start.3
  487.5 9.9 copy-start.30
  504.4 489.9 %all-reduce.6.cloned.1.call-start = ((), (), s32[]{:S(2)}) async-start(), calls=%async_computation.3 | async-start | bytes 14942208 | tf_op jit(solution)/shard_map/psum | solution.py:507
  515.1 4.5 copy-start.6
  519.6 4.5 copy-start.13
  817.5 10.4 %slice-start = ((s8[4718592]{0:T(1024)(128)(4,1)}), s8[4194304]{0:T(1024)(128)(4,1)S(1)}, s32[]{:S(2)}) async-start(s8[4718592]{0:T(1024)(128)(4,1)} %bitcast.61), calls=%async_computation.5 | async-start | bytes 8388608
  820.5 7.4 slice-start.1
  999.4 3.9 copy-start.1
  (24 other events, 65.6 us)
Sparse Core Ops, SparseCore 0:
  504.5 312.9 all-reduce.7
  825.5 168.7 all-reduce.5

commit v2 on v1

v2 whole, which is shorter than its diff:
```python
import functools

import jax
import jax.numpy as jnp
from jax import lax
from jax.experimental import pallas as pl
from jax.experimental.pallas import tpu as pltpu
from jax.sharding import Mesh, PartitionSpec as P

HEADS = 12
HEAD_DIM = 64
PAIR = 2 * HEAD_DIM
KEY_CHUNK = 512
LOG2E = 1.4426950408889634
SWAP = [(0, 1), (1, 0)]
F32 = jnp.float32
BF16 = jnp.bfloat16
NN = (((1,), (0,)), ((), ()))
NT = (((1,), (1,)), ((), ()))
TN = (((0,), (0,)), ((), ()))


def mm(left, right, dims=NN):
    return lax.dot_general(left, right, dims, preferred_element_type=F32)


def params(mib):
    return pltpu.CompilerParams(vmem_limit_bytes=mib * 2**20)


def cost(flops, moved):
    return pl.CostEstimate(flops=flops, bytes_accessed=moved, transcendentals=0)


def hot(left, right):
    return (left == right).astype(BF16)


def route_kernel(
    rows_dev, capacity, top_ref, gene_ref, know_ref, req_ref, gene_slot_ref, know_slot_ref
):
    tokens = gene_ref.shape[0]
    devices, slots_all = req_ref.shape
    group = devices // 2
    lane = lax.broadcasted_iota(jnp.int32, (tokens, devices), 1)
    mine = lane < group
    top = top_ref[0]
    first = jnp.where(mine, lane + top * group, lane - top * group) * rows_dev
    earlier = (
        lax.broadcasted_iota(jnp.int32, (tokens, tokens), 0)
        > lax.broadcasted_iota(jnp.int32, (tokens, tokens), 1)
    ).astype(F32).astype(BF16)
    rank_lane = lax.broadcasted_iota(jnp.int32, (tokens, capacity), 1)
    asked = []
    for which, (ids_ref, slot_ref) in enumerate(((gene_ref, gene_slot_ref), (know_ref, know_slot_ref))):
        row = ids_ref[...] - first
        hit = (row >= 0) & (row < rows_dev)
        before = mm(earlier, hit.astype(F32).astype(BF16))
        rank = jnp.sum(jnp.where(hit, before, 0.0), axis=1, keepdims=True)
        owner = jnp.sum(jnp.where(hit, lane, 0).astype(F32), axis=1, keepdims=True)
        slot_ref[...] = (owner * slots_all + rank).astype(jnp.int32) + which * capacity
        rank_hit = (rank_lane == rank.astype(jnp.int32)).astype(F32).astype(BF16)
        coded = jnp.where(hit, row + 1, 0)
        high = (coded >> 4).astype(F32).astype(BF16)
        low = (coded & 15).astype(F32).astype(BF16)
        wanted = (mm(high, rank_hit, TN) * 16.0 + mm(low, rank_hit, TN)).astype(jnp.int32)
        asked.append(jnp.where(wanted > 0, wanted - 1 + which * rows_dev, -1))
    req_ref[:, :capacity] = asked[0]
    req_ref[:, capacity:] = asked[1]


def route(top, gene_ids, know_ids, rows_dev, capacity, devices):
    tokens = gene_ids.shape[0]
    return pl.pallas_call(
        functools.partial(route_kernel, rows_dev, capacity),
        in_specs=[pl.BlockSpec(memory_space=pltpu.SMEM)] + [pl.BlockSpec(memory_space=pltpu.VMEM)] * 2,
        out_shape=(
            jax.ShapeDtypeStruct((devices, 2 * capacity), jnp.int32),
            jax.ShapeDtypeStruct((tokens, 1), jnp.int32),
            jax.ShapeDtypeStruct((tokens, 1), jnp.int32),
        ),
        compiler_params=params(32),
        name="route",
    )(top.reshape(1), gene_ids[:, None], know_ids[:, None])


def fill_keys(aug_ref, key, first_key, count):
    lanes = lax.broadcasted_iota(jnp.int32, key.shape, 1)
    at = lax.broadcasted_iota(jnp.int32, key.shape, 0) + first_key
    bias = jnp.where(at < count, 0.0, -1e30).astype(BF16)
    none = jnp.zeros_like(key)
    aug_ref[:, :PAIR] = jnp.where(lanes < HEAD_DIM, key, jnp.where(lanes == HEAD_DIM, bias, none))
    aug_ref[:, PAIR : 2 * PAIR] = key
    aug_ref[:, 2 * PAIR :] = jnp.where(lanes >= HEAD_DIM, key, jnp.where(lanes == 0, bias, none))


def head_mask(shape, head):
    lanes = lax.broadcasted_iota(jnp.int32, shape, 1)
    return (lanes >= head * HEAD_DIM) & (lanes < (head + 1) * HEAD_DIM)


def spread_query(query, head):
    lanes = lax.broadcasted_iota(jnp.int32, query.shape, 1)
    scaled = query.astype(F32) * (HEAD_DIM ** (-0.5) * LOG2E)
    scaled = jnp.where(head_mask(query.shape, head), scaled, 0.0)
    high = scaled.astype(BF16)
    low = scaled - high.astype(F32)
    low = jnp.where(lanes == (1 - head) * HEAD_DIM, 1.0, low).astype(BF16)
    return jnp.concatenate([low, high] if head == 0 else [high, low], axis=1)


def fold_rows(value, how):
    return how(value.reshape(value.shape[0] // 8, 8, value.shape[1]), axis=0)


def attend_kernel(merge, where_ref, q_ref, k_ref, v_ref, *rest):
    if merge:
        out_in_ref, lse_in_ref, out_ref, lse_ref, aug_ref, vt_ref, score_ref = rest
    else:
        out_ref, lse_ref, aug_ref, vt_ref, score_ref = rest
    spans = [slice(c, c + KEY_CHUNK) for c in range(0, k_ref.shape[0], KEY_CHUNK)]
    fill_keys(aug_ref, k_ref[...], where_ref[0], where_ref[1])
    vt_ref[...] = v_ref[...].T
    outs = []
    for head in range(2):
        own = slice(head * HEAD_DIM, (head + 1) * HEAD_DIM)
        query = spread_query(q_ref[...], head)
        top = None
        for span in spans:
            scores = mm(aug_ref[span, head * PAIR : (head + 2) * PAIR], query, NT)
            score_ref[head, span, :] = scores
            high = fold_rows(scores, jnp.max)
            top = high if top is None else jnp.maximum(top, high)
        top = jnp.max(top, axis=0, keepdims=True)
        total = None
        acc = None
        for span in spans:
            probs = jnp.exp2(score_ref[head, span, :] - top)
            part = fold_rows(probs, jnp.sum)
            total = part if total is None else total + part
            part = mm(vt_ref[own, span], probs.astype(BF16))
            acc = part if acc is None else acc + part
        total = jnp.sum(total, axis=0, keepdims=True)
        lse = top + jnp.log2(total)
        if merge:
            before = lse_in_ref[0, head : head + 1, :]
            both = jnp.maximum(lse, before)
            both = both + jnp.log2(jnp.exp2(lse - both) + jnp.exp2(before - both))
            acc = acc * (jnp.exp2(lse - both) / total)
            acc = acc + out_in_ref[own, :] * jnp.exp2(before - both)
            lse = both
        else:
            acc = acc / total
        lse_ref[0, head : head + 1, :] = lse
        outs.append(acc)
    out = jnp.concatenate(outs, axis=0)
    out_ref[...] = out.T if merge else out


def attend(where, query, key, value, before=()):
    tokens, width = query.shape
    keys = key.shape[0]
    pairs = width // PAIR
    column = lambda rows: pl.BlockSpec((rows, PAIR), lambda p, w: (0, p))
    upright = pl.BlockSpec((PAIR, tokens), lambda p, w: (p, 0))
    stats = pl.BlockSpec((1, 2, tokens), lambda p, w: (p, 0, 0))
    merge = len(before) > 0
    return pl.pallas_call(
        functools.partial(attend_kernel, merge),
        grid_spec=pltpu.PrefetchScalarGridSpec(
            num_scalar_prefetch=1,
            grid=(pairs,),
            in_specs=[column(tokens), column(keys), column(keys)] + ([upright, stats] if merge else []),
            out_specs=[column(tokens) if merge else upright, stats],
            scratch_shapes=[
                pltpu.VMEM((keys, 3 * PAIR), BF16),
                pltpu.VMEM((PAIR, keys), BF16),
                pltpu.VMEM((2, keys, tokens), F32),
            ],
        ),
        out_shape=(
            jax.ShapeDtypeStruct((tokens, width) if merge else (width, tokens), F32),
            jax.ShapeDtypeStruct((pairs, 2, tokens), F32),
        ),
        compiler_params=params(48),
        cost_estimate=cost(16 * tokens * keys * width, 2 * tokens * width * 10),
        name="attend_more" if merge else "attend",
    )(where, query, key, value, *before)


def attend_back_kernel(
    add, untouched, where_ref, q_ref, g_ref, o_ref, lse_ref, k_ref, v_ref, *rest
):
    dq_in_ref = rest[0] if add else None
    dq_ref, dk_ref, dv_ref, aug_ref, kt_ref = rest[int(add) + untouched :]
    fill_keys(aug_ref, k_ref[...], where_ref[0], where_ref[1])
    kt_ref[...] = k_ref[...].T
    grad = g_ref[...]
    picks = (
        lax.broadcasted_iota(jnp.int32, (8, PAIR), 1) // HEAD_DIM
        == lax.broadcasted_iota(jnp.int32, (8, PAIR), 0)
    ).astype(F32)
    inner = lax.dot_general(
        picks,
        grad.astype(F32) * o_ref[...],
        NT,
        precision=lax.Precision.HIGHEST,
        preferred_element_type=F32,
    )
    scaled = q_ref[...] * jnp.asarray(HEAD_DIM ** (-0.5), BF16)
    none = jnp.zeros_like(grad)
    masks = [head_mask(grad.shape, head) for head in range(2)]
    queries = [spread_query(q_ref[...], head) for head in range(2)]
    q_heads = [jnp.where(m, scaled, none) for m in masks]
    g_heads = [jnp.where(m, grad, none) for m in masks]
    dqs = [None, None]
    for first in range(0, k_ref.shape[0], KEY_CHUNK):
        span = slice(first, first + KEY_CHUNK)
        dk = None
        dv = None
        for head in range(2):
            own = slice(head * HEAD_DIM, (head + 1) * HEAD_DIM)
            scores = mm(aug_ref[span, head * PAIR : (head + 2) * PAIR], queries[head], NT)
            probs = jnp.exp2(scores - lse_ref[0, head : head + 1, :])
            grad_probs = mm(v_ref[span, :], g_heads[head], NT)
            grad_scores = (probs * (grad_probs - inner[head : head + 1, :])).astype(BF16)
            part = mm(kt_ref[own, span], grad_scores)
            dqs[head] = part if dqs[head] is None else dqs[head] + part
            part = mm(probs.astype(BF16), g_heads[head])
            dv = part if dv is None else dv + part
            part = mm(grad_scores, q_heads[head])
            dk = part if dk is None else dk + part
        dk_ref[span, :] = dk.astype(BF16)
        dv_ref[span, :] = dv.astype(BF16)
    dq = jnp.concatenate(dqs, axis=0).T * HEAD_DIM ** (-0.5)
    if add:
        dq = dq + dq_in_ref[...]
    dq_ref[...] = dq.astype(dq_ref.dtype)


def attend_back(where, query, grad, out, lse, key, value, first, count, before, into):
    tokens, width = query.shape
    keys = key.shape[0]
    column = lambda rows: pl.BlockSpec((rows, PAIR), lambda p, w: (0, p + first))
    untouched = pl.BlockSpec(memory_space=pl.ANY)
    add = len(before) > 0
    given = 7 + len(before)
    return pl.pallas_call(
        functools.partial(attend_back_kernel, add, len(into)),
        grid_spec=pltpu.PrefetchScalarGridSpec(
            num_scalar_prefetch=1,
            grid=(count,),
            in_specs=[column(tokens)] * 3
            + [pl.BlockSpec((1, 2, tokens), lambda p, w: (p + first, 0, 0))]
            + [column(keys)] * 2
            + [column(tokens)] * len(before)
            + [untouched] * len(into),
            out_specs=[column(tokens), column(keys), column(keys)],
            scratch_shapes=[
                pltpu.VMEM((keys, 3 * PAIR), BF16),
                pltpu.VMEM((PAIR, keys), BF16),
            ],
        ),
        out_shape=(
            jax.ShapeDtypeStruct((tokens, width), BF16 if add else F32),
            jax.ShapeDtypeStruct((keys, width), BF16),
            jax.ShapeDtypeStruct((keys, width), BF16),
        ),
        input_output_aliases={given + i: i for i in range(len(into))},
        compiler_params=params(56),
        cost_estimate=cost(40 * tokens * keys * PAIR * count, 2 * tokens * PAIR * count * 12),
        name=("attend_back_more" if add else "attend_back") + str(first),
    )(where, query, grad, out, lse, key, value, *before, *into)


def norm_parts(value):
    centre = jnp.mean(value, axis=-1, keepdims=True)
    centred = value - centre
    variance = jnp.mean(centred * centred, axis=-1, keepdims=True)
    inverse = lax.rsqrt(variance + 1e-05)
    return centred * inverse, inverse


def norm_back(grad, unit, inverse, gain):
    grad_unit = grad * gain
    return inverse * (
        grad_unit
        - jnp.mean(grad_unit, axis=-1, keepdims=True)
        - unit * jnp.mean(grad_unit * unit, axis=-1, keepdims=True)
    )


def middle_kernel(
    ctx_ref,
    emb_ref,
    cot_ref,
    w_out_ref,
    w_up_ref,
    w_down_ref,
    small_ref,
    b_up_ref,
    out_ref,
    ctx_low_ref,
    normed_ref,
    act_ref,
    gffn_ref,
    gpre_ref,
    gattn_ref,
    gone_ref,
    gctx_ref,
    sums_ref,
    up_sums_ref,
    slope_ref,
):
    step = pl.program_id(0)
    width = emb_ref.shape[1]
    wide = w_up_ref.shape[1]

    @pl.when(step == 0)
    def _():
        sums_ref[...] = jnp.zeros_like(sums_ref)
        up_sums_ref[...] = jnp.zeros_like(up_sums_ref)

    b_out, gain_one, shift_one, b_down, gain_two, shift_two = (
        small_ref[i : i + 1, :] for i in range(6)
    )
    ctx_low = ctx_ref[...].astype(BF16)
    ctx_low_ref[...] = ctx_low
    unit_one, inv_one = norm_parts(emb_ref[...] + mm(ctx_low, w_out_ref[...]) + b_out)
    normed = unit_one * gain_one + shift_one
    normed_low = normed.astype(BF16)
    normed_ref[...] = normed_low
    ffn = None
    for c in range(wide // width):
        span = slice(c * width, (c + 1) * width)
        pre = mm(normed_low, w_up_ref[:, span]) + b_up_ref[:, span]
        below = 0.5 * (1.0 + lax.erf(pre * 0.7071067811865476))
        act = (pre * below).astype(BF16)
        act_ref[:, span] = act
        slope_ref[:, span] = below + pre * (0.3989422804014327 * jnp.exp(-0.5 * pre * pre))
        part = mm(act, w_down_ref[span, :])
        ffn = part if ffn is None else ffn + part
    unit_two, inv_two = norm_parts(normed + ffn + b_down)
    out_ref[...] = (unit_two * gain_two + shift_two).astype(BF16)
    grad = cot_ref[...].astype(F32)
    sums_ref[0:8, :] += fold_rows(grad * unit_two, jnp.sum)
    sums_ref[8:16, :] += fold_rows(grad, jnp.sum)
    grad_two = norm_back(grad, unit_two, inv_two, gain_two)
    gffn = grad_two.astype(BF16)
    gffn_ref[...] = gffn
    sums_ref[16:24, :] += fold_rows(gffn.astype(F32), jnp.sum)
    grad_normed = grad_two
    for c in range(wide // width):
        span = slice(c * width, (c + 1) * width)
        gpre = (mm(gffn, w_down_ref[span, :], NT) * slope_ref[:, span]).astype(BF16)
        gpre_ref[:, span] = gpre
        up_sums_ref[:, span] += fold_rows(gpre.astype(F32), jnp.sum)
        grad_normed = grad_normed + mm(gpre, w_up_ref[:, span], NT)
    sums_ref[24:32, :] += fold_rows(grad_normed * unit_one, jnp.sum)
    sums_ref[32:40, :] += fold_rows(grad_normed, jnp.sum)
    grad_one = norm_back(grad_normed, unit_one, inv_one, gain_one)
    gone_ref[...] = grad_one
    gattn = grad_one.astype(BF16)
    gattn_ref[...] = gattn
    sums_ref[40:48, :] += fold_rows(gattn.astype(F32), jnp.sum)
    gctx_ref[...] = mm(gattn, w_out_ref[...], NT).astype(BF16)


def middle(ctx, embedded, cotangent, w_out, w_up, w_down, small, b_up, block=256):
    tokens, width = embedded.shape
    wide = w_up.shape[1]
    whole = lambda a: pl.BlockSpec(a.shape, lambda i: (0, 0), pipeline_mode=pl.Buffered(1))
    rows = lambda n: pl.BlockSpec((block, n), lambda i: (i, 0))
    fixed = lambda r, n: pl.BlockSpec((r, n), lambda i: (0, 0))
    shape = lambda n, dtype: jax.ShapeDtypeStruct((tokens, n), dtype)
    return pl.pallas_call(
        middle_kernel,
        grid=(tokens // block,),
        in_specs=[rows(width)] * 3 + [whole(w_out), whole(w_up), whole(w_down), whole(small), whole(b_up)],
        out_specs=[
            rows(width),
            rows(width),
            rows(width),
            rows(wide),
            rows(width),
            rows(wide),
            rows(width),
            rows(width),
            rows(width),
            fixed(48, width),
            fixed(8, wide),
        ],
        out_shape=[
            shape(width, BF16),
            shape(width, BF16),
            shape(width, BF16),
            shape(wide, BF16),
            shape(width, BF16),
            shape(wide, BF16),
            shape(width, BF16),
            shape(width, F32),
            shape(width, BF16),
            jax.ShapeDtypeStruct((48, width), F32),
            jax.ShapeDtypeStruct((8, wide), F32),
        ],
        scratch_shapes=[pltpu.VMEM((block, wide), F32)],
        compiler_params=params(60),
        cost_estimate=cost(tokens * width * (8 * wide + 4 * width) * 2, 2 * tokens * (2 * wide + 14 * width)),
        name="middle",
    )(ctx, embedded, cotangent, w_out, w_up, w_down, small, b_up)


def cut(value, axis):
    rows = value.shape[0] // 2
    me = lax.axis_index(axis)
    keep = lax.dynamic_slice_in_dim(value, me * rows, rows, 0)
    return keep, lax.dynamic_slice_in_dim(value, (1 - me) * rows, rows, 0)


def halve(value, axis):
    keep, send = cut(value, axis)
    return keep + lax.ppermute(send, axis, SWAP)


def double(value, axis):
    first = lax.axis_index(axis) == 0
    other = lax.ppermute(value, axis, SWAP)
    return jnp.concatenate([jnp.where(first, value, other), jnp.where(first, other, value)], axis=0)


def orders_of(dp_axes):
    core, near, far = dp_axes[-1], dp_axes[-2], dp_axes[-3::-1]
    return (core, near, "seq", *far), (core, "seq", near, *far)


def doubled(pieces, orders):
    for step in reversed(range(len(orders[0]))):
        pieces = [double(p, order[step]) for p, order in zip(pieces, orders)]
    return pieces


def sum_everywhere(value, orders):
    pieces = jnp.split(halve(value, orders[0][0]), 2, axis=0)
    for step in range(1, len(orders[0])):
        pieces = [halve(p, order[step]) for p, order in zip(pieces, orders)]
    pieces = doubled(pieces, [order[1:] for order in orders])
    return double(jnp.concatenate(pieces, axis=0), orders[0][0])


def local(
    dp_axes,
    gene_ids,
    homolog_ids,
    knowledge_ids,
    expr_bins,
    species,
    cell_lengths,
    gene_table,
    knowledge_tables,
    expr_table,
    w_query,
    b_query,
    w_key,
    w_value,
    b_value,
    w_out,
    b_out,
    gain_one,
    shift_one,
    w_up,
    b_up,
    w_down,
    b_down,
    gain_two,
    shift_two,
    cotangent,
):
    tokens = gene_ids.shape[1]
    rows_dev, width = gene_table.shape
    wide = w_up.shape[1]
    every = (*dp_axes, "seq")
    top_axis, group_axes = dp_axes[0], (*dp_axes[1:], "seq")
    devices = lax.axis_size(every)
    group = devices // 2
    capacity = 2 * tokens // devices
    slots_all = 2 * capacity
    slots = group * slots_all
    bins = expr_table.shape[0]
    me = lax.axis_index("seq")

    def exchange(value, axis):
        return lax.all_to_all(value, group_axes, split_axis=axis, concat_axis=axis, tiled=True)

    gene_table, knowledge_tables = lax.optimization_barrier((gene_table, knowledge_tables))
    gene_other = lax.ppermute(gene_table, top_axis, SWAP)
    know_sum = jnp.sum(knowledge_tables.astype(F32), axis=0).astype(BF16)
    chosen = jnp.where(species[0] == 1, homolog_ids, gene_ids).reshape(-1)
    requests, gene_slot, know_slot = route(
        lax.axis_index(top_axis), chosen, knowledge_ids.reshape(-1), rows_dev, capacity, devices
    )
    asked = exchange(requests.reshape(2, group, slots_all), 1).reshape(2, slots)
    asked, gene_other, know_sum = lax.optimization_barrier((asked, gene_other, know_sum))
    know_other = lax.ppermute(know_sum, top_axis, SWAP)
    tables = [
        jnp.concatenate([gene_table, know_sum], axis=0),
        jnp.concatenate([gene_other, know_other], axis=0),
    ]
    row_at = jnp.arange(2 * rows_dev)
    slot_at = jnp.arange(slots)
    bin_hot = hot(expr_bins.reshape(-1)[:, None], jnp.arange(bins)[None, :])
    embedded = mm(bin_hot, expr_table)
    slot_hots = []
    for part in range(2):
        found = mm(hot(asked[part][:, None], row_at[None, :]), tables[part]).astype(BF16)
        fetched = exchange(found.reshape(group, slots_all, width), 0).reshape(slots, width)
        at = slot_at[None, :] + part * slots
        slot_hots.append(((at == gene_slot) | (at == know_slot)).astype(BF16))
        embedded = embedded + mm(slot_hots[part], fetched)
    x_low = embedded.astype(BF16)

    x_other = lax.ppermute(x_low, "seq", SWAP)
    query = (mm(x_low, w_query) + b_query).astype(BF16)
    key, key_other = (mm(x, w_key).astype(BF16) for x in (x_low, x_other))
    value, value_other = ((mm(x, w_value) + b_value).astype(BF16) for x in (x_low, x_other))
    mine = jnp.stack([me * tokens, cell_lengths[0]]).astype(jnp.int32)
    others = jnp.stack([(1 - me) * tokens, cell_lengths[0]]).astype(jnp.int32)
    context, lse = attend(
        others, query, key_other, value_other, attend(mine, query, key, value)
    )

    small = jnp.stack([b_out, gain_one, shift_one, b_down, gain_two, shift_two])
    (
        layer_output,
        ctx_low,
        normed_low,
        activated,
        grad_ffn,
        grad_pre,
        grad_attn,
        grad_one,
        grad_ctx,
        sums,
        up_sums,
    ) = middle(
        context, embedded, cotangent.reshape(tokens, width), w_out, w_up, w_down, small, b_up[None, :]
    )

    orders = orders_of(dp_axes)
    step = 0
    ffn_grads = [mm(activated, grad_ffn, TN).astype(BF16), mm(normed_low, grad_pre, TN).astype(BF16)]
    ffn_grads, grad_ctx = lax.optimization_barrier((ffn_grads, grad_ctx))
    w_out_grad = mm(ctx_low, grad_attn, TN)
    ffn_grads = [halve(g, order[0]) for g, order in zip(ffn_grads, orders)]
    pairs = width // PAIR
    sides = ((others, key_other, value_other), (mine, key, value))
    grads = []
    before = ()
    dx_from_other = None
    for side, (place, keys, values) in enumerate(sides):
        into = ()
        for part in range(2):
            step += 1
            cuts = [cut(g, order[step]) for g, order in zip(ffn_grads, orders)]
            cuts, grad_ctx, into, before = lax.optimization_barrier((cuts, grad_ctx, into, before))
            arrived = [lax.ppermute(c[1], order[step], SWAP) for c, order in zip(cuts, orders)]
            into = attend_back(
                place,
                query,
                grad_ctx,
                context,
                lse,
                keys,
                values,
                part * pairs // 2,
                pairs // 2,
                before,
                into,
            )
            arrived, into = lax.optimization_barrier((arrived, into))
            ffn_grads = [c[0] + a for c, a in zip(cuts, arrived)]
        grads.append(into)
        if side == 0:
            before = into[:1]
            dx_other = (mm(into[1], w_key, NT) + mm(into[2], w_value, NT)).astype(BF16)
            dx_other, before = lax.optimization_barrier((dx_other, before))
            dx_from_other = lax.ppermute(dx_other, "seq", SWAP)
    for order_step in range(step + 1, len(orders[0])):
        ffn_grads = [halve(g, order[order_step]) for g, order in zip(ffn_grads, orders)]
    (_, dk_other, dv_other), (dq, dk, dv) = grads
    dq, dk, dv, dx_from_other = lax.optimization_barrier((dq, dk, dv, dx_from_other))
    grad_embedded = (
        grad_one
        + mm(dq, w_query, NT)
        + mm(dk, w_key, NT)
        + mm(dv, w_value, NT)
        + dx_from_other.astype(F32)
    )
    grad_low = grad_embedded.astype(BF16)

    owned = [row_at[:, None] == asked[part][None, :] for part in range(2)]
    counts = [jnp.sum(o.astype(jnp.int32), axis=1) for o in owned]
    row_counts = counts[0] + lax.ppermute(counts[1], top_axis, SWAP)
    table_parts = [None, None]
    outgoing = [mm(hots, grad_low, TN).astype(BF16) for hots in slot_hots]
    outgoing, ffn_grads, dq, dk, dv = lax.optimization_barrier((outgoing, ffn_grads, dq, dk, dv))
    for part in (1, 0):
        returned = exchange(outgoing[part].reshape(group, slots_all, width), 0).reshape(slots, width)
        table_parts[part] = mm(owned[part].astype(BF16), returned)
    table_grads = table_parts[0] + lax.ppermute(
        table_parts[1].astype(BF16), top_axis, SWAP
    ).astype(F32)

    w_query_grad = mm(x_low, dq, TN)
    w_key_grad = mm(x_low, dk, TN) + mm(x_other, dk_other, TN)
    w_value_grad = mm(x_low, dv, TN) + mm(x_other, dv_other, TN)
    b_query_grad = jnp.sum(dq.astype(F32), axis=0)
    b_value_grad = jnp.sum(dv.astype(F32), axis=0) + jnp.sum(dv_other.astype(F32), axis=0)
    grad_rest = (grad_embedded - grad_low.astype(F32)).astype(BF16)
    expr_grad = mm(bin_hot, grad_low, TN) + mm(bin_hot, grad_rest, TN)
    late = [
        w_query_grad,
        w_key_grad,
        w_value_grad,
        w_out_grad,
        expr_grad,
        b_query_grad[None, :],
        b_value_grad[None, :],
        jnp.sum(sums.reshape(6, 8, width), axis=1),
        jnp.sum(up_sums, axis=0).reshape(wide // width, width),
    ]
    heights = [item.shape[0] for item in late]
    late.append(jnp.zeros((-sum(heights) % 512, width), F32))
    late = sum_everywhere(jnp.concatenate([item.astype(BF16) for item in late], axis=0), orders)
    w_down_grad, w_up_grad = (g.astype(F32) for g in doubled(ffn_grads, orders))
    taken = []
    for height in heights:
        at = sum(item.shape[0] for item in taken)
        taken.append(late[at : at + height].astype(F32))
    w_query_grad, w_key_grad, w_value_grad, w_out_grad, *taken = taken
    expr_grad, b_query_grad, b_value_grad, sums, b_up_grad = taken
    gain_two_grad, shift_two_grad, b_down_grad, gain_one_grad, shift_one_grad, b_out_grad = (
        sums[i] for i in range(6)
    )
    return (
        layer_output.reshape(1, tokens, width),
        table_grads[:rows_dev],
        table_grads[rows_dev:],
        expr_grad,
        w_query_grad,
        b_query_grad[0],
        w_key_grad,
        w_value_grad,
        b_value_grad[0],
        w_out_grad,
        b_out_grad,
        gain_one_grad,
        shift_one_grad,
        w_up_grad,
        b_up_grad.reshape(wide),
        w_down_grad,
        b_down_grad,
        gain_two_grad,
        shift_two_grad,
        row_counts.reshape(2, rows_dev),
    )


def solution(mesh):
    bits = mesh.shape["dp"].bit_length() - 1
    dp_axes = tuple(f"dp{i}" for i in range(bits))
    fine = Mesh(mesh.devices.reshape((2,) * bits + (mesh.shape["seq"],)), (*dp_axes, "seq"))
    every = (*dp_axes, "seq")
    whole = P()
    placed = (
        (P(dp_axes, "seq"),) * 4
        + (P(dp_axes),) * 2
        + (P(every, None), P(None, every, None))
        + (whole,) * 16
        + (P(dp_axes, "seq", None),)
    )
    given = (
        (P(dp_axes, "seq", None),)
        + (P(every, None),) * 2
        + (whole,) * 16
        + (P(None, every),)
    )
    return jax.shard_map(
        functools.partial(local, dp_axes), mesh=fine, in_specs=placed, out_specs=given, check_vma=False
    )
```

time: 1020 us -> 777 us (0.76)
  blocking collectives: 162 us -> 0 us
  waiting for transfers between devices: 445 us -> 311 us
  starting transfers between devices: 15.8 us -> 73.7 us
  Pallas kernels: 222 us -> 168 us
  other arithmetic: 23.3 us -> 62.4 us
  local copies, waits for them, and re-layouts: 15.9 us -> 51.9 us
  between operations: 16.5 us -> 3.91 us
  matrix products: 110 us -> 98.8 us
    psum x2 -> x0, waiting for transfers between devices: 277 us -> none  [the longest x1 154 us: local(): lax.psum((expr_grad, w_query_grad, w_key_grad, w_value_grad, b_query_grad...]
    ppermute x2 -> x44, waiting for transfers between devices: 23.3 us -> 269 us  [the longest x19 149 us: double(): other = lax.ppermute(value, axis, SWAP)]
    psum x1 -> x0, blocking collectives: 162 us -> none  [local(): lax.psum((expr_grad, w_query_grad, w_key_grad, w_value_grad, b_query_grad...]
    all_to_all x3 -> x5, waiting for transfers between devices: 145 us -> 42.3 us  [exchange(): lax.all_to_all(value, group_axes, split_axis=axis, concat_axis=axis, tile...]
    pallas_call x4 -> x7, Pallas kernels: 185 us -> 130 us  [the longest x4 83.8 us: attend_back(): pl.pallas_call(functools.partial(attend_back_kernel, add, len(into)), gri...]
    ppermute x2 -> x44, starting transfers between devices: 0.28 us -> 46.8 us  [the longest x19 16.7 us: double(): other = lax.ppermute(value, axis, SWAP)]
    concatenate x0 -> x1, local copies, waits for them, and re-layouts: none -> 30.1 us  [local(): jnp.concatenate([item.astype(BF16) for item in late], axis=0)]
    select_n x0 -> x19, other arithmetic: none -> 16.4 us  [double(): jnp.where(first, value, other)]
  transfers between devices with their start and end apart: 7 -> 49, of which waited for: 5 -> 26; matrix products, arithmetic and copies ran while one was open for 9% -> 16% of each run, Pallas kernels for 6% -> 14%
where the time goes in v2:
time: 777 us; the launch traced here: 770 us
  waiting for transfers between devices  311 us (40%)
  Pallas kernels  168 us (22%)
  matrix products  98.8 us (13%)
  starting transfers between devices  73.7 us (9%)
  other arithmetic  62.4 us (8%)
  local copies, waits for them, and re-layouts  51.9 us (7%)
    ppermute x19, waiting for transfers between devices, double(): other = lax.ppermute(value, axis, SWAP)  149 us
    dot_general x29, matrix products, mm(): return lax.dot_general(left, right, dims, preferred_element_type=F32)  98.8 us
    pallas_call x4, Pallas kernels, attend_back(): pl.pallas_call(functools.partial(attend_back_kernel, add, len(into)), gri...  83.8 us
    ppermute x1, waiting for transfers between devices, local(): know_other = lax.ppermute(know_sum, top_axis, SWAP)  51.8 us
    pallas_call x2, Pallas kernels, attend(): pl.pallas_call(functools.partial(attend_kernel, merge), grid_spec=pltpu.P...  43.5 us
    all_to_all x5, waiting for transfers between devices, exchange(): lax.all_to_all(value, group_axes, split_axis=axis, concat_axis=axis, tile...  42.3 us
    pallas_call x1, Pallas kernels, middle(): pl.pallas_call(middle_kernel, grid=(tokens // block,), in_specs=[rows(wid...  37.2 us
    ppermute x1, waiting for transfers between devices, local(): lax.ppermute(table_parts[1].astype(BF16), top_axis, SWAP).astype(F32)  30.1 us
  transfers between devices with their start and end apart: 49, of which 26 were waited for; matrix products, arithmetic and copies ran while one was open for 16% of the time, Pallas kernels for 14%

profile of v2, /device:TPU:0, one launch (start us, length us, event | category | flops | bytes accessed | tf_op | source)
XLA Modules:
  0.0 769.8 jit_solution(13159075231500919022)
XLA Ops:
  17.8 8.9 %all-to-all-done = s32[2,16,128]{2,0,1:T(2,128)S(1)} async-done(((s32[2,16,128]{2,0,1:T(2,128)}), s32[2,16,128]{2,0,1:T(2,128)S(1)}, u32[]{:S(2)}, u32[]{:S(2)}) %all-to-all-start) | async-done | bytes 16416 | tf_op jit(solution)/shard_map/all_to_all | solution.py:492
  37.5 51.8 %collective-permute-done.1 = bf16[288,768]{1,0:T(8,128)(2,1)S(1)} collective-permute-done((bf16[288,768]{1,0:T(8,128)(2,1)S(1)}, bf16[288,768]{1,0:T(8,128)(2,1)S(1)}, u32[]{:S(2)}, u32[]{:S(2)}) %collective-permute-start.1) | collective-permute-done | bytes 442400 | tf_op jit(solution)/shard_map/ppermute | solution.py:503
  94.4 6.4 all-to-all-start.2
  102.9 7.9 %fusion.5 = f32[1024,768]{1,0:T(8,128)} fusion(bf16[2048,768]{1,0:T(8,128)(2,1)} %bitcast.10, s32[1024]{0:T(1024)S(1)} %reduce.3, s32[1024]{0:T(1024)S(1)} %reduce.2), kind=kOutput, calls=%fused_computation.7 | convolution fusion | flops 3227516928 | bytes 6299648 | tf_op jit(solution)/shard_map/dot_general | solution.py:24
  110.7 33.4 %all-to-all-done.2 = bf16[16,128,768]{2,1,0:T(8,128)(2,1)} async-done(((bf16[16,128,768]{2,1,0:T(8,128)(2,1)}), bf16[16,128,768]{2,1,0:T(8,128)(2,1)}, u32[]{:S(2)}, u32[]{:S(2)}) %all-to-all-start.2) | async-done | bytes 3145760 | tf_op jit(solution)/shard_map/all_to_all | solution.py:492
  158.0 21.1 %attend.1 = (f32[768,1024]{1,0:T(8,128)}, f32[6,2,1024]{2,1,0:T(2,128)S(1)}) custom-call(s32[2]{0:T(128)S(1)} %pad_add_fusion.1.where_ref, bf16[1024,768]{1,0:T(8,128)(2,1)S(1)} %add_convert_fusion.3.q_ref, bf16[1024,768]{1,0:T(8,128)(2,1)S(1)} %convolution_convert_fusion.2.k_ref, bf16[1024,768]{1,0:T(8,128)(2,1)S(1)} %add_convert_fusion.1.v_ref), custom_call_target="tpu_custom_call" | custom-call | flops 12884901888 | bytes 15728640 | tf_op jit(solution)/shard_map/attend/pallas_call | solution.py:168
  179.1 9.9 %collective-permute-done.2 = bf16[1024,768]{1,0:T(8,128)(2,1)S(1)} collective-permute-done((bf16[1024,768]{1,0:T(8,128)(2,1)S(1)}, bf16[1024,768]{1,0:T(8,128)(2,1)S(1)}, u32[]{:S(2)}, u32[]{:S(2)}) %collective-permute-start.2) | collective-permute-done | bytes 1572896 | tf_op jit(solution)/shard_map/ppermute | solution.py:521
  191.8 22.4 %attend_more.1 = (f32[1024,768]{1,0:T(8,128)}, f32[6,2,1024]{2,1,0:T(2,128)S(1)}) custom-call(s32[2]{0:T(128)S(1)} %pad_add_fusion.where_ref, bf16[1024,768]{1,0:T(8,128)(2,1)S(1)} %add_convert_fusion.3.q_ref, bf16[1024,768]{1,0:T(8,128)(2,1)S(1)} %convolution_convert_fusion.3.k_ref, bf16[1024,768]{1,0:T(8,128)(2,1)S(1)} %add_convert_fusion.2.v_ref, ...), custom_call_target="tpu_custom_call" | custom-call | flops 12884901888 | bytes 15728640 | tf_op jit(solution)/shard_map/attend_more/pallas_call | solution.py:168
  214.8 37.2 %middle.1 = (bf16[1024,768]{1,0:T(8,128)(2,1)}, bf16[1024,768]{1,0:T(8,128)(2,1)}, bf16[1024,768]{1,0:T(8,128)(2,1)}, bf16[1024,3072]{1,0:T(8,128)(2,1)}, bf16[1...) custom-call(f32[1024,768]{1,0:T(8,128)} %get-tuple-element.129.ctx_r, ...), custom_call_target="tpu_custom_call" | custom-call | flops 43486543872 | bytes 34603008 | tf_op jit(solution)/shard_map/middle/pallas_call | solution.py:376
  252.1 9.3 %convolution_convert_fusion.1 = bf16[3072,768]{1,0:T(8,128)(2,1)} fusion(bf16[1024,3072]{1,0:T(8,128)(2,1)} %get-tuple-element.132, bf16[1024,768]{1,0:T(8,128)(2,1)} %get-tuple-element.133), kind=kOutput, calls=%fused_computation.13 | convolution fusion | flops 4834197504 | bytes 12582912 | tf_op jit(solution)/shard_map/dot_general | solution.py:24
  286.2 20.6 %attend_back0.1 = (f32[1024,768]{1,0:T(8,128)}, bf16[1024,768]{1,0:T(8,128)(2,1)}, bf16[1024,768]{1,0:T(8,128)(2,1)}) custom-call(s32[2]{0:T(128)} %copy-done.2, bf16[1024,768]{1,0:T(8,128)(2,1)} %copy-done.5, bf16[1024,768]{1,0:T(8,128)(2,1)} %get-tuple-element.187.g_ref, f32[1024,768]{1,0:T(8,128)} %get-tuple-element.129.ctx_ref.o_ref, ...), custom_call_target="tpu_custom_call" | custom-call | flops 16106127360 | bytes 9437184 | tf_op jit(solution)/shard_map/attend_back0/pallas_call | solution.py:248
  316.0 20.9 %attend_back3.1 = (f32[1024,768]{1,0:T(8,128)}, bf16[1024,768]{1,0:T(8,128)(2,1)}, bf16[1024,768]{1,0:T(8,128)(2,1)}) custom-call(s32[2]{0:T(128)} %copy-done.2, bf16[1024,768]{1,0:T(8,128)(2,1)} %copy-done.5, bf16[1024,768]{1,0:T(8,128)(2,1)} %get-tuple-element.187.g_ref, ...), custom_call_target="tpu_custom_call", output_to_operand_aliasing={{0}: (7, {}), {1}: (8, {}), {2}: (9, {})} | custom-call | flops 16106127360 | bytes 9437184 | tf_op jit(solution)/shard_map/attend_back3/pallas_call | solution.py:248
  345.4 21.0 %attend_back_more0.1 = (bf16[1024,768]{1,0:T(8,128)(2,1)}, bf16[1024,768]{1,0:T(8,128)(2,1)}, bf16[1024,768]{1,0:T(8,128)(2,1)}) custom-call(s32[2]{0:T(128)} %copy-done.1, bf16[1024,768]{1,0:T(8,128)(2,1)} %copy-done.5, bf16[1024,768]{1,0:T(8,128)(2,1)} %get-tuple-element.187.g_ref, f32[1024,768]{1,0:T(8,128)} %get-tuple-element.129.ctx_ref.o_ref, ...), custom_call_target="tpu_custom_call" | custom-call | flops 16106127360 | bytes 9437184 | tf_op jit(solution)/shard_map/attend_back_more0/pallas_call | solution.py:248
  369.9 21.2 %attend_back_more3.1 = (bf16[1024,768]{1,0:T(8,128)(2,1)}, bf16[1024,768]{1,0:T(8,128)(2,1)}, bf16[1024,768]{1,0:T(8,128)(2,1)}) custom-call(s32[2]{0:T(128)} %copy-done.1, bf16[1024,768]{1,0:T(8,128)(2,1)} %copy-done.5, bf16[1024,768]{1,0:T(8,128)(2,1)} %get-tuple-element.187.g_ref, ...), custom_call_target="tpu_custom_call", output_to_operand_aliasing={{0}: (8, {}), {1}: (9, {}), {2}: (10, {})} | custom-call | flops 16106127360 | bytes 9437184 | tf_op jit(solution)/shard_map/attend_back_more3/pallas_call | solution.py:248
  406.7 6.5 fusion.23
  434.2 30.1 %concatenate.65 = bf16[3584,768]{1,0:T(8,128)(2,1)} concatenate(bf16[768,768]{1,0:T(8,128)(2,1)} %convolution_convert_fusion.5, bf16[768,768]{1,0:T(8,128)(2,1)} %add_convert_fusion.5, bf16[768,768]{1,0:T(8,128)(2,1)} %add_convert_fusion.4, bf16[768,768]{1,0:T(8,128)(2,1)} %convolution_convert_fusion.4, bf16[128,768]{1,0:T(8,128)(2,1)S(1)} %fusion.35, ...), dimensions={0} | concatenate | bytes 11010048 | tf_op jit(solution)/shard_map/concatenate | solution.py:633
  472.0 7.5 collective-permute-done.35
  494.0 52.8 %collective-permute-done.40 = bf16[384,768]{1,0:T(8,128)(2,1)S(1)} collective-permute-done((bf16[384,768]{1,0:T(8,128)(2,1)}, bf16[384,768]{1,0:T(8,128)(2,1)S(1)}, u32[]{:S(2)}, u32[]{:S(2)}) %collective-permute-start.40) | collective-permute-done | bytes 589856 | tf_op jit(solution)/shard_map/ppermute | solution.py:427
  556.4 19.7 %collective-permute-done.41 = bf16[768,768]{1,0:T(8,128)(2,1)S(1)} collective-permute-done((bf16[768,768]{1,0:T(8,128)(2,1)S(1)}, bf16[768,768]{1,0:T(8,128)(2,1)S(1)}, u32[]{:S(2)}, u32[]{:S(2)}) %collective-permute-start.41) | collective-permute-done | bytes 1179680 | tf_op jit(solution)/shard_map/ppermute | solution.py:427
  580.8 6.9 collective-permute-done.16
  611.7 6.7 all-to-all-start.3
  622.5 45.9 %collective-permute-done.29 = bf16[112,768]{1,0:T(8,128)(2,1)S(1)} collective-permute-done((bf16[112,768]{1,0:T(8,128)(2,1)S(1)}, bf16[112,768]{1,0:T(8,128)(2,1)S(1)}, u32[]{:S(2)}, u32[]{:S(2)}) %collective-permute-start.29) | collective-permute-done | bytes 172064 | tf_op jit(solution)/shard_map/ppermute | solution.py:427
  685.7 10.3 %collective-permute-done.31 = bf16[448,768]{1,0:T(8,128)(2,1)S(1)} collective-permute-done((bf16[448,768]{1,0:T(8,128)(2,1)S(1)}, bf16[448,768]{1,0:T(8,128)(2,1)S(1)}, u32[]{:S(2)}, u32[]{:S(2)}) %collective-permute-start.31) | collective-permute-done | bytes 688160 | tf_op jit(solution)/shard_map/ppermute | solution.py:427
  719.4 30.1 %collective-permute-done.14 = bf16[576,768]{1,0:T(8,128)(2,1)} collective-permute-done((bf16[576,768]{1,0:T(8,128)(2,1)}, bf16[576,768]{1,0:T(8,128)(2,1)}, u32[]{:S(2)}, u32[]{:S(2)}) %collective-permute-start.14) | collective-permute-done | bytes 884768 | tf_op jit(solution)/shard_map/ppermute | solution.py:609
  (367 shorter events, 257.5 us)
Async XLA Ops:
  0.7 26.0 %collective-permute-start = (bf16[288,768]{1,0:T(8,128)(2,1)}, bf16[288,768]{1,0:T(8,128)(2,1)}, u32[]{:S(2)}, u32[]{:S(2)}) collective-permute-start(bf16[288,768]{1,0:T(8,128)(2,1)} %param.31), channel_id=1, source_target_pairs={{0,16},{16,0},{1,17},{17,1},{2,18},{18,2},{3,19},{19,3},{4,20},{20... | collective-permute-start | bytes 1327112 | tf_op jit(solution)/shard_map/ppermute | solution.py:495
  31.9 62.5 %all-to-all-start.1 = ((bf16[16,128,768]{2,1,0:T(8,128)(2,1)}), bf16[16,128,768]{2,1,0:T(8,128)(2,1)}, u32[]{:S(2)}, u32[]{:S(2)}) async-start(bf16[16,128,768]{2,1,0:T(8,128)(2,1)} %bitcast.77), calls=%async_computation.1 | async-start | bytes 6291456 | tf_op jit(solution)/shard_map/all_to_all | solution.py:492
  36.4 52.9 %collective-permute-start.1 = (bf16[288,768]{1,0:T(8,128)(2,1)S(1)}, bf16[288,768]{1,0:T(8,128)(2,1)S(1)}, u32[]{:S(2)}, u32[]{:S(2)}) collective-permute-start(bf16[288,768]{1,0:T(8,128)(2,1)S(1)} %reduce_sum.78), channel_id=1, source_target_pairs={{0,16},{16,0},{1,17},{17,1},{2,18},{18,2},{3,19},{19,3},{4,20},{20... | collective-permute-start | bytes 1327112 | tf_op jit(solution)/shard_map/ppermute | solution.py:503
  94.4 49.7 %all-to-all-start.2 = ((bf16[16,128,768]{2,1,0:T(8,128)(2,1)}), bf16[16,128,768]{2,1,0:T(8,128)(2,1)}, u32[]{:S(2)}, u32[]{:S(2)}) async-start(bf16[16,128,768]{2,1,0:T(8,128)(2,1)} %bitcast.76), calls=%async_computation.2 | async-start | bytes 6291456 | tf_op jit(solution)/shard_map/all_to_all | solution.py:492
  152.3 36.6 %collective-permute-start.2 = (bf16[1024,768]{1,0:T(8,128)(2,1)S(1)}, bf16[1024,768]{1,0:T(8,128)(2,1)S(1)}, u32[]{:S(2)}, u32[]{:S(2)}) collective-permute-start(bf16[1024,768]{1,0:T(8,128)(2,1)S(1)} %get-tuple-element.292), channel_id=1, source_target_pairs={{0,1},{1,0},{2,3},{3,2},{4,5},{5,4},{6,7},{7,6},{8,9},{9,8},{10,11... | collective-permute-start | bytes 4718600 | tf_op jit(solution)/shard_map/ppermute | solution.py:521
  284.8 27.9 %collective-permute-start.5 = (bf16[768,768]{1,0:T(8,128)(2,1)S(1)}, bf16[768,768]{1,0:T(8,128)(2,1)S(1)}, u32[]{:S(2)}, u32[]{:S(2)}) collective-permute-start(bf16[768,768]{1,0:T(8,128)(2,1)S(1)} %get-tuple-element.141), channel_id=1, source_target_pairs={{0,4},{4,0},{1,5},{5,1},{2,6},{6,2},{3,7},{7,3},{8,12},{12,8},{9,1... | collective-permute-start | bytes 3538952 | tf_op jit(solution)/shard_map/ppermute | solution.py:565
  285.7 28.1 %collective-permute-start.6 = (bf16[192,3072]{1,0:T(8,128)(2,1)S(1)}, bf16[192,3072]{1,0:T(8,128)(2,1)S(1)}, u32[]{:S(2)}, u32[]{:S(2)}) collective-permute-start(bf16[192,3072]{1,0:T(8,128)(2,1)S(1)} %get-tuple-element.142), channel_id=1, source_target_pairs={{0,1},{1,0},{2,3},{3,2},{4,5},{5,4},{6,7},{7,6},{8,9},{9,8},{10,11... | collective-permute-start | bytes 3538952 | tf_op jit(solution)/shard_map/ppermute | solution.py:565
  341.9 24.8 %collective-permute-start.9 = (bf16[192,768]{1,0:T(8,128)(2,1)S(1)}, bf16[192,768]{1,0:T(8,128)(2,1)S(1)}, u32[]{:S(2)}, u32[]{:S(2)}) collective-permute-start(bf16[192,768]{1,0:T(8,128)(2,1)S(1)} %get-tuple-element.172), channel_id=1, source_target_pairs={{0,8},{8,0},{1,9},{9,1},{2,10},{10,2},{3,11},{11,3},{4,12},{12,4},... | collective-permute-start | bytes 884744 | tf_op jit(solution)/shard_map/ppermute | solution.py:565
  344.0 47.3 %collective-permute-start.13 = (bf16[1024,768]{1,0:T(8,128)(2,1)S(1)}, bf16[1024,768]{1,0:T(8,128)(2,1)S(1)}, u32[]{:S(2)}, u32[]{:S(2)}) collective-permute-start(bf16[1024,768]{1,0:T(8,128)(2,1)S(1)} %add_convert_fusion), channel_id=1, source_target_pairs={{0,1},{1,0},{2,3},{3,2},{4,5},{5,4},{6,7},{7,6},{8,9},{9,8},{10,11... | collective-permute-start | bytes 4718600 | tf_op jit(solution)/shard_map/ppermute | solution.py:586
  423.8 46.4 %collective-permute-start.38 = (bf16[96,768]{1,0:T(8,128)(2,1)S(1)}, bf16[96,768]{1,0:T(8,128)(2,1)S(1)}, u32[]{:S(2)}, u32[]{:S(2)}) collective-permute-start(bf16[96,768]{1,0:T(8,128)(2,1)S(1)} %add.287), channel_id=1, source_target_pairs={{0,16},{16,0},{1,17},{17,1},{2,18},{18,2},{3,19},{19,3},{4,20},{20... | collective-permute-start | bytes 442376 | tf_op jit(solution)/shard_map/ppermute | solution.py:427
  433.4 30.9 %collective-permute-start.34 = (bf16[48,3072]{1,0:T(8,128)(2,1)}, bf16[48,3072]{1,0:T(8,128)(2,1)}, u32[]{:S(2)}, u32[]{:S(2)}) collective-permute-start(bf16[48,3072]{1,0:T(8,128)(2,1)} %pad_maximum_fusion.12), channel_id=1, source_target_pairs={{0,8},{8,0},{1,9},{9,1},{2,10},{10,2},{3,11},{11,3},{4,12},{12,4},... | collective-permute-start | bytes 884744 | tf_op jit(solution)/shard_map/ppermute | solution.py:427
  470.2 82.2 %collective-permute-start.15 = (bf16[1792,768]{1,0:T(8,128)(2,1)}, bf16[1792,768]{1,0:T(8,128)(2,1)}, u32[]{:S(2)}, u32[]{:S(2)}) collective-permute-start(bf16[1792,768]{1,0:T(8,128)(2,1)} %constant_dynamic-slice_fusion.8), channel_id=1, source_target_pairs={{0,2},{2,0},{1,3},{3,1},{4,6},{6,4},{5,7},{7,5},{8,10},{10,8},{9,1... | collective-permute-start | bytes 8257544 | tf_op jit(solution)/shard_map/ppermute | solution.py:422
  479.9 69.0 %collective-permute-start.36 = (bf16[192,3072]{1,0:T(8,128)(2,1)S(1)}, bf16[192,3072]{1,0:T(8,128)(2,1)}, u32[]{:S(2)}, u32[]{:S(2)}) collective-permute-start(bf16[192,3072]{1,0:T(8,128)(2,1)S(1)} %pad_maximum_fusion.4), channel_id=1, source_target_pairs={{0,1},{1,0},{2,3},{3,2},{4,5},{5,4},{6,7},{7,6},{8,9},{9,8},{10,11... | collective-permute-start | bytes 3538952 | tf_op jit(solution)/shard_map/ppermute | solution.py:427
  481.4 65.4 %collective-permute-start.40 = (bf16[384,768]{1,0:T(8,128)(2,1)}, bf16[384,768]{1,0:T(8,128)(2,1)S(1)}, u32[]{:S(2)}, u32[]{:S(2)}) collective-permute-start(bf16[384,768]{1,0:T(8,128)(2,1)} %pad_maximum_fusion.9), channel_id=1, source_target_pairs={{0,1},{1,0},{2,3},{3,2},{4,5},{5,4},{6,7},{7,6},{8,9},{9,8},{10,11... | collective-permute-start | bytes 1769480 | tf_op jit(solution)/shard_map/ppermute | solution.py:427
  489.5 122.3 %all-to-all-start.4 = ((bf16[16,128,768]{2,1,0:T(8,128)(2,1)}), bf16[16,128,768]{2,1,0:T(8,128)(2,1)}, u32[]{:S(2)}, u32[]{:S(2)}) async-start(bf16[16,128,768]{2,1,0:T(8,128)(2,1)} %bitcast.75), calls=%async_computation.4 | async-start | bytes 6291456 | tf_op jit(solution)/shard_map/all_to_all | solution.py:492
  547.1 29.0 %collective-permute-start.41 = (bf16[768,768]{1,0:T(8,128)(2,1)S(1)}, bf16[768,768]{1,0:T(8,128)(2,1)S(1)}, u32[]{:S(2)}, u32[]{:S(2)}) collective-permute-start(bf16[768,768]{1,0:T(8,128)(2,1)S(1)} %pad_maximum_fusion.5), channel_id=1, source_target_pairs={{0,4},{4,0},{1,5},{5,1},{2,6},{6,2},{3,7},{7,3},{8,12},{12,8},{9,1... | collective-permute-start | bytes 3538952 | tf_op jit(solution)/shard_map/ppermute | solution.py:427
  552.3 130.6 %collective-permute-start.37 = (bf16[384,3072]{1,0:T(8,128)(2,1)}, bf16[384,3072]{1,0:T(8,128)(2,1)}, u32[]{:S(2)}, u32[]{:S(2)}) collective-permute-start(bf16[384,3072]{1,0:T(8,128)(2,1)} %pad_maximum_fusion.1), channel_id=1, source_target_pairs={{0,2},{2,0},{1,3},{3,1},{4,6},{6,4},{5,7},{7,5},{8,10},{10,8},{9,1... | collective-permute-start | bytes 7077896 | tf_op jit(solution)/shard_map/ppermute | solution.py:427
  555.7 32.0 %collective-permute-start.16 = (bf16[448,768]{1,0:T(8,128)(2,1)S(1)}, bf16[448,768]{1,0:T(8,128)(2,1)S(1)}, u32[]{:S(2)}, u32[]{:S(2)}) collective-permute-start(bf16[448,768]{1,0:T(8,128)(2,1)S(1)} %constant_dynamic-slice_fusion.7), channel_id=1, source_target_pairs={{0,4},{4,0},{1,5},{5,1},{2,6},{6,2},{3,7},{7,3},{8,12},{12,8},{9,1... | collective-permute-start | bytes 2064392 | tf_op jit(solution)/shard_map/ppermute | solution.py:422
  578.8 120.9 %collective-permute-start.42 = (bf16[1536,768]{1,0:T(8,128)(2,1)}, bf16[1536,768]{1,0:T(8,128)(2,1)}, u32[]{:S(2)}, u32[]{:S(2)}) collective-permute-start(bf16[1536,768]{1,0:T(8,128)(2,1)} %pad_maximum_fusion.2), channel_id=1, source_target_pairs={{0,2},{2,0},{1,3},{3,1},{4,6},{6,4},{5,7},{7,5},{8,10},{10,8},{9,1... | collective-permute-start | bytes 7077896 | tf_op jit(solution)/shard_map/ppermute | solution.py:427
  611.7 107.7 %all-to-all-start.3 = ((bf16[16,128,768]{2,1,0:T(8,128)(2,1)}), bf16[16,128,768]{2,1,0:T(8,128)(2,1)}, u32[]{:S(2)}, u32[]{:S(2)}) async-start(bf16[16,128,768]{2,1,0:T(8,128)(2,1)} %bitcast.74), calls=%async_computation.3 | async-start | bytes 6291456 | tf_op jit(solution)/shard_map/all_to_all | solution.py:492
  619.3 49.0 %collective-permute-start.29 = (bf16[112,768]{1,0:T(8,128)(2,1)S(1)}, bf16[112,768]{1,0:T(8,128)(2,1)S(1)}, u32[]{:S(2)}, u32[]{:S(2)}) collective-permute-start(bf16[112,768]{1,0:T(8,128)(2,1)S(1)} %pad_maximum_fusion.15), channel_id=1, source_target_pairs={{0,8},{8,0},{1,9},{9,1},{2,10},{10,2},{3,11},{11,3},{4,12},{12,4},... | collective-permute-start | bytes 516104 | tf_op jit(solution)/shard_map/ppermute | solution.py:427
  622.4 49.1 %collective-permute-start.21 = (bf16[112,768]{1,0:T(8,128)(2,1)S(1)}, bf16[112,768]{1,0:T(8,128)(2,1)S(1)}, u32[]{:S(2)}, u32[]{:S(2)}) collective-permute-start(bf16[112,768]{1,0:T(8,128)(2,1)S(1)} %pad_maximum_fusion.14), channel_id=1, source_target_pairs={{0,8},{8,0},{1,9},{9,1},{2,10},{10,2},{3,11},{11,3},{4,12},{12,4},... | collective-permute-start | bytes 516104 | tf_op jit(solution)/shard_map/ppermute | solution.py:427
  699.7 55.5 %collective-permute-start.32 = (bf16[1792,768]{1,0:T(8,128)(2,1)}, bf16[1792,768]{1,0:T(8,128)(2,1)}, u32[]{:S(2)}, u32[]{:S(2)}) collective-permute-start(bf16[1792,768]{1,0:T(8,128)(2,1)} %pad_maximum_fusion), channel_id=1, source_target_pairs={{0,2},{2,0},{1,3},{3,1},{4,6},{6,4},{5,7},{7,5},{8,10},{10,8},{9,1... | collective-permute-start | bytes 8257544 | tf_op jit(solution)/shard_map/ppermute | solution.py:427
  708.4 41.2 %collective-permute-start.14 = (bf16[576,768]{1,0:T(8,128)(2,1)}, bf16[576,768]{1,0:T(8,128)(2,1)}, u32[]{:S(2)}, u32[]{:S(2)}) collective-permute-start(bf16[576,768]{1,0:T(8,128)(2,1)} %fusion.32), channel_id=1, source_target_pairs={{0,16},{16,0},{1,17},{17,1},{2,18},{18,2},{3,19},{19,3},{4,20},{20... | collective-permute-start | bytes 2654216 | tf_op jit(solution)/shard_map/ppermute | solution.py:609
  (94 other events, 1291.9 us)

commit v3 on v2

--- a/solution.py
+++ b/solution.py
@@ -499,8 +499,8 @@
         lax.axis_index(top_axis), chosen, knowledge_ids.reshape(-1), rows_dev, capacity, devices
     )
     asked = exchange(requests.reshape(2, group, slots_all), 1).reshape(2, slots)
-    asked, gene_other, know_sum = lax.optimization_barrier((asked, gene_other, know_sum))
     know_other = lax.ppermute(know_sum, top_axis, SWAP)
+    asked, gene_other, know_other = lax.optimization_barrier((asked, gene_other, know_other))
     tables = [
         jnp.concatenate([gene_table, know_sum], axis=0),
         jnp.concatenate([gene_other, know_other], axis=0),
@@ -600,15 +600,12 @@
     owned = [row_at[:, None] == asked[part][None, :] for part in range(2)]
     counts = [jnp.sum(o.astype(jnp.int32), axis=1) for o in owned]
     row_counts = counts[0] + lax.ppermute(counts[1], top_axis, SWAP)
-    table_parts = [None, None]
     outgoing = [mm(hots, grad_low, TN).astype(BF16) for hots in slot_hots]
-    outgoing, ffn_grads, dq, dk, dv = lax.optimization_barrier((outgoing, ffn_grads, dq, dk, dv))
-    for part in (1, 0):
-        returned = exchange(outgoing[part].reshape(group, slots_all, width), 0).reshape(slots, width)
-        table_parts[part] = mm(owned[part].astype(BF16), returned)
-    table_grads = table_parts[0] + lax.ppermute(
-        table_parts[1].astype(BF16), top_axis, SWAP
-    ).astype(F32)
+    outgoing, dq, dk, dv = lax.optimization_barrier((outgoing, dq, dk, dv))
+    returned = [
+        exchange(rows.reshape(group, slots_all, width), 0).reshape(slots, width)
+        for rows in outgoing[::-1]
+    ][::-1]
 
     w_query_grad = mm(x_low, dq, TN)
     w_key_grad = mm(x_low, dk, TN) + mm(x_other, dk_other, TN)
@@ -617,46 +614,53 @@
     b_value_grad = jnp.sum(dv.astype(F32), axis=0) + jnp.sum(dv_other.astype(F32), axis=0)
     grad_rest = (grad_embedded - grad_low.astype(F32)).astype(BF16)
     expr_grad = mm(bin_hot, grad_low, TN) + mm(bin_hot, grad_rest, TN)
-    late = [
-        w_query_grad,
-        w_key_grad,
-        w_value_grad,
-        w_out_grad,
-        expr_grad,
-        b_query_grad[None, :],
-        b_value_grad[None, :],
-        jnp.sum(sums.reshape(6, 8, width), axis=1),
-        jnp.sum(up_sums, axis=0).reshape(wide // width, width),
-    ]
+    short = jnp.concatenate(
+        [
+            jnp.sum(sums.reshape(6, 8, width), axis=1),
+            jnp.sum(up_sums, axis=0).reshape(wide // width, width),
+            b_query_grad[None, :],
+            b_value_grad[None, :],
+        ],
+        axis=0,
+    )
+    short = jnp.pad(short, ((0, -short.shape[0] % 16), (0, 0)))
+    late = [w_query_grad, w_key_grad, w_value_grad, w_out_grad, expr_grad, short]
     heights = [item.shape[0] for item in late]
     late.append(jnp.zeros((-sum(heights) % 512, width), F32))
-    late = sum_everywhere(jnp.concatenate([item.astype(BF16) for item in late], axis=0), orders)
+    late = jnp.concatenate([item.astype(BF16) for item in late], axis=0)
+    returned, late, ffn_grads = lax.optimization_barrier((returned, late, ffn_grads))
+    table_parts = [mm(owned[part].astype(BF16), returned[part]) for part in range(2)]
+    table_grads = table_parts[0] + lax.ppermute(
+        table_parts[1].astype(BF16), top_axis, SWAP
+    ).astype(F32)
+    late = sum_everywhere(late, orders)
     w_down_grad, w_up_grad = (g.astype(F32) for g in doubled(ffn_grads, orders))
     taken = []
     for height in heights:
         at = sum(item.shape[0] for item in taken)
         taken.append(late[at : at + height].astype(F32))
-    w_query_grad, w_key_grad, w_value_grad, w_out_grad, *taken = taken
-    expr_grad, b_query_grad, b_value_grad, sums, b_up_grad = taken
+    w_query_grad, w_key_grad, w_value_grad, w_out_grad, expr_grad, short = taken
     gain_two_grad, shift_two_grad, b_down_grad, gain_one_grad, shift_one_grad, b_out_grad = (
-        sums[i] for i in range(6)
-    )
+        short[i] for i in range(6)
+    )
+    b_up_grad = short[6 : 6 + wide // width].reshape(wide)
+    b_query_grad, b_value_grad = short[6 + wide // width], short[7 + wide // width]
     return (
         layer_output.reshape(1, tokens, width),
         table_grads[:rows_dev],
         table_grads[rows_dev:],
         expr_grad,
         w_query_grad,
-        b_query_grad[0],
+        b_query_grad,
         w_key_grad,
         w_value_grad,
-        b_value_grad[0],
+        b_value_grad,
         w_out_grad,
         b_out_grad,
         gain_one_grad,
         shift_one_grad,
         w_up_grad,
-        b_up_grad.reshape(wide),
+        b_up_grad,
         w_down_grad,
         b_down_grad,
         gain_two_grad,

time: 777 us -> 746 us (0.960)
  blocking collectives: 0 us -> 56.1 us
  waiting for transfers between devices: 311 us -> 271 us
  local copies, waits for them, and re-layouts: 51.9 us -> 18.1 us
  other arithmetic: 62.4 us -> 49.6 us
    ppermute x19, waiting for transfers between devices: 149 us -> 90.7 us  [double(): other = lax.ppermute(value, axis, SWAP)]
    all_to_all x0 -> x2, blocking collectives: none -> 56.1 us  [exchange(): lax.all_to_all(value, group_axes, split_axis=axis, concat_axis=axis, tile...]
    ppermute x1, waiting for transfers between devices: 51.8 us -> 10.9 us  [local(): know_other = lax.ppermute(know_sum, top_axis, SWAP)]
    ppermute x1, waiting for transfers between devices: 2.05 us -> 39.5 us  [local(): row_counts = counts[0] + lax.ppermute(counts[1], top_axis, SWAP)]
    all_to_all x5 -> x3, waiting for transfers between devices: 42.3 us -> 73.5 us  [exchange(): lax.all_to_all(value, group_axes, split_axis=axis, concat_axis=axis, tile...]
    ppermute x1, waiting for transfers between devices: 30.1 us -> 0.01 us  [local(): lax.ppermute(table_parts[1].astype(BF16), top_axis, SWAP).astype(F32)]
    concatenate x1, local copies, waits for them, and re-layouts: 30.1 us -> 0.84 us  [local(): late = jnp.concatenate([item.astype(BF16) for item in late], axis=0)]
    ppermute x19, starting transfers between devices: 16.7 us -> 34.2 us  [double(): other = lax.ppermute(value, axis, SWAP)]
  transfers between devices with their start and end apart: 49 -> 47, of which waited for: 26 -> 29; matrix products, arithmetic and copies ran while one was open for 16% -> 11% of each run, Pallas kernels for 14% -> 15%
where the time goes in v3:
time: 746 us; the launch traced here: 740 us
  waiting for transfers between devices  271 us (36%)
  Pallas kernels  168 us (23%)
  matrix products  93 us (12%)
  starting transfers between devices  80.8 us (11%)
  blocking collectives  56.1 us (8%)
  other arithmetic  49.6 us (7%)
  local copies, waits for them, and re-layouts  18.1 us (2%)
    dot_general x29, matrix products, mm(): return lax.dot_general(left, right, dims, preferred_element_type=F32)  93 us
    ppermute x19, waiting for transfers between devices, double(): other = lax.ppermute(value, axis, SWAP)  90.7 us
    pallas_call x4, Pallas kernels, attend_back(): pl.pallas_call(functools.partial(attend_back_kernel, add, len(into)), gri...  83.7 us
    all_to_all x3, waiting for transfers between devices, exchange(): lax.all_to_all(value, group_axes, split_axis=axis, concat_axis=axis, tile...  73.5 us
    all_to_all x2, blocking collectives, exchange(): lax.all_to_all(value, group_axes, split_axis=axis, concat_axis=axis, tile...  56.1 us
    pallas_call x2, Pallas kernels, attend(): pl.pallas_call(functools.partial(attend_kernel, merge), grid_spec=pltpu.P...  43.5 us
    ppermute x1, waiting for transfers between devices, local(): row_counts = counts[0] + lax.ppermute(counts[1], top_axis, SWAP)  39.5 us
    pallas_call x1, Pallas kernels, middle(): pl.pallas_call(middle_kernel, grid=(tokens // block,), in_specs=[rows(wid...  37.5 us
  transfers between devices with their start and end apart: 47, of which 29 were waited for; matrix products, arithmetic and copies ran while one was open for 11% of the time, Pallas kernels for 15%

profile of v3, /device:TPU:0, one launch (start us, length us, event | category | flops | bytes accessed | tf_op | source)
XLA Modules:
  0.0 739.7 jit_solution(7297407129673693194)
XLA Ops:
  12.5 14.3 %all_to_all.25 = s32[2,16,128]{2,0,1:T(2,128)S(1)} all-to-all(s32[2,16,128]{2,0,1:T(2,128)S(1)} %copy.58), channel_id=1, replica_groups=mesh['dp0'=2,'dp1'=2,'dp2'=2,'dp3'=2,'seq'=2] {'dp1','dp2','dp3','seq'}, dimensions={1} | all-to-all | bytes 32768 | tf_op jit(solution)/shard_map/all_to_all | solution.py:492
  26.8 10.9 %collective-permute-done.1 = bf16[288,768]{1,0:T(8,128)(2,1)} collective-permute-done((bf16[288,768]{1,0:T(8,128)(2,1)}, bf16[288,768]{1,0:T(8,128)(2,1)}, u32[]{:S(2)}, u32[]{:S(2)}) %collective-permute-start.1) | collective-permute-done | bytes 442400 | tf_op jit(solution)/shard_map/ppermute | solution.py:502
  37.7 8.7 %collective-permute-done = bf16[288,768]{1,0:T(8,128)(2,1)} collective-permute-done((bf16[288,768]{1,0:T(8,128)(2,1)}, bf16[288,768]{1,0:T(8,128)(2,1)}, u32[]{:S(2)}, u32[]{:S(2)}) %collective-permute-start) | collective-permute-done | bytes 442400 | tf_op jit(solution)/shard_map/ppermute | solution.py:495
  61.4 38.2 %all-to-all-done.1 = bf16[16,128,768]{2,1,0:T(8,128)(2,1)} async-done(((bf16[16,128,768]{2,1,0:T(8,128)(2,1)}), bf16[16,128,768]{2,1,0:T(8,128)(2,1)}, u32[]{:S(2)}, u32[]{:S(2)}) %all-to-all-start.1) | async-done | bytes 3145760 | tf_op jit(solution)/shard_map/all_to_all | solution.py:492
  107.7 7.9 %fusion.5 = f32[1024,768]{1,0:T(8,128)} fusion(bf16[2048,768]{1,0:T(8,128)(2,1)} %bitcast.10, s32[1024]{0:T(1024)S(1)} %reduce.3, s32[1024]{0:T(1024)S(1)} %reduce.2), kind=kOutput, calls=%fused_computation.7 | convolution fusion | flops 3227516928 | bytes 6299648 | tf_op jit(solution)/shard_map/dot_general | solution.py:24
  115.6 35.3 %all-to-all-done.2 = bf16[16,128,768]{2,1,0:T(8,128)(2,1)} async-done(((bf16[16,128,768]{2,1,0:T(8,128)(2,1)}), bf16[16,128,768]{2,1,0:T(8,128)(2,1)}, u32[]{:S(2)}, u32[]{:S(2)}) %all-to-all-start.2) | async-done | bytes 3145760 | tf_op jit(solution)/shard_map/all_to_all | solution.py:492
  163.9 21.1 %attend.1 = (f32[768,1024]{1,0:T(8,128)}, f32[6,2,1024]{2,1,0:T(2,128)S(1)}) custom-call(s32[2]{0:T(128)S(1)} %pad_add_fusion.1.where_ref, bf16[1024,768]{1,0:T(8,128)(2,1)S(1)} %add_convert_fusion.3.q_ref, bf16[1024,768]{1,0:T(8,128)(2,1)S(1)} %convolution_convert_fusion.2.k_ref, bf16[1024,768]{1,0:T(8,128)(2,1)S(1)} %add_convert_fusion.1.v_ref), custom_call_target="tpu_custom_call" | custom-call | flops 12884901888 | bytes 15728640 | tf_op jit(solution)/shard_map/attend/pallas_call | solution.py:168
  185.1 10.2 %collective-permute-done.2 = bf16[1024,768]{1,0:T(8,128)(2,1)S(1)} collective-permute-done((bf16[1024,768]{1,0:T(8,128)(2,1)S(1)}, bf16[1024,768]{1,0:T(8,128)(2,1)S(1)}, u32[]{:S(2)}, u32[]{:S(2)}) %collective-permute-start.2) | collective-permute-done | bytes 1572896 | tf_op jit(solution)/shard_map/ppermute | solution.py:521
  198.1 22.4 %attend_more.1 = (f32[1024,768]{1,0:T(8,128)}, f32[6,2,1024]{2,1,0:T(2,128)S(1)}) custom-call(s32[2]{0:T(128)S(1)} %pad_add_fusion.where_ref, bf16[1024,768]{1,0:T(8,128)(2,1)S(1)} %add_convert_fusion.3.q_ref, bf16[1024,768]{1,0:T(8,128)(2,1)S(1)} %convolution_convert_fusion.3.k_ref, bf16[1024,768]{1,0:T(8,128)(2,1)S(1)} %add_convert_fusion.2.v_ref, ...), custom_call_target="tpu_custom_call" | custom-call | flops 12884901888 | bytes 15728640 | tf_op jit(solution)/shard_map/attend_more/pallas_call | solution.py:168
  221.1 37.5 %middle.1 = (bf16[1024,768]{1,0:T(8,128)(2,1)}, bf16[1024,768]{1,0:T(8,128)(2,1)}, bf16[1024,768]{1,0:T(8,128)(2,1)}, bf16[1024,3072]{1,0:T(8,128)(2,1)}, bf16[1...) custom-call(f32[1024,768]{1,0:T(8,128)} %get-tuple-element.132.ctx_r, ...), custom_call_target="tpu_custom_call" | custom-call | flops 43486543872 | bytes 34603008 | tf_op jit(solution)/shard_map/middle/pallas_call | solution.py:376
  258.6 9.3 %convolution_convert_fusion.1 = bf16[3072,768]{1,0:T(8,128)(2,1)} fusion(bf16[1024,3072]{1,0:T(8,128)(2,1)} %get-tuple-element.135, bf16[1024,768]{1,0:T(8,128)(2,1)} %get-tuple-element.136), kind=kOutput, calls=%fused_computation.13 | convolution fusion | flops 4834197504 | bytes 12582912 | tf_op jit(solution)/shard_map/dot_general | solution.py:24
  288.7 20.6 %attend_back0.1 = (f32[1024,768]{1,0:T(8,128)}, bf16[1024,768]{1,0:T(8,128)(2,1)}, bf16[1024,768]{1,0:T(8,128)(2,1)}) custom-call(s32[2]{0:T(128)} %copy-done.2, bf16[1024,768]{1,0:T(8,128)(2,1)} %copy-done.5, bf16[1024,768]{1,0:T(8,128)(2,1)} %get-tuple-element.190.g_ref, f32[1024,768]{1,0:T(8,128)} %get-tuple-element.132.ctx_ref.o_ref, ...), custom_call_target="tpu_custom_call" | custom-call | flops 16106127360 | bytes 9437184 | tf_op jit(solution)/shard_map/attend_back0/pallas_call | solution.py:248
  309.3 6.9 collective-permute-done.5
  319.4 20.9 %attend_back3.1 = (f32[1024,768]{1,0:T(8,128)}, bf16[1024,768]{1,0:T(8,128)(2,1)}, bf16[1024,768]{1,0:T(8,128)(2,1)}) custom-call(s32[2]{0:T(128)} %copy-done.2, bf16[1024,768]{1,0:T(8,128)(2,1)} %copy-done.5, bf16[1024,768]{1,0:T(8,128)(2,1)} %get-tuple-element.190.g_ref, ...), custom_call_target="tpu_custom_call", output_to_operand_aliasing={{0}: (7, {}), {1}: (8, {}), {2}: (9, {})} | custom-call | flops 16106127360 | bytes 9437184 | tf_op jit(solution)/shard_map/attend_back3/pallas_call | solution.py:248
  349.0 21.2 %attend_back_more0.1 = (bf16[1024,768]{1,0:T(8,128)(2,1)}, bf16[1024,768]{1,0:T(8,128)(2,1)}, bf16[1024,768]{1,0:T(8,128)(2,1)}) custom-call(s32[2]{0:T(128)} %copy-done.1, bf16[1024,768]{1,0:T(8,128)(2,1)} %copy-done.5, bf16[1024,768]{1,0:T(8,128)(2,1)} %get-tuple-element.190.g_ref, f32[1024,768]{1,0:T(8,128)} %get-tuple-element.132.ctx_ref.o_ref, ...), custom_call_target="tpu_custom_call" | custom-call | flops 16106127360 | bytes 9437184 | tf_op jit(solution)/shard_map/attend_back_more0/pallas_call | solution.py:248
  373.6 21.0 %attend_back_more3.1 = (bf16[1024,768]{1,0:T(8,128)(2,1)}, bf16[1024,768]{1,0:T(8,128)(2,1)}, bf16[1024,768]{1,0:T(8,128)(2,1)}) custom-call(s32[2]{0:T(128)} %copy-done.1, bf16[1024,768]{1,0:T(8,128)(2,1)} %copy-done.5, bf16[1024,768]{1,0:T(8,128)(2,1)} %get-tuple-element.190.g_ref, ...), custom_call_target="tpu_custom_call", output_to_operand_aliasing={{0}: (8, {}), {1}: (9, {}), {2}: (10, {})} | custom-call | flops 16106127360 | bytes 9437184 | tf_op jit(solution)/shard_map/attend_back_more3/pallas_call | solution.py:248
  408.1 6.8 fusion.23
  414.9 41.8 %all_to_all.26 = bf16[16,128,768]{2,1,0:T(8,128)(2,1)} all-to-all(bf16[16,128,768]{2,1,0:T(8,128)(2,1)S(1)} %bitcast.76), channel_id=1, replica_groups=mesh['dp0'=2,'dp1'=2,'dp2'=2,'dp3'=2,'seq'=2] {'dp1','dp2','dp3','seq'}, dimensions={0} | all-to-all | bytes 6291456 | tf_op jit(solution)/shard_map/all_to_all | solution.py:492
  465.4 39.5 %collective-permute-done.43 = s32[576]{0:T(1024)S(1)} collective-permute-done((s32[576]{0:T(1024)S(1)}, s32[576]{0:T(1024)S(1)}, u32[]{:S(2)}, u32[]{:S(2)}) %collective-permute-start.43) | collective-permute-done | bytes 2336 | tf_op jit(solution)/shard_map/ppermute | solution.py:602
  541.1 20.4 %collective-permute-start.34 = (bf16[48,3072]{1,0:T(8,128)(2,1)S(1)}, bf16[48,3072]{1,0:T(8,128)(2,1)S(1)}, u32[]{:S(2)}, u32[]{:S(2)}) collective-permute-start(bf16[48,3072]{1,0:T(8,128)(2,1)S(1)} %pad_maximum_fusion.12), channel_id=1, source_target_pairs={{0,8},{8,0},{1,9},{9,1},{2,10},{10,2},{3,11},{11,3},{4,12},{12,4},... | collective-permute-start | bytes 884744 | tf_op jit(solution)/shard_map/ppermute | solution.py:427
  564.7 24.4 %collective-permute-done.34 = bf16[48,3072]{1,0:T(8,128)(2,1)S(1)} collective-permute-done((bf16[48,3072]{1,0:T(8,128)(2,1)S(1)}, bf16[48,3072]{1,0:T(8,128)(2,1)S(1)}, u32[]{:S(2)}, u32[]{:S(2)}) %collective-permute-start.34) | collective-permute-done | bytes 294944 | tf_op jit(solution)/shard_map/ppermute | solution.py:427
  618.4 22.7 %collective-permute-done.41 = bf16[768,768]{1,0:T(8,128)(2,1)S(1)} collective-permute-done((bf16[768,768]{1,0:T(8,128)(2,1)S(1)}, bf16[768,768]{1,0:T(8,128)(2,1)S(1)}, u32[]{:S(2)}, u32[]{:S(2)}) %collective-permute-start.41) | collective-permute-done | bytes 1179680 | tf_op jit(solution)/shard_map/ppermute | solution.py:427
  641.7 9.1 %collective-permute-done.24 = bf16[448,768]{1,0:T(8,128)(2,1)S(1)} collective-permute-done((bf16[448,768]{1,0:T(8,128)(2,1)S(1)}, bf16[448,768]{1,0:T(8,128)(2,1)S(1)}, u32[]{:S(2)}, u32[]{:S(2)}) %collective-permute-start.24) | collective-permute-done | bytes 688160 | tf_op jit(solution)/shard_map/ppermute | solution.py:422
  704.4 6.6 collective-permute-done.31
  (344 shorter events, 258.5 us)
Async XLA Ops:
  3.4 34.3 %collective-permute-start.1 = (bf16[288,768]{1,0:T(8,128)(2,1)}, bf16[288,768]{1,0:T(8,128)(2,1)}, u32[]{:S(2)}, u32[]{:S(2)}) collective-permute-start(bf16[288,768]{1,0:T(8,128)(2,1)} %reduce_sum.75), channel_id=1, source_target_pairs={{0,16},{16,0},{1,17},{17,1},{2,18},{18,2},{3,19},{19,3},{4,20},{20... | collective-permute-start | bytes 1327112 | tf_op jit(solution)/shard_map/ppermute | solution.py:502
  7.4 38.9 %collective-permute-start = (bf16[288,768]{1,0:T(8,128)(2,1)}, bf16[288,768]{1,0:T(8,128)(2,1)}, u32[]{:S(2)}, u32[]{:S(2)}) collective-permute-start(bf16[288,768]{1,0:T(8,128)(2,1)} %param.31), channel_id=1, source_target_pairs={{0,16},{16,0},{1,17},{17,1},{2,18},{18,2},{3,19},{19,3},{4,20},{20... | collective-permute-start | bytes 1327112 | tf_op jit(solution)/shard_map/ppermute | solution.py:495
  51.6 48.0 %all-to-all-start.1 = ((bf16[16,128,768]{2,1,0:T(8,128)(2,1)}), bf16[16,128,768]{2,1,0:T(8,128)(2,1)}, u32[]{:S(2)}, u32[]{:S(2)}) async-start(bf16[16,128,768]{2,1,0:T(8,128)(2,1)} %bitcast.75), calls=%async_computation.1 | async-start | bytes 6291456 | tf_op jit(solution)/shard_map/all_to_all | solution.py:492
  99.7 51.2 %all-to-all-start.2 = ((bf16[16,128,768]{2,1,0:T(8,128)(2,1)}), bf16[16,128,768]{2,1,0:T(8,128)(2,1)}, u32[]{:S(2)}, u32[]{:S(2)}) async-start(bf16[16,128,768]{2,1,0:T(8,128)(2,1)} %bitcast.74), calls=%async_computation.2 | async-start | bytes 6291456 | tf_op jit(solution)/shard_map/all_to_all | solution.py:492
  159.0 36.2 %collective-permute-start.2 = (bf16[1024,768]{1,0:T(8,128)(2,1)S(1)}, bf16[1024,768]{1,0:T(8,128)(2,1)S(1)}, u32[]{:S(2)}, u32[]{:S(2)}) collective-permute-start(bf16[1024,768]{1,0:T(8,128)(2,1)S(1)} %get-tuple-element.298), channel_id=1, source_target_pairs={{0,1},{1,0},{2,3},{3,2},{4,5},{5,4},{6,7},{7,6},{8,9},{9,8},{10,11... | collective-permute-start | bytes 4718600 | tf_op jit(solution)/shard_map/ppermute | solution.py:521
  288.3 28.0 %collective-permute-start.5 = (bf16[768,768]{1,0:T(8,128)(2,1)S(1)}, bf16[768,768]{1,0:T(8,128)(2,1)S(1)}, u32[]{:S(2)}, u32[]{:S(2)}) collective-permute-start(bf16[768,768]{1,0:T(8,128)(2,1)S(1)} %get-tuple-element.144), channel_id=1, source_target_pairs={{0,4},{4,0},{1,5},{5,1},{2,6},{6,2},{3,7},{7,3},{8,12},{12,8},{9,1... | collective-permute-start | bytes 3538952 | tf_op jit(solution)/shard_map/ppermute | solution.py:565
  288.3 28.2 %collective-permute-start.6 = (bf16[192,3072]{1,0:T(8,128)(2,1)}, bf16[192,3072]{1,0:T(8,128)(2,1)S(1)}, u32[]{:S(2)}, u32[]{:S(2)}) collective-permute-start(bf16[192,3072]{1,0:T(8,128)(2,1)} %get-tuple-element.145), channel_id=1, source_target_pairs={{0,1},{1,0},{2,3},{3,2},{4,5},{5,4},{6,7},{7,6},{8,9},{9,8},{10,11... | collective-permute-start | bytes 3538952 | tf_op jit(solution)/shard_map/ppermute | solution.py:565
  317.4 22.9 %collective-permute-start.7 = (bf16[384,768]{1,0:T(8,128)(2,1)S(1)}, bf16[384,768]{1,0:T(8,128)(2,1)S(1)}, u32[]{:S(2)}, u32[]{:S(2)}) collective-permute-start(bf16[384,768]{1,0:T(8,128)(2,1)S(1)} %get-tuple-element.158), channel_id=1, source_target_pairs={{0,1},{1,0},{2,3},{3,2},{4,5},{5,4},{6,7},{7,6},{8,9},{9,8},{10,11... | collective-permute-start | bytes 1769480 | tf_op jit(solution)/shard_map/ppermute | solution.py:565
  345.1 25.1 %collective-permute-start.9 = (bf16[192,768]{1,0:T(8,128)(2,1)S(1)}, bf16[192,768]{1,0:T(8,128)(2,1)S(1)}, u32[]{:S(2)}, u32[]{:S(2)}) collective-permute-start(bf16[192,768]{1,0:T(8,128)(2,1)S(1)} %get-tuple-element.175), channel_id=1, source_target_pairs={{0,8},{8,0},{1,9},{9,1},{2,10},{10,2},{3,11},{11,3},{4,12},{12,4},... | collective-permute-start | bytes 884744 | tf_op jit(solution)/shard_map/ppermute | solution.py:565
  347.2 23.0 %collective-permute-start.10 = (bf16[48,3072]{1,0:T(8,128)(2,1)S(1)}, bf16[48,3072]{1,0:T(8,128)(2,1)S(1)}, u32[]{:S(2)}, u32[]{:S(2)}) collective-permute-start(bf16[48,3072]{1,0:T(8,128)(2,1)S(1)} %get-tuple-element.176), channel_id=1, source_target_pairs={{0,8},{8,0},{1,9},{9,1},{2,10},{10,2},{3,11},{11,3},{4,12},{12,4},... | collective-permute-start | bytes 884744 | tf_op jit(solution)/shard_map/ppermute | solution.py:565
  347.3 47.3 %collective-permute-start.13 = (bf16[1024,768]{1,0:T(8,128)(2,1)S(1)}, bf16[1024,768]{1,0:T(8,128)(2,1)S(1)}, u32[]{:S(2)}, u32[]{:S(2)}) collective-permute-start(bf16[1024,768]{1,0:T(8,128)(2,1)S(1)} %add_convert_fusion), channel_id=1, source_target_pairs={{0,1},{1,0},{2,3},{3,2},{4,5},{5,4},{6,7},{7,6},{8,9},{9,8},{10,11... | collective-permute-start | bytes 4718600 | tf_op jit(solution)/shard_map/ppermute | solution.py:586
  370.5 24.2 %collective-permute-start.11 = (bf16[96,768]{1,0:T(8,128)(2,1)S(1)}, bf16[96,768]{1,0:T(8,128)(2,1)S(1)}, u32[]{:S(2)}, u32[]{:S(2)}) collective-permute-start(bf16[96,768]{1,0:T(8,128)(2,1)S(1)} %get-tuple-element.188), channel_id=1, source_target_pairs={{0,16},{16,0},{1,17},{17,1},{2,18},{18,2},{3,19},{19,3},{4,20},{20... | collective-permute-start | bytes 442376 | tf_op jit(solution)/shard_map/ppermute | solution.py:565
  456.7 71.8 %all-to-all-start.3 = ((bf16[16,128,768]{2,1,0:T(8,128)(2,1)}), bf16[16,128,768]{2,1,0:T(8,128)(2,1)}, u32[]{:S(2)}, u32[]{:S(2)}) async-start(bf16[16,128,768]{2,1,0:T(8,128)(2,1)} %bitcast.73), calls=%async_computation.3 | async-start | bytes 6291456 | tf_op jit(solution)/shard_map/all_to_all | solution.py:492
  461.9 42.9 %collective-permute-start.43 = (s32[576]{0:T(1024)S(1)}, s32[576]{0:T(1024)S(1)}, u32[]{:S(2)}, u32[]{:S(2)}) collective-permute-start(s32[576]{0:T(1024)S(1)} %convert_reduce_fusion), channel_id=1, source_target_pairs={{0,16},{16,0},{1,17},{17,1},{2,18},{18,2},{3,19},{19,3},{4,20},{20... | collective-permute-start | bytes 6920 | tf_op jit(solution)/shard_map/ppermute | solution.py:602
  531.8 32.8 %collective-permute-start.38 = (bf16[96,768]{1,0:T(8,128)(2,1)S(1)}, bf16[96,768]{1,0:T(8,128)(2,1)S(1)}, u32[]{:S(2)}, u32[]{:S(2)}) collective-permute-start(bf16[96,768]{1,0:T(8,128)(2,1)S(1)} %add.296), channel_id=1, source_target_pairs={{0,16},{16,0},{1,17},{17,1},{2,18},{18,2},{3,19},{19,3},{4,20},{20... | collective-permute-start | bytes 442376 | tf_op jit(solution)/shard_map/ppermute | solution.py:427
  536.0 60.7 %collective-permute-start.14 = (bf16[576,768]{1,0:T(8,128)(2,1)S(1)}, bf16[576,768]{1,0:T(8,128)(2,1)S(1)}, u32[]{:S(2)}, u32[]{:S(2)}) collective-permute-start(bf16[576,768]{1,0:T(8,128)(2,1)S(1)} %fusion.36), channel_id=1, source_target_pairs={{0,16},{16,0},{1,17},{17,1},{2,18},{18,2},{3,19},{19,3},{4,20},{20... | collective-permute-start | bytes 2654216 | tf_op jit(solution)/shard_map/ppermute | solution.py:633
  541.0 71.2 %collective-permute-start.15 = (bf16[1792,768]{1,0:T(8,128)(2,1)S(1)}, bf16[1792,768]{1,0:T(8,128)(2,1)S(1)}, u32[]{:S(2)}, u32[]{:S(2)}) collective-permute-start(bf16[1792,768]{1,0:T(8,128)(2,1)S(1)} %constant_dynamic-slice_fusion.8), channel_id=1, source_target_pairs={{0,2},{2,0},{1,3},{3,1},{4,6},{6,4},{5,7},{7,5},{8,10},{10,8},{9,1... | collective-permute-start | bytes 8257544 | tf_op jit(solution)/shard_map/ppermute | solution.py:422
  541.1 48.0 %collective-permute-start.34 = (bf16[48,3072]{1,0:T(8,128)(2,1)S(1)}, bf16[48,3072]{1,0:T(8,128)(2,1)S(1)}, u32[]{:S(2)}, u32[]{:S(2)}) collective-permute-start(bf16[48,3072]{1,0:T(8,128)(2,1)S(1)} %pad_maximum_fusion.12), channel_id=1, source_target_pairs={{0,8},{8,0},{1,9},{9,1},{2,10},{10,2},{3,11},{11,3},{4,12},{12,4},... | collective-permute-start | bytes 884744 | tf_op jit(solution)/shard_map/ppermute | solution.py:427
  564.6 30.7 %collective-permute-start.39 = (bf16[192,768]{1,0:T(8,128)(2,1)S(1)}, bf16[192,768]{1,0:T(8,128)(2,1)S(1)}, u32[]{:S(2)}, u32[]{:S(2)}) collective-permute-start(bf16[192,768]{1,0:T(8,128)(2,1)S(1)} %pad_maximum_fusion.13), channel_id=1, source_target_pairs={{0,8},{8,0},{1,9},{9,1},{2,10},{10,2},{3,11},{11,3},{4,12},{12,4},... | collective-permute-start | bytes 884744 | tf_op jit(solution)/shard_map/ppermute | solution.py:427
  604.8 98.7 %collective-permute-start.36 = (bf16[192,3072]{1,0:T(8,128)(2,1)S(1)}, bf16[192,3072]{1,0:T(8,128)(2,1)S(1)}, u32[]{:S(2)}, u32[]{:S(2)}) collective-permute-start(bf16[192,3072]{1,0:T(8,128)(2,1)S(1)} %pad_maximum_fusion.4), channel_id=1, source_target_pairs={{0,1},{1,0},{2,3},{3,2},{4,5},{5,4},{6,7},{7,6},{8,9},{9,8},{10,11... | collective-permute-start | bytes 3538952 | tf_op jit(solution)/shard_map/ppermute | solution.py:427
  612.1 29.0 %collective-permute-start.41 = (bf16[768,768]{1,0:T(8,128)(2,1)S(1)}, bf16[768,768]{1,0:T(8,128)(2,1)S(1)}, u32[]{:S(2)}, u32[]{:S(2)}) collective-permute-start(bf16[768,768]{1,0:T(8,128)(2,1)S(1)} %pad_maximum_fusion.5), channel_id=1, source_target_pairs={{0,4},{4,0},{1,5},{5,1},{2,6},{6,2},{3,7},{7,3},{8,12},{12,8},{9,1... | collective-permute-start | bytes 3538952 | tf_op jit(solution)/shard_map/ppermute | solution.py:427
  615.0 35.8 %collective-permute-start.24 = (bf16[448,768]{1,0:T(8,128)(2,1)S(1)}, bf16[448,768]{1,0:T(8,128)(2,1)S(1)}, u32[]{:S(2)}, u32[]{:S(2)}) collective-permute-start(bf16[448,768]{1,0:T(8,128)(2,1)S(1)} %constant_dynamic-slice_fusion.3), channel_id=1, source_target_pairs={{0,1},{1,0},{2,3},{3,2},{4,5},{5,4},{6,7},{7,6},{8,9},{9,8},{10,11... | collective-permute-start | bytes 2064392 | tf_op jit(solution)/shard_map/ppermute | solution.py:422
  616.3 36.8 %collective-permute-start.16 = (bf16[448,768]{1,0:T(8,128)(2,1)S(1)}, bf16[448,768]{1,0:T(8,128)(2,1)S(1)}, u32[]{:S(2)}, u32[]{:S(2)}) collective-permute-start(bf16[448,768]{1,0:T(8,128)(2,1)S(1)} %constant_dynamic-slice_fusion.7), channel_id=1, source_target_pairs={{0,4},{4,0},{1,5},{5,1},{2,6},{6,2},{3,7},{7,3},{8,12},{12,8},{9,1... | collective-permute-start | bytes 2064392 | tf_op jit(solution)/shard_map/ppermute | solution.py:422
  641.7 74.7 %collective-permute-start.42 = (bf16[1536,768]{1,0:T(8,128)(2,1)S(1)}, bf16[1536,768]{1,0:T(8,128)(2,1)S(1)}, u32[]{:S(2)}, u32[]{:S(2)}) collective-permute-start(bf16[1536,768]{1,0:T(8,128)(2,1)S(1)} %pad_maximum_fusion.2), channel_id=1, source_target_pairs={{0,2},{2,0},{1,3},{3,1},{4,6},{6,4},{5,7},{7,5},{8,10},{10,8},{9,1... | collective-permute-start | bytes 7077896 | tf_op jit(solution)/shard_map/ppermute | solution.py:427
  (82 other events, 1059.5 us)

commit v4 on v3

--- a/solution.py
+++ b/solution.py
@@ -410,6 +410,47 @@
     )(ctx, embedded, cotangent, w_out, w_up, w_down, small, b_up)
 
 
+def weight_sums_kernel(counts, half_ref, act_ref, gffn_ref, gpre_ref, norm_ref, ctx_ref, gattn_ref, out_ref):
+    at = pl.program_id(0) + half_ref[0] * pl.num_programs(0)
+    first = 0
+    for count, left, right in zip(counts, (act_ref, gpre_ref, ctx_ref), (gffn_ref, norm_ref, gattn_ref)):
+        @pl.when((at >= first) & (at < first + count))
+        def _(left=left, right=right):
+            out_ref[...] = mm(left[...], right[...], TN).astype(BF16)
+        first += count
+
+
+def weight_sums(half, activated, grad_ffn, grad_pre, normed, ctx, grad_attn, block=384):
+    tokens, width = grad_ffn.shape
+    lefts = (activated, grad_pre, ctx)
+    counts = [left.shape[1] // block for left in lefts]
+    steps = sum(counts) // 2
+    specs = []
+    first = 0
+    for left, right, count in zip(lefts, (grad_ffn, normed, grad_attn), counts):
+        specs.append(
+            pl.BlockSpec(
+                (tokens, block),
+                lambda i, h, first=first, count=count: (0, jnp.clip(i + h[0] * steps - first, 0, count - 1)),
+            )
+        )
+        specs.append(pl.BlockSpec((tokens, width), lambda i, h: (0, 0), pipeline_mode=pl.Buffered(1)))
+        first += count
+    return pl.pallas_call(
+        functools.partial(weight_sums_kernel, counts),
+        grid_spec=pltpu.PrefetchScalarGridSpec(
+            num_scalar_prefetch=1,
+            grid=(steps,),
+            in_specs=specs,
+            out_specs=pl.BlockSpec((block, width), lambda i, h: (i, 0)),
+        ),
+        out_shape=jax.ShapeDtypeStruct((steps * block, width), BF16),
+        compiler_params=params(40),
+        cost_estimate=cost(2 * tokens * width * block * steps, 2 * steps * block * (tokens + width)),
+        name="weight_sums",
+    )(half.reshape(1), activated, grad_ffn, grad_pre, normed, ctx, grad_attn)
+
+
 def cut(value, axis):
     rows = value.shape[0] // 2
     me = lax.axis_index(axis)
@@ -417,34 +458,49 @@
     return keep, lax.dynamic_slice_in_dim(value, (1 - me) * rows, rows, 0)
 
 
-def halve(value, axis):
-    keep, send = cut(value, axis)
-    return keep + lax.ppermute(send, axis, SWAP)
-
-
-def double(value, axis):
+def swap(value, axis):
+    return lax.ppermute(value, axis, SWAP)
+
+
+def join(value, other, axis):
     first = lax.axis_index(axis) == 0
-    other = lax.ppermute(value, axis, SWAP)
     return jnp.concatenate([jnp.where(first, value, other), jnp.where(first, other, value)], axis=0)
 
 
-def orders_of(dp_axes):
-    core, near, far = dp_axes[-1], dp_axes[-2], dp_axes[-3::-1]
-    return (core, near, "seq", *far), (core, "seq", near, *far)
-
-
-def doubled(pieces, orders):
-    for step in reversed(range(len(orders[0]))):
-        pieces = [double(p, order[step]) for p, order in zip(pieces, orders)]
+def stages_of(dp_axes):
+    near, far = dp_axes[-2], dp_axes[-3::-1]
+    down = [((near, "seq"), True), (("seq", near), True)] + [((axis,), True) for axis in far]
+    return down + [(axes, False) for axes, _ in down[::-1]]
+
+
+def begin(pieces, stage):
+    axes, halves = stage
+    if len(pieces) < len(axes):
+        pieces = jnp.split(pieces[0], 2, axis=0)
+    if len(pieces) > len(axes):
+        pieces = [jnp.concatenate(pieces, axis=0)]
+    if halves:
+        keeps, sends = zip(*(cut(p, axis) for p, axis in zip(pieces, axes)))
+        return list(keeps), list(sends)
+    return list(pieces), list(pieces)
+
+
+def travel(sends, stage):
+    return [swap(s, axis) for s, axis in zip(sends, stage[0])]
+
+
+def end(keeps, arrived, stage):
+    axes, halves = stage
+    if halves:
+        return [k + a for k, a in zip(keeps, arrived)]
+    return [join(k, a, axis) for k, a, axis in zip(keeps, arrived, axes)]
+
+
+def run_stages(pieces, stages):
+    for stage in stages:
+        keeps, sends = begin(pieces, stage)
+        pieces = end(keeps, travel(sends, stage), stage)
     return pieces
-
-
-def sum_everywhere(value, orders):
-    pieces = jnp.split(halve(value, orders[0][0]), 2, axis=0)
-    for step in range(1, len(orders[0])):
-        pieces = [halve(p, order[step]) for p, order in zip(pieces, orders)]
-    pieces = doubled(pieces, [order[1:] for order in orders])
-    return double(jnp.concatenate(pieces, axis=0), orders[0][0])
 
 
 def local(
@@ -524,9 +580,13 @@
     value, value_other = ((mm(x, w_value) + b_value).astype(BF16) for x in (x_low, x_other))
     mine = jnp.stack([me * tokens, cell_lengths[0]]).astype(jnp.int32)
     others = jnp.stack([(1 - me) * tokens, cell_lengths[0]]).astype(jnp.int32)
-    context, lse = attend(
-        others, query, key_other, value_other, attend(mine, query, key, value)
-    )
+    owned = [row_at[:, None] == asked[part][None, :] for part in range(2)]
+    counts = [jnp.sum(o.astype(jnp.int32), axis=1) for o in owned]
+    counts_back = lax.ppermute(counts[1], top_axis, SWAP)
+    first_part = attend(mine, query, key, value)
+    first_part, counts_back = lax.optimization_barrier((first_part, counts_back))
+    row_counts = counts[0] + counts_back
+    context, lse = attend(others, query, key_other, value_other, first_part)
 
     small = jnp.stack([b_out, gain_one, shift_one, b_down, gain_two, shift_two])
     (
@@ -545,49 +605,49 @@
         context, embedded, cotangent.reshape(tokens, width), w_out, w_up, w_down, small, b_up[None, :]
     )
 
-    orders = orders_of(dp_axes)
-    step = 0
-    ffn_grads = [mm(activated, grad_ffn, TN).astype(BF16), mm(normed_low, grad_pre, TN).astype(BF16)]
-    ffn_grads, grad_ctx = lax.optimization_barrier((ffn_grads, grad_ctx))
-    w_out_grad = mm(ctx_low, grad_attn, TN)
-    ffn_grads = [halve(g, order[0]) for g, order in zip(ffn_grads, orders)]
+    core = dp_axes[-1]
+    stages = stages_of(dp_axes)
+    my_core = lax.axis_index(core)
+    lefts_rights = (activated, grad_ffn, grad_pre, normed_low, ctx_low, grad_attn)
+    sent = weight_sums(1 - my_core, *lefts_rights)
+    sent, lefts_rights = lax.optimization_barrier((sent, lefts_rights))
+    arrived = swap(sent, core)
+    kept = weight_sums(my_core, *lefts_rights)
+    kept, arrived, grad_ctx = lax.optimization_barrier((kept, arrived, grad_ctx))
+    early = jnp.split(kept + arrived, 2, axis=0)
     pairs = width // PAIR
+    third = pairs // 3
     sides = ((others, key_other, value_other), (mine, key, value))
+    parts = (((0, 2 * third), (2 * third, third)), ((0, third), (third, third), (2 * third, third)))
+    done = 0
     grads = []
     before = ()
-    dx_from_other = None
     for side, (place, keys, values) in enumerate(sides):
         into = ()
-        for part in range(2):
-            step += 1
-            cuts = [cut(g, order[step]) for g, order in zip(ffn_grads, orders)]
-            cuts, grad_ctx, into, before = lax.optimization_barrier((cuts, grad_ctx, into, before))
-            arrived = [lax.ppermute(c[1], order[step], SWAP) for c, order in zip(cuts, orders)]
+        for first, count in parts[side]:
+            keeps, sends = begin(early, stages[done])
+            keeps, sends, grad_ctx, into, before = lax.optimization_barrier(
+                (keeps, sends, grad_ctx, into, before)
+            )
+            came = travel(sends, stages[done])
             into = attend_back(
-                place,
-                query,
-                grad_ctx,
-                context,
-                lse,
-                keys,
-                values,
-                part * pairs // 2,
-                pairs // 2,
-                before,
-                into,
+                place, query, grad_ctx, context, lse, keys, values, first, count, before, into
             )
-            arrived, into = lax.optimization_barrier((arrived, into))
-            ffn_grads = [c[0] + a for c, a in zip(cuts, arrived)]
+            came, into = lax.optimization_barrier((came, into))
+            early = end(keeps, came, stages[done])
+            done += 1
         grads.append(into)
         if side == 0:
             before = into[:1]
             dx_other = (mm(into[1], w_key, NT) + mm(into[2], w_value, NT)).astype(BF16)
             dx_other, before = lax.optimization_barrier((dx_other, before))
-            dx_from_other = lax.ppermute(dx_other, "seq", SWAP)
-    for order_step in range(step + 1, len(orders[0])):
-        ffn_grads = [halve(g, order[order_step]) for g, order in zip(ffn_grads, orders)]
+            dx_from_other = swap(dx_other, "seq")
     (_, dk_other, dv_other), (dq, dk, dv) = grads
-    dq, dk, dv, dx_from_other = lax.optimization_barrier((dq, dk, dv, dx_from_other))
+    keeps, sends = begin(early, stages[done])
+    keeps, sends, dq, dk, dv, dx_from_other = lax.optimization_barrier(
+        (keeps, sends, dq, dk, dv, dx_from_other)
+    )
+    came = travel(sends, stages[done])
     grad_embedded = (
         grad_one
         + mm(dq, w_query, NT)
@@ -597,16 +657,15 @@
     )
     grad_low = grad_embedded.astype(BF16)
 
-    owned = [row_at[:, None] == asked[part][None, :] for part in range(2)]
-    counts = [jnp.sum(o.astype(jnp.int32), axis=1) for o in owned]
-    row_counts = counts[0] + lax.ppermute(counts[1], top_axis, SWAP)
     outgoing = [mm(hots, grad_low, TN).astype(BF16) for hots in slot_hots]
-    outgoing, dq, dk, dv = lax.optimization_barrier((outgoing, dq, dk, dv))
-    returned = [
-        exchange(rows.reshape(group, slots_all, width), 0).reshape(slots, width)
-        for rows in outgoing[::-1]
-    ][::-1]
-
+    outgoing, dq, dk, dv, came = lax.optimization_barrier((outgoing, dq, dk, dv, came))
+    early = end(keeps, came, stages[done])
+    done += 1
+
+    def give_back(rows):
+        return exchange(rows.reshape(group, slots_all, width), 0).reshape(slots, width)
+
+    returned_other = give_back(outgoing[1])
     w_query_grad = mm(x_low, dq, TN)
     w_key_grad = mm(x_low, dk, TN) + mm(x_other, dk_other, TN)
     w_value_grad = mm(x_low, dv, TN) + mm(x_other, dv_other, TN)
@@ -624,22 +683,36 @@
         axis=0,
     )
     short = jnp.pad(short, ((0, -short.shape[0] % 16), (0, 0)))
-    late = [w_query_grad, w_key_grad, w_value_grad, w_out_grad, expr_grad, short]
+    late = [w_query_grad, w_key_grad, w_value_grad, expr_grad, short]
     heights = [item.shape[0] for item in late]
     late.append(jnp.zeros((-sum(heights) % 512, width), F32))
     late = jnp.concatenate([item.astype(BF16) for item in late], axis=0)
-    returned, late, ffn_grads = lax.optimization_barrier((returned, late, ffn_grads))
-    table_parts = [mm(owned[part].astype(BF16), returned[part]) for part in range(2)]
-    table_grads = table_parts[0] + lax.ppermute(
-        table_parts[1].astype(BF16), top_axis, SWAP
-    ).astype(F32)
-    late = sum_everywhere(late, orders)
-    w_down_grad, w_up_grad = (g.astype(F32) for g in doubled(ffn_grads, orders))
+    keep, send = cut(late, core)
+    keep, send, outgoing, returned_other = lax.optimization_barrier(
+        (keep, send, outgoing, returned_other)
+    )
+    returned = give_back(outgoing[0])
+    from_other = swap(mm(owned[1].astype(BF16), returned_other).astype(BF16), top_axis)
+    late = jnp.split(keep + swap(send, core), 2, axis=0)
+    returned, late, early, from_other = lax.optimization_barrier((returned, late, early, from_other))
+    table_grads = mm(owned[0].astype(BF16), returned) + from_other.astype(F32)
+    early = run_stages(early, stages[done:])
+    early = jnp.concatenate(early, axis=0)
+    early = join(early, swap(early, core), core)
+    w_down_grad = early[:wide].astype(F32)
+    w_up_grad = early[wide : 2 * wide].T.astype(F32)
+    w_out_grad = early[2 * wide :].astype(F32)
+    late = run_stages(late, stages[:-2])
+    late, w_down_grad, w_up_grad, w_out_grad = lax.optimization_barrier(
+        (late, w_down_grad, w_up_grad, w_out_grad)
+    )
+    late = jnp.concatenate(run_stages(late, stages[-2:]), axis=0)
+    late = join(late, swap(late, core), core)
     taken = []
     for height in heights:
         at = sum(item.shape[0] for item in taken)
         taken.append(late[at : at + height].astype(F32))
-    w_query_grad, w_key_grad, w_value_grad, w_out_grad, expr_grad, short = taken
+    w_query_grad, w_key_grad, w_value_grad, expr_grad, short = taken
     gain_two_grad, shift_two_grad, b_down_grad, gain_one_grad, shift_one_grad, b_out_grad = (
         short[i] for i in range(6)
     )

time: 746 us -> 732 us (0.981)
  blocking collectives: 56.1 us -> 15 us
  Pallas kernels: 168 us -> 193 us
  local copies, waits for them, and re-layouts: 18.1 us -> 39.9 us
  starting transfers between devices: 80.8 us -> 59.8 us
  other arithmetic: 49.6 us -> 60.7 us
  matrix products: 93 us -> 81.9 us
    all_to_all x2 -> x1, blocking collectives: 56.1 us -> 15 us  [exchange(): lax.all_to_all(value, group_axes, split_axis=axis, concat_axis=axis, tile...]
    ppermute x41 -> x31, starting transfers between devices: 61.6 us -> 34.4 us  [the longest x30 31.4 us: swap(): return lax.ppermute(value, axis, SWAP)]
    pallas_call x0 -> x2, Pallas kernels: none -> 22 us  [weight_sums(): pl.pallas_call(functools.partial(weight_sums_kernel, counts), grid_spec=p...]
    unnamed x118 -> x153, local copies, waits for them, and re-layouts: 3.63 us -> 25.5 us
    all_to_all x3 -> x4, waiting for transfers between devices: 73.5 us -> 87.5 us  [exchange(): lax.all_to_all(value, group_axes, split_axis=axis, concat_axis=axis, tile...]
    ppermute x41 -> x31, waiting for transfers between devices: 167 us -> 154 us  [the longest x30 154 us: swap(): return lax.ppermute(value, axis, SWAP)]
    dot_general x29 -> x26, matrix products: 93 us -> 81.9 us  [mm(): return lax.dot_general(left, right, dims, preferred_element_type=F32)]
    all_to_all x3 -> x4, starting transfers between devices: 15.1 us -> 21.3 us  [exchange(): lax.all_to_all(value, group_axes, split_axis=axis, concat_axis=axis, tile...]
  transfers between devices with their start and end apart: 47 -> 38, of which waited for: 29 -> 24; matrix products, arithmetic and copies ran while one was open for 11% -> 15% of each run, Pallas kernels for 15% -> 17%
where the time goes in v4:
time: 732 us; the launch traced here: 725 us
  waiting for transfers between devices  271 us (37%)
  Pallas kernels  193 us (26%)
  matrix products  81.9 us (11%)
  other arithmetic  60.7 us (8%)
  starting transfers between devices  59.8 us (8%)
  local copies, waits for them, and re-layouts  39.9 us (5%)
  blocking collectives  15 us (2%)
    ppermute x30, waiting for transfers between devices, swap(): return lax.ppermute(value, axis, SWAP)  154 us
    all_to_all x4, waiting for transfers between devices, exchange(): lax.all_to_all(value, group_axes, split_axis=axis, concat_axis=axis, tile...  87.5 us
    pallas_call x5, Pallas kernels, attend_back(): pl.pallas_call(functools.partial(attend_back_kernel, add, len(into)), gri...  86.9 us
    dot_general x26, matrix products, mm(): return lax.dot_general(left, right, dims, preferred_element_type=F32)  81.9 us
    pallas_call x2, Pallas kernels, attend(): pl.pallas_call(functools.partial(attend_kernel, merge), grid_spec=pltpu.P...  43.5 us
    pallas_call x1, Pallas kernels, middle(): pl.pallas_call(middle_kernel, grid=(tokens // block,), in_specs=[rows(wid...  37.2 us
    ppermute x30, starting transfers between devices, swap(): return lax.ppermute(value, axis, SWAP)  31.4 us
    unnamed x153, local copies, waits for them, and re-layouts  25.5 us
  transfers between devices with their start and end apart: 38, of which 24 were waited for; matrix products, arithmetic and copies ran while one was open for 15% of the time, Pallas kernels for 17%

profile of v4, /device:TPU:0, one launch (start us, length us, event | category | flops | bytes accessed | tf_op | source)
XLA Modules:
  0.0 724.5 jit_solution(13393876245850009708)
XLA Ops:
  11.8 15.0 %all_to_all.25 = s32[2,16,128]{2,0,1:T(2,128)S(1)} all-to-all(s32[2,16,128]{2,0,1:T(2,128)S(1)} %copy.64), channel_id=1, replica_groups=mesh['dp0'=2,'dp1'=2,'dp2'=2,'dp3'=2,'seq'=2] {'dp1','dp2','dp3','seq'}, dimensions={1} | all-to-all | bytes 32768 | tf_op jit(solution)/shard_map/all_to_all | solution.py:548
  26.8 10.9 %collective-permute-done.1 = bf16[288,768]{1,0:T(8,128)(2,1)} collective-permute-done((bf16[288,768]{1,0:T(8,128)(2,1)}, bf16[288,768]{1,0:T(8,128)(2,1)}, u32[]{:S(2)}, u32[]{:S(2)}) %collective-permute-start.1) | collective-permute-done | bytes 442400 | tf_op jit(solution)/shard_map/ppermute | solution.py:558
  37.7 8.7 %collective-permute-done = bf16[288,768]{1,0:T(8,128)(2,1)} collective-permute-done((bf16[288,768]{1,0:T(8,128)(2,1)}, bf16[288,768]{1,0:T(8,128)(2,1)}, u32[]{:S(2)}, u32[]{:S(2)}) %collective-permute-start) | collective-permute-done | bytes 442400 | tf_op jit(solution)/shard_map/ppermute | solution.py:551
  61.4 38.2 %all-to-all-done.1 = bf16[16,128,768]{2,1,0:T(8,128)(2,1)} async-done(((bf16[16,128,768]{2,1,0:T(8,128)(2,1)}), bf16[16,128,768]{2,1,0:T(8,128)(2,1)}, u32[]{:S(2)}, u32[]{:S(2)}) %all-to-all-start.1) | async-done | bytes 3145760 | tf_op jit(solution)/shard_map/all_to_all | solution.py:548
  111.5 7.9 %fusion.5 = f32[1024,768]{1,0:T(8,128)} fusion(bf16[2048,768]{1,0:T(8,128)(2,1)} %bitcast.10, s32[1024]{0:T(1024)S(1)} %reduce.3, s32[1024]{0:T(1024)S(1)} %reduce.2), kind=kOutput, calls=%fused_computation.8 | convolution fusion | flops 3227516928 | bytes 6299648 | tf_op jit(solution)/shard_map/dot_general | solution.py:24
  119.3 31.6 %all-to-all-done.2 = bf16[16,128,768]{2,1,0:T(8,128)(2,1)} async-done(((bf16[16,128,768]{2,1,0:T(8,128)(2,1)}), bf16[16,128,768]{2,1,0:T(8,128)(2,1)}, u32[]{:S(2)}, u32[]{:S(2)}) %all-to-all-start.2) | async-done | bytes 3145760 | tf_op jit(solution)/shard_map/all_to_all | solution.py:548
  164.3 21.1 %attend.1 = (f32[768,1024]{1,0:T(8,128)}, f32[6,2,1024]{2,1,0:T(2,128)S(1)}) custom-call(s32[2]{0:T(128)S(1)} %pad_add_fusion.1.where_ref, bf16[1024,768]{1,0:T(8,128)(2,1)S(1)} %add_convert_fusion.3.q_ref, bf16[1024,768]{1,0:T(8,128)(2,1)S(1)} %convolution_convert_fusion.k_ref, bf16[1024,768]{1,0:T(8,128)(2,1)S(1)} %add_convert_fusion.1.v_ref), custom_call_target="tpu_custom_call" | custom-call | flops 12884901888 | bytes 15728640 | tf_op jit(solution)/shard_map/attend/pallas_call | solution.py:168
  185.5 9.8 %collective-permute-done.2 = bf16[1024,768]{1,0:T(8,128)(2,1)S(1)} collective-permute-done((bf16[1024,768]{1,0:T(8,128)(2,1)S(1)}, bf16[1024,768]{1,0:T(8,128)(2,1)S(1)}, u32[]{:S(2)}, u32[]{:S(2)}) %collective-permute-start.2) | collective-permute-done | bytes 1572896 | tf_op jit(solution)/shard_map/ppermute | solution.py:577
  198.2 22.4 %attend_more.1 = (f32[1024,768]{1,0:T(8,128)}, f32[6,2,1024]{2,1,0:T(2,128)S(1)}) custom-call(s32[2]{0:T(128)S(1)} %pad_add_fusion.where_ref, bf16[1024,768]{1,0:T(8,128)(2,1)S(1)} %add_convert_fusion.3.q_ref, bf16[1024,768]{1,0:T(8,128)(2,1)S(1)} %convolution_convert_fusion.1.k_ref, bf16[1024,768]{1,0:T(8,128)(2,1)S(1)} %add_convert_fusion.2.v_ref, ...), custom_call_target="tpu_custom_call" | custom-call | flops 12884901888 | bytes 15728640 | tf_op jit(solution)/shard_map/attend_more/pallas_call | solution.py:168
  221.2 37.2 %middle.1 = (bf16[1024,768]{1,0:T(8,128)(2,1)}, bf16[1024,768]{1,0:T(8,128)(2,1)}, bf16[1024,768]{1,0:T(8,128)(2,1)}, bf16[1024,3072]{1,0:T(8,128)(2,1)}, bf16[1...) custom-call(f32[1024,768]{1,0:T(8,128)} %get-tuple-element.163.ctx_r, ...), custom_call_target="tpu_custom_call" | custom-call | flops 43486543872 | bytes 34603008 | tf_op jit(solution)/shard_map/middle/pallas_call | solution.py:376
  264.1 11.7 %weight_sums.2 = bf16[3456,768]{1,0:T(8,128)(2,1)} custom-call(s32[1]{0:T(128)} %bitcast.19.half_ref, bf16[1024,3072]{1,0:T(8,128)(2,1)} %get-tuple-element.172.act_ref, bf16[1024,768]{1,0:T(8,128)(2,1)S(1)} %copy-done.5, bf16[1024,3072]{1,0:T(8,128)(2,1)} %get-tuple-element.174.gpre_ref, bf16[1024,768]{1,0:T(8,128)(2,1)S(1)} %copy-done.3, ...), custom_call_target="tpu_custom_call" | custom-call | flops 5435817984 | bytes 12386304 | tf_op jit(solution)/shard_map/weight_sums/pallas_call | solution.py:439
  280.0 10.4 %weight_sums.3 = bf16[3456,768]{1,0:T(8,128)(2,1)S(1)} custom-call(s32[1]{0:T(128)} %bitcast.18.half_ref, bf16[1024,3072]{1,0:T(8,128)(2,1)} %get-tuple-element.172.act_ref, bf16[1024,768]{1,0:T(8,128)(2,1)S(1)} %copy-done.6, bf16[1024,3072]{1,0:T(8,128)(2,1)} %get-tuple-element.174.gpre_ref, bf16[1024,768]{1,0:T(8,128)(2,1)S(1)} %copy-done.4, ...), custom_call_target="tpu_custom_call" | custom-call | flops 5435817984 | bytes 12386304 | tf_op jit(solution)/shard_map/weight_sums/pallas_call | solution.py:439
  296.7 26.5 %attend_back0.1 = (f32[1024,768]{1,0:T(8,128)}, bf16[1024,768]{1,0:T(8,128)(2,1)}, bf16[1024,768]{1,0:T(8,128)(2,1)}) custom-call(s32[2]{0:T(128)} %copy-done.10, bf16[1024,768]{1,0:T(8,128)(2,1)} %copy-done.13, bf16[1024,768]{1,0:T(8,128)(2,1)} %get-tuple-element.241.g_ref, f32[1024,768]{1,0:T(8,128)} %get-tuple-element.163.ctx_ref.o_ref, ...), custom_call_target="tpu_custom_call" | custom-call | flops 21474836480 | bytes 12582912 | tf_op jit(solution)/shard_map/attend_back0/pallas_call | solution.py:248
  330.4 15.1 %attend_back4.1 = (f32[1024,768]{1,0:T(8,128)}, bf16[1024,768]{1,0:T(8,128)(2,1)}, bf16[1024,768]{1,0:T(8,128)(2,1)}) custom-call(s32[2]{0:T(128)} %copy-done.10, bf16[1024,768]{1,0:T(8,128)(2,1)} %copy-done.13, bf16[1024,768]{1,0:T(8,128)(2,1)} %get-tuple-element.241.g_ref, ...), custom_call_target="tpu_custom_call", output_to_operand_aliasing={{0}: (7, {}), {1}: (8, {}), {2}: (9, {})} | custom-call | flops 10737418240 | bytes 6291456 | tf_op jit(solution)/shard_map/attend_back4/pallas_call | solution.py:248
  354.6 15.0 %attend_back_more0.1 = (bf16[1024,768]{1,0:T(8,128)(2,1)}, bf16[1024,768]{1,0:T(8,128)(2,1)}, bf16[1024,768]{1,0:T(8,128)(2,1)}) custom-call(s32[2]{0:T(128)} %copy-done.9, bf16[1024,768]{1,0:T(8,128)(2,1)} %copy-done.13, bf16[1024,768]{1,0:T(8,128)(2,1)} %get-tuple-element.241.g_ref, f32[1024,768]{1,0:T(8,128)} %get-tuple-element.163.ctx_ref.o_ref, ...), custom_call_target="tpu_custom_call" | custom-call | flops 10737418240 | bytes 6291456 | tf_op jit(solution)/shard_map/attend_back_more0/pallas_call | solution.py:248
  373.0 14.9 %attend_back_more2.1 = (bf16[1024,768]{1,0:T(8,128)(2,1)}, bf16[1024,768]{1,0:T(8,128)(2,1)}, bf16[1024,768]{1,0:T(8,128)(2,1)}) custom-call(s32[2]{0:T(128)} %copy-done.9, bf16[1024,768]{1,0:T(8,128)(2,1)} %copy-done.13, bf16[1024,768]{1,0:T(8,128)(2,1)} %get-tuple-element.241.g_ref, ...), custom_call_target="tpu_custom_call", output_to_operand_aliasing={{0}: (8, {}), {1}: (9, {}), {2}: (10, {})} | custom-call | flops 10737418240 | bytes 6291456 | tf_op jit(solution)/shard_map/attend_back_more2/pallas_call | solution.py:248
  388.1 15.2 %attend_back_more4.1 = (bf16[1024,768]{1,0:T(8,128)(2,1)}, bf16[1024,768]{1,0:T(8,128)(2,1)}, bf16[1024,768]{1,0:T(8,128)(2,1)}) custom-call(s32[2]{0:T(128)} %copy-done.9, bf16[1024,768]{1,0:T(8,128)(2,1)} %copy-done.13, bf16[1024,768]{1,0:T(8,128)(2,1)} %get-tuple-element.241.g_ref, ...), custom_call_target="tpu_custom_call", output_to_operand_aliasing={{0}: (8, {}), {1}: (9, {}), {2}: (10, {})} | custom-call | flops 10737418240 | bytes 6291456 | tf_op jit(solution)/shard_map/attend_back_more4/pallas_call | solution.py:248
  458.2 17.7 %all-to-all-done.3 = bf16[16,128,768]{2,1,0:T(8,128)(2,1)} async-done(((bf16[16,128,768]{2,1,0:T(8,128)(2,1)}), bf16[16,128,768]{2,1,0:T(8,128)(2,1)}, u32[]{:S(2)}, u32[]{:S(2)}) %all-to-all-start.3) | async-done | bytes 3145760 | tf_op jit(solution)/shard_map/all_to_all | solution.py:548
  495.3 50.9 %collective-permute-done.15 = bf16[576,768]{1,0:T(8,128)(2,1)} collective-permute-done((bf16[576,768]{1,0:T(8,128)(2,1)}, bf16[576,768]{1,0:T(8,128)(2,1)}, u32[]{:S(2)}, u32[]{:S(2)}) %collective-permute-start.15) | collective-permute-done | bytes 884768 | tf_op jit(solution)/shard_map/ppermute | solution.py:462
  547.4 17.0 %collective-permute-done.24 = bf16[432,768]{1,0:T(8,128)(2,1)} collective-permute-done((bf16[432,768]{1,0:T(8,128)(2,1)}, bf16[432,768]{1,0:T(8,128)(2,1)}, u32[]{:S(2)}, u32[]{:S(2)}) %collective-permute-start.24) | collective-permute-done | bytes 663584 | tf_op jit(solution)/shard_map/ppermute | solution.py:462
  568.8 28.3 %collective-permute-done.27 = bf16[864,768]{1,0:T(8,128)(2,1)S(1)} collective-permute-done((bf16[864,768]{1,0:T(8,128)(2,1)S(1)}, bf16[864,768]{1,0:T(8,128)(2,1)S(1)}, u32[]{:S(2)}, u32[]{:S(2)}) %collective-permute-start.27) | collective-permute-done | bytes 1327136 | tf_op jit(solution)/shard_map/ppermute | solution.py:462
  607.1 10.5 %collective-permute-done.18 = bf16[320,768]{1,0:T(8,128)(2,1)} collective-permute-done((bf16[320,768]{1,0:T(8,128)(2,1)}, bf16[320,768]{1,0:T(8,128)(2,1)}, u32[]{:S(2)}, u32[]{:S(2)}) %collective-permute-start.18) | collective-permute-done | bytes 491552 | tf_op jit(solution)/shard_map/ppermute | solution.py:462
  666.3 10.2 %convert_bitcast_fusion = (f32[768,3072]{0,1:T(8,128)}, f32[3072,768]{1,0:T(8,128)}) fusion(bf16[3456,768]{1,0:T(8,128)(2,1)S(1)} %get-tuple-element.372, bf16[3456,768]{1,0:T(8,128)(2,1)S(1)} %get-tuple-element.373), kind=kLoop, calls=%fused_computation | loop fusion | flops 11796480 | bytes 34209792 | tf_op jit(solution)/shard_map/convert_element_type | solution.py:703
  704.5 9.6 %copy.65 = f32[768,3072]{1,0:T(8,128)} copy(f32[768,3072]{0,1:T(8,128)} %get-tuple-element.355) | data formatting | bytes 18874368
  (338 shorter events, 265.0 us)
Async XLA Ops:
  3.4 34.3 %collective-permute-start.1 = (bf16[288,768]{1,0:T(8,128)(2,1)}, bf16[288,768]{1,0:T(8,128)(2,1)}, u32[]{:S(2)}, u32[]{:S(2)}) collective-permute-start(bf16[288,768]{1,0:T(8,128)(2,1)} %reduce_sum.75), channel_id=1, source_target_pairs={{0,16},{16,0},{1,17},{17,1},{2,18},{18,2},{3,19},{19,3},{4,20},{20... | collective-permute-start | bytes 1327112 | tf_op jit(solution)/shard_map/ppermute | solution.py:558
  7.4 38.9 %collective-permute-start = (bf16[288,768]{1,0:T(8,128)(2,1)}, bf16[288,768]{1,0:T(8,128)(2,1)}, u32[]{:S(2)}, u32[]{:S(2)}) collective-permute-start(bf16[288,768]{1,0:T(8,128)(2,1)} %param.31), channel_id=1, source_target_pairs={{0,16},{16,0},{1,17},{17,1},{2,18},{18,2},{3,19},{19,3},{4,20},{20... | collective-permute-start | bytes 1327112 | tf_op jit(solution)/shard_map/ppermute | solution.py:551
  51.7 48.0 %all-to-all-start.1 = ((bf16[16,128,768]{2,1,0:T(8,128)(2,1)}), bf16[16,128,768]{2,1,0:T(8,128)(2,1)}, u32[]{:S(2)}, u32[]{:S(2)}) async-start(bf16[16,128,768]{2,1,0:T(8,128)(2,1)} %bitcast.71), calls=%async_computation.1 | async-start | bytes 6291456 | tf_op jit(solution)/shard_map/all_to_all | solution.py:548
  99.7 51.3 %all-to-all-start.2 = ((bf16[16,128,768]{2,1,0:T(8,128)(2,1)}), bf16[16,128,768]{2,1,0:T(8,128)(2,1)}, u32[]{:S(2)}, u32[]{:S(2)}) async-start(bf16[16,128,768]{2,1,0:T(8,128)(2,1)} %bitcast.70), calls=%async_computation.2 | async-start | bytes 6291456 | tf_op jit(solution)/shard_map/all_to_all | solution.py:548
  108.4 77.0 %collective-permute-start.3 = (s32[576]{0:T(1024)S(1)}, s32[576]{0:T(1024)S(1)}, u32[]{:S(2)}, u32[]{:S(2)}) collective-permute-start(s32[576]{0:T(1024)S(1)} %convert_reduce_fusion.1), channel_id=1, source_target_pairs={{0,16},{16,0},{1,17},{17,1},{2,18},{18,2},{3,19},{19,3},{4,20},{20... | collective-permute-start | bytes 6920 | tf_op jit(solution)/shard_map/ppermute | solution.py:585
  159.1 36.2 %collective-permute-start.2 = (bf16[1024,768]{1,0:T(8,128)(2,1)S(1)}, bf16[1024,768]{1,0:T(8,128)(2,1)S(1)}, u32[]{:S(2)}, u32[]{:S(2)}) collective-permute-start(bf16[1024,768]{1,0:T(8,128)(2,1)S(1)} %get-tuple-element.435), channel_id=1, source_target_pairs={{0,1},{1,0},{2,3},{3,2},{4,5},{5,4},{6,7},{7,6},{8,9},{9,8},{10,11... | collective-permute-start | bytes 4718600 | tf_op jit(solution)/shard_map/ppermute | solution.py:577
  296.0 31.7 %collective-permute-start.5 = (bf16[864,768]{1,0:T(8,128)(2,1)}, bf16[864,768]{1,0:T(8,128)(2,1)S(1)}, u32[]{:S(2)}, u32[]{:S(2)}) collective-permute-start(bf16[864,768]{1,0:T(8,128)(2,1)} %get-tuple-element.184), channel_id=1, source_target_pairs={{0,4},{4,0},{1,5},{5,1},{2,6},{6,2},{3,7},{7,3},{8,12},{12,8},{9,1... | collective-permute-start | bytes 3981320 | tf_op jit(solution)/shard_map/ppermute | solution.py:462
  296.3 31.4 %collective-permute-start.6 = (bf16[864,768]{1,0:T(8,128)(2,1)S(1)}, bf16[864,768]{1,0:T(8,128)(2,1)S(1)}, u32[]{:S(2)}, u32[]{:S(2)}) collective-permute-start(bf16[864,768]{1,0:T(8,128)(2,1)S(1)} %get-tuple-element.185), channel_id=1, source_target_pairs={{0,1},{1,0},{2,3},{3,2},{4,5},{5,4},{6,7},{7,6},{8,9},{9,8},{10,11... | collective-permute-start | bytes 3981320 | tf_op jit(solution)/shard_map/ppermute | solution.py:462
  328.5 17.0 %collective-permute-start.7 = (bf16[432,768]{1,0:T(8,128)(2,1)S(1)}, bf16[432,768]{1,0:T(8,128)(2,1)S(1)}, u32[]{:S(2)}, u32[]{:S(2)}) collective-permute-start(bf16[432,768]{1,0:T(8,128)(2,1)S(1)} %get-tuple-element.198), channel_id=1, source_target_pairs={{0,1},{1,0},{2,3},{3,2},{4,5},{5,4},{6,7},{7,6},{8,9},{9,8},{10,11... | collective-permute-start | bytes 1990664 | tf_op jit(solution)/shard_map/ppermute | solution.py:462
  328.9 16.7 %collective-permute-start.8 = (bf16[432,768]{1,0:T(8,128)(2,1)S(1)}, bf16[432,768]{1,0:T(8,128)(2,1)S(1)}, u32[]{:S(2)}, u32[]{:S(2)}) collective-permute-start(bf16[432,768]{1,0:T(8,128)(2,1)S(1)} %get-tuple-element.199), channel_id=1, source_target_pairs={{0,4},{4,0},{1,5},{5,1},{2,6},{6,2},{3,7},{7,3},{8,12},{12,8},{9,1... | collective-permute-start | bytes 1990664 | tf_op jit(solution)/shard_map/ppermute | solution.py:462
  352.2 17.4 %collective-permute-start.9 = (bf16[432,768]{1,0:T(8,128)(2,1)S(1)}, bf16[432,768]{1,0:T(8,128)(2,1)S(1)}, u32[]{:S(2)}, u32[]{:S(2)}) collective-permute-start(bf16[432,768]{1,0:T(8,128)(2,1)S(1)} %get-tuple-element.215), channel_id=1, source_target_pairs={{0,8},{8,0},{1,9},{9,1},{2,10},{10,2},{3,11},{11,3},{4,12},{12,4},... | collective-permute-start | bytes 1990664 | tf_op jit(solution)/shard_map/ppermute | solution.py:462
  354.3 49.7 %collective-permute-start.12 = (bf16[1024,768]{1,0:T(8,128)(2,1)S(1)}, bf16[1024,768]{1,0:T(8,128)(2,1)S(1)}, u32[]{:S(2)}, u32[]{:S(2)}) collective-permute-start(bf16[1024,768]{1,0:T(8,128)(2,1)S(1)} %add_convert_fusion), channel_id=1, source_target_pairs={{0,1},{1,0},{2,3},{3,2},{4,5},{5,4},{6,7},{7,6},{8,9},{9,8},{10,11... | collective-permute-start | bytes 4718600 | tf_op jit(solution)/shard_map/ppermute | solution.py:462
  369.9 18.0 %collective-permute-start.10 = (bf16[216,768]{1,0:T(8,128)(2,1)S(1)}, bf16[216,768]{1,0:T(8,128)(2,1)S(1)}, u32[]{:S(2)}, u32[]{:S(2)}) collective-permute-start(bf16[216,768]{1,0:T(8,128)(2,1)S(1)} %get-tuple-element.226), channel_id=1, source_target_pairs={{0,16},{16,0},{1,17},{17,1},{2,18},{18,2},{3,19},{19,3},{4,20},{20... | collective-permute-start | bytes 995336 | tf_op jit(solution)/shard_map/ppermute | solution.py:462
  404.0 23.8 %collective-permute-start.13 = (bf16[432,768]{1,0:T(8,128)(2,1)S(1)}, bf16[432,768]{1,0:T(8,128)(2,1)}, u32[]{:S(2)}, u32[]{:S(2)}) collective-permute-start(bf16[432,768]{1,0:T(8,128)(2,1)S(1)} %pad_maximum_fusion.7), channel_id=1, source_target_pairs={{0,8},{8,0},{1,9},{9,1},{2,10},{10,2},{3,11},{11,3},{4,12},{12,4},... | collective-permute-start | bytes 1990664 | tf_op jit(solution)/shard_map/ppermute | solution.py:462
  427.8 48.1 %all-to-all-start.3 = ((bf16[16,128,768]{2,1,0:T(8,128)(2,1)}), bf16[16,128,768]{2,1,0:T(8,128)(2,1)}, u32[]{:S(2)}, u32[]{:S(2)}) async-start(bf16[16,128,768]{2,1,0:T(8,128)(2,1)} %bitcast.69), calls=%async_computation.3 | async-start | bytes 6291456 | tf_op jit(solution)/shard_map/all_to_all | solution.py:548
  475.9 70.3 %all-to-all-start.4 = ((bf16[16,128,768]{2,1,0:T(8,128)(2,1)}), bf16[16,128,768]{2,1,0:T(8,128)(2,1)}, u32[]{:S(2)}, u32[]{:S(2)}) async-start(bf16[16,128,768]{2,1,0:T(8,128)(2,1)} %bitcast.68), calls=%async_computation.4 | async-start | bytes 6291456 | tf_op jit(solution)/shard_map/all_to_all | solution.py:548
  487.5 58.8 %collective-permute-start.15 = (bf16[576,768]{1,0:T(8,128)(2,1)}, bf16[576,768]{1,0:T(8,128)(2,1)}, u32[]{:S(2)}, u32[]{:S(2)}) collective-permute-start(bf16[576,768]{1,0:T(8,128)(2,1)} %fusion.35), channel_id=1, source_target_pairs={{0,16},{16,0},{1,17},{17,1},{2,18},{18,2},{3,19},{19,3},{4,20},{20... | collective-permute-start | bytes 2654216 | tf_op jit(solution)/shard_map/ppermute | solution.py:462
  547.4 17.0 %collective-permute-start.24 = (bf16[432,768]{1,0:T(8,128)(2,1)}, bf16[432,768]{1,0:T(8,128)(2,1)}, u32[]{:S(2)}, u32[]{:S(2)}) collective-permute-start(bf16[432,768]{1,0:T(8,128)(2,1)} %get-tuple-element.403), channel_id=1, source_target_pairs={{0,1},{1,0},{2,3},{3,2},{4,5},{5,4},{6,7},{7,6},{8,9},{9,8},{10,11... | collective-permute-start | bytes 1990664 | tf_op jit(solution)/shard_map/ppermute | solution.py:462
  547.4 17.4 %collective-permute-start.26 = (bf16[432,768]{1,0:T(8,128)(2,1)}, bf16[432,768]{1,0:T(8,128)(2,1)}, u32[]{:S(2)}, u32[]{:S(2)}) collective-permute-start(bf16[432,768]{1,0:T(8,128)(2,1)} %get-tuple-element.404), channel_id=1, source_target_pairs={{0,4},{4,0},{1,5},{5,1},{2,6},{6,2},{3,7},{7,3},{8,12},{12,8},{9,1... | collective-permute-start | bytes 1990664 | tf_op jit(solution)/shard_map/ppermute | solution.py:462
  566.4 30.6 %collective-permute-start.27 = (bf16[864,768]{1,0:T(8,128)(2,1)S(1)}, bf16[864,768]{1,0:T(8,128)(2,1)S(1)}, u32[]{:S(2)}, u32[]{:S(2)}) collective-permute-start(bf16[864,768]{1,0:T(8,128)(2,1)S(1)} %pad_maximum_fusion.5), channel_id=1, source_target_pairs={{0,1},{1,0},{2,3},{3,2},{4,5},{5,4},{6,7},{7,6},{8,9},{9,8},{10,11... | collective-permute-start | bytes 3981320 | tf_op jit(solution)/shard_map/ppermute | solution.py:462
  568.1 30.1 %collective-permute-start.25 = (bf16[864,768]{1,0:T(8,128)(2,1)S(1)}, bf16[864,768]{1,0:T(8,128)(2,1)S(1)}, u32[]{:S(2)}, u32[]{:S(2)}) collective-permute-start(bf16[864,768]{1,0:T(8,128)(2,1)S(1)} %pad_maximum_fusion.4), channel_id=1, source_target_pairs={{0,4},{4,0},{1,5},{5,1},{2,6},{6,2},{3,7},{7,3},{8,12},{12,8},{9,1... | collective-permute-start | bytes 3981320 | tf_op jit(solution)/shard_map/ppermute | solution.py:462
  601.9 57.9 %collective-permute-start.28 = (bf16[3456,768]{1,0:T(8,128)(2,1)}, bf16[3456,768]{1,0:T(8,128)(2,1)}, u32[]{:S(2)}, u32[]{:S(2)}) collective-permute-start(bf16[3456,768]{1,0:T(8,128)(2,1)} %pad_maximum_fusion), channel_id=1, source_target_pairs={{0,2},{2,0},{1,3},{3,1},{4,6},{6,4},{5,7},{7,5},{8,10},{10,8},{9,1... | collective-permute-start | bytes 15925256 | tf_op jit(solution)/shard_map/ppermute | solution.py:462
  605.3 16.2 %collective-permute-start.16 = (bf16[320,768]{1,0:T(8,128)(2,1)}, bf16[320,768]{1,0:T(8,128)(2,1)}, u32[]{:S(2)}, u32[]{:S(2)}) collective-permute-start(bf16[320,768]{1,0:T(8,128)(2,1)} %constant_dynamic-slice_fusion.4), channel_id=1, source_target_pairs={{0,4},{4,0},{1,5},{5,1},{2,6},{6,2},{3,7},{7,3},{8,12},{12,8},{9,1... | collective-permute-start | bytes 1474568 | tf_op jit(solution)/shard_map/ppermute | solution.py:462
  697.7 16.4 %collective-permute-start.33 = (bf16[1280,768]{1,0:T(8,128)(2,1)S(1)}, bf16[1280,768]{1,0:T(8,128)(2,1)}, u32[]{:S(2)}, u32[]{:S(2)}) collective-permute-start(bf16[1280,768]{1,0:T(8,128)(2,1)S(1)} %pad_maximum_fusion.2), channel_id=1, source_target_pairs={{0,2},{2,0},{1,3},{3,1},{4,6},{6,4},{5,7},{7,5},{8,10},{10,8},{9,1... | collective-permute-start | bytes 5898248 | tf_op jit(solution)/shard_map/ppermute | solution.py:462
  (90 other events, 956.1 us)

commit v5 on v4

--- a/solution.py
+++ b/solution.py
@@ -445,10 +445,53 @@
             out_specs=pl.BlockSpec((block, width), lambda i, h: (i, 0)),
         ),
         out_shape=jax.ShapeDtypeStruct((steps * block, width), BF16),
-        compiler_params=params(40),
+        compiler_params=params(60),
         cost_estimate=cost(2 * tokens * width * block * steps, 2 * steps * block * (tokens + width)),
         name="weight_sums",
     )(half.reshape(1), activated, grad_ffn, grad_pre, normed, ctx, grad_attn)
+
+
+def unpack_kernel(counts, upright, core_ref, own_ref, other_ref, *out_refs):
+    at = pl.program_id(0)
+    half = pl.num_programs(0) // 2
+    mine = jnp.where(at < half, 0, 1) == core_ref[0]
+    rows = jnp.where(mine, own_ref[...], other_ref[...]).astype(F32)
+    first = 0
+    for count, turn, out_ref in zip(counts, upright, out_refs):
+
+        @pl.when((at >= first) & (at < first + count))
+        def _(turn=turn, out_ref=out_ref):
+            out_ref[...] = rows.T if turn else rows
+
+        first += count
+
+
+def unpack(core, own, other, heights, upright, block):
+    half, width = own.shape
+    steps = 2 * half // block
+    counts = [height // block for height in heights]
+    source = pl.BlockSpec((block, width), lambda i, c: (i % (steps // 2), 0))
+    specs, shapes = [], []
+    first = 0
+    for height, count, turn in zip(heights, counts, upright):
+        place = lambda i, first=first, count=count: jnp.clip(i - first, 0, count - 1)
+        if turn:
+            specs.append(pl.BlockSpec((width, block), lambda i, c, place=place: (0, place(i))))
+            shapes.append(jax.ShapeDtypeStruct((width, height), F32))
+        else:
+            specs.append(pl.BlockSpec((block, width), lambda i, c, place=place: (place(i), 0)))
+            shapes.append(jax.ShapeDtypeStruct((height, width), F32))
+        first += count
+    return pl.pallas_call(
+        functools.partial(unpack_kernel, counts, upright),
+        grid_spec=pltpu.PrefetchScalarGridSpec(
+            num_scalar_prefetch=1, grid=(steps,), in_specs=[source, source], out_specs=specs
+        ),
+        out_shape=shapes,
+        compiler_params=params(60),
+        cost_estimate=cost(2 * half * width, 2 * half * width * 8),
+        name="unpack",
+    )(core.reshape(1), own, other)
 
 
 def cut(value, axis):
@@ -555,8 +598,8 @@
         lax.axis_index(top_axis), chosen, knowledge_ids.reshape(-1), rows_dev, capacity, devices
     )
     asked = exchange(requests.reshape(2, group, slots_all), 1).reshape(2, slots)
+    asked, gene_other, know_sum = lax.optimization_barrier((asked, gene_other, know_sum))
     know_other = lax.ppermute(know_sum, top_axis, SWAP)
-    asked, gene_other, know_other = lax.optimization_barrier((asked, gene_other, know_other))
     tables = [
         jnp.concatenate([gene_table, know_sum], axis=0),
         jnp.concatenate([gene_other, know_other], axis=0),
@@ -656,6 +699,11 @@
         + dx_from_other.astype(F32)
     )
     grad_low = grad_embedded.astype(BF16)
+    grad_low, came = lax.optimization_barrier((grad_low, came))
+    keeps, sends = begin(end(keeps, came, stages[done]), stages[done + 1])
+    done += 1
+    keeps, sends, grad_low = lax.optimization_barrier((keeps, sends, grad_low))
+    came = travel(sends, stages[done])
 
     outgoing = [mm(hots, grad_low, TN).astype(BF16) for hots in slot_hots]
     outgoing, dq, dk, dv, came = lax.optimization_barrier((outgoing, dq, dk, dv, came))
@@ -682,10 +730,10 @@
         ],
         axis=0,
     )
-    short = jnp.pad(short, ((0, -short.shape[0] % 16), (0, 0)))
+    block = 128
+    short = jnp.pad(short, ((0, -short.shape[0] % block), (0, 0)))
     late = [w_query_grad, w_key_grad, w_value_grad, expr_grad, short]
     heights = [item.shape[0] for item in late]
-    late.append(jnp.zeros((-sum(heights) % 512, width), F32))
     late = jnp.concatenate([item.astype(BF16) for item in late], axis=0)
     keep, send = cut(late, core)
     keep, send, outgoing, returned_other = lax.optimization_barrier(
@@ -696,23 +744,34 @@
     late = jnp.split(keep + swap(send, core), 2, axis=0)
     returned, late, early, from_other = lax.optimization_barrier((returned, late, early, from_other))
     table_grads = mm(owned[0].astype(BF16), returned) + from_other.astype(F32)
-    early = run_stages(early, stages[done:])
-    early = jnp.concatenate(early, axis=0)
-    early = join(early, swap(early, core), core)
-    w_down_grad = early[:wide].astype(F32)
-    w_up_grad = early[wide : 2 * wide].T.astype(F32)
-    w_out_grad = early[2 * wide :].astype(F32)
-    late = run_stages(late, stages[:-2])
-    late, w_down_grad, w_up_grad, w_out_grad = lax.optimization_barrier(
-        (late, w_down_grad, w_up_grad, w_out_grad)
-    )
-    late = jnp.concatenate(run_stages(late, stages[-2:]), axis=0)
-    late = join(late, swap(late, core), core)
-    taken = []
-    for height in heights:
-        at = sum(item.shape[0] for item in taken)
-        taken.append(late[at : at + height].astype(F32))
-    w_query_grad, w_key_grad, w_value_grad, expr_grad, short = taken
+    late = run_stages(late, stages[:2])
+    late, early = lax.optimization_barrier((late, early))
+    early_step = begin(early, stages[done])
+    last = len(stages) - 1
+    for at, stage in enumerate(stages[2:], start=2):
+        keeps, sends = begin(late, stage)
+        if at in (2, last):
+            keeps, sends, early_step = lax.optimization_barrier((keeps, sends, early_step))
+        came = travel(sends, stage)
+        if at == 2:
+            early_came = travel(early_step[1], stages[done])
+        if at == last:
+            early = unpack(
+                my_core, *early_step, (wide, wide, width), (False, True, False), 384
+            )
+            came, early = lax.optimization_barrier((came, early))
+        late = end(keeps, came, stage)
+        if at == last - 2:
+            late, early_came = lax.optimization_barrier((late, early_came))
+            early = end(early_step[0], early_came, stages[done])
+            early = jnp.concatenate(run_stages(early, stages[done + 1 :]), axis=0)
+            early_step = (early, swap(early, core))
+    w_down_grad, w_up_grad, w_out_grad = early
+    late = jnp.concatenate(late, axis=0)
+    late_other = swap(late, core)
+    w_query_grad, w_key_grad, w_value_grad, expr_grad, short = unpack(
+        my_core, late, late_other, heights, (False,) * 5, block
+    )
     gain_two_grad, shift_two_grad, b_down_grad, gain_one_grad, shift_one_grad, b_out_grad = (
         short[i] for i in range(6)
     )

time: 732 us -> 688 us (0.940)
  Pallas kernels: 193 us -> 236 us
  waiting for transfers between devices: 271 us -> 244 us
  other arithmetic: 60.7 us -> 33.8 us
  local copies, waits for them, and re-layouts: 39.9 us -> 23 us
  blocking collectives: 15 us -> 0 us
    ppermute x1, waiting for transfers between devices: 10.9 us -> 51.8 us  [local(): know_other = lax.ppermute(know_sum, top_axis, SWAP)]
    pallas_call x0 -> x2, Pallas kernels: none -> 37 us  [unpack(): pl.pallas_call(functools.partial(unpack_kernel, counts, upright), grid_sp...]
    ppermute x30, waiting for transfers between devices: 154 us -> 123 us  [swap(): return lax.ppermute(value, axis, SWAP)]
    all_to_all x4 -> x5, waiting for transfers between devices: 87.5 us -> 59.9 us  [exchange(): lax.all_to_all(value, group_axes, split_axis=axis, concat_axis=axis, tile...]
    convert_element_type x5 -> x0, other arithmetic: 17.2 us -> none  [the longest x1 10.2 us: local(): w_up_grad = early[wide:2 * wide].T.astype(F32)]
    unnamed x153 -> x139, local copies, waits for them, and re-layouts: 25.5 us -> 10 us
    all_to_all x1 -> x0, blocking collectives: 15 us -> none  [exchange(): lax.all_to_all(value, group_axes, split_axis=axis, concat_axis=axis, tile...]
    ppermute x1, waiting for transfers between devices: 8.65 us -> 0.01 us  [local(): gene_other = lax.ppermute(gene_table, top_axis, SWAP)]
  transfers between devices with their start and end apart: 38 -> 39, of which waited for: 24 -> 23; matrix products, arithmetic and copies ran while one was open for 15% -> 14% of each run, Pallas kernels for 17% -> 22%
where the time goes in v5:
time: 688 us; the launch traced here: 680 us
  waiting for transfers between devices  244 us (35%)
  Pallas kernels  236 us (34%)
  matrix products  78.7 us (11%)
  starting transfers between devices  61.7 us (9%)
  other arithmetic  33.8 us (5%)
  local copies, waits for them, and re-layouts  23 us (3%)
    ppermute x30, waiting for transfers between devices, swap(): return lax.ppermute(value, axis, SWAP)  123 us
    pallas_call x5, Pallas kernels, attend_back(): pl.pallas_call(functools.partial(attend_back_kernel, add, len(into)), gri...  87.1 us
    dot_general x26, matrix products, mm(): return lax.dot_general(left, right, dims, preferred_element_type=F32)  78.7 us
    all_to_all x5, waiting for transfers between devices, exchange(): lax.all_to_all(value, group_axes, split_axis=axis, concat_axis=axis, tile...  59.9 us
    ppermute x1, waiting for transfers between devices, local(): know_other = lax.ppermute(know_sum, top_axis, SWAP)  51.8 us
    pallas_call x2, Pallas kernels, attend(): pl.pallas_call(functools.partial(attend_kernel, merge), grid_spec=pltpu.P...  43.5 us
    pallas_call x1, Pallas kernels, middle(): pl.pallas_call(middle_kernel, grid=(tokens // block,), in_specs=[rows(wid...  37.3 us
    pallas_call x2, Pallas kernels, unpack(): pl.pallas_call(functools.partial(unpack_kernel, counts, upright), grid_sp...  37 us
  transfers between devices with their start and end apart: 39, of which 23 were waited for; matrix products, arithmetic and copies ran while one was open for 14% of the time, Pallas kernels for 22%

profile of v5, /device:TPU:0, one launch (start us, length us, event | category | flops | bytes accessed | tf_op | source)
XLA Modules:
  0.0 680.3 jit_solution(13857350987841829394)
XLA Ops:
  17.8 8.9 %all-to-all-done = s32[2,16,128]{2,0,1:T(2,128)S(1)} async-done(((s32[2,16,128]{2,0,1:T(2,128)}), s32[2,16,128]{2,0,1:T(2,128)S(1)}, u32[]{:S(2)}, u32[]{:S(2)}) %all-to-all-start) | async-done | bytes 16416 | tf_op jit(solution)/shard_map/all_to_all | solution.py:591
  37.5 51.8 %collective-permute-done.1 = bf16[288,768]{1,0:T(8,128)(2,1)S(1)} collective-permute-done((bf16[288,768]{1,0:T(8,128)(2,1)S(1)}, bf16[288,768]{1,0:T(8,128)(2,1)S(1)}, u32[]{:S(2)}, u32[]{:S(2)}) %collective-permute-start.1) | collective-permute-done | bytes 442400 | tf_op jit(solution)/shard_map/ppermute | solution.py:602
  105.3 7.9 %fusion.5 = f32[1024,768]{1,0:T(8,128)} fusion(bf16[2048,768]{1,0:T(8,128)(2,1)} %bitcast.10, s32[1024]{0:T(1024)S(1)} %reduce.3, s32[1024]{0:T(1024)S(1)} %reduce.2), kind=kOutput, calls=%fused_computation.7 | convolution fusion | flops 3227516928 | bytes 6299648 | tf_op jit(solution)/shard_map/dot_general | solution.py:24
  113.2 31.0 %all-to-all-done.2 = bf16[16,128,768]{2,1,0:T(8,128)(2,1)} async-done(((bf16[16,128,768]{2,1,0:T(8,128)(2,1)}), bf16[16,128,768]{2,1,0:T(8,128)(2,1)}, u32[]{:S(2)}, u32[]{:S(2)}) %all-to-all-start.2) | async-done | bytes 3145760 | tf_op jit(solution)/shard_map/all_to_all | solution.py:591
  158.2 21.1 %attend.1 = (f32[768,1024]{1,0:T(8,128)}, f32[6,2,1024]{2,1,0:T(2,128)S(1)}) custom-call(s32[2]{0:T(128)S(1)} %pad_add_fusion.1.where_ref, bf16[1024,768]{1,0:T(8,128)(2,1)S(1)} %add_convert_fusion.3.q_ref, bf16[1024,768]{1,0:T(8,128)(2,1)S(1)} %convolution_convert_fusion.k_ref, bf16[1024,768]{1,0:T(8,128)(2,1)S(1)} %add_convert_fusion.1.v_ref), custom_call_target="tpu_custom_call" | custom-call | flops 12884901888 | bytes 15728640 | tf_op jit(solution)/shard_map/attend/pallas_call | solution.py:168
  179.3 9.6 %collective-permute-done.2 = bf16[1024,768]{1,0:T(8,128)(2,1)S(1)} collective-permute-done((bf16[1024,768]{1,0:T(8,128)(2,1)S(1)}, bf16[1024,768]{1,0:T(8,128)(2,1)S(1)}, u32[]{:S(2)}, u32[]{:S(2)}) %collective-permute-start.2) | collective-permute-done | bytes 1572896 | tf_op jit(solution)/shard_map/ppermute | solution.py:620
  191.8 22.4 %attend_more.1 = (f32[1024,768]{1,0:T(8,128)}, f32[6,2,1024]{2,1,0:T(2,128)S(1)}) custom-call(s32[2]{0:T(128)S(1)} %pad_add_fusion.where_ref, bf16[1024,768]{1,0:T(8,128)(2,1)S(1)} %add_convert_fusion.3.q_ref, bf16[1024,768]{1,0:T(8,128)(2,1)S(1)} %convolution_convert_fusion.1.k_ref, bf16[1024,768]{1,0:T(8,128)(2,1)S(1)} %add_convert_fusion.2.v_ref, ...), custom_call_target="tpu_custom_call" | custom-call | flops 12884901888 | bytes 15728640 | tf_op jit(solution)/shard_map/attend_more/pallas_call | solution.py:168
  214.8 37.3 %middle.1 = (bf16[1024,768]{1,0:T(8,128)(2,1)}, bf16[1024,768]{1,0:T(8,128)(2,1)}, bf16[1024,768]{1,0:T(8,128)(2,1)}, bf16[1024,3072]{1,0:T(8,128)(2,1)}, bf16[1...) custom-call(f32[1024,768]{1,0:T(8,128)} %get-tuple-element.200.ctx_r, ...), custom_call_target="tpu_custom_call" | custom-call | flops 43486543872 | bytes 34603008 | tf_op jit(solution)/shard_map/middle/pallas_call | solution.py:376
  252.1 13.8 %weight_sums.2 = bf16[3456,768]{1,0:T(8,128)(2,1)} custom-call(s32[1]{0:T(128)} %bitcast.19.half_ref, bf16[1024,3072]{1,0:T(8,128)(2,1)} %get-tuple-element.208.act_ref, bf16[1024,768]{1,0:T(8,128)(2,1)} %get-tuple-element.209.gffn_ref, bf16[1024,3072]{1,0:T(8,128)(2,1)} %get-tuple-element.210.gpre_ref, bf16[1024,768]{1,0:T(8,128)(2,1)} %get-tuple-element.211.norm_ref, ...), custom_call_target="tpu_custom_call" | custom-call | flops 5435817984 | bytes 12386304 | tf_op jit(solution)/shard_map/weight_sums/pallas_call | solution.py:439
  265.9 13.6 %weight_sums.3 = bf16[3456,768]{1,0:T(8,128)(2,1)} custom-call(s32[1]{0:T(128)} %bitcast.18.half_ref.core_ref, bf16[1024,3072]{1,0:T(8,128)(2,1)} %get-tuple-element.208.act_ref, bf16[1024,768]{1,0:T(8,128)(2,1)} %get-tuple-element.209.gffn_ref, bf16[1024,3072]{1,0:T(8,128)(2,1)} %get-tuple-element.210.gpre_ref, ...), custom_call_target="tpu_custom_call" | custom-call | flops 5435817984 | bytes 12386304 | tf_op jit(solution)/shard_map/weight_sums/pallas_call | solution.py:439
  288.1 26.6 %attend_back0.1 = (f32[1024,768]{1,0:T(8,128)}, bf16[1024,768]{1,0:T(8,128)(2,1)}, bf16[1024,768]{1,0:T(8,128)(2,1)}) custom-call(s32[2]{0:T(128)} %copy-done.2, bf16[1024,768]{1,0:T(8,128)(2,1)} %copy-done.5, bf16[1024,768]{1,0:T(8,128)(2,1)} %get-tuple-element.277.g_ref, f32[1024,768]{1,0:T(8,128)} %get-tuple-element.200.ctx_ref.o_ref, ...), custom_call_target="tpu_custom_call" | custom-call | flops 21474836480 | bytes 12582912 | tf_op jit(solution)/shard_map/attend_back0/pallas_call | solution.py:248
  322.0 15.1 %attend_back4.1 = (f32[1024,768]{1,0:T(8,128)}, bf16[1024,768]{1,0:T(8,128)(2,1)}, bf16[1024,768]{1,0:T(8,128)(2,1)}) custom-call(s32[2]{0:T(128)} %copy-done.2, bf16[1024,768]{1,0:T(8,128)(2,1)} %copy-done.5, bf16[1024,768]{1,0:T(8,128)(2,1)} %get-tuple-element.277.g_ref, ...), custom_call_target="tpu_custom_call", output_to_operand_aliasing={{0}: (7, {}), {1}: (8, {}), {2}: (9, {})} | custom-call | flops 10737418240 | bytes 6291456 | tf_op jit(solution)/shard_map/attend_back4/pallas_call | solution.py:248
  346.2 15.2 %attend_back_more0.1 = (bf16[1024,768]{1,0:T(8,128)(2,1)}, bf16[1024,768]{1,0:T(8,128)(2,1)}, bf16[1024,768]{1,0:T(8,128)(2,1)}) custom-call(s32[2]{0:T(128)} %copy-done.1, bf16[1024,768]{1,0:T(8,128)(2,1)} %copy-done.5, bf16[1024,768]{1,0:T(8,128)(2,1)} %get-tuple-element.277.g_ref, f32[1024,768]{1,0:T(8,128)} %get-tuple-element.200.ctx_ref.o_ref, ...), custom_call_target="tpu_custom_call" | custom-call | flops 10737418240 | bytes 6291456 | tf_op jit(solution)/shard_map/attend_back_more0/pallas_call | solution.py:248
  363.8 14.9 %attend_back_more2.1 = (bf16[1024,768]{1,0:T(8,128)(2,1)}, bf16[1024,768]{1,0:T(8,128)(2,1)}, bf16[1024,768]{1,0:T(8,128)(2,1)}) custom-call(s32[2]{0:T(128)} %copy-done.1, bf16[1024,768]{1,0:T(8,128)(2,1)} %copy-done.5, bf16[1024,768]{1,0:T(8,128)(2,1)} %get-tuple-element.277.g_ref, ...), custom_call_target="tpu_custom_call", output_to_operand_aliasing={{0}: (8, {}), {1}: (9, {}), {2}: (10, {})} | custom-call | flops 10737418240 | bytes 6291456 | tf_op jit(solution)/shard_map/attend_back_more2/pallas_call | solution.py:248
  379.7 15.4 %attend_back_more4.1 = (bf16[1024,768]{1,0:T(8,128)(2,1)}, bf16[1024,768]{1,0:T(8,128)(2,1)}, bf16[1024,768]{1,0:T(8,128)(2,1)}) custom-call(s32[2]{0:T(128)} %copy-done.1, bf16[1024,768]{1,0:T(8,128)(2,1)} %copy-done.5, bf16[1024,768]{1,0:T(8,128)(2,1)} %get-tuple-element.277.g_ref, ...), custom_call_target="tpu_custom_call", output_to_operand_aliasing={{0}: (8, {}), {1}: (9, {}), {2}: (10, {})} | custom-call | flops 10737418240 | bytes 6291456 | tf_op jit(solution)/shard_map/attend_back_more4/pallas_call | solution.py:248
  404.7 7.7 %collective-permute-done.13 = bf16[432,768]{1,0:T(8,128)(2,1)S(1)} collective-permute-done((bf16[432,768]{1,0:T(8,128)(2,1)S(1)}, bf16[432,768]{1,0:T(8,128)(2,1)S(1)}, u32[]{:S(2)}, u32[]{:S(2)}) %collective-permute-start.13) | collective-permute-done | bytes 663584 | tf_op jit(solution)/shard_map/ppermute | solution.py:505
  458.3 20.1 %all-to-all-done.3 = bf16[16,128,768]{2,1,0:T(8,128)(2,1)} async-done(((bf16[16,128,768]{2,1,0:T(8,128)(2,1)}), bf16[16,128,768]{2,1,0:T(8,128)(2,1)}, u32[]{:S(2)}, u32[]{:S(2)}) %all-to-all-start.3) | async-done | bytes 3145760 | tf_op jit(solution)/shard_map/all_to_all | solution.py:591
  494.6 54.0 %collective-permute-done.17 = bf16[576,768]{1,0:T(8,128)(2,1)} collective-permute-done((bf16[576,768]{1,0:T(8,128)(2,1)S(1)}, bf16[576,768]{1,0:T(8,128)(2,1)}, u32[]{:S(2)}, u32[]{:S(2)}) %collective-permute-start.17) | collective-permute-done | bytes 884768 | tf_op jit(solution)/shard_map/ppermute | solution.py:505
  550.3 12.5 %collective-permute-done.20 = bf16[320,768]{1,0:T(8,128)(2,1)} collective-permute-done((bf16[320,768]{1,0:T(8,128)(2,1)}, bf16[320,768]{1,0:T(8,128)(2,1)}, u32[]{:S(2)}, u32[]{:S(2)}) %collective-permute-start.20) | collective-permute-done | bytes 491552 | tf_op jit(solution)/shard_map/ppermute | solution.py:505
  574.2 6.6 collective-permute-done.22
  600.7 10.6 %collective-permute-done.26 = bf16[864,768]{1,0:T(8,128)(2,1)} collective-permute-done((bf16[864,768]{1,0:T(8,128)(2,1)S(1)}, bf16[864,768]{1,0:T(8,128)(2,1)}, u32[]{:S(2)}, u32[]{:S(2)}) %collective-permute-start.26) | collective-permute-done | bytes 1327136 | tf_op jit(solution)/shard_map/ppermute | solution.py:505
  620.0 6.8 collective-permute-done.29
  632.3 22.2 %unpack.2 = (f32[3072,768]{1,0:T(8,128)}, f32[768,3072]{1,0:T(8,128)}, f32[768,768]{1,0:T(8,128)}) custom-call(s32[1]{0:T(128)} %bitcast.18.half_ref.core_ref, bf16[3456,768]{1,0:T(8,128)(2,1)} %copy-done.9, bf16[3456,768]{1,0:T(8,128)(2,1)} %copy-done.12), custom_call_target="tpu_custom_call" | custom-call | flops 5308416 | bytes 42467328 | tf_op jit(solution)/shard_map/unpack/pallas_call | solution.py:485
  662.2 14.8 %unpack.3 = (f32[768,768]{1,0:T(8,128)}, f32[768,768]{1,0:T(8,128)}, f32[768,768]{1,0:T(8,128)}, f32[128,768]{1,0:T(8,128)}, f32[128,768]{1,0:T(8,128)}) custom-call(s32[1]{0:T(128)} %bitcast.18.half_ref.core_ref, bf16[1280,768]{1,0:T(8,128)(2,1)} %copy-done.11, bf16[1280,768]{1,0:T(8,128)(2,1)} %collective-permute-done.33.other_ref), custom_call_target="tpu_custom_call" | custom-call | flops 1966080 | bytes 15728640 | tf_op jit(solution)/shard_map/unpack/pallas_call | solution.py:485
  (319 shorter events, 217.1 us)
Async XLA Ops:
  0.7 26.0 %collective-permute-start = (bf16[288,768]{1,0:T(8,128)(2,1)}, bf16[288,768]{1,0:T(8,128)(2,1)}, u32[]{:S(2)}, u32[]{:S(2)}) collective-permute-start(bf16[288,768]{1,0:T(8,128)(2,1)} %param.31), channel_id=1, source_target_pairs={{0,16},{16,0},{1,17},{17,1},{2,18},{18,2},{3,19},{19,3},{4,20},{20... | collective-permute-start | bytes 1327112 | tf_op jit(solution)/shard_map/ppermute | solution.py:594
  11.1 15.6 %all-to-all-start = ((s32[2,16,128]{2,0,1:T(2,128)}), s32[2,16,128]{2,0,1:T(2,128)S(1)}, u32[]{:S(2)}, u32[]{:S(2)}) async-start(s32[2,16,128]{2,0,1:T(2,128)} %copy.61), calls=%async_computation | async-start | bytes 32768 | tf_op jit(solution)/shard_map/all_to_all | solution.py:591
  31.9 62.5 %all-to-all-start.1 = ((bf16[16,128,768]{2,1,0:T(8,128)(2,1)}), bf16[16,128,768]{2,1,0:T(8,128)(2,1)}, u32[]{:S(2)}, u32[]{:S(2)}) async-start(bf16[16,128,768]{2,1,0:T(8,128)(2,1)} %bitcast.69), calls=%async_computation.1 | async-start | bytes 6291456 | tf_op jit(solution)/shard_map/all_to_all | solution.py:591
  36.4 52.9 %collective-permute-start.1 = (bf16[288,768]{1,0:T(8,128)(2,1)S(1)}, bf16[288,768]{1,0:T(8,128)(2,1)S(1)}, u32[]{:S(2)}, u32[]{:S(2)}) collective-permute-start(bf16[288,768]{1,0:T(8,128)(2,1)S(1)} %reduce_sum.75), channel_id=1, source_target_pairs={{0,16},{16,0},{1,17},{17,1},{2,18},{18,2},{3,19},{19,3},{4,20},{20... | collective-permute-start | bytes 1327112 | tf_op jit(solution)/shard_map/ppermute | solution.py:602
  94.4 49.8 %all-to-all-start.2 = ((bf16[16,128,768]{2,1,0:T(8,128)(2,1)}), bf16[16,128,768]{2,1,0:T(8,128)(2,1)}, u32[]{:S(2)}, u32[]{:S(2)}) async-start(bf16[16,128,768]{2,1,0:T(8,128)(2,1)} %bitcast.68), calls=%async_computation.2 | async-start | bytes 6291456 | tf_op jit(solution)/shard_map/all_to_all | solution.py:591
  103.2 76.1 %collective-permute-start.3 = (s32[576]{0:T(1024)S(1)}, s32[576]{0:T(1024)S(1)}, u32[]{:S(2)}, u32[]{:S(2)}) collective-permute-start(s32[576]{0:T(1024)S(1)} %convert_reduce_fusion.1), channel_id=1, source_target_pairs={{0,16},{16,0},{1,17},{17,1},{2,18},{18,2},{3,19},{19,3},{4,20},{20... | collective-permute-start | bytes 6920 | tf_op jit(solution)/shard_map/ppermute | solution.py:628
  152.4 36.6 %collective-permute-start.2 = (bf16[1024,768]{1,0:T(8,128)(2,1)S(1)}, bf16[1024,768]{1,0:T(8,128)(2,1)S(1)}, u32[]{:S(2)}, u32[]{:S(2)}) collective-permute-start(bf16[1024,768]{1,0:T(8,128)(2,1)S(1)} %get-tuple-element.418), channel_id=1, source_target_pairs={{0,1},{1,0},{2,3},{3,2},{4,5},{5,4},{6,7},{7,6},{8,9},{9,8},{10,11... | collective-permute-start | bytes 4718600 | tf_op jit(solution)/shard_map/ppermute | solution.py:620
  286.7 32.2 %collective-permute-start.5 = (bf16[864,768]{1,0:T(8,128)(2,1)}, bf16[864,768]{1,0:T(8,128)(2,1)S(1)}, u32[]{:S(2)}, u32[]{:S(2)}) collective-permute-start(bf16[864,768]{1,0:T(8,128)(2,1)} %get-tuple-element.220), channel_id=1, source_target_pairs={{0,4},{4,0},{1,5},{5,1},{2,6},{6,2},{3,7},{7,3},{8,12},{12,8},{9,1... | collective-permute-start | bytes 3981320 | tf_op jit(solution)/shard_map/ppermute | solution.py:505
  287.6 31.3 %collective-permute-start.6 = (bf16[864,768]{1,0:T(8,128)(2,1)S(1)}, bf16[864,768]{1,0:T(8,128)(2,1)S(1)}, u32[]{:S(2)}, u32[]{:S(2)}) collective-permute-start(bf16[864,768]{1,0:T(8,128)(2,1)S(1)} %get-tuple-element.221), channel_id=1, source_target_pairs={{0,1},{1,0},{2,3},{3,2},{4,5},{5,4},{6,7},{7,6},{8,9},{9,8},{10,11... | collective-permute-start | bytes 3981320 | tf_op jit(solution)/shard_map/ppermute | solution.py:505
  319.8 17.3 %collective-permute-start.7 = (bf16[432,768]{1,0:T(8,128)(2,1)S(1)}, bf16[432,768]{1,0:T(8,128)(2,1)S(1)}, u32[]{:S(2)}, u32[]{:S(2)}) collective-permute-start(bf16[432,768]{1,0:T(8,128)(2,1)S(1)} %get-tuple-element.234), channel_id=1, source_target_pairs={{0,1},{1,0},{2,3},{3,2},{4,5},{5,4},{6,7},{7,6},{8,9},{9,8},{10,11... | collective-permute-start | bytes 1990664 | tf_op jit(solution)/shard_map/ppermute | solution.py:505
  320.4 16.7 %collective-permute-start.8 = (bf16[432,768]{1,0:T(8,128)(2,1)S(1)}, bf16[432,768]{1,0:T(8,128)(2,1)S(1)}, u32[]{:S(2)}, u32[]{:S(2)}) collective-permute-start(bf16[432,768]{1,0:T(8,128)(2,1)S(1)} %get-tuple-element.235), channel_id=1, source_target_pairs={{0,4},{4,0},{1,5},{5,1},{2,6},{6,2},{3,7},{7,3},{8,12},{12,8},{9,1... | collective-permute-start | bytes 1990664 | tf_op jit(solution)/shard_map/ppermute | solution.py:505
  343.8 17.6 %collective-permute-start.9 = (bf16[432,768]{1,0:T(8,128)(2,1)S(1)}, bf16[432,768]{1,0:T(8,128)(2,1)S(1)}, u32[]{:S(2)}, u32[]{:S(2)}) collective-permute-start(bf16[432,768]{1,0:T(8,128)(2,1)S(1)} %get-tuple-element.251), channel_id=1, source_target_pairs={{0,8},{8,0},{1,9},{9,1},{2,10},{10,2},{3,11},{11,3},{4,12},{12,4},... | collective-permute-start | bytes 1990664 | tf_op jit(solution)/shard_map/ppermute | solution.py:505
  345.7 49.8 %collective-permute-start.12 = (bf16[1024,768]{1,0:T(8,128)(2,1)S(1)}, bf16[1024,768]{1,0:T(8,128)(2,1)S(1)}, u32[]{:S(2)}, u32[]{:S(2)}) collective-permute-start(bf16[1024,768]{1,0:T(8,128)(2,1)S(1)} %add_convert_fusion), channel_id=1, source_target_pairs={{0,1},{1,0},{2,3},{3,2},{4,5},{5,4},{6,7},{7,6},{8,9},{9,8},{10,11... | collective-permute-start | bytes 4718600 | tf_op jit(solution)/shard_map/ppermute | solution.py:505
  361.6 17.0 %collective-permute-start.10 = (bf16[216,768]{1,0:T(8,128)(2,1)S(1)}, bf16[216,768]{1,0:T(8,128)(2,1)S(1)}, u32[]{:S(2)}, u32[]{:S(2)}) collective-permute-start(bf16[216,768]{1,0:T(8,128)(2,1)S(1)} %get-tuple-element.262), channel_id=1, source_target_pairs={{0,16},{16,0},{1,17},{17,1},{2,18},{18,2},{3,19},{19,3},{4,20},{20... | collective-permute-start | bytes 995336 | tf_op jit(solution)/shard_map/ppermute | solution.py:505
  378.8 16.6 %collective-permute-start.11 = (bf16[216,768]{1,0:T(8,128)(2,1)S(1)}, bf16[216,768]{1,0:T(8,128)(2,1)S(1)}, u32[]{:S(2)}, u32[]{:S(2)}) collective-permute-start(bf16[216,768]{1,0:T(8,128)(2,1)S(1)} %add.234), channel_id=1, source_target_pairs={{0,16},{16,0},{1,17},{17,1},{2,18},{18,2},{3,19},{19,3},{4,20},{20... | collective-permute-start | bytes 995336 | tf_op jit(solution)/shard_map/ppermute | solution.py:505
  395.5 16.9 %collective-permute-start.13 = (bf16[432,768]{1,0:T(8,128)(2,1)S(1)}, bf16[432,768]{1,0:T(8,128)(2,1)S(1)}, u32[]{:S(2)}, u32[]{:S(2)}) collective-permute-start(bf16[432,768]{1,0:T(8,128)(2,1)S(1)} %pad_maximum_fusion.4), channel_id=1, source_target_pairs={{0,8},{8,0},{1,9},{9,1},{2,10},{10,2},{3,11},{11,3},{4,12},{12,4},... | collective-permute-start | bytes 1990664 | tf_op jit(solution)/shard_map/ppermute | solution.py:505
  412.5 16.0 %collective-permute-start.14 = (bf16[432,768]{1,0:T(8,128)(2,1)S(1)}, bf16[432,768]{1,0:T(8,128)(2,1)S(1)}, u32[]{:S(2)}, u32[]{:S(2)}) collective-permute-start(bf16[432,768]{1,0:T(8,128)(2,1)S(1)} %get-tuple-element.312), channel_id=1, source_target_pairs={{0,1},{1,0},{2,3},{3,2},{4,5},{5,4},{6,7},{7,6},{8,9},{9,8},{10,11... | collective-permute-start | bytes 1990664 | tf_op jit(solution)/shard_map/ppermute | solution.py:505
  430.3 48.1 %all-to-all-start.3 = ((bf16[16,128,768]{2,1,0:T(8,128)(2,1)}), bf16[16,128,768]{2,1,0:T(8,128)(2,1)}, u32[]{:S(2)}, u32[]{:S(2)}) async-start(bf16[16,128,768]{2,1,0:T(8,128)(2,1)} %bitcast.67), calls=%async_computation.3 | async-start | bytes 6291456 | tf_op jit(solution)/shard_map/all_to_all | solution.py:591
  478.4 70.2 %all-to-all-start.4 = ((bf16[16,128,768]{2,1,0:T(8,128)(2,1)}), bf16[16,128,768]{2,1,0:T(8,128)(2,1)}, u32[]{:S(2)}, u32[]{:S(2)}) async-start(bf16[16,128,768]{2,1,0:T(8,128)(2,1)} %bitcast.66), calls=%async_computation.4 | async-start | bytes 6291456 | tf_op jit(solution)/shard_map/all_to_all | solution.py:591
  489.2 59.4 %collective-permute-start.17 = (bf16[576,768]{1,0:T(8,128)(2,1)S(1)}, bf16[576,768]{1,0:T(8,128)(2,1)}, u32[]{:S(2)}, u32[]{:S(2)}) collective-permute-start(bf16[576,768]{1,0:T(8,128)(2,1)S(1)} %fusion.35), channel_id=1, source_target_pairs={{0,16},{16,0},{1,17},{17,1},{2,18},{18,2},{3,19},{19,3},{4,20},{20... | collective-permute-start | bytes 2654216 | tf_op jit(solution)/shard_map/ppermute | solution.py:505
  583.7 27.5 %collective-permute-start.26 = (bf16[864,768]{1,0:T(8,128)(2,1)S(1)}, bf16[864,768]{1,0:T(8,128)(2,1)}, u32[]{:S(2)}, u32[]{:S(2)}) collective-permute-start(bf16[864,768]{1,0:T(8,128)(2,1)S(1)} %copy-done.13), channel_id=1, source_target_pairs={{0,4},{4,0},{1,5},{5,1},{2,6},{6,2},{3,7},{7,3},{8,12},{12,8},{9,1... | collective-permute-start | bytes 3981320 | tf_op jit(solution)/shard_map/ppermute | solution.py:505
  586.4 26.2 %collective-permute-start.27 = (bf16[864,768]{1,0:T(8,128)(2,1)}, bf16[864,768]{1,0:T(8,128)(2,1)}, u32[]{:S(2)}, u32[]{:S(2)}) collective-permute-start(bf16[864,768]{1,0:T(8,128)(2,1)} %pad_maximum_fusion.3), channel_id=1, source_target_pairs={{0,1},{1,0},{2,3},{3,2},{4,5},{5,4},{6,7},{7,6},{8,9},{9,8},{10,11... | collective-permute-start | bytes 3981320 | tf_op jit(solution)/shard_map/ppermute | solution.py:505
  629.7 24.8 %collective-permute-start.31 = (bf16[320,768]{1,0:T(8,128)(2,1)S(1)}, bf16[320,768]{1,0:T(8,128)(2,1)S(1)}, u32[]{:S(2)}, u32[]{:S(2)}) collective-permute-start(bf16[320,768]{1,0:T(8,128)(2,1)S(1)} %pad_maximum_fusion.6), channel_id=1, source_target_pairs={{0,4},{4,0},{1,5},{5,1},{2,6},{6,2},{3,7},{7,3},{8,12},{12,8},{9,1... | collective-permute-start | bytes 1474568 | tf_op jit(solution)/shard_map/ppermute | solution.py:505
  631.1 23.4 %collective-permute-start.32 = (bf16[320,768]{1,0:T(8,128)(2,1)S(1)}, bf16[320,768]{1,0:T(8,128)(2,1)S(1)}, u32[]{:S(2)}, u32[]{:S(2)}) collective-permute-start(bf16[320,768]{1,0:T(8,128)(2,1)S(1)} %pad_maximum_fusion.7), channel_id=1, source_target_pairs={{0,1},{1,0},{2,3},{3,2},{4,5},{5,4},{6,7},{7,6},{8,9},{9,8},{10,11... | collective-permute-start | bytes 1474568 | tf_op jit(solution)/shard_map/ppermute | solution.py:505
  (84 other events, 1006.8 us)

commit v6 on v5

--- a/solution.py
+++ b/solution.py
@@ -470,7 +470,11 @@
     half, width = own.shape
     steps = 2 * half // block
     counts = [height // block for height in heights]
-    source = pl.BlockSpec((block, width), lambda i, c: (i % (steps // 2), 0))
+    last = steps // 2 - 1
+    source = lambda turn: pl.BlockSpec(
+        (block, width),
+        lambda i, c: (jnp.clip(i - (c[0] if turn == 0 else 1 - c[0]) * (last + 1), 0, last), 0),
+    )
     specs, shapes = [], []
     first = 0
     for height, count, turn in zip(heights, counts, upright):
@@ -485,12 +489,40 @@
     return pl.pallas_call(
         functools.partial(unpack_kernel, counts, upright),
         grid_spec=pltpu.PrefetchScalarGridSpec(
-            num_scalar_prefetch=1, grid=(steps,), in_specs=[source, source], out_specs=specs
+            num_scalar_prefetch=1, grid=(steps,), in_specs=[source(0), source(1)], out_specs=specs
         ),
         out_shape=shapes,
         compiler_params=params(60),
         cost_estimate=cost(2 * half * width, 2 * half * width * 8),
         name="unpack",
+    )(core.reshape(1), own, other)
+
+
+def unpack_whole_kernel(heights, core_ref, own_ref, other_ref, *out_refs):
+    half = own_ref.shape[0]
+    lower = core_ref[0] == 0
+    first = 0
+    for height, out_ref in zip(heights, out_refs):
+        for part in range(2):
+            start, stop = max(first, part * half), min(first + height, (part + 1) * half)
+            if start < stop:
+                span = slice(start - part * half, stop - part * half)
+                near, far = (own_ref, other_ref) if part == 0 else (other_ref, own_ref)
+                rows = jnp.where(lower, near[span, :], far[span, :])
+                out_ref[start - first : stop - first, :] = rows.astype(F32)
+        first += height
+
+
+def unpack_whole(core, own, other, heights):
+    width = own.shape[1]
+    vmem = pl.BlockSpec(memory_space=pltpu.VMEM)
+    return pl.pallas_call(
+        functools.partial(unpack_whole_kernel, heights),
+        in_specs=[pl.BlockSpec(memory_space=pltpu.SMEM), vmem, vmem],
+        out_specs=[vmem] * len(heights),
+        out_shape=[jax.ShapeDtypeStruct((height, width), F32) for height in heights],
+        compiler_params=params(60),
+        name="unpack_whole",
     )(core.reshape(1), own, other)
 
 
@@ -750,27 +782,27 @@
     last = len(stages) - 1
     for at, stage in enumerate(stages[2:], start=2):
         keeps, sends = begin(late, stage)
-        if at in (2, last):
+        if at == 2:
             keeps, sends, early_step = lax.optimization_barrier((keeps, sends, early_step))
         came = travel(sends, stage)
         if at == 2:
             early_came = travel(early_step[1], stages[done])
-        if at == last:
-            early = unpack(
-                my_core, *early_step, (wide, wide, width), (False, True, False), 384
-            )
-            came, early = lax.optimization_barrier((came, early))
+        if at == 4:
+            came, table_grads = lax.optimization_barrier((came, table_grads))
         late = end(keeps, came, stage)
-        if at == last - 2:
+        if at == last - 1:
             late, early_came = lax.optimization_barrier((late, early_came))
             early = end(early_step[0], early_came, stages[done])
             early = jnp.concatenate(run_stages(early, stages[done + 1 :]), axis=0)
             early_step = (early, swap(early, core))
-    w_down_grad, w_up_grad, w_out_grad = early
     late = jnp.concatenate(late, axis=0)
     late_other = swap(late, core)
-    w_query_grad, w_key_grad, w_value_grad, expr_grad, short = unpack(
-        my_core, late, late_other, heights, (False,) * 5, block
+    late, early_step = lax.optimization_barrier((late, early_step))
+    early = unpack(my_core, *early_step, (wide, wide, width), (False, True, False), 384)
+    late_other, early = lax.optimization_barrier((late_other, early))
+    w_down_grad, w_up_grad, w_out_grad = early
+    w_query_grad, w_key_grad, w_value_grad, expr_grad, short = unpack_whole(
+        my_core, late, late_other, heights
     )
     gain_two_grad, shift_two_grad, b_down_grad, gain_one_grad, shift_one_grad, b_out_grad = (
         short[i] for i in range(6)

time: 688 us -> 686 us (level)
  Pallas kernels: 236 us -> 222 us
  waiting for transfers between devices: 244 us -> 257 us
    pallas_call x2 -> x1, Pallas kernels: 37 us -> 18.7 us  [unpack(): pl.pallas_call(functools.partial(unpack_kernel, counts, upright), grid_sp...]
    ppermute x30, waiting for transfers between devices: 123 us -> 136 us  [swap(): return lax.ppermute(value, axis, SWAP)]
  transfers between devices with their start and end apart: 39 -> 39, of which waited for: 23 -> 22; matrix products, arithmetic and copies ran while one was open for 14% -> 14% of each run, Pallas kernels for 22% -> 21%
where the time goes in v6:
time: 686 us; the launch traced here: 678 us
  waiting for transfers between devices  257 us (37%)
  Pallas kernels  222 us (32%)
  matrix products  79.9 us (12%)
  starting transfers between devices  63.3 us (9%)
  other arithmetic  32.7 us (5%)
  local copies, waits for them, and re-layouts  19.6 us (3%)
    ppermute x30, waiting for transfers between devices, swap(): return lax.ppermute(value, axis, SWAP)  136 us
    pallas_call x5, Pallas kernels, attend_back(): pl.pallas_call(functools.partial(attend_back_kernel, add, len(into)), gri...  87 us
    dot_general x26, matrix products, mm(): return lax.dot_general(left, right, dims, preferred_element_type=F32)  79.9 us
    all_to_all x5, waiting for transfers between devices, exchange(): lax.all_to_all(value, group_axes, split_axis=axis, concat_axis=axis, tile...  60 us
    ppermute x1, waiting for transfers between devices, local(): know_other = lax.ppermute(know_sum, top_axis, SWAP)  51.7 us
    pallas_call x2, Pallas kernels, attend(): pl.pallas_call(functools.partial(attend_kernel, merge), grid_spec=pltpu.P...  43.5 us
    pallas_call x1, Pallas kernels, middle(): pl.pallas_call(middle_kernel, grid=(tokens // block,), in_specs=[rows(wid...  37.2 us
    ppermute x30, starting transfers between devices, swap(): return lax.ppermute(value, axis, SWAP)  28.6 us
  transfers between devices with their start and end apart: 39, of which 22 were waited for; matrix products, arithmetic and copies ran while one was open for 14% of the time, Pallas kernels for 21%

profile of v6, /device:TPU:0, one launch (start us, length us, event | category | flops | bytes accessed | tf_op | source)
XLA Modules:
  0.0 678.4 jit_solution(6058245861773104393)
XLA Ops:
  17.8 8.9 %all-to-all-done = s32[2,16,128]{2,0,1:T(2,128)S(1)} async-done(((s32[2,16,128]{2,0,1:T(2,128)}), s32[2,16,128]{2,0,1:T(2,128)S(1)}, u32[]{:S(2)}, u32[]{:S(2)}) %all-to-all-start) | async-done | bytes 16416 | tf_op jit(solution)/shard_map/all_to_all | solution.py:623
  37.5 51.7 %collective-permute-done.1 = bf16[288,768]{1,0:T(8,128)(2,1)S(1)} collective-permute-done((bf16[288,768]{1,0:T(8,128)(2,1)S(1)}, bf16[288,768]{1,0:T(8,128)(2,1)S(1)}, u32[]{:S(2)}, u32[]{:S(2)}) %collective-permute-start.1) | collective-permute-done | bytes 442400 | tf_op jit(solution)/shard_map/ppermute | solution.py:634
  105.3 7.9 %fusion.5 = f32[1024,768]{1,0:T(8,128)} fusion(bf16[2048,768]{1,0:T(8,128)(2,1)} %bitcast.10, s32[1024]{0:T(1024)S(1)} %reduce.3, s32[1024]{0:T(1024)S(1)} %reduce.2), kind=kOutput, calls=%fused_computation.7 | convolution fusion | flops 3227516928 | bytes 6299648 | tf_op jit(solution)/shard_map/dot_general | solution.py:24
  113.2 31.0 %all-to-all-done.2 = bf16[16,128,768]{2,1,0:T(8,128)(2,1)} async-done(((bf16[16,128,768]{2,1,0:T(8,128)(2,1)}), bf16[16,128,768]{2,1,0:T(8,128)(2,1)}, u32[]{:S(2)}, u32[]{:S(2)}) %all-to-all-start.2) | async-done | bytes 3145760 | tf_op jit(solution)/shard_map/all_to_all | solution.py:623
  158.2 21.1 %attend.1 = (f32[768,1024]{1,0:T(8,128)}, f32[6,2,1024]{2,1,0:T(2,128)S(1)}) custom-call(s32[2]{0:T(128)S(1)} %pad_add_fusion.1.where_ref, bf16[1024,768]{1,0:T(8,128)(2,1)S(1)} %add_convert_fusion.3.q_ref, bf16[1024,768]{1,0:T(8,128)(2,1)S(1)} %convolution_convert_fusion.k_ref, bf16[1024,768]{1,0:T(8,128)(2,1)S(1)} %add_convert_fusion.1.v_ref), custom_call_target="tpu_custom_call" | custom-call | flops 12884901888 | bytes 15728640 | tf_op jit(solution)/shard_map/attend/pallas_call | solution.py:168
  179.3 9.6 %collective-permute-done.2 = bf16[1024,768]{1,0:T(8,128)(2,1)S(1)} collective-permute-done((bf16[1024,768]{1,0:T(8,128)(2,1)S(1)}, bf16[1024,768]{1,0:T(8,128)(2,1)S(1)}, u32[]{:S(2)}, u32[]{:S(2)}) %collective-permute-start.2) | collective-permute-done | bytes 1572896 | tf_op jit(solution)/shard_map/ppermute | solution.py:652
  191.8 22.4 %attend_more.1 = (f32[1024,768]{1,0:T(8,128)}, f32[6,2,1024]{2,1,0:T(2,128)S(1)}) custom-call(s32[2]{0:T(128)S(1)} %pad_add_fusion.where_ref, bf16[1024,768]{1,0:T(8,128)(2,1)S(1)} %add_convert_fusion.3.q_ref, bf16[1024,768]{1,0:T(8,128)(2,1)S(1)} %convolution_convert_fusion.1.k_ref, bf16[1024,768]{1,0:T(8,128)(2,1)S(1)} %add_convert_fusion.2.v_ref, ...), custom_call_target="tpu_custom_call" | custom-call | flops 12884901888 | bytes 15728640 | tf_op jit(solution)/shard_map/attend_more/pallas_call | solution.py:168
  214.8 37.2 %middle.1 = (bf16[1024,768]{1,0:T(8,128)(2,1)}, bf16[1024,768]{1,0:T(8,128)(2,1)}, bf16[1024,768]{1,0:T(8,128)(2,1)}, bf16[1024,3072]{1,0:T(8,128)(2,1)}, bf16[1...) custom-call(f32[1024,768]{1,0:T(8,128)} %get-tuple-element.199.ctx_r, ...), custom_call_target="tpu_custom_call" | custom-call | flops 43486543872 | bytes 34603008 | tf_op jit(solution)/shard_map/middle/pallas_call | solution.py:376
  252.1 13.8 %weight_sums.2 = bf16[3456,768]{1,0:T(8,128)(2,1)} custom-call(s32[1]{0:T(128)} %bitcast.19.half_ref, bf16[1024,3072]{1,0:T(8,128)(2,1)} %get-tuple-element.207.act_ref, bf16[1024,768]{1,0:T(8,128)(2,1)} %get-tuple-element.208.gffn_ref, bf16[1024,3072]{1,0:T(8,128)(2,1)} %get-tuple-element.209.gpre_ref, bf16[1024,768]{1,0:T(8,128)(2,1)} %get-tuple-element.210.norm_ref, ...), custom_call_target="tpu_custom_call" | custom-call | flops 5435817984 | bytes 12386304 | tf_op jit(solution)/shard_map/weight_sums/pallas_call | solution.py:439
  265.9 13.6 %weight_sums.3 = bf16[3456,768]{1,0:T(8,128)(2,1)} custom-call(s32[1]{0:T(128)} %bitcast.18.half_ref.core_ref, bf16[1024,3072]{1,0:T(8,128)(2,1)} %get-tuple-element.207.act_ref, bf16[1024,768]{1,0:T(8,128)(2,1)} %get-tuple-element.208.gffn_ref, bf16[1024,3072]{1,0:T(8,128)(2,1)} %get-tuple-element.209.gpre_ref, ...), custom_call_target="tpu_custom_call" | custom-call | flops 5435817984 | bytes 12386304 | tf_op jit(solution)/shard_map/weight_sums/pallas_call | solution.py:439
  288.0 26.6 %attend_back0.1 = (f32[1024,768]{1,0:T(8,128)}, bf16[1024,768]{1,0:T(8,128)(2,1)}, bf16[1024,768]{1,0:T(8,128)(2,1)}) custom-call(s32[2]{0:T(128)} %copy-done.2, bf16[1024,768]{1,0:T(8,128)(2,1)} %copy-done.5, bf16[1024,768]{1,0:T(8,128)(2,1)} %get-tuple-element.276.g_ref, f32[1024,768]{1,0:T(8,128)} %get-tuple-element.199.ctx_ref.o_ref, ...), custom_call_target="tpu_custom_call" | custom-call | flops 21474836480 | bytes 12582912 | tf_op jit(solution)/shard_map/attend_back0/pallas_call | solution.py:248
  321.9 15.1 %attend_back4.1 = (f32[1024,768]{1,0:T(8,128)}, bf16[1024,768]{1,0:T(8,128)(2,1)}, bf16[1024,768]{1,0:T(8,128)(2,1)}) custom-call(s32[2]{0:T(128)} %copy-done.2, bf16[1024,768]{1,0:T(8,128)(2,1)} %copy-done.5, bf16[1024,768]{1,0:T(8,128)(2,1)} %get-tuple-element.276.g_ref, ...), custom_call_target="tpu_custom_call", output_to_operand_aliasing={{0}: (7, {}), {1}: (8, {}), {2}: (9, {})} | custom-call | flops 10737418240 | bytes 6291456 | tf_op jit(solution)/shard_map/attend_back4/pallas_call | solution.py:248
  346.2 15.0 %attend_back_more0.1 = (bf16[1024,768]{1,0:T(8,128)(2,1)}, bf16[1024,768]{1,0:T(8,128)(2,1)}, bf16[1024,768]{1,0:T(8,128)(2,1)}) custom-call(s32[2]{0:T(128)} %copy-done.1, bf16[1024,768]{1,0:T(8,128)(2,1)} %copy-done.5, bf16[1024,768]{1,0:T(8,128)(2,1)} %get-tuple-element.276.g_ref, f32[1024,768]{1,0:T(8,128)} %get-tuple-element.199.ctx_ref.o_ref, ...), custom_call_target="tpu_custom_call" | custom-call | flops 10737418240 | bytes 6291456 | tf_op jit(solution)/shard_map/attend_back_more0/pallas_call | solution.py:248
  363.6 14.8 %attend_back_more2.1 = (bf16[1024,768]{1,0:T(8,128)(2,1)}, bf16[1024,768]{1,0:T(8,128)(2,1)}, bf16[1024,768]{1,0:T(8,128)(2,1)}) custom-call(s32[2]{0:T(128)} %copy-done.1, bf16[1024,768]{1,0:T(8,128)(2,1)} %copy-done.5, bf16[1024,768]{1,0:T(8,128)(2,1)} %get-tuple-element.276.g_ref, ...), custom_call_target="tpu_custom_call", output_to_operand_aliasing={{0}: (8, {}), {1}: (9, {}), {2}: (10, {})} | custom-call | flops 10737418240 | bytes 6291456 | tf_op jit(solution)/shard_map/attend_back_more2/pallas_call | solution.py:248
  379.5 15.4 %attend_back_more4.1 = (bf16[1024,768]{1,0:T(8,128)(2,1)}, bf16[1024,768]{1,0:T(8,128)(2,1)}, bf16[1024,768]{1,0:T(8,128)(2,1)}) custom-call(s32[2]{0:T(128)} %copy-done.1, bf16[1024,768]{1,0:T(8,128)(2,1)} %copy-done.5, bf16[1024,768]{1,0:T(8,128)(2,1)} %get-tuple-element.276.g_ref, ...), custom_call_target="tpu_custom_call", output_to_operand_aliasing={{0}: (8, {}), {1}: (9, {}), {2}: (10, {})} | custom-call | flops 10737418240 | bytes 6291456 | tf_op jit(solution)/shard_map/attend_back_more4/pallas_call | solution.py:248
  404.5 7.6 %collective-permute-done.13 = bf16[432,768]{1,0:T(8,128)(2,1)S(1)} collective-permute-done((bf16[432,768]{1,0:T(8,128)(2,1)S(1)}, bf16[432,768]{1,0:T(8,128)(2,1)S(1)}, u32[]{:S(2)}, u32[]{:S(2)}) %collective-permute-start.13) | collective-permute-done | bytes 663584 | tf_op jit(solution)/shard_map/ppermute | solution.py:537
  420.1 6.5 fusion.23
  458.1 20.1 %all-to-all-done.3 = bf16[16,128,768]{2,1,0:T(8,128)(2,1)} async-done(((bf16[16,128,768]{2,1,0:T(8,128)(2,1)}), bf16[16,128,768]{2,1,0:T(8,128)(2,1)}, u32[]{:S(2)}, u32[]{:S(2)}) %all-to-all-start.3) | async-done | bytes 3145760 | tf_op jit(solution)/shard_map/all_to_all | solution.py:623
  494.5 53.8 %collective-permute-done.17 = bf16[576,768]{1,0:T(8,128)(2,1)} collective-permute-done((bf16[576,768]{1,0:T(8,128)(2,1)S(1)}, bf16[576,768]{1,0:T(8,128)(2,1)}, u32[]{:S(2)}, u32[]{:S(2)}) %collective-permute-start.17) | collective-permute-done | bytes 884768 | tf_op jit(solution)/shard_map/ppermute | solution.py:537
  550.0 12.5 %collective-permute-done.20 = bf16[320,768]{1,0:T(8,128)(2,1)} collective-permute-done((bf16[320,768]{1,0:T(8,128)(2,1)}, bf16[320,768]{1,0:T(8,128)(2,1)}, u32[]{:S(2)}, u32[]{:S(2)}) %collective-permute-start.20) | collective-permute-done | bytes 491552 | tf_op jit(solution)/shard_map/ppermute | solution.py:537
  573.0 6.4 collective-permute-done.22
  603.6 24.3 %collective-permute-done.27 = bf16[160,768]{1,0:T(8,128)(2,1)S(1)} collective-permute-done((bf16[160,768]{1,0:T(8,128)(2,1)S(1)}, bf16[160,768]{1,0:T(8,128)(2,1)S(1)}, u32[]{:S(2)}, u32[]{:S(2)}) %collective-permute-start.27) | collective-permute-done | bytes 245792 | tf_op jit(solution)/shard_map/ppermute | solution.py:537
  634.7 11.5 %collective-permute-done.30 = bf16[320,768]{1,0:T(8,128)(2,1)S(1)} collective-permute-done((bf16[320,768]{1,0:T(8,128)(2,1)S(1)}, bf16[320,768]{1,0:T(8,128)(2,1)S(1)}, u32[]{:S(2)}, u32[]{:S(2)}) %collective-permute-start.30) | collective-permute-done | bytes 491552 | tf_op jit(solution)/shard_map/ppermute | solution.py:537
  650.7 18.7 %unpack.1 = (f32[3072,768]{1,0:T(8,128)}, f32[768,3072]{1,0:T(8,128)}, f32[768,768]{1,0:T(8,128)}) custom-call(s32[1]{0:T(128)} %bitcast.18.half_ref.core_ref, bf16[3456,768]{1,0:T(8,128)(2,1)} %pad_maximum_fusion.own_ref, bf16[3456,768]{1,0:T(8,128)(2,1)} %collective-permute-done.32.other_ref), custom_call_target="tpu_custom_call" | custom-call | flops 5308416 | bytes 42467328 | tf_op jit(solution)/shard_map/unpack/pallas_call | solution.py:489
  (314 shorter events, 209.4 us)
Async XLA Ops:
  0.7 26.0 %collective-permute-start = (bf16[288,768]{1,0:T(8,128)(2,1)}, bf16[288,768]{1,0:T(8,128)(2,1)}, u32[]{:S(2)}, u32[]{:S(2)}) collective-permute-start(bf16[288,768]{1,0:T(8,128)(2,1)} %param.31), channel_id=1, source_target_pairs={{0,16},{16,0},{1,17},{17,1},{2,18},{18,2},{3,19},{19,3},{4,20},{20... | collective-permute-start | bytes 1327112 | tf_op jit(solution)/shard_map/ppermute | solution.py:626
  31.9 62.5 %all-to-all-start.1 = ((bf16[16,128,768]{2,1,0:T(8,128)(2,1)}), bf16[16,128,768]{2,1,0:T(8,128)(2,1)}, u32[]{:S(2)}, u32[]{:S(2)}) async-start(bf16[16,128,768]{2,1,0:T(8,128)(2,1)} %bitcast.69), calls=%async_computation.1 | async-start | bytes 6291456 | tf_op jit(solution)/shard_map/all_to_all | solution.py:623
  36.4 52.9 %collective-permute-start.1 = (bf16[288,768]{1,0:T(8,128)(2,1)S(1)}, bf16[288,768]{1,0:T(8,128)(2,1)S(1)}, u32[]{:S(2)}, u32[]{:S(2)}) collective-permute-start(bf16[288,768]{1,0:T(8,128)(2,1)S(1)} %reduce_sum.75), channel_id=1, source_target_pairs={{0,16},{16,0},{1,17},{17,1},{2,18},{18,2},{3,19},{19,3},{4,20},{20... | collective-permute-start | bytes 1327112 | tf_op jit(solution)/shard_map/ppermute | solution.py:634
  94.4 49.8 %all-to-all-start.2 = ((bf16[16,128,768]{2,1,0:T(8,128)(2,1)}), bf16[16,128,768]{2,1,0:T(8,128)(2,1)}, u32[]{:S(2)}, u32[]{:S(2)}) async-start(bf16[16,128,768]{2,1,0:T(8,128)(2,1)} %bitcast.68), calls=%async_computation.2 | async-start | bytes 6291456 | tf_op jit(solution)/shard_map/all_to_all | solution.py:623
  103.2 76.1 %collective-permute-start.3 = (s32[576]{0:T(1024)S(1)}, s32[576]{0:T(1024)S(1)}, u32[]{:S(2)}, u32[]{:S(2)}) collective-permute-start(s32[576]{0:T(1024)S(1)} %convert_reduce_fusion.1), channel_id=1, source_target_pairs={{0,16},{16,0},{1,17},{17,1},{2,18},{18,2},{3,19},{19,3},{4,20},{20... | collective-permute-start | bytes 6920 | tf_op jit(solution)/shard_map/ppermute | solution.py:660
  152.4 36.6 %collective-permute-start.2 = (bf16[1024,768]{1,0:T(8,128)(2,1)S(1)}, bf16[1024,768]{1,0:T(8,128)(2,1)S(1)}, u32[]{:S(2)}, u32[]{:S(2)}) collective-permute-start(bf16[1024,768]{1,0:T(8,128)(2,1)S(1)} %get-tuple-element.412), channel_id=1, source_target_pairs={{0,1},{1,0},{2,3},{3,2},{4,5},{5,4},{6,7},{7,6},{8,9},{9,8},{10,11... | collective-permute-start | bytes 4718600 | tf_op jit(solution)/shard_map/ppermute | solution.py:652
  286.7 32.2 %collective-permute-start.5 = (bf16[864,768]{1,0:T(8,128)(2,1)}, bf16[864,768]{1,0:T(8,128)(2,1)S(1)}, u32[]{:S(2)}, u32[]{:S(2)}) collective-permute-start(bf16[864,768]{1,0:T(8,128)(2,1)} %get-tuple-element.219), channel_id=1, source_target_pairs={{0,4},{4,0},{1,5},{5,1},{2,6},{6,2},{3,7},{7,3},{8,12},{12,8},{9,1... | collective-permute-start | bytes 3981320 | tf_op jit(solution)/shard_map/ppermute | solution.py:537
  287.6 31.3 %collective-permute-start.6 = (bf16[864,768]{1,0:T(8,128)(2,1)S(1)}, bf16[864,768]{1,0:T(8,128)(2,1)S(1)}, u32[]{:S(2)}, u32[]{:S(2)}) collective-permute-start(bf16[864,768]{1,0:T(8,128)(2,1)S(1)} %get-tuple-element.220), channel_id=1, source_target_pairs={{0,1},{1,0},{2,3},{3,2},{4,5},{5,4},{6,7},{7,6},{8,9},{9,8},{10,11... | collective-permute-start | bytes 3981320 | tf_op jit(solution)/shard_map/ppermute | solution.py:537
  319.8 17.3 %collective-permute-start.7 = (bf16[432,768]{1,0:T(8,128)(2,1)S(1)}, bf16[432,768]{1,0:T(8,128)(2,1)S(1)}, u32[]{:S(2)}, u32[]{:S(2)}) collective-permute-start(bf16[432,768]{1,0:T(8,128)(2,1)S(1)} %get-tuple-element.233), channel_id=1, source_target_pairs={{0,1},{1,0},{2,3},{3,2},{4,5},{5,4},{6,7},{7,6},{8,9},{9,8},{10,11... | collective-permute-start | bytes 1990664 | tf_op jit(solution)/shard_map/ppermute | solution.py:537
  320.4 16.7 %collective-permute-start.8 = (bf16[432,768]{1,0:T(8,128)(2,1)S(1)}, bf16[432,768]{1,0:T(8,128)(2,1)S(1)}, u32[]{:S(2)}, u32[]{:S(2)}) collective-permute-start(bf16[432,768]{1,0:T(8,128)(2,1)S(1)} %get-tuple-element.234), channel_id=1, source_target_pairs={{0,4},{4,0},{1,5},{5,1},{2,6},{6,2},{3,7},{7,3},{8,12},{12,8},{9,1... | collective-permute-start | bytes 1990664 | tf_op jit(solution)/shard_map/ppermute | solution.py:537
  343.7 17.5 %collective-permute-start.9 = (bf16[432,768]{1,0:T(8,128)(2,1)S(1)}, bf16[432,768]{1,0:T(8,128)(2,1)S(1)}, u32[]{:S(2)}, u32[]{:S(2)}) collective-permute-start(bf16[432,768]{1,0:T(8,128)(2,1)S(1)} %get-tuple-element.250), channel_id=1, source_target_pairs={{0,8},{8,0},{1,9},{9,1},{2,10},{10,2},{3,11},{11,3},{4,12},{12,4},... | collective-permute-start | bytes 1990664 | tf_op jit(solution)/shard_map/ppermute | solution.py:537
  345.7 49.5 %collective-permute-start.12 = (bf16[1024,768]{1,0:T(8,128)(2,1)S(1)}, bf16[1024,768]{1,0:T(8,128)(2,1)S(1)}, u32[]{:S(2)}, u32[]{:S(2)}) collective-permute-start(bf16[1024,768]{1,0:T(8,128)(2,1)S(1)} %add_convert_fusion), channel_id=1, source_target_pairs={{0,1},{1,0},{2,3},{3,2},{4,5},{5,4},{6,7},{7,6},{8,9},{9,8},{10,11... | collective-permute-start | bytes 4718600 | tf_op jit(solution)/shard_map/ppermute | solution.py:537
  361.5 16.9 %collective-permute-start.10 = (bf16[216,768]{1,0:T(8,128)(2,1)S(1)}, bf16[216,768]{1,0:T(8,128)(2,1)S(1)}, u32[]{:S(2)}, u32[]{:S(2)}) collective-permute-start(bf16[216,768]{1,0:T(8,128)(2,1)S(1)} %get-tuple-element.261), channel_id=1, source_target_pairs={{0,16},{16,0},{1,17},{17,1},{2,18},{18,2},{3,19},{19,3},{4,20},{20... | collective-permute-start | bytes 995336 | tf_op jit(solution)/shard_map/ppermute | solution.py:537
  378.5 16.6 %collective-permute-start.11 = (bf16[216,768]{1,0:T(8,128)(2,1)S(1)}, bf16[216,768]{1,0:T(8,128)(2,1)S(1)}, u32[]{:S(2)}, u32[]{:S(2)}) collective-permute-start(bf16[216,768]{1,0:T(8,128)(2,1)S(1)} %add.234), channel_id=1, source_target_pairs={{0,16},{16,0},{1,17},{17,1},{2,18},{18,2},{3,19},{19,3},{4,20},{20... | collective-permute-start | bytes 995336 | tf_op jit(solution)/shard_map/ppermute | solution.py:537
  395.3 16.9 %collective-permute-start.13 = (bf16[432,768]{1,0:T(8,128)(2,1)S(1)}, bf16[432,768]{1,0:T(8,128)(2,1)S(1)}, u32[]{:S(2)}, u32[]{:S(2)}) collective-permute-start(bf16[432,768]{1,0:T(8,128)(2,1)S(1)} %pad_maximum_fusion.4), channel_id=1, source_target_pairs={{0,8},{8,0},{1,9},{9,1},{2,10},{10,2},{3,11},{11,3},{4,12},{12,4},... | collective-permute-start | bytes 1990664 | tf_op jit(solution)/shard_map/ppermute | solution.py:537
  430.0 48.1 %all-to-all-start.3 = ((bf16[16,128,768]{2,1,0:T(8,128)(2,1)}), bf16[16,128,768]{2,1,0:T(8,128)(2,1)}, u32[]{:S(2)}, u32[]{:S(2)}) async-start(bf16[16,128,768]{2,1,0:T(8,128)(2,1)} %bitcast.67), calls=%async_computation.3 | async-start | bytes 6291456 | tf_op jit(solution)/shard_map/all_to_all | solution.py:623
  478.1 70.2 %all-to-all-start.4 = ((bf16[16,128,768]{2,1,0:T(8,128)(2,1)}), bf16[16,128,768]{2,1,0:T(8,128)(2,1)}, u32[]{:S(2)}, u32[]{:S(2)}) async-start(bf16[16,128,768]{2,1,0:T(8,128)(2,1)} %bitcast.66), calls=%async_computation.4 | async-start | bytes 6291456 | tf_op jit(solution)/shard_map/all_to_all | solution.py:623
  488.9 59.4 %collective-permute-start.17 = (bf16[576,768]{1,0:T(8,128)(2,1)S(1)}, bf16[576,768]{1,0:T(8,128)(2,1)}, u32[]{:S(2)}, u32[]{:S(2)}) collective-permute-start(bf16[576,768]{1,0:T(8,128)(2,1)S(1)} %fusion.35), channel_id=1, source_target_pairs={{0,16},{16,0},{1,17},{17,1},{2,18},{18,2},{3,19},{19,3},{4,20},{20... | collective-permute-start | bytes 2654216 | tf_op jit(solution)/shard_map/ppermute | solution.py:537
  597.3 32.0 %collective-permute-start.28 = (bf16[864,768]{1,0:T(8,128)(2,1)S(1)}, bf16[864,768]{1,0:T(8,128)(2,1)S(1)}, u32[]{:S(2)}, u32[]{:S(2)}) collective-permute-start(bf16[864,768]{1,0:T(8,128)(2,1)S(1)} %copy-done.11), channel_id=1, source_target_pairs={{0,4},{4,0},{1,5},{5,1},{2,6},{6,2},{3,7},{7,3},{8,12},{12,8},{9,1... | collective-permute-start | bytes 3981320 | tf_op jit(solution)/shard_map/ppermute | solution.py:537
  598.8 30.5 %collective-permute-start.29 = (bf16[864,768]{1,0:T(8,128)(2,1)S(1)}, bf16[864,768]{1,0:T(8,128)(2,1)S(1)}, u32[]{:S(2)}, u32[]{:S(2)}) collective-permute-start(bf16[864,768]{1,0:T(8,128)(2,1)S(1)} %copy-done.12), channel_id=1, source_target_pairs={{0,1},{1,0},{2,3},{3,2},{4,5},{5,4},{6,7},{7,6},{8,9},{9,8},{10,11... | collective-permute-start | bytes 3981320 | tf_op jit(solution)/shard_map/ppermute | solution.py:537
  601.6 26.4 %collective-permute-start.27 = (bf16[160,768]{1,0:T(8,128)(2,1)S(1)}, bf16[160,768]{1,0:T(8,128)(2,1)S(1)}, u32[]{:S(2)}, u32[]{:S(2)}) collective-permute-start(bf16[160,768]{1,0:T(8,128)(2,1)S(1)} %get-tuple-element.402), channel_id=1, source_target_pairs={{0,4},{4,0},{1,5},{5,1},{2,6},{6,2},{3,7},{7,3},{8,12},{12,8},{9,1... | collective-permute-start | bytes 737288 | tf_op jit(solution)/shard_map/ppermute | solution.py:537
  603.6 25.6 %collective-permute-start.26 = (bf16[160,768]{1,0:T(8,128)(2,1)S(1)}, bf16[160,768]{1,0:T(8,128)(2,1)S(1)}, u32[]{:S(2)}, u32[]{:S(2)}) collective-permute-start(bf16[160,768]{1,0:T(8,128)(2,1)S(1)} %get-tuple-element.403), channel_id=1, source_target_pairs={{0,1},{1,0},{2,3},{3,2},{4,5},{5,4},{6,7},{7,6},{8,9},{9,8},{10,11... | collective-permute-start | bytes 737288 | tf_op jit(solution)/shard_map/ppermute | solution.py:537
  632.6 18.1 %collective-permute-start.32 = (bf16[3456,768]{1,0:T(8,128)(2,1)}, bf16[3456,768]{1,0:T(8,128)(2,1)}, u32[]{:S(2)}, u32[]{:S(2)}) collective-permute-start(bf16[3456,768]{1,0:T(8,128)(2,1)} %pad_maximum_fusion.own_ref), channel_id=1, source_target_pairs={{0,2},{2,0},{1,3},{3,1},{4,6},{6,4},{5,7},{7,5},{8,10},{10,8},{9,1... | collective-permute-start | bytes 15925256 | tf_op jit(solution)/shard_map/ppermute | solution.py:537
  646.6 22.8 %collective-permute-start.33 = (bf16[1280,768]{1,0:T(8,128)(2,1)S(1)}, bf16[1280,768]{1,0:T(8,128)(2,1)}, u32[]{:S(2)}, u32[]{:S(2)}) collective-permute-start(bf16[1280,768]{1,0:T(8,128)(2,1)S(1)} %pad_maximum_fusion.1.own_ref), channel_id=1, source_target_pairs={{0,2},{2,0},{1,3},{3,1},{4,6},{6,4},{5,7},{7,5},{8,10},{10,8},{9,1... | collective-permute-start | bytes 5898248 | tf_op jit(solution)/shard_map/ppermute | solution.py:537
  (82 other events, 1041.5 us)

commit v7 on v6

--- a/solution.py
+++ b/solution.py
@@ -451,51 +451,63 @@
     )(half.reshape(1), activated, grad_ffn, grad_pre, normed, ctx, grad_attn)
 
 
-def unpack_kernel(counts, upright, core_ref, own_ref, other_ref, *out_refs):
+def unpack_early_kernel(upper, core_ref, *refs):
+    (down_own, down_other, up_own, up_other, out_own, out_other, down_ref, up_ref, out_ref) = refs
     at = pl.program_id(0)
-    half = pl.num_programs(0) // 2
-    mine = jnp.where(at < half, 0, 1) == core_ref[0]
-    rows = jnp.where(mine, own_ref[...], other_ref[...]).astype(F32)
-    first = 0
-    for count, turn, out_ref in zip(counts, upright, out_refs):
-
-        @pl.when((at >= first) & (at < first + count))
-        def _(turn=turn, out_ref=out_ref):
-            out_ref[...] = rows.T if turn else rows
-
-        first += count
-
-
-def unpack(core, own, other, heights, upright, block):
+    low = core_ref[0] == 0
+    down_ref[...] = jnp.where(low, down_own[...], down_other[...]).astype(F32)
+    mine = jnp.where(at < upper, low, jnp.logical_not(low))
+    up_ref[...] = jnp.where(mine, up_own[...], up_other[...]).astype(F32).T
+
+    @pl.when(at < out_ref.shape[0])
+    def _():
+        out_ref[at] = jnp.where(low, out_other[...], out_own[...]).astype(F32)
+
+
+def unpack_early(core, own, other, wide, block=384):
     half, width = own.shape
-    steps = 2 * half // block
-    counts = [height // block for height in heights]
-    last = steps // 2 - 1
-    source = lambda turn: pl.BlockSpec(
-        (block, width),
-        lambda i, c: (jnp.clip(i - (c[0] if turn == 0 else 1 - c[0]) * (last + 1), 0, last), 0),
-    )
-    specs, shapes = [], []
-    first = 0
-    for height, count, turn in zip(heights, counts, upright):
-        place = lambda i, first=first, count=count: jnp.clip(i - first, 0, count - 1)
-        if turn:
-            specs.append(pl.BlockSpec((width, block), lambda i, c, place=place: (0, place(i))))
-            shapes.append(jax.ShapeDtypeStruct((width, height), F32))
-        else:
-            specs.append(pl.BlockSpec((block, width), lambda i, c, place=place: (place(i), 0)))
-            shapes.append(jax.ShapeDtypeStruct((height, width), F32))
-        first += count
-    return pl.pallas_call(
-        functools.partial(unpack_kernel, counts, upright),
+    steps, blocks = wide // block, half // block
+    upper = blocks - steps
+    outs = width // block
+    last = blocks - 1
+    pick = lambda use, place: jnp.where(use, place, last)
+
+    def pair(place, in_low):
+        return [
+            pl.BlockSpec(
+                (block, width),
+                lambda i, c, turn=turn: (pick(in_low(i) == (c[0] == turn), place(i)), 0),
+            )
+            for turn in range(2)
+        ]
+
+    sources = (
+        pair(lambda i: i, lambda i: i >= 0)
+        + pair(lambda i: jnp.where(i < upper, steps + i, i - upper), lambda i: i < upper)
+        + pair(lambda i: blocks - outs + jnp.minimum(i, outs - 1), lambda i: i < 0)
+    )
+    down, up, out = pl.pallas_call(
+        functools.partial(unpack_early_kernel, upper),
         grid_spec=pltpu.PrefetchScalarGridSpec(
-            num_scalar_prefetch=1, grid=(steps,), in_specs=[source(0), source(1)], out_specs=specs
+            num_scalar_prefetch=1,
+            grid=(steps,),
+            in_specs=sources,
+            out_specs=[
+                pl.BlockSpec((block, width), lambda i, c: (i, 0)),
+                pl.BlockSpec((width, block), lambda i, c: (0, i)),
+                pl.BlockSpec((outs, block, width), lambda i, c: (0, 0, 0)),
+            ],
         ),
-        out_shape=shapes,
+        out_shape=[
+            jax.ShapeDtypeStruct((wide, width), F32),
+            jax.ShapeDtypeStruct((width, wide), F32),
+            jax.ShapeDtypeStruct((outs, block, width), F32),
+        ],
         compiler_params=params(60),
-        cost_estimate=cost(2 * half * width, 2 * half * width * 8),
-        name="unpack",
-    )(core.reshape(1), own, other)
+        cost_estimate=cost(2 * half * width, 2 * half * width * 6),
+        name="unpack_early",
+    )(core.reshape(1), *(own, other) * 3)
+    return down, up, out.reshape(width, width)
 
 
 def unpack_whole_kernel(heights, core_ref, own_ref, other_ref, *out_refs):
@@ -772,34 +784,37 @@
         (keep, send, outgoing, returned_other)
     )
     returned = give_back(outgoing[0])
-    from_other = swap(mm(owned[1].astype(BF16), returned_other).astype(BF16), top_axis)
+    for_other = mm(owned[1].astype(BF16), returned_other).astype(BF16)
     late = jnp.split(keep + swap(send, core), 2, axis=0)
-    returned, late, early, from_other = lax.optimization_barrier((returned, late, early, from_other))
-    table_grads = mm(owned[0].astype(BF16), returned) + from_other.astype(F32)
-    late = run_stages(late, stages[:2])
-    late, early = lax.optimization_barrier((late, early))
+    returned, late, early, for_other = lax.optimization_barrier((returned, late, early, for_other))
+    table_own = mm(owned[0].astype(BF16), returned)
+    from_other = swap(for_other, top_axis)
+    last = len(stages) - 1
     early_step = begin(early, stages[done])
-    last = len(stages) - 1
-    for at, stage in enumerate(stages[2:], start=2):
+    for at, stage in enumerate(stages):
         keeps, sends = begin(late, stage)
+        if at == 1:
+            keeps, sends, early_step = lax.optimization_barrier((keeps, sends, early_step))
+            early_came = travel(early_step[1], stages[done])
         if at == 2:
-            keeps, sends, early_step = lax.optimization_barrier((keeps, sends, early_step))
-        came = travel(sends, stage)
-        if at == 2:
-            early_came = travel(early_step[1], stages[done])
-        if at == 4:
-            came, table_grads = lax.optimization_barrier((came, table_grads))
-        late = end(keeps, came, stage)
-        if at == last - 1:
-            late, early_came = lax.optimization_barrier((late, early_came))
+            keeps, sends, from_other = lax.optimization_barrier((keeps, sends, from_other))
+        if at == 3:
+            keeps, sends, early_came = lax.optimization_barrier((keeps, sends, early_came))
             early = end(early_step[0], early_came, stages[done])
             early = jnp.concatenate(run_stages(early, stages[done + 1 :]), axis=0)
             early_step = (early, swap(early, core))
+        if at == last - 2:
+            keeps, sends, early_step = lax.optimization_barrier((keeps, sends, early_step))
+        came = travel(sends, stage)
+        if at == 4:
+            table_grads = table_own + from_other.astype(F32)
+            came, table_grads = lax.optimization_barrier((came, table_grads))
+        if at == last - 2:
+            early = unpack_early(my_core, *early_step, wide)
+            came, early = lax.optimization_barrier((came, early))
+        late = end(keeps, came, stage)
     late = jnp.concatenate(late, axis=0)
     late_other = swap(late, core)
-    late, early_step = lax.optimization_barrier((late, early_step))
-    early = unpack(my_core, *early_step, (wide, wide, width), (False, True, False), 384)
-    late_other, early = lax.optimization_barrier((late_other, early))
     w_down_grad, w_up_grad, w_out_grad = early
     w_query_grad, w_key_grad, w_value_grad, expr_grad, short = unpack_whole(
         my_core, late, late_other, heights

time: 686 us -> 676 us (0.985)
  waiting for transfers between devices: 257 us -> 248 us
    ppermute x30, waiting for transfers between devices: 136 us -> 93.4 us  [swap(): return lax.ppermute(value, axis, SWAP)]
    all_to_all x5, waiting for transfers between devices: 60 us -> 93.1 us  [exchange(): lax.all_to_all(value, group_axes, split_axis=axis, concat_axis=axis, tile...]
  transfers between devices with their start and end apart: 39 -> 39, of which waited for: 22 -> 21; matrix products, arithmetic and copies ran while one was open for 14% -> 15% of each run, Pallas kernels for 21% -> 21%
where the time goes in v7:
time: 676 us; the launch traced here: 668 us
  waiting for transfers between devices  248 us (37%)
  Pallas kernels  218 us (32%)
  matrix products  81 us (12%)
  starting transfers between devices  58.1 us (9%)
  other arithmetic  37.8 us (6%)
  local copies, waits for them, and re-layouts  22.5 us (3%)
    ppermute x30, waiting for transfers between devices, swap(): return lax.ppermute(value, axis, SWAP)  93.4 us
    all_to_all x5, waiting for transfers between devices, exchange(): lax.all_to_all(value, group_axes, split_axis=axis, concat_axis=axis, tile...  93.1 us
    pallas_call x5, Pallas kernels, attend_back(): pl.pallas_call(functools.partial(attend_back_kernel, add, len(into)), gri...  87.1 us
    dot_general x26, matrix products, mm(): return lax.dot_general(left, right, dims, preferred_element_type=F32)  81 us
    ppermute x1, waiting for transfers between devices, local(): know_other = lax.ppermute(know_sum, top_axis, SWAP)  51.8 us
    pallas_call x2, Pallas kernels, attend(): pl.pallas_call(functools.partial(attend_kernel, merge), grid_spec=pltpu.P...  43.5 us
    pallas_call x1, Pallas kernels, middle(): pl.pallas_call(middle_kernel, grid=(tokens // block,), in_specs=[rows(wid...  37.3 us
    pallas_call x2, Pallas kernels, weight_sums(): pl.pallas_call(functools.partial(weight_sums_kernel, counts), grid_spec=p...  27.4 us
  transfers between devices with their start and end apart: 39, of which 21 were waited for; matrix products, arithmetic and copies ran while one was open for 15% of the time, Pallas kernels for 21%

profile of v7, /device:TPU:0, one launch (start us, length us, event | category | flops | bytes accessed | tf_op | source)
XLA Modules:
  0.0 668.4 jit_solution(16515002290670168072)
XLA Ops:
  17.8 8.9 %all-to-all-done = s32[2,16,128]{2,0,1:T(2,128)S(1)} async-done(((s32[2,16,128]{2,0,1:T(2,128)}), s32[2,16,128]{2,0,1:T(2,128)S(1)}, u32[]{:S(2)}, u32[]{:S(2)}) %all-to-all-start) | async-done | bytes 16416 | tf_op jit(solution)/shard_map/all_to_all | solution.py:635
  37.5 51.8 %collective-permute-done.1 = bf16[288,768]{1,0:T(8,128)(2,1)S(1)} collective-permute-done((bf16[288,768]{1,0:T(8,128)(2,1)S(1)}, bf16[288,768]{1,0:T(8,128)(2,1)S(1)}, u32[]{:S(2)}, u32[]{:S(2)}) %collective-permute-start.1) | collective-permute-done | bytes 442400 | tf_op jit(solution)/shard_map/ppermute | solution.py:646
  105.3 7.9 %fusion.5 = f32[1024,768]{1,0:T(8,128)} fusion(bf16[2048,768]{1,0:T(8,128)(2,1)} %bitcast.10, s32[1024]{0:T(1024)S(1)} %reduce.3, s32[1024]{0:T(1024)S(1)} %reduce.2), kind=kOutput, calls=%fused_computation.7 | convolution fusion | flops 3227516928 | bytes 6299648 | tf_op jit(solution)/shard_map/dot_general | solution.py:24
  113.2 31.0 %all-to-all-done.2 = bf16[16,128,768]{2,1,0:T(8,128)(2,1)} async-done(((bf16[16,128,768]{2,1,0:T(8,128)(2,1)}), bf16[16,128,768]{2,1,0:T(8,128)(2,1)}, u32[]{:S(2)}, u32[]{:S(2)}) %all-to-all-start.2) | async-done | bytes 3145760 | tf_op jit(solution)/shard_map/all_to_all | solution.py:635
  158.2 21.1 %attend.1 = (f32[768,1024]{1,0:T(8,128)}, f32[6,2,1024]{2,1,0:T(2,128)S(1)}) custom-call(s32[2]{0:T(128)S(1)} %pad_add_fusion.1.where_ref, bf16[1024,768]{1,0:T(8,128)(2,1)S(1)} %add_convert_fusion.3.q_ref, bf16[1024,768]{1,0:T(8,128)(2,1)S(1)} %convolution_convert_fusion.k_ref, bf16[1024,768]{1,0:T(8,128)(2,1)S(1)} %add_convert_fusion.1.v_ref), custom_call_target="tpu_custom_call" | custom-call | flops 12884901888 | bytes 15728640 | tf_op jit(solution)/shard_map/attend/pallas_call | solution.py:168
  179.3 9.6 %collective-permute-done.2 = bf16[1024,768]{1,0:T(8,128)(2,1)S(1)} collective-permute-done((bf16[1024,768]{1,0:T(8,128)(2,1)S(1)}, bf16[1024,768]{1,0:T(8,128)(2,1)S(1)}, u32[]{:S(2)}, u32[]{:S(2)}) %collective-permute-start.2) | collective-permute-done | bytes 1572896 | tf_op jit(solution)/shard_map/ppermute | solution.py:664
  191.8 22.4 %attend_more.1 = (f32[1024,768]{1,0:T(8,128)}, f32[6,2,1024]{2,1,0:T(2,128)S(1)}) custom-call(s32[2]{0:T(128)S(1)} %pad_add_fusion.where_ref, bf16[1024,768]{1,0:T(8,128)(2,1)S(1)} %add_convert_fusion.3.q_ref, bf16[1024,768]{1,0:T(8,128)(2,1)S(1)} %convolution_convert_fusion.1.k_ref, bf16[1024,768]{1,0:T(8,128)(2,1)S(1)} %add_convert_fusion.2.v_ref, ...), custom_call_target="tpu_custom_call" | custom-call | flops 12884901888 | bytes 15728640 | tf_op jit(solution)/shard_map/attend_more/pallas_call | solution.py:168
  214.8 37.3 %middle.1 = (bf16[1024,768]{1,0:T(8,128)(2,1)}, bf16[1024,768]{1,0:T(8,128)(2,1)}, bf16[1024,768]{1,0:T(8,128)(2,1)}, bf16[1024,3072]{1,0:T(8,128)(2,1)}, bf16[1...) custom-call(f32[1024,768]{1,0:T(8,128)} %get-tuple-element.201.ctx_r, ...), custom_call_target="tpu_custom_call" | custom-call | flops 43486543872 | bytes 34603008 | tf_op jit(solution)/shard_map/middle/pallas_call | solution.py:376
  252.1 13.8 %weight_sums.2 = bf16[3456,768]{1,0:T(8,128)(2,1)} custom-call(s32[1]{0:T(128)} %bitcast.19.half_ref, bf16[1024,3072]{1,0:T(8,128)(2,1)} %get-tuple-element.209.act_ref, bf16[1024,768]{1,0:T(8,128)(2,1)} %get-tuple-element.210.gffn_ref, bf16[1024,3072]{1,0:T(8,128)(2,1)} %get-tuple-element.211.gpre_ref, bf16[1024,768]{1,0:T(8,128)(2,1)} %get-tuple-element.212.norm_ref, ...), custom_call_target="tpu_custom_call" | custom-call | flops 5435817984 | bytes 12386304 | tf_op jit(solution)/shard_map/weight_sums/pallas_call | solution.py:439
  265.9 13.6 %weight_sums.3 = bf16[3456,768]{1,0:T(8,128)(2,1)} custom-call(s32[1]{0:T(128)} %bitcast.18.half_ref.core_ref, bf16[1024,3072]{1,0:T(8,128)(2,1)} %get-tuple-element.209.act_ref, bf16[1024,768]{1,0:T(8,128)(2,1)} %get-tuple-element.210.gffn_ref, bf16[1024,3072]{1,0:T(8,128)(2,1)} %get-tuple-element.211.gpre_ref, ...), custom_call_target="tpu_custom_call" | custom-call | flops 5435817984 | bytes 12386304 | tf_op jit(solution)/shard_map/weight_sums/pallas_call | solution.py:439
  288.1 26.6 %attend_back0.1 = (f32[1024,768]{1,0:T(8,128)}, bf16[1024,768]{1,0:T(8,128)(2,1)}, bf16[1024,768]{1,0:T(8,128)(2,1)}) custom-call(s32[2]{0:T(128)} %copy-done.2, bf16[1024,768]{1,0:T(8,128)(2,1)} %copy-done.5, bf16[1024,768]{1,0:T(8,128)(2,1)} %get-tuple-element.278.g_ref, f32[1024,768]{1,0:T(8,128)} %get-tuple-element.201.ctx_ref.o_ref, ...), custom_call_target="tpu_custom_call" | custom-call | flops 21474836480 | bytes 12582912 | tf_op jit(solution)/shard_map/attend_back0/pallas_call | solution.py:248
  322.0 15.1 %attend_back4.1 = (f32[1024,768]{1,0:T(8,128)}, bf16[1024,768]{1,0:T(8,128)(2,1)}, bf16[1024,768]{1,0:T(8,128)(2,1)}) custom-call(s32[2]{0:T(128)} %copy-done.2, bf16[1024,768]{1,0:T(8,128)(2,1)} %copy-done.5, bf16[1024,768]{1,0:T(8,128)(2,1)} %get-tuple-element.278.g_ref, ...), custom_call_target="tpu_custom_call", output_to_operand_aliasing={{0}: (7, {}), {1}: (8, {}), {2}: (9, {})} | custom-call | flops 10737418240 | bytes 6291456 | tf_op jit(solution)/shard_map/attend_back4/pallas_call | solution.py:248
  346.2 15.2 %attend_back_more0.1 = (bf16[1024,768]{1,0:T(8,128)(2,1)}, bf16[1024,768]{1,0:T(8,128)(2,1)}, bf16[1024,768]{1,0:T(8,128)(2,1)}) custom-call(s32[2]{0:T(128)} %copy-done.1, bf16[1024,768]{1,0:T(8,128)(2,1)} %copy-done.5, bf16[1024,768]{1,0:T(8,128)(2,1)} %get-tuple-element.278.g_ref, f32[1024,768]{1,0:T(8,128)} %get-tuple-element.201.ctx_ref.o_ref, ...), custom_call_target="tpu_custom_call" | custom-call | flops 10737418240 | bytes 6291456 | tf_op jit(solution)/shard_map/attend_back_more0/pallas_call | solution.py:248
  363.8 14.9 %attend_back_more2.1 = (bf16[1024,768]{1,0:T(8,128)(2,1)}, bf16[1024,768]{1,0:T(8,128)(2,1)}, bf16[1024,768]{1,0:T(8,128)(2,1)}) custom-call(s32[2]{0:T(128)} %copy-done.1, bf16[1024,768]{1,0:T(8,128)(2,1)} %copy-done.5, bf16[1024,768]{1,0:T(8,128)(2,1)} %get-tuple-element.278.g_ref, ...), custom_call_target="tpu_custom_call", output_to_operand_aliasing={{0}: (8, {}), {1}: (9, {}), {2}: (10, {})} | custom-call | flops 10737418240 | bytes 6291456 | tf_op jit(solution)/shard_map/attend_back_more2/pallas_call | solution.py:248
  379.7 15.4 %attend_back_more4.1 = (bf16[1024,768]{1,0:T(8,128)(2,1)}, bf16[1024,768]{1,0:T(8,128)(2,1)}, bf16[1024,768]{1,0:T(8,128)(2,1)}) custom-call(s32[2]{0:T(128)} %copy-done.1, bf16[1024,768]{1,0:T(8,128)(2,1)} %copy-done.5, bf16[1024,768]{1,0:T(8,128)(2,1)} %get-tuple-element.278.g_ref, ...), custom_call_target="tpu_custom_call", output_to_operand_aliasing={{0}: (8, {}), {1}: (9, {}), {2}: (10, {})} | custom-call | flops 10737418240 | bytes 6291456 | tf_op jit(solution)/shard_map/attend_back_more4/pallas_call | solution.py:248
  404.7 7.7 %collective-permute-done.13 = bf16[432,768]{1,0:T(8,128)(2,1)S(1)} collective-permute-done((bf16[432,768]{1,0:T(8,128)(2,1)S(1)}, bf16[432,768]{1,0:T(8,128)(2,1)S(1)}, u32[]{:S(2)}, u32[]{:S(2)}) %collective-permute-start.13) | collective-permute-done | bytes 663584 | tf_op jit(solution)/shard_map/ppermute | solution.py:549
  420.4 6.5 fusion.23
  458.3 20.1 %all-to-all-done.3 = bf16[16,128,768]{2,1,0:T(8,128)(2,1)} async-done(((bf16[16,128,768]{2,1,0:T(8,128)(2,1)}), bf16[16,128,768]{2,1,0:T(8,128)(2,1)}, u32[]{:S(2)}, u32[]{:S(2)}) %all-to-all-start.3) | async-done | bytes 3145760 | tf_op jit(solution)/shard_map/all_to_all | solution.py:635
  496.4 33.2 %all-to-all-done.4 = bf16[16,128,768]{2,1,0:T(8,128)(2,1)} async-done(((bf16[16,128,768]{2,1,0:T(8,128)(2,1)}), bf16[16,128,768]{2,1,0:T(8,128)(2,1)}, u32[]{:S(2)}, u32[]{:S(2)}) %all-to-all-start.4) | async-done | bytes 3145760 | tf_op jit(solution)/shard_map/all_to_all | solution.py:635
  531.4 12.4 %collective-permute-done.18 = bf16[320,768]{1,0:T(8,128)(2,1)} collective-permute-done((bf16[320,768]{1,0:T(8,128)(2,1)}, bf16[320,768]{1,0:T(8,128)(2,1)}, u32[]{:S(2)}, u32[]{:S(2)}) %collective-permute-start.18) | collective-permute-done | bytes 491552 | tf_op jit(solution)/shard_map/ppermute | solution.py:549
  551.2 32.7 %collective-permute-done.19 = bf16[160,768]{1,0:T(8,128)(2,1)} collective-permute-done((bf16[160,768]{1,0:T(8,128)(2,1)S(1)}, bf16[160,768]{1,0:T(8,128)(2,1)}, u32[]{:S(2)}, u32[]{:S(2)}) %collective-permute-start.19) | collective-permute-done | bytes 245792 | tf_op jit(solution)/shard_map/ppermute | solution.py:549
  590.3 7.9 %collective-permute-done.22 = bf16[160,768]{1,0:T(8,128)(2,1)S(1)} collective-permute-done((bf16[160,768]{1,0:T(8,128)(2,1)S(1)}, bf16[160,768]{1,0:T(8,128)(2,1)S(1)}, u32[]{:S(2)}, u32[]{:S(2)}) %collective-permute-start.22) | collective-permute-done | bytes 245792 | tf_op jit(solution)/shard_map/ppermute | solution.py:549
  620.0 13.7 %unpack_early.1 = (f32[3072,768]{1,0:T(8,128)}, f32[768,3072]{1,0:T(8,128)}, f32[2,384,768]{2,1,0:T(8,128)}) custom-call(s32[1]{0:T(128)} %bitcast.18.half_ref.core_ref, bf16[3456,768]{1,0:T(8,128)(2,1)} %copy-done.9, bf16[3456,768]{1,0:T(8,128)(2,1)} %copy-done.10, bf16[3456,768]{1,0:T(8,128)(2,1)} %copy-done.9, bf16[3456,768]{1,0:T(8,128)(2,1)} %copy-done.10, ...), custom_call_target="tpu_custom_call" | custom-call | flops 5308416 | bytes 31850496 | tf_op jit(solution)/shard_map/unpack_early/pallas_call | solution.py:489
  644.8 8.4 %collective-permute-done.30 = bf16[320,768]{1,0:T(8,128)(2,1)S(1)} collective-permute-done((bf16[320,768]{1,0:T(8,128)(2,1)S(1)}, bf16[320,768]{1,0:T(8,128)(2,1)S(1)}, u32[]{:S(2)}, u32[]{:S(2)}) %collective-permute-start.30) | collective-permute-done | bytes 491552 | tf_op jit(solution)/shard_map/ppermute | solution.py:549
  (311 shorter events, 218.1 us)
Async XLA Ops:
  0.7 26.0 %collective-permute-start = (bf16[288,768]{1,0:T(8,128)(2,1)}, bf16[288,768]{1,0:T(8,128)(2,1)}, u32[]{:S(2)}, u32[]{:S(2)}) collective-permute-start(bf16[288,768]{1,0:T(8,128)(2,1)} %param.31), channel_id=1, source_target_pairs={{0,16},{16,0},{1,17},{17,1},{2,18},{18,2},{3,19},{19,3},{4,20},{20... | collective-permute-start | bytes 1327112 | tf_op jit(solution)/shard_map/ppermute | solution.py:638
  11.1 15.6 %all-to-all-start = ((s32[2,16,128]{2,0,1:T(2,128)}), s32[2,16,128]{2,0,1:T(2,128)S(1)}, u32[]{:S(2)}, u32[]{:S(2)}) async-start(s32[2,16,128]{2,0,1:T(2,128)} %copy.61), calls=%async_computation | async-start | bytes 32768 | tf_op jit(solution)/shard_map/all_to_all | solution.py:635
  31.9 62.5 %all-to-all-start.1 = ((bf16[16,128,768]{2,1,0:T(8,128)(2,1)}), bf16[16,128,768]{2,1,0:T(8,128)(2,1)}, u32[]{:S(2)}, u32[]{:S(2)}) async-start(bf16[16,128,768]{2,1,0:T(8,128)(2,1)} %bitcast.70), calls=%async_computation.1 | async-start | bytes 6291456 | tf_op jit(solution)/shard_map/all_to_all | solution.py:635
  36.4 52.9 %collective-permute-start.1 = (bf16[288,768]{1,0:T(8,128)(2,1)S(1)}, bf16[288,768]{1,0:T(8,128)(2,1)S(1)}, u32[]{:S(2)}, u32[]{:S(2)}) collective-permute-start(bf16[288,768]{1,0:T(8,128)(2,1)S(1)} %reduce_sum.75), channel_id=1, source_target_pairs={{0,16},{16,0},{1,17},{17,1},{2,18},{18,2},{3,19},{19,3},{4,20},{20... | collective-permute-start | bytes 1327112 | tf_op jit(solution)/shard_map/ppermute | solution.py:646
  94.4 49.8 %all-to-all-start.2 = ((bf16[16,128,768]{2,1,0:T(8,128)(2,1)}), bf16[16,128,768]{2,1,0:T(8,128)(2,1)}, u32[]{:S(2)}, u32[]{:S(2)}) async-start(bf16[16,128,768]{2,1,0:T(8,128)(2,1)} %bitcast.69), calls=%async_computation.2 | async-start | bytes 6291456 | tf_op jit(solution)/shard_map/all_to_all | solution.py:635
  103.2 76.1 %collective-permute-start.3 = (s32[576]{0:T(1024)S(1)}, s32[576]{0:T(1024)S(1)}, u32[]{:S(2)}, u32[]{:S(2)}) collective-permute-start(s32[576]{0:T(1024)S(1)} %convert_reduce_fusion.1), channel_id=1, source_target_pairs={{0,16},{16,0},{1,17},{17,1},{2,18},{18,2},{3,19},{19,3},{4,20},{20... | collective-permute-start | bytes 6920 | tf_op jit(solution)/shard_map/ppermute | solution.py:672
  152.4 36.6 %collective-permute-start.2 = (bf16[1024,768]{1,0:T(8,128)(2,1)S(1)}, bf16[1024,768]{1,0:T(8,128)(2,1)S(1)}, u32[]{:S(2)}, u32[]{:S(2)}) collective-permute-start(bf16[1024,768]{1,0:T(8,128)(2,1)S(1)} %get-tuple-element.422), channel_id=1, source_target_pairs={{0,1},{1,0},{2,3},{3,2},{4,5},{5,4},{6,7},{7,6},{8,9},{9,8},{10,11... | collective-permute-start | bytes 4718600 | tf_op jit(solution)/shard_map/ppermute | solution.py:664
  286.7 32.2 %collective-permute-start.5 = (bf16[864,768]{1,0:T(8,128)(2,1)}, bf16[864,768]{1,0:T(8,128)(2,1)S(1)}, u32[]{:S(2)}, u32[]{:S(2)}) collective-permute-start(bf16[864,768]{1,0:T(8,128)(2,1)} %get-tuple-element.221), channel_id=1, source_target_pairs={{0,4},{4,0},{1,5},{5,1},{2,6},{6,2},{3,7},{7,3},{8,12},{12,8},{9,1... | collective-permute-start | bytes 3981320 | tf_op jit(solution)/shard_map/ppermute | solution.py:549
  287.6 31.3 %collective-permute-start.6 = (bf16[864,768]{1,0:T(8,128)(2,1)S(1)}, bf16[864,768]{1,0:T(8,128)(2,1)S(1)}, u32[]{:S(2)}, u32[]{:S(2)}) collective-permute-start(bf16[864,768]{1,0:T(8,128)(2,1)S(1)} %get-tuple-element.222), channel_id=1, source_target_pairs={{0,1},{1,0},{2,3},{3,2},{4,5},{5,4},{6,7},{7,6},{8,9},{9,8},{10,11... | collective-permute-start | bytes 3981320 | tf_op jit(solution)/shard_map/ppermute | solution.py:549
  319.8 17.3 %collective-permute-start.7 = (bf16[432,768]{1,0:T(8,128)(2,1)S(1)}, bf16[432,768]{1,0:T(8,128)(2,1)S(1)}, u32[]{:S(2)}, u32[]{:S(2)}) collective-permute-start(bf16[432,768]{1,0:T(8,128)(2,1)S(1)} %get-tuple-element.235), channel_id=1, source_target_pairs={{0,1},{1,0},{2,3},{3,2},{4,5},{5,4},{6,7},{7,6},{8,9},{9,8},{10,11... | collective-permute-start | bytes 1990664 | tf_op jit(solution)/shard_map/ppermute | solution.py:549
  320.4 16.7 %collective-permute-start.8 = (bf16[432,768]{1,0:T(8,128)(2,1)S(1)}, bf16[432,768]{1,0:T(8,128)(2,1)S(1)}, u32[]{:S(2)}, u32[]{:S(2)}) collective-permute-start(bf16[432,768]{1,0:T(8,128)(2,1)S(1)} %get-tuple-element.236), channel_id=1, source_target_pairs={{0,4},{4,0},{1,5},{5,1},{2,6},{6,2},{3,7},{7,3},{8,12},{12,8},{9,1... | collective-permute-start | bytes 1990664 | tf_op jit(solution)/shard_map/ppermute | solution.py:549
  343.8 17.6 %collective-permute-start.9 = (bf16[432,768]{1,0:T(8,128)(2,1)S(1)}, bf16[432,768]{1,0:T(8,128)(2,1)S(1)}, u32[]{:S(2)}, u32[]{:S(2)}) collective-permute-start(bf16[432,768]{1,0:T(8,128)(2,1)S(1)} %get-tuple-element.252), channel_id=1, source_target_pairs={{0,8},{8,0},{1,9},{9,1},{2,10},{10,2},{3,11},{11,3},{4,12},{12,4},... | collective-permute-start | bytes 1990664 | tf_op jit(solution)/shard_map/ppermute | solution.py:549
  345.7 49.8 %collective-permute-start.12 = (bf16[1024,768]{1,0:T(8,128)(2,1)S(1)}, bf16[1024,768]{1,0:T(8,128)(2,1)S(1)}, u32[]{:S(2)}, u32[]{:S(2)}) collective-permute-start(bf16[1024,768]{1,0:T(8,128)(2,1)S(1)} %add_convert_fusion), channel_id=1, source_target_pairs={{0,1},{1,0},{2,3},{3,2},{4,5},{5,4},{6,7},{7,6},{8,9},{9,8},{10,11... | collective-permute-start | bytes 4718600 | tf_op jit(solution)/shard_map/ppermute | solution.py:549
  361.6 17.0 %collective-permute-start.10 = (bf16[216,768]{1,0:T(8,128)(2,1)S(1)}, bf16[216,768]{1,0:T(8,128)(2,1)S(1)}, u32[]{:S(2)}, u32[]{:S(2)}) collective-permute-start(bf16[216,768]{1,0:T(8,128)(2,1)S(1)} %get-tuple-element.263), channel_id=1, source_target_pairs={{0,16},{16,0},{1,17},{17,1},{2,18},{18,2},{3,19},{19,3},{4,20},{20... | collective-permute-start | bytes 995336 | tf_op jit(solution)/shard_map/ppermute | solution.py:549
  378.8 16.6 %collective-permute-start.11 = (bf16[216,768]{1,0:T(8,128)(2,1)S(1)}, bf16[216,768]{1,0:T(8,128)(2,1)S(1)}, u32[]{:S(2)}, u32[]{:S(2)}) collective-permute-start(bf16[216,768]{1,0:T(8,128)(2,1)S(1)} %add.234), channel_id=1, source_target_pairs={{0,16},{16,0},{1,17},{17,1},{2,18},{18,2},{3,19},{19,3},{4,20},{20... | collective-permute-start | bytes 995336 | tf_op jit(solution)/shard_map/ppermute | solution.py:549
  395.5 16.9 %collective-permute-start.13 = (bf16[432,768]{1,0:T(8,128)(2,1)S(1)}, bf16[432,768]{1,0:T(8,128)(2,1)S(1)}, u32[]{:S(2)}, u32[]{:S(2)}) collective-permute-start(bf16[432,768]{1,0:T(8,128)(2,1)S(1)} %pad_maximum_fusion.4), channel_id=1, source_target_pairs={{0,8},{8,0},{1,9},{9,1},{2,10},{10,2},{3,11},{11,3},{4,12},{12,4},... | collective-permute-start | bytes 1990664 | tf_op jit(solution)/shard_map/ppermute | solution.py:549
  412.5 16.0 %collective-permute-start.14 = (bf16[432,768]{1,0:T(8,128)(2,1)S(1)}, bf16[432,768]{1,0:T(8,128)(2,1)S(1)}, u32[]{:S(2)}, u32[]{:S(2)}) collective-permute-start(bf16[432,768]{1,0:T(8,128)(2,1)S(1)} %get-tuple-element.313), channel_id=1, source_target_pairs={{0,1},{1,0},{2,3},{3,2},{4,5},{5,4},{6,7},{7,6},{8,9},{9,8},{10,11... | collective-permute-start | bytes 1990664 | tf_op jit(solution)/shard_map/ppermute | solution.py:549
  430.3 48.1 %all-to-all-start.3 = ((bf16[16,128,768]{2,1,0:T(8,128)(2,1)}), bf16[16,128,768]{2,1,0:T(8,128)(2,1)}, u32[]{:S(2)}, u32[]{:S(2)}) async-start(bf16[16,128,768]{2,1,0:T(8,128)(2,1)} %bitcast.68), calls=%async_computation.3 | async-start | bytes 6291456 | tf_op jit(solution)/shard_map/all_to_all | solution.py:635
  478.4 51.2 %all-to-all-start.4 = ((bf16[16,128,768]{2,1,0:T(8,128)(2,1)}), bf16[16,128,768]{2,1,0:T(8,128)(2,1)}, u32[]{:S(2)}, u32[]{:S(2)}) async-start(bf16[16,128,768]{2,1,0:T(8,128)(2,1)} %bitcast.67), calls=%async_computation.4 | async-start | bytes 6291456 | tf_op jit(solution)/shard_map/all_to_all | solution.py:635
  547.0 51.3 %collective-permute-start.23 = (bf16[864,768]{1,0:T(8,128)(2,1)S(1)}, bf16[864,768]{1,0:T(8,128)(2,1)}, u32[]{:S(2)}, u32[]{:S(2)}) collective-permute-start(bf16[864,768]{1,0:T(8,128)(2,1)S(1)} %copy-done.13), channel_id=1, source_target_pairs={{0,4},{4,0},{1,5},{5,1},{2,6},{6,2},{3,7},{7,3},{8,12},{12,8},{9,1... | collective-permute-start | bytes 3981320 | tf_op jit(solution)/shard_map/ppermute | solution.py:549
  547.1 51.2 %collective-permute-start.24 = (bf16[864,768]{1,0:T(8,128)(2,1)}, bf16[864,768]{1,0:T(8,128)(2,1)}, u32[]{:S(2)}, u32[]{:S(2)}) collective-permute-start(bf16[864,768]{1,0:T(8,128)(2,1)} %pad_maximum_fusion.3), channel_id=1, source_target_pairs={{0,1},{1,0},{2,3},{3,2},{4,5},{5,4},{6,7},{7,6},{8,9},{9,8},{10,11... | collective-permute-start | bytes 3981320 | tf_op jit(solution)/shard_map/ppermute | solution.py:549
  548.9 41.4 %collective-permute-start.21 = (bf16[576,768]{1,0:T(8,128)(2,1)}, bf16[576,768]{1,0:T(8,128)(2,1)}, u32[]{:S(2)}, u32[]{:S(2)}) collective-permute-start(bf16[576,768]{1,0:T(8,128)(2,1)} %fusion.35), channel_id=1, source_target_pairs={{0,16},{16,0},{1,17},{17,1},{2,18},{18,2},{3,19},{19,3},{4,20},{20... | collective-permute-start | bytes 2654216 | tf_op jit(solution)/shard_map/ppermute | solution.py:549
  549.0 34.8 %collective-permute-start.19 = (bf16[160,768]{1,0:T(8,128)(2,1)S(1)}, bf16[160,768]{1,0:T(8,128)(2,1)}, u32[]{:S(2)}, u32[]{:S(2)}) collective-permute-start(bf16[160,768]{1,0:T(8,128)(2,1)S(1)} %get-tuple-element.323), channel_id=1, source_target_pairs={{0,1},{1,0},{2,3},{3,2},{4,5},{5,4},{6,7},{7,6},{8,9},{9,8},{10,11... | collective-permute-start | bytes 737288 | tf_op jit(solution)/shard_map/ppermute | solution.py:549
  549.2 35.6 %collective-permute-start.20 = (bf16[160,768]{1,0:T(8,128)(2,1)}, bf16[160,768]{1,0:T(8,128)(2,1)S(1)}, u32[]{:S(2)}, u32[]{:S(2)}) collective-permute-start(bf16[160,768]{1,0:T(8,128)(2,1)} %get-tuple-element.325), channel_id=1, source_target_pairs={{0,4},{4,0},{1,5},{5,1},{2,6},{6,2},{3,7},{7,3},{8,12},{12,8},{9,1... | collective-permute-start | bytes 737288 | tf_op jit(solution)/shard_map/ppermute | solution.py:549
  (81 other events, 1032.0 us)

commit v8 on v7

--- a/solution.py
+++ b/solution.py
@@ -41,11 +41,10 @@
 ):
     tokens = gene_ref.shape[0]
     devices, slots_all = req_ref.shape
-    group = devices // 2
     lane = lax.broadcasted_iota(jnp.int32, (tokens, devices), 1)
-    mine = lane < group
     top = top_ref[0]
-    first = jnp.where(mine, lane + top * group, lane - top * group) * rows_dev
+    half = jnp.where((lane & 1) == 0, top, 1 - top)
+    first = (half * (devices // 2) + (lane >> 1)) * rows_dev
     earlier = (
         lax.broadcasted_iota(jnp.int32, (tokens, tokens), 0)
         > lax.broadcasted_iota(jnp.int32, (tokens, tokens), 1)
@@ -451,63 +450,40 @@
     )(half.reshape(1), activated, grad_ffn, grad_pre, normed, ctx, grad_attn)
 
 
-def unpack_early_kernel(upper, core_ref, *refs):
-    (down_own, down_other, up_own, up_other, out_own, out_other, down_ref, up_ref, out_ref) = refs
-    at = pl.program_id(0)
-    low = core_ref[0] == 0
-    down_ref[...] = jnp.where(low, down_own[...], down_other[...]).astype(F32)
-    mine = jnp.where(at < upper, low, jnp.logical_not(low))
-    up_ref[...] = jnp.where(mine, up_own[...], up_other[...]).astype(F32).T
-
-    @pl.when(at < out_ref.shape[0])
-    def _():
-        out_ref[at] = jnp.where(low, out_other[...], out_own[...]).astype(F32)
-
-
-def unpack_early(core, own, other, wide, block=384):
-    half, width = own.shape
-    steps, blocks = wide // block, half // block
-    upper = blocks - steps
-    outs = width // block
-    last = blocks - 1
-    pick = lambda use, place: jnp.where(use, place, last)
-
-    def pair(place, in_low):
-        return [
-            pl.BlockSpec(
-                (block, width),
-                lambda i, c, turn=turn: (pick(in_low(i) == (c[0] == turn), place(i)), 0),
-            )
-            for turn in range(2)
-        ]
-
-    sources = (
-        pair(lambda i: i, lambda i: i >= 0)
-        + pair(lambda i: jnp.where(i < upper, steps + i, i - upper), lambda i: i < upper)
-        + pair(lambda i: blocks - outs + jnp.minimum(i, outs - 1), lambda i: i < 0)
-    )
-    down, up, out = pl.pallas_call(
-        functools.partial(unpack_early_kernel, upper),
+def unpack_kernel(first, half, turn, core_ref, own_ref, other_ref, out_ref):
+    at = pl.program_id(0) + first
+    mine = (at >= half) == (core_ref[0] == 1)
+    rows = jnp.where(mine, own_ref[...], other_ref[...]).astype(F32)
+    out_ref[...] = rows.T if turn else rows
+
+
+def unpack(core, own, other, first, rows, turn, block=384):
+    half, width = own.shape[0] // block, own.shape[1]
+    first, steps = first // block, rows // block
+
+    def place(i, c, owner):
+        at = i + first
+        inside = (at >= half) == (c[0] == owner)
+        return jnp.where(inside, at % half, half - 1), 0
+
+    return pl.pallas_call(
+        functools.partial(unpack_kernel, first, half, turn),
         grid_spec=pltpu.PrefetchScalarGridSpec(
             num_scalar_prefetch=1,
             grid=(steps,),
-            in_specs=sources,
-            out_specs=[
-                pl.BlockSpec((block, width), lambda i, c: (i, 0)),
-                pl.BlockSpec((width, block), lambda i, c: (0, i)),
-                pl.BlockSpec((outs, block, width), lambda i, c: (0, 0, 0)),
+            in_specs=[
+                pl.BlockSpec((block, width), functools.partial(place, owner=1)),
+                pl.BlockSpec((block, width), functools.partial(place, owner=0)),
             ],
+            out_specs=pl.BlockSpec((width, block), lambda i, c: (0, i))
+            if turn
+            else pl.BlockSpec((block, width), lambda i, c: (i, 0)),
         ),
-        out_shape=[
-            jax.ShapeDtypeStruct((wide, width), F32),
-            jax.ShapeDtypeStruct((width, wide), F32),
-            jax.ShapeDtypeStruct((outs, block, width), F32),
-        ],
+        out_shape=jax.ShapeDtypeStruct((width, rows) if turn else (rows, width), F32),
         compiler_params=params(60),
-        cost_estimate=cost(2 * half * width, 2 * half * width * 6),
-        name="unpack_early",
-    )(core.reshape(1), *(own, other) * 3)
-    return down, up, out.reshape(width, width)
+        cost_estimate=cost(rows * width, rows * width * 6),
+        name="unpack" + str(first),
+    )(core.reshape(1), own, other)
 
 
 def unpack_whole_kernel(heights, core_ref, own_ref, other_ref, *out_refs):
@@ -627,12 +603,12 @@
     group = devices // 2
     capacity = 2 * tokens // devices
     slots_all = 2 * capacity
-    slots = group * slots_all
+    slots = devices * slots_all
     bins = expr_table.shape[0]
     me = lax.axis_index("seq")
 
-    def exchange(value, axis):
-        return lax.all_to_all(value, group_axes, split_axis=axis, concat_axis=axis, tiled=True)
+    def exchange(value):
+        return lax.all_to_all(value, group_axes, split_axis=0, concat_axis=0, tiled=True)
 
     gene_table, knowledge_tables = lax.optimization_barrier((gene_table, knowledge_tables))
     gene_other = lax.ppermute(gene_table, top_axis, SWAP)
@@ -641,24 +617,20 @@
     requests, gene_slot, know_slot = route(
         lax.axis_index(top_axis), chosen, knowledge_ids.reshape(-1), rows_dev, capacity, devices
     )
-    asked = exchange(requests.reshape(2, group, slots_all), 1).reshape(2, slots)
-    asked, gene_other, know_sum = lax.optimization_barrier((asked, gene_other, know_sum))
+    asked = exchange(requests.reshape(group, 2 * slots_all))
     know_other = lax.ppermute(know_sum, top_axis, SWAP)
-    tables = [
-        jnp.concatenate([gene_table, know_sum], axis=0),
-        jnp.concatenate([gene_other, know_other], axis=0),
-    ]
-    row_at = jnp.arange(2 * rows_dev)
-    slot_at = jnp.arange(slots)
+    asked, gene_other, know_other = lax.optimization_barrier((asked, gene_other, know_other))
+    asked = asked.reshape(group, 2, slots_all)
+    shift = jnp.arange(2)[None, :, None] * (2 * rows_dev)
+    asked = jnp.where(asked >= 0, asked + shift, -1).reshape(slots)
+    tables = jnp.concatenate([gene_table, know_sum, gene_other, know_other], axis=0)
+    row_at = jnp.arange(4 * rows_dev)
     bin_hot = hot(expr_bins.reshape(-1)[:, None], jnp.arange(bins)[None, :])
-    embedded = mm(bin_hot, expr_table)
-    slot_hots = []
-    for part in range(2):
-        found = mm(hot(asked[part][:, None], row_at[None, :]), tables[part]).astype(BF16)
-        fetched = exchange(found.reshape(group, slots_all, width), 0).reshape(slots, width)
-        at = slot_at[None, :] + part * slots
-        slot_hots.append(((at == gene_slot) | (at == know_slot)).astype(BF16))
-        embedded = embedded + mm(slot_hots[part], fetched)
+    found = mm(hot(asked[:, None], row_at[None, :]), tables).astype(BF16)
+    fetched = exchange(found.reshape(group, 2 * slots_all, width)).reshape(slots, width)
+    slot_at = jnp.arange(slots)[None, :]
+    slot_hot = ((slot_at == gene_slot) | (slot_at == know_slot)).astype(BF16)
+    embedded = mm(slot_hot, fetched) + mm(bin_hot, expr_table)
     x_low = embedded.astype(BF16)
 
     x_other = lax.ppermute(x_low, "seq", SWAP)
@@ -667,7 +639,8 @@
     value, value_other = ((mm(x, w_value) + b_value).astype(BF16) for x in (x_low, x_other))
     mine = jnp.stack([me * tokens, cell_lengths[0]]).astype(jnp.int32)
     others = jnp.stack([(1 - me) * tokens, cell_lengths[0]]).astype(jnp.int32)
-    owned = [row_at[:, None] == asked[part][None, :] for part in range(2)]
+    block_rows = 2 * rows_dev
+    owned = [row_at[at : at + block_rows, None] == asked[None, :] for at in (0, block_rows)]
     counts = [jnp.sum(o.astype(jnp.int32), axis=1) for o in owned]
     counts_back = lax.ppermute(counts[1], top_axis, SWAP)
     first_part = attend(mine, query, key, value)
@@ -749,15 +722,11 @@
     keeps, sends, grad_low = lax.optimization_barrier((keeps, sends, grad_low))
     came = travel(sends, stages[done])
 
-    outgoing = [mm(hots, grad_low, TN).astype(BF16) for hots in slot_hots]
+    outgoing = mm(slot_hot, grad_low, TN).astype(BF16)
     outgoing, dq, dk, dv, came = lax.optimization_barrier((outgoing, dq, dk, dv, came))
     early = end(keeps, came, stages[done])
     done += 1
-
-    def give_back(rows):
-        return exchange(rows.reshape(group, slots_all, width), 0).reshape(slots, width)
-
-    returned_other = give_back(outgoing[1])
+    returned = exchange(outgoing.reshape(group, 2 * slots_all, width)).reshape(slots, width)
     w_query_grad = mm(x_low, dq, TN)
     w_key_grad = mm(x_low, dk, TN) + mm(x_other, dk_other, TN)
     w_value_grad = mm(x_low, dv, TN) + mm(x_other, dv_other, TN)
@@ -780,24 +749,18 @@
     heights = [item.shape[0] for item in late]
     late = jnp.concatenate([item.astype(BF16) for item in late], axis=0)
     keep, send = cut(late, core)
-    keep, send, outgoing, returned_other = lax.optimization_barrier(
-        (keep, send, outgoing, returned_other)
-    )
-    returned = give_back(outgoing[0])
-    for_other = mm(owned[1].astype(BF16), returned_other).astype(BF16)
     late = jnp.split(keep + swap(send, core), 2, axis=0)
-    returned, late, early, for_other = lax.optimization_barrier((returned, late, early, for_other))
+    returned, late, early = lax.optimization_barrier((returned, late, early))
+    from_other = swap(mm(owned[1].astype(BF16), returned).astype(BF16), top_axis)
     table_own = mm(owned[0].astype(BF16), returned)
-    from_other = swap(for_other, top_axis)
     last = len(stages) - 1
+    early_parts = []
     early_step = begin(early, stages[done])
     for at, stage in enumerate(stages):
         keeps, sends = begin(late, stage)
         if at == 1:
             keeps, sends, early_step = lax.optimization_barrier((keeps, sends, early_step))
             early_came = travel(early_step[1], stages[done])
-        if at == 2:
-            keeps, sends, from_other = lax.optimization_barrier((keeps, sends, from_other))
         if at == 3:
             keeps, sends, early_came = lax.optimization_barrier((keeps, sends, early_came))
             early = end(early_step[0], early_came, stages[done])
@@ -806,16 +769,27 @@
         if at == last - 2:
             keeps, sends, early_step = lax.optimization_barrier((keeps, sends, early_step))
         came = travel(sends, stage)
+        if at == 1:
+            came, from_other, table_own = lax.optimization_barrier((came, from_other, table_own))
         if at == 4:
             table_grads = table_own + from_other.astype(F32)
             came, table_grads = lax.optimization_barrier((came, table_grads))
-        if at == last - 2:
-            early = unpack_early(my_core, *early_step, wide)
-            came, early = lax.optimization_barrier((came, early))
+        if at >= last - 2:
+            part = at - last + 2
+            early_parts.append(
+                unpack(
+                    my_core,
+                    *early_step,
+                    part * wide,
+                    (wide, wide, width)[part],
+                    part == 1,
+                )
+            )
+            came, early_parts = lax.optimization_barrier((came, early_parts))
         late = end(keeps, came, stage)
     late = jnp.concatenate(late, axis=0)
     late_other = swap(late, core)
-    w_down_grad, w_up_grad, w_out_grad = early
+    w_down_grad, w_up_grad, w_out_grad = early_parts
     w_query_grad, w_key_grad, w_value_grad, expr_grad, short = unpack_whole(
         my_core, late, late_other, heights
     )

time: 676 us -> 677 us (level)
  starting transfers between devices: 58.1 us -> 48.2 us
    all_to_all x5 -> x3, waiting for transfers between devices: 93.1 us -> 143 us  [exchange(): lax.all_to_all(value, group_axes, split_axis=0, concat_axis=0, tiled=True)]
    ppermute x1, waiting for transfers between devices: 51.8 us -> 10.9 us  [local(): know_other = lax.ppermute(know_sum, top_axis, SWAP)]
    ppermute x30, waiting for transfers between devices: 93.4 us -> 78.9 us  [swap(): return lax.ppermute(value, axis, SWAP)]
    all_to_all x5 -> x3, starting transfers between devices: 26 us -> 15.4 us  [exchange(): lax.all_to_all(value, group_axes, split_axis=0, concat_axis=0, tiled=True)]
    ppermute x1, waiting for transfers between devices: 0.01 us -> 8.65 us  [local(): gene_other = lax.ppermute(gene_table, top_axis, SWAP)]
    pallas_call x1 -> x3, Pallas kernels: 13.7 us -> 19.1 us  [unpack(): pl.pallas_call(functools.partial(unpack_kernel, first, half, turn), grid_...]
    dot_general x26 -> x23, matrix products: 81 us -> 83.7 us  [mm(): return lax.dot_general(left, right, dims, preferred_element_type=F32)]
  transfers between devices with their start and end apart: 39 -> 37, of which waited for: 21 -> 22; matrix products, arithmetic and copies ran while one was open for 15% -> 13% of each run, Pallas kernels for 21% -> 22%
where the time goes in v8:
time: 677 us; the launch traced here: 669 us
  waiting for transfers between devices  251 us (37%)
  Pallas kernels  224 us (33%)
  matrix products  83.7 us (12%)
  starting transfers between devices  48.2 us (7%)
  other arithmetic  35 us (5%)
  local copies, waits for them, and re-layouts  24.2 us (4%)
    all_to_all x3, waiting for transfers between devices, exchange(): lax.all_to_all(value, group_axes, split_axis=0, concat_axis=0, tiled=True)  143 us
    pallas_call x5, Pallas kernels, attend_back(): pl.pallas_call(functools.partial(attend_back_kernel, add, len(into)), gri...  86.9 us
    dot_general x23, matrix products, mm(): return lax.dot_general(left, right, dims, preferred_element_type=F32)  83.7 us
    ppermute x30, waiting for transfers between devices, swap(): return lax.ppermute(value, axis, SWAP)  78.9 us
    pallas_call x2, Pallas kernels, attend(): pl.pallas_call(functools.partial(attend_kernel, merge), grid_spec=pltpu.P...  43.7 us
    pallas_call x1, Pallas kernels, middle(): pl.pallas_call(middle_kernel, grid=(tokens // block,), in_specs=[rows(wid...  37.1 us
    pallas_call x2, Pallas kernels, weight_sums(): pl.pallas_call(functools.partial(weight_sums_kernel, counts), grid_spec=p...  27.6 us
    ppermute x30, starting transfers between devices, swap(): return lax.ppermute(value, axis, SWAP)  24.6 us
  transfers between devices with their start and end apart: 37, of which 22 were waited for; matrix products, arithmetic and copies ran while one was open for 13% of the time, Pallas kernels for 22%

profile of v8, /device:TPU:0, one launch (start us, length us, event | category | flops | bytes accessed | tf_op | source)
XLA Modules:
  0.0 669.2 jit_solution(13926950697223391797)
XLA Ops:
  17.5 9.2 %all-to-all-done = s32[16,1,256]{2,1,0:T(1,128)S(1)} async-done(((s32[16,1,256]{2,1,0:T(1,128)}), s32[16,1,256]{2,1,0:T(1,128)S(1)}, u32[]{:S(2)}, u32[]{:S(2)}) %all-to-all-start) | async-done | bytes 16416 | tf_op jit(solution)/shard_map/all_to_all | solution.py:611
  26.8 10.9 %collective-permute-done.1 = bf16[288,768]{1,0:T(8,128)(2,1)} collective-permute-done((bf16[288,768]{1,0:T(8,128)(2,1)}, bf16[288,768]{1,0:T(8,128)(2,1)}, u32[]{:S(2)}, u32[]{:S(2)}) %collective-permute-start.1) | collective-permute-done | bytes 442400 | tf_op jit(solution)/shard_map/ppermute | solution.py:621
  37.7 8.7 %collective-permute-done = bf16[288,768]{1,0:T(8,128)(2,1)} collective-permute-done((bf16[288,768]{1,0:T(8,128)(2,1)}, bf16[288,768]{1,0:T(8,128)(2,1)}, u32[]{:S(2)}, u32[]{:S(2)}) %collective-permute-start) | collective-permute-done | bytes 442400 | tf_op jit(solution)/shard_map/ppermute | solution.py:614
  46.5 12.4 %fusion.20 = bf16[4096,768]{1,0:T(8,128)(2,1)} fusion(s32[4096]{0:T(1024)S(1)} %add_select_fusion, bf16[288,768]{1,0:T(8,128)(2,1)} %collective-permute-done.1, bf16[288,768]{1,0:T(8,128)(2,1)} %collective-permute-done, bf16[288,768]{1,0:T(8,128)(2,1)} %reduce_sum.75, bf16[288,768]{1,0:T(8,128)(2,1)} %param.31), kind=kOutput, calls=%fused_computation.21 | convolution fusion | flops 7262699520 | bytes 8077312 | tf_op jit(solution)/shard_map/dot_general | solution.py:24
  71.6 80.0 %all-to-all-done.1 = bf16[16,256,768]{2,1,0:T(8,128)(2,1)} async-done(((bf16[16,256,768]{2,1,0:T(8,128)(2,1)}), bf16[16,256,768]{2,1,0:T(8,128)(2,1)}, u32[]{:S(2)}, u32[]{:S(2)}) %all-to-all-start.1) | async-done | bytes 6291488 | tf_op jit(solution)/shard_map/all_to_all | solution.py:611
  151.6 11.3 %fusion.4 = f32[1024,768]{1,0:T(8,128)S(1)} fusion(bf16[4096,768]{1,0:T(8,128)(2,1)} %bitcast.8, s32[1024]{0:T(1024)S(1)} %reduce.3, s32[1024]{0:T(1024)S(1)} %reduce.2), kind=kOutput, calls=%fused_computation.6 | convolution fusion | flops 6455033856 | bytes 9445376 | tf_op jit(solution)/shard_map/dot_general | solution.py:24
  171.0 21.1 %attend.1 = (f32[768,1024]{1,0:T(8,128)}, f32[6,2,1024]{2,1,0:T(2,128)S(1)}) custom-call(s32[2]{0:T(128)S(1)} %pad_add_fusion.1.where_ref, bf16[1024,768]{1,0:T(8,128)(2,1)S(1)} %add_convert_fusion.3.q_ref, bf16[1024,768]{1,0:T(8,128)(2,1)S(1)} %convolution_convert_fusion.k_ref, bf16[1024,768]{1,0:T(8,128)(2,1)S(1)} %add_convert_fusion.1.v_ref), custom_call_target="tpu_custom_call" | custom-call | flops 12884901888 | bytes 15728640 | tf_op jit(solution)/shard_map/attend/pallas_call | solution.py:167
  192.1 9.3 %collective-permute-done.2 = bf16[1024,768]{1,0:T(8,128)(2,1)S(1)} collective-permute-done((bf16[1024,768]{1,0:T(8,128)(2,1)S(1)}, bf16[1024,768]{1,0:T(8,128)(2,1)S(1)}, u32[]{:S(2)}, u32[]{:S(2)}) %collective-permute-start.2) | collective-permute-done | bytes 1572896 | tf_op jit(solution)/shard_map/ppermute | solution.py:636
  204.3 22.6 %attend_more.1 = (f32[1024,768]{1,0:T(8,128)}, f32[6,2,1024]{2,1,0:T(2,128)S(1)}) custom-call(s32[2]{0:T(128)S(1)} %pad_add_fusion.where_ref, bf16[1024,768]{1,0:T(8,128)(2,1)S(1)} %add_convert_fusion.3.q_ref, bf16[1024,768]{1,0:T(8,128)(2,1)S(1)} %convolution_convert_fusion.1.k_ref, bf16[1024,768]{1,0:T(8,128)(2,1)S(1)} %add_convert_fusion.2.v_ref, ...), custom_call_target="tpu_custom_call" | custom-call | flops 12884901888 | bytes 15728640 | tf_op jit(solution)/shard_map/attend_more/pallas_call | solution.py:167
  227.6 37.1 %middle.1 = (bf16[1024,768]{1,0:T(8,128)(2,1)}, bf16[1024,768]{1,0:T(8,128)(2,1)}, bf16[1024,768]{1,0:T(8,128)(2,1)}, bf16[1024,3072]{1,0:T(8,128)(2,1)}, bf16[1...) custom-call(f32[1024,768]{1,0:T(8,128)} %get-tuple-element.200.ctx_r, ...), custom_call_target="tpu_custom_call" | custom-call | flops 43486543872 | bytes 34603008 | tf_op jit(solution)/shard_map/middle/pallas_call | solution.py:375
  264.7 13.8 %weight_sums.2 = bf16[3456,768]{1,0:T(8,128)(2,1)} custom-call(s32[1]{0:T(128)} %bitcast.15.half_ref, bf16[1024,3072]{1,0:T(8,128)(2,1)} %get-tuple-element.208.act_ref, bf16[1024,768]{1,0:T(8,128)(2,1)} %get-tuple-element.209.gffn_ref, bf16[1024,3072]{1,0:T(8,128)(2,1)} %get-tuple-element.210.gpre_ref, bf16[1024,768]{1,0:T(8,128)(2,1)} %get-tuple-element.211.norm_ref, ...), custom_call_target="tpu_custom_call" | custom-call | flops 5435817984 | bytes 12386304 | tf_op jit(solution)/shard_map/weight_sums/pallas_call | solution.py:438
  278.5 13.8 %weight_sums.3 = bf16[3456,768]{1,0:T(8,128)(2,1)} custom-call(s32[1]{0:T(128)} %bitcast.14.half_ref.core_ref, bf16[1024,3072]{1,0:T(8,128)(2,1)} %get-tuple-element.208.act_ref, bf16[1024,768]{1,0:T(8,128)(2,1)} %get-tuple-element.209.gffn_ref, bf16[1024,3072]{1,0:T(8,128)(2,1)} %get-tuple-element.210.gpre_ref, ...), custom_call_target="tpu_custom_call" | custom-call | flops 5435817984 | bytes 12386304 | tf_op jit(solution)/shard_map/weight_sums/pallas_call | solution.py:438
  299.8 26.5 %attend_back0.1 = (f32[1024,768]{1,0:T(8,128)}, bf16[1024,768]{1,0:T(8,128)(2,1)}, bf16[1024,768]{1,0:T(8,128)(2,1)}) custom-call(s32[2]{0:T(128)} %copy-done.2, bf16[1024,768]{1,0:T(8,128)(2,1)} %copy-done.5, bf16[1024,768]{1,0:T(8,128)(2,1)} %get-tuple-element.277.g_ref, f32[1024,768]{1,0:T(8,128)} %get-tuple-element.200.ctx_ref.o_ref, ...), custom_call_target="tpu_custom_call" | custom-call | flops 21474836480 | bytes 12582912 | tf_op jit(solution)/shard_map/attend_back0/pallas_call | solution.py:247
  335.8 14.9 %attend_back4.1 = (f32[1024,768]{1,0:T(8,128)}, bf16[1024,768]{1,0:T(8,128)(2,1)}, bf16[1024,768]{1,0:T(8,128)(2,1)}) custom-call(s32[2]{0:T(128)} %copy-done.2, bf16[1024,768]{1,0:T(8,128)(2,1)} %copy-done.5, bf16[1024,768]{1,0:T(8,128)(2,1)} %get-tuple-element.277.g_ref, ...), custom_call_target="tpu_custom_call", output_to_operand_aliasing={{0}: (7, {}), {1}: (8, {}), {2}: (9, {})} | custom-call | flops 10737418240 | bytes 6291456 | tf_op jit(solution)/shard_map/attend_back4/pallas_call | solution.py:247
  360.1 15.1 %attend_back_more0.1 = (bf16[1024,768]{1,0:T(8,128)(2,1)}, bf16[1024,768]{1,0:T(8,128)(2,1)}, bf16[1024,768]{1,0:T(8,128)(2,1)}) custom-call(s32[2]{0:T(128)} %copy-done.1, bf16[1024,768]{1,0:T(8,128)(2,1)} %copy-done.5, bf16[1024,768]{1,0:T(8,128)(2,1)} %get-tuple-element.277.g_ref, f32[1024,768]{1,0:T(8,128)} %get-tuple-element.200.ctx_ref.o_ref, ...), custom_call_target="tpu_custom_call" | custom-call | flops 10737418240 | bytes 6291456 | tf_op jit(solution)/shard_map/attend_back_more0/pallas_call | solution.py:247
  378.2 14.9 %attend_back_more2.1 = (bf16[1024,768]{1,0:T(8,128)(2,1)}, bf16[1024,768]{1,0:T(8,128)(2,1)}, bf16[1024,768]{1,0:T(8,128)(2,1)}) custom-call(s32[2]{0:T(128)} %copy-done.1, bf16[1024,768]{1,0:T(8,128)(2,1)} %copy-done.5, bf16[1024,768]{1,0:T(8,128)(2,1)} %get-tuple-element.277.g_ref, ...), custom_call_target="tpu_custom_call", output_to_operand_aliasing={{0}: (8, {}), {1}: (9, {}), {2}: (10, {})} | custom-call | flops 10737418240 | bytes 6291456 | tf_op jit(solution)/shard_map/attend_back_more2/pallas_call | solution.py:247
  393.4 15.5 %attend_back_more4.1 = (bf16[1024,768]{1,0:T(8,128)(2,1)}, bf16[1024,768]{1,0:T(8,128)(2,1)}, bf16[1024,768]{1,0:T(8,128)(2,1)}) custom-call(s32[2]{0:T(128)} %copy-done.1, bf16[1024,768]{1,0:T(8,128)(2,1)} %copy-done.5, bf16[1024,768]{1,0:T(8,128)(2,1)} %get-tuple-element.277.g_ref, ...), custom_call_target="tpu_custom_call", output_to_operand_aliasing={{0}: (8, {}), {1}: (9, {}), {2}: (10, {})} | custom-call | flops 10737418240 | bytes 6291456 | tf_op jit(solution)/shard_map/attend_back_more4/pallas_call | solution.py:247
  428.6 10.9 %fusion.17 = bf16[4096,768]{1,0:T(8,128)(2,1)} fusion(bf16[1024,768]{1,0:T(8,128)(2,1)S(1)} %get-tuple-element.299, s32[1024]{0:T(1024)S(1)} %copy-done.43, s32[1024]{0:T(1024)S(1)} %copy-done.41), kind=kOutput, calls=%fused_computation.20 | convolution fusion | flops 6458179584 | bytes 7872512 | tf_op jit(solution)/shard_map/dot_general | solution.py:24
  483.1 53.9 %all-to-all-done.2 = bf16[16,256,768]{2,1,0:T(8,128)(2,1)} async-done(((bf16[16,256,768]{2,1,0:T(8,128)(2,1)}), bf16[16,256,768]{2,1,0:T(8,128)(2,1)}, u32[]{:S(2)}, u32[]{:S(2)}) %all-to-all-start.2) | async-done | bytes 6291488 | tf_op jit(solution)/shard_map/all_to_all | solution.py:611
  565.1 22.4 %collective-permute-done.21 = bf16[576,768]{1,0:T(8,128)(2,1)S(1)} collective-permute-done((bf16[576,768]{1,0:T(8,128)(2,1)S(1)}, bf16[576,768]{1,0:T(8,128)(2,1)S(1)}, u32[]{:S(2)}, u32[]{:S(2)}) %collective-permute-start.21) | collective-permute-done | bytes 884768 | tf_op jit(solution)/shard_map/ppermute | solution.py:525
  588.7 8.4 %collective-permute-done.22 = bf16[160,768]{1,0:T(8,128)(2,1)S(1)} collective-permute-done((bf16[160,768]{1,0:T(8,128)(2,1)S(1)}, bf16[160,768]{1,0:T(8,128)(2,1)S(1)}, u32[]{:S(2)}, u32[]{:S(2)}) %collective-permute-start.22) | collective-permute-done | bytes 245792 | tf_op jit(solution)/shard_map/ppermute | solution.py:525
  623.3 7.9 %unpack0.1 = f32[3072,768]{1,0:T(8,128)} custom-call(s32[1]{0:T(128)} %bitcast.14.half_ref.core_ref, bf16[3456,768]{1,0:T(8,128)(2,1)} %copy-done.9, bf16[3456,768]{1,0:T(8,128)(2,1)} %copy-done.10), custom_call_target="tpu_custom_call" | custom-call | flops 2359296 | bytes 14155776 | tf_op jit(solution)/shard_map/unpack0/pallas_call | solution.py:469
  634.1 8.5 %unpack8.1 = f32[768,3072]{1,0:T(8,128)} custom-call(s32[1]{0:T(128)} %bitcast.14.half_ref.core_ref, bf16[3456,768]{1,0:T(8,128)(2,1)} %copy-done.9, bf16[3456,768]{1,0:T(8,128)(2,1)} %copy-done.10), custom_call_target="tpu_custom_call" | custom-call | flops 2359296 | bytes 14155776 | tf_op jit(solution)/shard_map/unpack8/pallas_call | solution.py:469
  646.9 8.6 %collective-permute-done.31 = bf16[320,768]{1,0:T(8,128)(2,1)S(1)} collective-permute-done((bf16[320,768]{1,0:T(8,128)(2,1)S(1)}, bf16[320,768]{1,0:T(8,128)(2,1)S(1)}, u32[]{:S(2)}, u32[]{:S(2)}) %collective-permute-start.31) | collective-permute-done | bytes 491552 | tf_op jit(solution)/shard_map/ppermute | solution.py:525
  (323 shorter events, 207.9 us)
Async XLA Ops:
  3.4 34.3 %collective-permute-start.1 = (bf16[288,768]{1,0:T(8,128)(2,1)}, bf16[288,768]{1,0:T(8,128)(2,1)}, u32[]{:S(2)}, u32[]{:S(2)}) collective-permute-start(bf16[288,768]{1,0:T(8,128)(2,1)} %reduce_sum.75), channel_id=1, source_target_pairs={{0,16},{16,0},{1,17},{17,1},{2,18},{18,2},{3,19},{19,3},{4,20},{20... | collective-permute-start | bytes 1327112 | tf_op jit(solution)/shard_map/ppermute | solution.py:621
  7.4 38.9 %collective-permute-start = (bf16[288,768]{1,0:T(8,128)(2,1)}, bf16[288,768]{1,0:T(8,128)(2,1)}, u32[]{:S(2)}, u32[]{:S(2)}) collective-permute-start(bf16[288,768]{1,0:T(8,128)(2,1)} %param.31), channel_id=1, source_target_pairs={{0,16},{16,0},{1,17},{17,1},{2,18},{18,2},{3,19},{19,3},{4,20},{20... | collective-permute-start | bytes 1327112 | tf_op jit(solution)/shard_map/ppermute | solution.py:614
  12.4 14.4 %all-to-all-start = ((s32[16,1,256]{2,1,0:T(1,128)}), s32[16,1,256]{2,1,0:T(1,128)S(1)}, u32[]{:S(2)}, u32[]{:S(2)}) async-start(s32[16,1,256]{2,1,0:T(1,128)} %bitcast.5), calls=%async_computation | async-start | bytes 32768 | tf_op jit(solution)/shard_map/all_to_all | solution.py:611
  58.9 92.7 %all-to-all-start.1 = ((bf16[16,256,768]{2,1,0:T(8,128)(2,1)}), bf16[16,256,768]{2,1,0:T(8,128)(2,1)}, u32[]{:S(2)}, u32[]{:S(2)}) async-start(bf16[16,256,768]{2,1,0:T(8,128)(2,1)} %bitcast.63), calls=%async_computation.1 | async-start | bytes 12582912 | tf_op jit(solution)/shard_map/all_to_all | solution.py:611
  68.8 123.3 %collective-permute-start.3 = (s32[576]{0:T(1024)S(1)}, s32[576]{0:T(1024)S(1)}, u32[]{:S(2)}, u32[]{:S(2)}) collective-permute-start(s32[576]{0:T(1024)S(1)} %get-tuple-element.365), channel_id=1, source_target_pairs={{0,16},{16,0},{1,17},{17,1},{2,18},{18,2},{3,19},{19,3},{4,20},{20... | collective-permute-start | bytes 6920 | tf_op jit(solution)/shard_map/ppermute | solution.py:645
  165.4 36.1 %collective-permute-start.2 = (bf16[1024,768]{1,0:T(8,128)(2,1)S(1)}, bf16[1024,768]{1,0:T(8,128)(2,1)S(1)}, u32[]{:S(2)}, u32[]{:S(2)}) collective-permute-start(bf16[1024,768]{1,0:T(8,128)(2,1)S(1)} %get-tuple-element.416), channel_id=1, source_target_pairs={{0,1},{1,0},{2,3},{3,2},{4,5},{5,4},{6,7},{7,6},{8,9},{9,8},{10,11... | collective-permute-start | bytes 4718600 | tf_op jit(solution)/shard_map/ppermute | solution.py:636
  278.5 13.8 %collective-permute-start.4 = (bf16[3456,768]{1,0:T(8,128)(2,1)}, bf16[3456,768]{1,0:T(8,128)(2,1)}, u32[]{:S(2)}, u32[]{:S(2)}) collective-permute-start(bf16[3456,768]{1,0:T(8,128)(2,1)} %weight_sums.2), channel_id=1, source_target_pairs={{0,2},{2,0},{1,3},{3,1},{4,6},{6,4},{5,7},{7,5},{8,10},{10,8},{9,1... | collective-permute-start | bytes 15925256 | tf_op jit(solution)/shard_map/ppermute | solution.py:525
  298.5 32.0 %collective-permute-start.5 = (bf16[864,768]{1,0:T(8,128)(2,1)S(1)}, bf16[864,768]{1,0:T(8,128)(2,1)S(1)}, u32[]{:S(2)}, u32[]{:S(2)}) collective-permute-start(bf16[864,768]{1,0:T(8,128)(2,1)S(1)} %get-tuple-element.220), channel_id=1, source_target_pairs={{0,4},{4,0},{1,5},{5,1},{2,6},{6,2},{3,7},{7,3},{8,12},{12,8},{9,1... | collective-permute-start | bytes 3981320 | tf_op jit(solution)/shard_map/ppermute | solution.py:525
  298.5 32.1 %collective-permute-start.6 = (bf16[864,768]{1,0:T(8,128)(2,1)S(1)}, bf16[864,768]{1,0:T(8,128)(2,1)}, u32[]{:S(2)}, u32[]{:S(2)}) collective-permute-start(bf16[864,768]{1,0:T(8,128)(2,1)S(1)} %get-tuple-element.221), channel_id=1, source_target_pairs={{0,1},{1,0},{2,3},{3,2},{4,5},{5,4},{6,7},{7,6},{8,9},{9,8},{10,11... | collective-permute-start | bytes 3981320 | tf_op jit(solution)/shard_map/ppermute | solution.py:525
  332.9 17.8 %collective-permute-start.7 = (bf16[432,768]{1,0:T(8,128)(2,1)S(1)}, bf16[432,768]{1,0:T(8,128)(2,1)S(1)}, u32[]{:S(2)}, u32[]{:S(2)}) collective-permute-start(bf16[432,768]{1,0:T(8,128)(2,1)S(1)} %get-tuple-element.234), channel_id=1, source_target_pairs={{0,1},{1,0},{2,3},{3,2},{4,5},{5,4},{6,7},{7,6},{8,9},{9,8},{10,11... | collective-permute-start | bytes 1990664 | tf_op jit(solution)/shard_map/ppermute | solution.py:525
  334.1 16.6 %collective-permute-start.8 = (bf16[432,768]{1,0:T(8,128)(2,1)S(1)}, bf16[432,768]{1,0:T(8,128)(2,1)S(1)}, u32[]{:S(2)}, u32[]{:S(2)}) collective-permute-start(bf16[432,768]{1,0:T(8,128)(2,1)S(1)} %get-tuple-element.235), channel_id=1, source_target_pairs={{0,4},{4,0},{1,5},{5,1},{2,6},{6,2},{3,7},{7,3},{8,12},{12,8},{9,1... | collective-permute-start | bytes 1990664 | tf_op jit(solution)/shard_map/ppermute | solution.py:525
  357.3 17.8 %collective-permute-start.9 = (bf16[432,768]{1,0:T(8,128)(2,1)S(1)}, bf16[432,768]{1,0:T(8,128)(2,1)S(1)}, u32[]{:S(2)}, u32[]{:S(2)}) collective-permute-start(bf16[432,768]{1,0:T(8,128)(2,1)S(1)} %get-tuple-element.251), channel_id=1, source_target_pairs={{0,8},{8,0},{1,9},{9,1},{2,10},{10,2},{3,11},{11,3},{4,12},{12,4},... | collective-permute-start | bytes 1990664 | tf_op jit(solution)/shard_map/ppermute | solution.py:525
  359.5 50.2 %collective-permute-start.12 = (bf16[1024,768]{1,0:T(8,128)(2,1)S(1)}, bf16[1024,768]{1,0:T(8,128)(2,1)S(1)}, u32[]{:S(2)}, u32[]{:S(2)}) collective-permute-start(bf16[1024,768]{1,0:T(8,128)(2,1)S(1)} %add_convert_fusion), channel_id=1, source_target_pairs={{0,1},{1,0},{2,3},{3,2},{4,5},{5,4},{6,7},{7,6},{8,9},{9,8},{10,11... | collective-permute-start | bytes 4718600 | tf_op jit(solution)/shard_map/ppermute | solution.py:525
  375.4 17.7 %collective-permute-start.10 = (bf16[216,768]{1,0:T(8,128)(2,1)S(1)}, bf16[216,768]{1,0:T(8,128)(2,1)S(1)}, u32[]{:S(2)}, u32[]{:S(2)}) collective-permute-start(bf16[216,768]{1,0:T(8,128)(2,1)S(1)} %get-tuple-element.262), channel_id=1, source_target_pairs={{0,16},{16,0},{1,17},{17,1},{2,18},{18,2},{3,19},{19,3},{4,20},{20... | collective-permute-start | bytes 995336 | tf_op jit(solution)/shard_map/ppermute | solution.py:525
  393.2 16.4 %collective-permute-start.11 = (bf16[216,768]{1,0:T(8,128)(2,1)S(1)}, bf16[216,768]{1,0:T(8,128)(2,1)S(1)}, u32[]{:S(2)}, u32[]{:S(2)}) collective-permute-start(bf16[216,768]{1,0:T(8,128)(2,1)S(1)} %add.236), channel_id=1, source_target_pairs={{0,16},{16,0},{1,17},{17,1},{2,18},{18,2},{3,19},{19,3},{4,20},{20... | collective-permute-start | bytes 995336 | tf_op jit(solution)/shard_map/ppermute | solution.py:525
  409.7 16.9 %collective-permute-start.13 = (bf16[432,768]{1,0:T(8,128)(2,1)S(1)}, bf16[432,768]{1,0:T(8,128)(2,1)S(1)}, u32[]{:S(2)}, u32[]{:S(2)}) collective-permute-start(bf16[432,768]{1,0:T(8,128)(2,1)S(1)} %pad_maximum_fusion.4), channel_id=1, source_target_pairs={{0,8},{8,0},{1,9},{9,1},{2,10},{10,2},{3,11},{11,3},{4,12},{12,4},... | collective-permute-start | bytes 1990664 | tf_op jit(solution)/shard_map/ppermute | solution.py:525
  426.7 16.0 %collective-permute-start.14 = (bf16[432,768]{1,0:T(8,128)(2,1)S(1)}, bf16[432,768]{1,0:T(8,128)(2,1)S(1)}, u32[]{:S(2)}, u32[]{:S(2)}) collective-permute-start(bf16[432,768]{1,0:T(8,128)(2,1)S(1)} %get-tuple-element.308), channel_id=1, source_target_pairs={{0,1},{1,0},{2,3},{3,2},{4,5},{5,4},{6,7},{7,6},{8,9},{9,8},{10,11... | collective-permute-start | bytes 1990664 | tf_op jit(solution)/shard_map/ppermute | solution.py:525
  427.8 15.7 %collective-permute-start.15 = (bf16[432,768]{1,0:T(8,128)(2,1)S(1)}, bf16[432,768]{1,0:T(8,128)(2,1)S(1)}, u32[]{:S(2)}, u32[]{:S(2)}) collective-permute-start(bf16[432,768]{1,0:T(8,128)(2,1)S(1)} %get-tuple-element.310), channel_id=1, source_target_pairs={{0,4},{4,0},{1,5},{5,1},{2,6},{6,2},{3,7},{7,3},{8,12},{12,8},{9,1... | collective-permute-start | bytes 1990664 | tf_op jit(solution)/shard_map/ppermute | solution.py:525
  444.4 92.6 %all-to-all-start.2 = ((bf16[16,256,768]{2,1,0:T(8,128)(2,1)}), bf16[16,256,768]{2,1,0:T(8,128)(2,1)}, u32[]{:S(2)}, u32[]{:S(2)}) async-start(bf16[16,256,768]{2,1,0:T(8,128)(2,1)} %bitcast.62), calls=%async_computation.2 | async-start | bytes 12582912 | tf_op jit(solution)/shard_map/all_to_all | solution.py:611
  539.6 13.3 %collective-permute-start.17 = (bf16[320,768]{1,0:T(8,128)(2,1)S(1)}, bf16[320,768]{1,0:T(8,128)(2,1)S(1)}, u32[]{:S(2)}, u32[]{:S(2)}) collective-permute-start(bf16[320,768]{1,0:T(8,128)(2,1)S(1)} %constant_dynamic-slice_fusion.7), channel_id=1, source_target_pairs={{0,4},{4,0},{1,5},{5,1},{2,6},{6,2},{3,7},{7,3},{8,12},{12,8},{9,1... | collective-permute-start | bytes 1474568 | tf_op jit(solution)/shard_map/ppermute | solution.py:525
  546.7 40.8 %collective-permute-start.21 = (bf16[576,768]{1,0:T(8,128)(2,1)S(1)}, bf16[576,768]{1,0:T(8,128)(2,1)S(1)}, u32[]{:S(2)}, u32[]{:S(2)}) collective-permute-start(bf16[576,768]{1,0:T(8,128)(2,1)S(1)} %fusion.36), channel_id=1, source_target_pairs={{0,16},{16,0},{1,17},{17,1},{2,18},{18,2},{3,19},{19,3},{4,20},{20... | collective-permute-start | bytes 2654216 | tf_op jit(solution)/shard_map/ppermute | solution.py:525
  553.3 44.1 %collective-permute-start.23 = (bf16[864,768]{1,0:T(8,128)(2,1)S(1)}, bf16[864,768]{1,0:T(8,128)(2,1)}, u32[]{:S(2)}, u32[]{:S(2)}) collective-permute-start(bf16[864,768]{1,0:T(8,128)(2,1)S(1)} %pad_maximum_fusion.2), channel_id=1, source_target_pairs={{0,4},{4,0},{1,5},{5,1},{2,6},{6,2},{3,7},{7,3},{8,12},{12,8},{9,1... | collective-permute-start | bytes 3981320 | tf_op jit(solution)/shard_map/ppermute | solution.py:525
  555.3 42.1 %collective-permute-start.24 = (bf16[864,768]{1,0:T(8,128)(2,1)}, bf16[864,768]{1,0:T(8,128)(2,1)}, u32[]{:S(2)}, u32[]{:S(2)}) collective-permute-start(bf16[864,768]{1,0:T(8,128)(2,1)} %pad_maximum_fusion.3), channel_id=1, source_target_pairs={{0,1},{1,0},{2,3},{3,2},{4,5},{5,4},{6,7},{7,6},{8,9},{9,8},{10,11... | collective-permute-start | bytes 3981320 | tf_op jit(solution)/shard_map/ppermute | solution.py:525
  603.6 17.4 %collective-permute-start.27 = (bf16[3456,768]{1,0:T(8,128)(2,1)S(1)}, bf16[3456,768]{1,0:T(8,128)(2,1)S(1)}, u32[]{:S(2)}, u32[]{:S(2)}) collective-permute-start(bf16[3456,768]{1,0:T(8,128)(2,1)S(1)} %pad_maximum_fusion.own_ref), channel_id=1, source_target_pairs={{0,2},{2,0},{1,3},{3,1},{4,6},{6,4},{5,7},{7,5},{8,10},{10,8},{9,1... | collective-permute-start | bytes 15925256 | tf_op jit(solution)/shard_map/ppermute | solution.py:525
  (86 other events, 1435.0 us)

commit v9 on v8

--- a/solution.py
+++ b/solution.py
@@ -618,19 +618,32 @@
         lax.axis_index(top_axis), chosen, knowledge_ids.reshape(-1), rows_dev, capacity, devices
     )
     asked = exchange(requests.reshape(group, 2 * slots_all))
+    asked, gene_other, know_sum = lax.optimization_barrier((asked, gene_other, know_sum))
     know_other = lax.ppermute(know_sum, top_axis, SWAP)
-    asked, gene_other, know_other = lax.optimization_barrier((asked, gene_other, know_other))
     asked = asked.reshape(group, 2, slots_all)
     shift = jnp.arange(2)[None, :, None] * (2 * rows_dev)
-    asked = jnp.where(asked >= 0, asked + shift, -1).reshape(slots)
-    tables = jnp.concatenate([gene_table, know_sum, gene_other, know_other], axis=0)
+    asked = jnp.where(asked >= 0, asked + shift, -1).reshape(group, 2 * slots_all)
     row_at = jnp.arange(4 * rows_dev)
+    slot_at = jnp.arange(slots).reshape(group, 2 * slots_all)
     bin_hot = hot(expr_bins.reshape(-1)[:, None], jnp.arange(bins)[None, :])
-    found = mm(hot(asked[:, None], row_at[None, :]), tables).astype(BF16)
-    fetched = exchange(found.reshape(group, 2 * slots_all, width)).reshape(slots, width)
-    slot_at = jnp.arange(slots)[None, :]
+    embedded = mm(bin_hot, expr_table)
+    fetched = gene_other
+    tables = jnp.concatenate([gene_table, know_sum, gene_other], axis=0)
+    late_rows = slice(slots_all + capacity, 2 * slots_all)
+    early_rows = slice(0, slots_all + capacity)
+    for columns, rows, table in (
+        (early_rows, row_at[: 3 * rows_dev], tables),
+        (late_rows, row_at[3 * rows_dev :], know_other),
+    ):
+        wanted = asked[:, columns].reshape(-1)
+        found = mm(hot(wanted[:, None], rows[None, :]), table).astype(BF16)
+        found, _ = lax.optimization_barrier((found, fetched))
+        fetched = exchange(found.reshape(group, -1, width)).reshape(-1, width)
+        at = slot_at[:, columns].reshape(1, -1)
+        embedded = embedded + mm(((at == gene_slot) | (at == know_slot)).astype(BF16), fetched)
+    asked = asked.reshape(slots)
+    slot_at = slot_at.reshape(1, slots)
     slot_hot = ((slot_at == gene_slot) | (slot_at == know_slot)).astype(BF16)
-    embedded = mm(slot_hot, fetched) + mm(bin_hot, expr_table)
     x_low = embedded.astype(BF16)
 
     x_other = lax.ppermute(x_low, "seq", SWAP)
@@ -750,13 +763,16 @@
     late = jnp.concatenate([item.astype(BF16) for item in late], axis=0)
     keep, send = cut(late, core)
     late = jnp.split(keep + swap(send, core), 2, axis=0)
-    returned, late, early = lax.optimization_barrier((returned, late, early))
+    keeps, sends = begin(late, stages[0])
+    came = travel(sends, stages[0])
+    returned, keeps, came, early = lax.optimization_barrier((returned, keeps, came, early))
+    late = end(keeps, came, stages[0])
     from_other = swap(mm(owned[1].astype(BF16), returned).astype(BF16), top_axis)
     table_own = mm(owned[0].astype(BF16), returned)
     last = len(stages) - 1
     early_parts = []
     early_step = begin(early, stages[done])
-    for at, stage in enumerate(stages):
+    for at, stage in enumerate(stages[1:], start=1):
         keeps, sends = begin(late, stage)
         if at == 1:
             keeps, sends, early_step = lax.optimization_barrier((keeps, sends, early_step))

time: 677 us -> 668 us (0.987)
  waiting for transfers between devices: 251 us -> 234 us
    all_to_all x3 -> x4, waiting for transfers between devices: 143 us -> 13.4 us  [exchange(): lax.all_to_all(value, group_axes, split_axis=0, concat_axis=0, tiled=True)]
    ppermute x1, waiting for transfers between devices: 10.9 us -> 73.8 us  [local(): know_other = lax.ppermute(know_sum, top_axis, SWAP)]
    ppermute x30, waiting for transfers between devices: 78.9 us -> 136 us  [swap(): return lax.ppermute(value, axis, SWAP)]
    ppermute x1, waiting for transfers between devices: 8.65 us -> 0.01 us  [local(): gene_other = lax.ppermute(gene_table, top_axis, SWAP)]
    all_to_all x3 -> x4, starting transfers between devices: 15.4 us -> 20.6 us  [exchange(): lax.all_to_all(value, group_axes, split_axis=0, concat_axis=0, tiled=True)]
    dot_general x23 -> x25, matrix products: 83.7 us -> 83.5 us  [mm(): return lax.dot_general(left, right, dims, preferred_element_type=F32)]
  transfers between devices with their start and end apart: 37 -> 38, of which waited for: 22 -> 21; matrix products, arithmetic and copies ran while one was open for 13% -> 15% of each run, Pallas kernels for 22% -> 22%
where the time goes in v9:
time: 668 us; the launch traced here: 661 us
  waiting for transfers between devices  234 us (35%)
  Pallas kernels  224 us (34%)
  matrix products  83.5 us (12%)
  starting transfers between devices  54 us (8%)
  other arithmetic  37.5 us (6%)
  local copies, waits for them, and re-layouts  24.8 us (4%)
    ppermute x30, waiting for transfers between devices, swap(): return lax.ppermute(value, axis, SWAP)  136 us
    pallas_call x5, Pallas kernels, attend_back(): pl.pallas_call(functools.partial(attend_back_kernel, add, len(into)), gri...  86.9 us
    dot_general x25, matrix products, mm(): return lax.dot_general(left, right, dims, preferred_element_type=F32)  83.5 us
    ppermute x1, waiting for transfers between devices, local(): know_other = lax.ppermute(know_sum, top_axis, SWAP)  73.8 us
    pallas_call x2, Pallas kernels, attend(): pl.pallas_call(functools.partial(attend_kernel, merge), grid_spec=pltpu.P...  43.5 us
    pallas_call x1, Pallas kernels, middle(): pl.pallas_call(middle_kernel, grid=(tokens // block,), in_specs=[rows(wid...  37.3 us
    pallas_call x2, Pallas kernels, weight_sums(): pl.pallas_call(functools.partial(weight_sums_kernel, counts), grid_spec=p...  27.6 us
    ppermute x30, starting transfers between devices, swap(): return lax.ppermute(value, axis, SWAP)  25.6 us
  transfers between devices with their start and end apart: 38, of which 21 were waited for; matrix products, arithmetic and copies ran while one was open for 15% of the time, Pallas kernels for 22%

profile of v9, /device:TPU:0, one launch (start us, length us, event | category | flops | bytes accessed | tf_op | source)
XLA Modules:
  0.0 660.6 jit_solution(15972114261238895055)
XLA Ops:
  17.9 8.8 %all-to-all-done = s32[16,1,256]{2,1,0:T(1,128)S(1)} async-done(((s32[16,1,256]{2,1,0:T(1,128)}), s32[16,1,256]{2,1,0:T(1,128)S(1)}, u32[]{:S(2)}, u32[]{:S(2)}) %all-to-all-start) | async-done | bytes 16416 | tf_op jit(solution)/shard_map/all_to_all | solution.py:611
  26.8 8.3 %fusion.25 = bf16[3072,768]{1,0:T(8,128)(2,1)} fusion(s32[864]{0:T(1024)S(1)} %iota_add_fusion.2, s32[3072]{0:T(1024)S(1)} %eq.199, bf16[288,768]{1,0:T(8,128)(2,1)} %collective-permute-done, bf16[288,768]{1,0:T(8,128)(2,1)S(1)} %reduce_sum.75, bf16[288,768]{1,0:T(8,128)(2,1)} %param.31), kind=kOutput, calls=%fused_computation.27 | convolution fusion | flops 4085858304 | bytes 6061440 | tf_op jit(solution)/shard_map/dot_general | solution.py:24
  40.9 73.8 %collective-permute-done.1 = bf16[288,768]{1,0:T(8,128)(2,1)S(1)} collective-permute-done((bf16[288,768]{1,0:T(8,128)(2,1)S(1)}, bf16[288,768]{1,0:T(8,128)(2,1)S(1)}, u32[]{:S(2)}, u32[]{:S(2)}) %collective-permute-start.1) | collective-permute-done | bytes 442400 | tf_op jit(solution)/shard_map/ppermute | solution.py:622
  130.9 9.5 %fusion.3 = f32[1024,768]{1,0:T(8,128)} fusion(bf16[3072,768]{1,0:T(8,128)(2,1)} %bitcast.9, s32[3072]{0:T(1024)S(1)} %eq.189, s32[1024]{0:T(1024)S(1)} %reduce.3, s32[1024]{0:T(1024)S(1)} %reduce.2), kind=kOutput, calls=%fused_computation.4 | convolution fusion | flops 4841275392 | bytes 7884800 | tf_op jit(solution)/shard_map/dot_general | solution.py:24
  155.9 21.1 %attend.1 = (f32[768,1024]{1,0:T(8,128)}, f32[6,2,1024]{2,1,0:T(2,128)S(1)}) custom-call(s32[2]{0:T(128)S(1)} %pad_add_fusion.1.where_ref, bf16[1024,768]{1,0:T(8,128)(2,1)S(1)} %add_convert_fusion.3.q_ref, bf16[1024,768]{1,0:T(8,128)(2,1)S(1)} %convolution_convert_fusion.k_ref, bf16[1024,768]{1,0:T(8,128)(2,1)S(1)} %add_convert_fusion.1.v_ref), custom_call_target="tpu_custom_call" | custom-call | flops 12884901888 | bytes 15728640 | tf_op jit(solution)/shard_map/attend/pallas_call | solution.py:167
  177.0 10.8 %collective-permute-done.2 = bf16[1024,768]{1,0:T(8,128)(2,1)S(1)} collective-permute-done((bf16[1024,768]{1,0:T(8,128)(2,1)S(1)}, bf16[1024,768]{1,0:T(8,128)(2,1)S(1)}, u32[]{:S(2)}, u32[]{:S(2)}) %collective-permute-start.2) | collective-permute-done | bytes 1572896 | tf_op jit(solution)/shard_map/ppermute | solution.py:649
  190.7 22.4 %attend_more.1 = (f32[1024,768]{1,0:T(8,128)}, f32[6,2,1024]{2,1,0:T(2,128)S(1)}) custom-call(s32[2]{0:T(128)S(1)} %pad_add_fusion.where_ref, bf16[1024,768]{1,0:T(8,128)(2,1)S(1)} %add_convert_fusion.3.q_ref, bf16[1024,768]{1,0:T(8,128)(2,1)S(1)} %convolution_convert_fusion.1.k_ref, bf16[1024,768]{1,0:T(8,128)(2,1)S(1)} %add_convert_fusion.2.v_ref, ...), custom_call_target="tpu_custom_call" | custom-call | flops 12884901888 | bytes 15728640 | tf_op jit(solution)/shard_map/attend_more/pallas_call | solution.py:167
  213.7 37.3 %middle.1 = (bf16[1024,768]{1,0:T(8,128)(2,1)}, bf16[1024,768]{1,0:T(8,128)(2,1)}, bf16[1024,768]{1,0:T(8,128)(2,1)}, bf16[1024,3072]{1,0:T(8,128)(2,1)}, bf16[1...) custom-call(f32[1024,768]{1,0:T(8,128)} %get-tuple-element.206.ctx_r, ...), custom_call_target="tpu_custom_call" | custom-call | flops 43486543872 | bytes 34603008 | tf_op jit(solution)/shard_map/middle/pallas_call | solution.py:375
  251.0 13.8 %weight_sums.2 = bf16[3456,768]{1,0:T(8,128)(2,1)} custom-call(s32[1]{0:T(128)} %bitcast.18.half_ref, bf16[1024,3072]{1,0:T(8,128)(2,1)} %get-tuple-element.214.act_ref, bf16[1024,768]{1,0:T(8,128)(2,1)} %get-tuple-element.215.gffn_ref, bf16[1024,3072]{1,0:T(8,128)(2,1)} %get-tuple-element.216.gpre_ref, bf16[1024,768]{1,0:T(8,128)(2,1)} %get-tuple-element.217.norm_ref, ...), custom_call_target="tpu_custom_call" | custom-call | flops 5435817984 | bytes 12386304 | tf_op jit(solution)/shard_map/weight_sums/pallas_call | solution.py:438
  264.9 13.8 %weight_sums.3 = bf16[3456,768]{1,0:T(8,128)(2,1)} custom-call(s32[1]{0:T(128)} %bitcast.17.half_ref.core_ref, bf16[1024,3072]{1,0:T(8,128)(2,1)} %get-tuple-element.214.act_ref, bf16[1024,768]{1,0:T(8,128)(2,1)} %get-tuple-element.215.gffn_ref, bf16[1024,3072]{1,0:T(8,128)(2,1)} %get-tuple-element.216.gpre_ref, ...), custom_call_target="tpu_custom_call" | custom-call | flops 5435817984 | bytes 12386304 | tf_op jit(solution)/shard_map/weight_sums/pallas_call | solution.py:438
  288.0 26.5 %attend_back0.1 = (f32[1024,768]{1,0:T(8,128)}, bf16[1024,768]{1,0:T(8,128)(2,1)}, bf16[1024,768]{1,0:T(8,128)(2,1)}) custom-call(s32[2]{0:T(128)} %copy-done.2, bf16[1024,768]{1,0:T(8,128)(2,1)} %copy-done.5, bf16[1024,768]{1,0:T(8,128)(2,1)} %get-tuple-element.283.g_ref, f32[1024,768]{1,0:T(8,128)} %get-tuple-element.206.ctx_ref.o_ref, ...), custom_call_target="tpu_custom_call" | custom-call | flops 21474836480 | bytes 12582912 | tf_op jit(solution)/shard_map/attend_back0/pallas_call | solution.py:247
  322.4 14.9 %attend_back4.1 = (f32[1024,768]{1,0:T(8,128)}, bf16[1024,768]{1,0:T(8,128)(2,1)}, bf16[1024,768]{1,0:T(8,128)(2,1)}) custom-call(s32[2]{0:T(128)} %copy-done.2, bf16[1024,768]{1,0:T(8,128)(2,1)} %copy-done.5, bf16[1024,768]{1,0:T(8,128)(2,1)} %get-tuple-element.283.g_ref, ...), custom_call_target="tpu_custom_call", output_to_operand_aliasing={{0}: (7, {}), {1}: (8, {}), {2}: (9, {})} | custom-call | flops 10737418240 | bytes 6291456 | tf_op jit(solution)/shard_map/attend_back4/pallas_call | solution.py:247
  346.4 15.1 %attend_back_more0.1 = (bf16[1024,768]{1,0:T(8,128)(2,1)}, bf16[1024,768]{1,0:T(8,128)(2,1)}, bf16[1024,768]{1,0:T(8,128)(2,1)}) custom-call(s32[2]{0:T(128)} %copy-done.1, bf16[1024,768]{1,0:T(8,128)(2,1)} %copy-done.5, bf16[1024,768]{1,0:T(8,128)(2,1)} %get-tuple-element.283.g_ref, f32[1024,768]{1,0:T(8,128)} %get-tuple-element.206.ctx_ref.o_ref, ...), custom_call_target="tpu_custom_call" | custom-call | flops 10737418240 | bytes 6291456 | tf_op jit(solution)/shard_map/attend_back_more0/pallas_call | solution.py:247
  363.9 14.9 %attend_back_more2.1 = (bf16[1024,768]{1,0:T(8,128)(2,1)}, bf16[1024,768]{1,0:T(8,128)(2,1)}, bf16[1024,768]{1,0:T(8,128)(2,1)}) custom-call(s32[2]{0:T(128)} %copy-done.1, bf16[1024,768]{1,0:T(8,128)(2,1)} %copy-done.5, bf16[1024,768]{1,0:T(8,128)(2,1)} %get-tuple-element.283.g_ref, ...), custom_call_target="tpu_custom_call", output_to_operand_aliasing={{0}: (8, {}), {1}: (9, {}), {2}: (10, {})} | custom-call | flops 10737418240 | bytes 6291456 | tf_op jit(solution)/shard_map/attend_back_more2/pallas_call | solution.py:247
  379.8 15.5 %attend_back_more4.1 = (bf16[1024,768]{1,0:T(8,128)(2,1)}, bf16[1024,768]{1,0:T(8,128)(2,1)}, bf16[1024,768]{1,0:T(8,128)(2,1)}) custom-call(s32[2]{0:T(128)} %copy-done.1, bf16[1024,768]{1,0:T(8,128)(2,1)} %copy-done.5, bf16[1024,768]{1,0:T(8,128)(2,1)} %get-tuple-element.283.g_ref, ...), custom_call_target="tpu_custom_call", output_to_operand_aliasing={{0}: (8, {}), {1}: (9, {}), {2}: (10, {})} | custom-call | flops 10737418240 | bytes 6291456 | tf_op jit(solution)/shard_map/attend_back_more4/pallas_call | solution.py:247
  414.0 10.9 %fusion.17 = bf16[4096,768]{1,0:T(8,128)(2,1)} fusion(bf16[1024,768]{1,0:T(8,128)(2,1)S(1)} %get-tuple-element.305, s32[1024]{0:T(1024)S(1)} %copy-done.43, s32[1024]{0:T(1024)S(1)} %copy-done.41), kind=kOutput, calls=%fused_computation.20 | convolution fusion | flops 6458179584 | bytes 7872512 | tf_op jit(solution)/shard_map/dot_general | solution.py:24
  473.9 54.6 %collective-permute-done.18 = bf16[320,768]{1,0:T(8,128)(2,1)} collective-permute-done((bf16[320,768]{1,0:T(8,128)(2,1)S(1)}, bf16[320,768]{1,0:T(8,128)(2,1)}, u32[]{:S(2)}, u32[]{:S(2)}) %collective-permute-start.18) | collective-permute-done | bytes 491552 | tf_op jit(solution)/shard_map/ppermute | solution.py:525
  543.0 7.9 %fusion.7 = f32[576,768]{1,0:T(8,128)} fusion(bf16[4096,768]{1,0:T(8,128)(2,1)} %bitcast.20, s32[4096]{0:T(1024)S(1)} %copy-done.39, s32[576]{0:T(1024)S(1)} %copy-done.54), kind=kOutput, calls=%fused_computation.9 | convolution fusion | flops 3626237952 | bytes 8079616 | tf_op jit(solution)/shard_map/dot_general | solution.py:24
  550.8 30.2 %collective-permute-done.21 = bf16[576,768]{1,0:T(8,128)(2,1)S(1)} collective-permute-done((bf16[576,768]{1,0:T(8,128)(2,1)S(1)}, bf16[576,768]{1,0:T(8,128)(2,1)S(1)}, u32[]{:S(2)}, u32[]{:S(2)}) %collective-permute-start.21) | collective-permute-done | bytes 884768 | tf_op jit(solution)/shard_map/ppermute | solution.py:525
  582.2 6.9 %collective-permute-done.22 = bf16[160,768]{1,0:T(8,128)(2,1)S(1)} collective-permute-done((bf16[160,768]{1,0:T(8,128)(2,1)S(1)}, bf16[160,768]{1,0:T(8,128)(2,1)S(1)}, u32[]{:S(2)}, u32[]{:S(2)}) %collective-permute-start.22) | collective-permute-done | bytes 245792 | tf_op jit(solution)/shard_map/ppermute | solution.py:525
  596.4 8.2 %collective-permute-done.25 = bf16[80,768]{1,0:T(8,128)(2,1)S(1)} collective-permute-done((bf16[80,768]{1,0:T(8,128)(2,1)S(1)}, bf16[80,768]{1,0:T(8,128)(2,1)S(1)}, u32[]{:S(2)}, u32[]{:S(2)}) %collective-permute-start.25) | collective-permute-done | bytes 122912 | tf_op jit(solution)/shard_map/ppermute | solution.py:525
  615.3 7.9 %unpack0.1 = f32[3072,768]{1,0:T(8,128)} custom-call(s32[1]{0:T(128)} %bitcast.17.half_ref.core_ref, bf16[3456,768]{1,0:T(8,128)(2,1)} %copy-done.9, bf16[3456,768]{1,0:T(8,128)(2,1)} %copy-done.10), custom_call_target="tpu_custom_call" | custom-call | flops 2359296 | bytes 14155776 | tf_op jit(solution)/shard_map/unpack0/pallas_call | solution.py:469
  625.7 8.5 %unpack8.1 = f32[768,3072]{1,0:T(8,128)} custom-call(s32[1]{0:T(128)} %bitcast.17.half_ref.core_ref, bf16[3456,768]{1,0:T(8,128)(2,1)} %copy-done.9, bf16[3456,768]{1,0:T(8,128)(2,1)} %copy-done.10), custom_call_target="tpu_custom_call" | custom-call | flops 2359296 | bytes 14155776 | tf_op jit(solution)/shard_map/unpack8/pallas_call | solution.py:469
  638.9 8.1 %collective-permute-done.31 = bf16[320,768]{1,0:T(8,128)(2,1)S(1)} collective-permute-done((bf16[320,768]{1,0:T(8,128)(2,1)S(1)}, bf16[320,768]{1,0:T(8,128)(2,1)S(1)}, u32[]{:S(2)}, u32[]{:S(2)}) %collective-permute-start.31) | collective-permute-done | bytes 491552 | tf_op jit(solution)/shard_map/ppermute | solution.py:525
  (334 shorter events, 207.2 us)
Async XLA Ops:
  0.7 26.0 %collective-permute-start = (bf16[288,768]{1,0:T(8,128)(2,1)}, bf16[288,768]{1,0:T(8,128)(2,1)}, u32[]{:S(2)}, u32[]{:S(2)}) collective-permute-start(bf16[288,768]{1,0:T(8,128)(2,1)} %param.31), channel_id=1, source_target_pairs={{0,16},{16,0},{1,17},{17,1},{2,18},{18,2},{3,19},{19,3},{4,20},{20... | collective-permute-start | bytes 1327112 | tf_op jit(solution)/shard_map/ppermute | solution.py:614
  35.1 81.8 %all-to-all-start.1 = ((bf16[16,192,768]{2,1,0:T(8,128)(2,1)}), bf16[16,192,768]{2,1,0:T(8,128)(2,1)}, u32[]{:S(2)}, u32[]{:S(2)}) async-start(bf16[16,192,768]{2,1,0:T(8,128)(2,1)} %bitcast.71), calls=%async_computation.1 | async-start | bytes 9437184 | tf_op jit(solution)/shard_map/all_to_all | solution.py:611
  39.7 75.0 %collective-permute-start.1 = (bf16[288,768]{1,0:T(8,128)(2,1)S(1)}, bf16[288,768]{1,0:T(8,128)(2,1)S(1)}, u32[]{:S(2)}, u32[]{:S(2)}) collective-permute-start(bf16[288,768]{1,0:T(8,128)(2,1)S(1)} %reduce_sum.75), channel_id=1, source_target_pairs={{0,16},{16,0},{1,17},{17,1},{2,18},{18,2},{3,19},{19,3},{4,20},{20... | collective-permute-start | bytes 1327112 | tf_op jit(solution)/shard_map/ppermute | solution.py:622
  116.9 28.1 %all-to-all-start.2 = ((bf16[16,64,768]{2,1,0:T(8,128)(2,1)}), bf16[16,64,768]{2,1,0:T(8,128)(2,1)}, u32[]{:S(2)}, u32[]{:S(2)}) async-start(bf16[16,64,768]{2,1,0:T(8,128)(2,1)} %bitcast.72), calls=%async_computation.2 | async-start | bytes 3145728 | tf_op jit(solution)/shard_map/all_to_all | solution.py:611
  128.8 48.2 %collective-permute-start.3 = (s32[576]{0:T(1024)S(1)}, s32[576]{0:T(1024)S(1)}, u32[]{:S(2)}, u32[]{:S(2)}) collective-permute-start(s32[576]{0:T(1024)S(1)} %get-tuple-element.373), channel_id=1, source_target_pairs={{0,16},{16,0},{1,17},{17,1},{2,18},{18,2},{3,19},{19,3},{4,20},{20... | collective-permute-start | bytes 6920 | tf_op jit(solution)/shard_map/ppermute | solution.py:658
  151.0 36.8 %collective-permute-start.2 = (bf16[1024,768]{1,0:T(8,128)(2,1)S(1)}, bf16[1024,768]{1,0:T(8,128)(2,1)S(1)}, u32[]{:S(2)}, u32[]{:S(2)}) collective-permute-start(bf16[1024,768]{1,0:T(8,128)(2,1)S(1)} %get-tuple-element.428), channel_id=1, source_target_pairs={{0,1},{1,0},{2,3},{3,2},{4,5},{5,4},{6,7},{7,6},{8,9},{9,8},{10,11... | collective-permute-start | bytes 4718600 | tf_op jit(solution)/shard_map/ppermute | solution.py:649
  284.8 32.1 %collective-permute-start.5 = (bf16[864,768]{1,0:T(8,128)(2,1)S(1)}, bf16[864,768]{1,0:T(8,128)(2,1)S(1)}, u32[]{:S(2)}, u32[]{:S(2)}) collective-permute-start(bf16[864,768]{1,0:T(8,128)(2,1)S(1)} %get-tuple-element.226), channel_id=1, source_target_pairs={{0,4},{4,0},{1,5},{5,1},{2,6},{6,2},{3,7},{7,3},{8,12},{12,8},{9,1... | collective-permute-start | bytes 3981320 | tf_op jit(solution)/shard_map/ppermute | solution.py:525
  287.2 31.8 %collective-permute-start.6 = (bf16[864,768]{1,0:T(8,128)(2,1)S(1)}, bf16[864,768]{1,0:T(8,128)(2,1)}, u32[]{:S(2)}, u32[]{:S(2)}) collective-permute-start(bf16[864,768]{1,0:T(8,128)(2,1)S(1)} %get-tuple-element.227), channel_id=1, source_target_pairs={{0,1},{1,0},{2,3},{3,2},{4,5},{5,4},{6,7},{7,6},{8,9},{9,8},{10,11... | collective-permute-start | bytes 3981320 | tf_op jit(solution)/shard_map/ppermute | solution.py:525
  321.2 16.7 %collective-permute-start.7 = (bf16[432,768]{1,0:T(8,128)(2,1)S(1)}, bf16[432,768]{1,0:T(8,128)(2,1)S(1)}, u32[]{:S(2)}, u32[]{:S(2)}) collective-permute-start(bf16[432,768]{1,0:T(8,128)(2,1)S(1)} %get-tuple-element.240), channel_id=1, source_target_pairs={{0,1},{1,0},{2,3},{3,2},{4,5},{5,4},{6,7},{7,6},{8,9},{9,8},{10,11... | collective-permute-start | bytes 1990664 | tf_op jit(solution)/shard_map/ppermute | solution.py:525
  322.0 16.3 %collective-permute-start.8 = (bf16[432,768]{1,0:T(8,128)(2,1)S(1)}, bf16[432,768]{1,0:T(8,128)(2,1)S(1)}, u32[]{:S(2)}, u32[]{:S(2)}) collective-permute-start(bf16[432,768]{1,0:T(8,128)(2,1)S(1)} %get-tuple-element.241), channel_id=1, source_target_pairs={{0,4},{4,0},{1,5},{5,1},{2,6},{6,2},{3,7},{7,3},{8,12},{12,8},{9,1... | collective-permute-start | bytes 1990664 | tf_op jit(solution)/shard_map/ppermute | solution.py:525
  345.0 16.6 %collective-permute-start.9 = (bf16[432,768]{1,0:T(8,128)(2,1)S(1)}, bf16[432,768]{1,0:T(8,128)(2,1)S(1)}, u32[]{:S(2)}, u32[]{:S(2)}) collective-permute-start(bf16[432,768]{1,0:T(8,128)(2,1)S(1)} %get-tuple-element.257), channel_id=1, source_target_pairs={{0,8},{8,0},{1,9},{9,1},{2,10},{10,2},{3,11},{11,3},{4,12},{12,4},... | collective-permute-start | bytes 1990664 | tf_op jit(solution)/shard_map/ppermute | solution.py:525
  345.1 50.4 %collective-permute-start.12 = (bf16[1024,768]{1,0:T(8,128)(2,1)S(1)}, bf16[1024,768]{1,0:T(8,128)(2,1)S(1)}, u32[]{:S(2)}, u32[]{:S(2)}) collective-permute-start(bf16[1024,768]{1,0:T(8,128)(2,1)S(1)} %add_convert_fusion), channel_id=1, source_target_pairs={{0,1},{1,0},{2,3},{3,2},{4,5},{5,4},{6,7},{7,6},{8,9},{9,8},{10,11... | collective-permute-start | bytes 4718600 | tf_op jit(solution)/shard_map/ppermute | solution.py:525
  361.8 16.9 %collective-permute-start.10 = (bf16[216,768]{1,0:T(8,128)(2,1)S(1)}, bf16[216,768]{1,0:T(8,128)(2,1)S(1)}, u32[]{:S(2)}, u32[]{:S(2)}) collective-permute-start(bf16[216,768]{1,0:T(8,128)(2,1)S(1)} %get-tuple-element.268), channel_id=1, source_target_pairs={{0,16},{16,0},{1,17},{17,1},{2,18},{18,2},{3,19},{19,3},{4,20},{20... | collective-permute-start | bytes 995336 | tf_op jit(solution)/shard_map/ppermute | solution.py:525
  378.8 16.5 %collective-permute-start.11 = (bf16[216,768]{1,0:T(8,128)(2,1)S(1)}, bf16[216,768]{1,0:T(8,128)(2,1)S(1)}, u32[]{:S(2)}, u32[]{:S(2)}) collective-permute-start(bf16[216,768]{1,0:T(8,128)(2,1)S(1)} %add.250), channel_id=1, source_target_pairs={{0,16},{16,0},{1,17},{17,1},{2,18},{18,2},{3,19},{19,3},{4,20},{20... | collective-permute-start | bytes 995336 | tf_op jit(solution)/shard_map/ppermute | solution.py:525
  395.5 16.5 %collective-permute-start.13 = (bf16[432,768]{1,0:T(8,128)(2,1)S(1)}, bf16[432,768]{1,0:T(8,128)(2,1)S(1)}, u32[]{:S(2)}, u32[]{:S(2)}) collective-permute-start(bf16[432,768]{1,0:T(8,128)(2,1)S(1)} %pad_maximum_fusion.4), channel_id=1, source_target_pairs={{0,8},{8,0},{1,9},{9,1},{2,10},{10,2},{3,11},{11,3},{4,12},{12,4},... | collective-permute-start | bytes 1990664 | tf_op jit(solution)/shard_map/ppermute | solution.py:525
  429.4 99.9 %all-to-all-start.3 = ((bf16[16,256,768]{2,1,0:T(8,128)(2,1)}), bf16[16,256,768]{2,1,0:T(8,128)(2,1)}, u32[]{:S(2)}, u32[]{:S(2)}) async-start(bf16[16,256,768]{2,1,0:T(8,128)(2,1)} %bitcast.70), calls=%async_computation.3 | async-start | bytes 12582912 | tf_op jit(solution)/shard_map/all_to_all | solution.py:611
  468.5 60.1 %collective-permute-start.18 = (bf16[320,768]{1,0:T(8,128)(2,1)S(1)}, bf16[320,768]{1,0:T(8,128)(2,1)}, u32[]{:S(2)}, u32[]{:S(2)}) collective-permute-start(bf16[320,768]{1,0:T(8,128)(2,1)S(1)} %get-tuple-element.406), channel_id=1, source_target_pairs={{0,1},{1,0},{2,3},{3,2},{4,5},{5,4},{6,7},{7,6},{8,9},{9,8},{10,11... | collective-permute-start | bytes 1474568 | tf_op jit(solution)/shard_map/ppermute | solution.py:525
  471.0 58.3 %collective-permute-start.17 = (bf16[320,768]{1,0:T(8,128)(2,1)S(1)}, bf16[320,768]{1,0:T(8,128)(2,1)}, u32[]{:S(2)}, u32[]{:S(2)}) collective-permute-start(bf16[320,768]{1,0:T(8,128)(2,1)S(1)} %get-tuple-element.408), channel_id=1, source_target_pairs={{0,4},{4,0},{1,5},{5,1},{2,6},{6,2},{3,7},{7,3},{8,12},{12,8},{9,1... | collective-permute-start | bytes 1474568 | tf_op jit(solution)/shard_map/ppermute | solution.py:525
  531.8 19.0 %collective-permute-start.19 = (bf16[160,768]{1,0:T(8,128)(2,1)S(1)}, bf16[160,768]{1,0:T(8,128)(2,1)S(1)}, u32[]{:S(2)}, u32[]{:S(2)}) collective-permute-start(bf16[160,768]{1,0:T(8,128)(2,1)S(1)} %get-tuple-element.325), channel_id=1, source_target_pairs={{0,1},{1,0},{2,3},{3,2},{4,5},{5,4},{6,7},{7,6},{8,9},{9,8},{10,11... | collective-permute-start | bytes 737288 | tf_op jit(solution)/shard_map/ppermute | solution.py:525
  533.3 17.6 %collective-permute-start.20 = (bf16[160,768]{1,0:T(8,128)(2,1)S(1)}, bf16[160,768]{1,0:T(8,128)(2,1)S(1)}, u32[]{:S(2)}, u32[]{:S(2)}) collective-permute-start(bf16[160,768]{1,0:T(8,128)(2,1)S(1)} %get-tuple-element.326), channel_id=1, source_target_pairs={{0,4},{4,0},{1,5},{5,1},{2,6},{6,2},{3,7},{7,3},{8,12},{12,8},{9,1... | collective-permute-start | bytes 737288 | tf_op jit(solution)/shard_map/ppermute | solution.py:525
  540.2 40.8 %collective-permute-start.21 = (bf16[576,768]{1,0:T(8,128)(2,1)S(1)}, bf16[576,768]{1,0:T(8,128)(2,1)S(1)}, u32[]{:S(2)}, u32[]{:S(2)}) collective-permute-start(bf16[576,768]{1,0:T(8,128)(2,1)S(1)} %fusion.44), channel_id=1, source_target_pairs={{0,16},{16,0},{1,17},{17,1},{2,18},{18,2},{3,19},{19,3},{4,20},{20... | collective-permute-start | bytes 2654216 | tf_op jit(solution)/shard_map/ppermute | solution.py:525
  540.3 49.2 %collective-permute-start.23 = (bf16[864,768]{1,0:T(8,128)(2,1)S(1)}, bf16[864,768]{1,0:T(8,128)(2,1)}, u32[]{:S(2)}, u32[]{:S(2)}) collective-permute-start(bf16[864,768]{1,0:T(8,128)(2,1)S(1)} %pad_maximum_fusion.2), channel_id=1, source_target_pairs={{0,4},{4,0},{1,5},{5,1},{2,6},{6,2},{3,7},{7,3},{8,12},{12,8},{9,1... | collective-permute-start | bytes 3981320 | tf_op jit(solution)/shard_map/ppermute | solution.py:525
  542.4 47.1 %collective-permute-start.24 = (bf16[864,768]{1,0:T(8,128)(2,1)}, bf16[864,768]{1,0:T(8,128)(2,1)}, u32[]{:S(2)}, u32[]{:S(2)}) collective-permute-start(bf16[864,768]{1,0:T(8,128)(2,1)} %pad_maximum_fusion.3), channel_id=1, source_target_pairs={{0,1},{1,0},{2,3},{3,2},{4,5},{5,4},{6,7},{7,6},{8,9},{9,8},{10,11... | collective-permute-start | bytes 3981320 | tf_op jit(solution)/shard_map/ppermute | solution.py:525
  595.7 17.3 %collective-permute-start.27 = (bf16[3456,768]{1,0:T(8,128)(2,1)S(1)}, bf16[3456,768]{1,0:T(8,128)(2,1)S(1)}, u32[]{:S(2)}, u32[]{:S(2)}) collective-permute-start(bf16[3456,768]{1,0:T(8,128)(2,1)S(1)} %pad_maximum_fusion.own_ref), channel_id=1, source_target_pairs={{0,2},{2,0},{1,3},{3,1},{4,6},{6,4},{5,7},{7,5},{8,10},{10,8},{9,1... | collective-permute-start | bytes 15925256 | tf_op jit(solution)/shard_map/ppermute | solution.py:525
  (85 other events, 911.5 us)

commit v10 on v9

--- a/solution.py
+++ b/solution.py
@@ -767,8 +767,6 @@
     came = travel(sends, stages[0])
     returned, keeps, came, early = lax.optimization_barrier((returned, keeps, came, early))
     late = end(keeps, came, stages[0])
-    from_other = swap(mm(owned[1].astype(BF16), returned).astype(BF16), top_axis)
-    table_own = mm(owned[0].astype(BF16), returned)
     last = len(stages) - 1
     early_parts = []
     early_step = begin(early, stages[done])
@@ -777,34 +775,44 @@
         if at == 1:
             keeps, sends, early_step = lax.optimization_barrier((keeps, sends, early_step))
             early_came = travel(early_step[1], stages[done])
-        if at == 3:
+        if at == 4:
             keeps, sends, early_came = lax.optimization_barrier((keeps, sends, early_came))
             early = end(early_step[0], early_came, stages[done])
             early = jnp.concatenate(run_stages(early, stages[done + 1 :]), axis=0)
             early_step = (early, swap(early, core))
-        if at == last - 2:
-            keeps, sends, early_step = lax.optimization_barrier((keeps, sends, early_step))
+        if at == last - 1:
+            keeps, sends, early_step, for_other = lax.optimization_barrier(
+                (keeps, sends, early_step, for_other)
+            )
+            from_other = [swap(part, top_axis) for part in jnp.split(for_other, 2, axis=0)]
+        if at == last:
+            keeps, sends, from_other[0] = lax.optimization_barrier((keeps, sends, from_other[0]))
         came = travel(sends, stage)
-        if at == 1:
-            came, from_other, table_own = lax.optimization_barrier((came, from_other, table_own))
-        if at == 4:
-            table_grads = table_own + from_other.astype(F32)
-            came, table_grads = lax.optimization_barrier((came, table_grads))
-        if at >= last - 2:
-            part = at - last + 2
+        if at == 2:
+            table_own = mm(owned[0].astype(BF16), returned)
+            came, table_own = lax.optimization_barrier((came, table_own))
+        if at == 3:
+            for_other = mm(owned[1].astype(BF16), returned).astype(BF16)
+            came, for_other = lax.optimization_barrier((came, for_other))
+        if at >= last - 1:
+            part = at - last + 1
             early_parts.append(
-                unpack(
-                    my_core,
-                    *early_step,
-                    part * wide,
-                    (wide, wide, width)[part],
-                    part == 1,
-                )
+                unpack(my_core, *early_step, part * wide, wide, part == 1)
             )
             came, early_parts = lax.optimization_barrier((came, early_parts))
+        if at == last:
+            came, from_other[1] = lax.optimization_barrier((came, from_other[1]))
         late = end(keeps, came, stage)
     late = jnp.concatenate(late, axis=0)
     late_other = swap(late, core)
+    early_parts.append(unpack(my_core, *early_step, 2 * wide, width, False))
+    late_other, early_parts, from_other = lax.optimization_barrier(
+        (late_other, early_parts, from_other)
+    )
+    gene_grad, know_grad = (
+        table_own[part * rows_dev : (part + 1) * rows_dev] + from_other[part].astype(F32)
+        for part in range(2)
+    )
     w_down_grad, w_up_grad, w_out_grad = early_parts
     w_query_grad, w_key_grad, w_value_grad, expr_grad, short = unpack_whole(
         my_core, late, late_other, heights
@@ -816,8 +824,8 @@
     b_query_grad, b_value_grad = short[6 + wide // width], short[7 + wide // width]
     return (
         layer_output.reshape(1, tokens, width),
-        table_grads[:rows_dev],
-        table_grads[rows_dev:],
+        gene_grad,
+        know_grad,
         expr_grad,
         w_query_grad,
         b_query_grad,

time: 668 us -> 673 us (level)
  waiting for transfers between devices: 234 us -> 242 us
    ppermute x30 -> x31, waiting for transfers between devices: 136 us -> 144 us  [swap(): return lax.ppermute(value, axis, SWAP)]
    ppermute x30 -> x31, starting transfers between devices: 25.6 us -> 24.7 us  [swap(): return lax.ppermute(value, axis, SWAP)]
  transfers between devices with their start and end apart: 38 -> 39, of which waited for: 21 -> 25; matrix products, arithmetic and copies ran while one was open for 15% -> 14% of each run, Pallas kernels for 22% -> 22%
where the time goes in v10:
time: 673 us; the launch traced here: 665 us
  waiting for transfers between devices  242 us (36%)
  Pallas kernels  224 us (33%)
  matrix products  82.5 us (12%)
  starting transfers between devices  53.2 us (8%)
  other arithmetic  37.6 us (6%)
  local copies, waits for them, and re-layouts  22.8 us (3%)
    ppermute x31, waiting for transfers between devices, swap(): return lax.ppermute(value, axis, SWAP)  144 us
    pallas_call x5, Pallas kernels, attend_back(): pl.pallas_call(functools.partial(attend_back_kernel, add, len(into)), gri...  86.9 us
    dot_general x25, matrix products, mm(): return lax.dot_general(left, right, dims, preferred_element_type=F32)  82.5 us
    ppermute x1, waiting for transfers between devices, local(): know_other = lax.ppermute(know_sum, top_axis, SWAP)  73.8 us
    pallas_call x2, Pallas kernels, attend(): pl.pallas_call(functools.partial(attend_kernel, merge), grid_spec=pltpu.P...  43.5 us
    pallas_call x1, Pallas kernels, middle(): pl.pallas_call(middle_kernel, grid=(tokens // block,), in_specs=[rows(wid...  37.3 us
    pallas_call x2, Pallas kernels, weight_sums(): pl.pallas_call(functools.partial(weight_sums_kernel, counts), grid_spec=p...  27.6 us
    ppermute x31, starting transfers between devices, swap(): return lax.ppermute(value, axis, SWAP)  24.7 us
  transfers between devices with their start and end apart: 39, of which 25 were waited for; matrix products, arithmetic and copies ran while one was open for 14% of the time, Pallas kernels for 22%

profile of v10, /device:TPU:0, one launch (start us, length us, event | category | flops | bytes accessed | tf_op | source)
XLA Modules:
  0.0 665.2 jit_solution(17724656054188072505)
XLA Ops:
  18.0 8.7 %all-to-all-done = s32[16,1,256]{2,1,0:T(1,128)S(1)} async-done(((s32[16,1,256]{2,1,0:T(1,128)}), s32[16,1,256]{2,1,0:T(1,128)S(1)}, u32[]{:S(2)}, u32[]{:S(2)}) %all-to-all-start) | async-done | bytes 16416 | tf_op jit(solution)/shard_map/all_to_all | solution.py:611
  26.8 8.2 %fusion.25 = bf16[3072,768]{1,0:T(8,128)(2,1)} fusion(s32[864]{0:T(1024)S(1)} %iota_add_fusion.2, s32[3072]{0:T(1024)S(1)} %eq.199, bf16[288,768]{1,0:T(8,128)(2,1)} %collective-permute-done, bf16[288,768]{1,0:T(8,128)(2,1)S(1)} %reduce_sum.75, bf16[288,768]{1,0:T(8,128)(2,1)S(1)} %copy-done.66), kind=kOutput, calls=%fused_computation.27 | convolution fusion | flops 4085858304 | bytes 6061440 | tf_op jit(solution)/shard_map/dot_general | solution.py:24
  40.8 73.8 %collective-permute-done.1 = bf16[288,768]{1,0:T(8,128)(2,1)S(1)} collective-permute-done((bf16[288,768]{1,0:T(8,128)(2,1)S(1)}, bf16[288,768]{1,0:T(8,128)(2,1)S(1)}, u32[]{:S(2)}, u32[]{:S(2)}) %collective-permute-start.1) | collective-permute-done | bytes 442400 | tf_op jit(solution)/shard_map/ppermute | solution.py:622
  130.8 9.5 %fusion.3 = f32[1024,768]{1,0:T(8,128)} fusion(bf16[3072,768]{1,0:T(8,128)(2,1)} %bitcast.9, s32[3072]{0:T(1024)S(1)} %eq.189, s32[1024]{0:T(1024)S(1)} %reduce.3, s32[1024]{0:T(1024)S(1)} %reduce.2), kind=kOutput, calls=%fused_computation.4 | convolution fusion | flops 4841275392 | bytes 7884800 | tf_op jit(solution)/shard_map/dot_general | solution.py:24
  155.8 21.1 %attend.1 = (f32[768,1024]{1,0:T(8,128)}, f32[6,2,1024]{2,1,0:T(2,128)S(1)}) custom-call(s32[2]{0:T(128)S(1)} %pad_add_fusion.1.where_ref, bf16[1024,768]{1,0:T(8,128)(2,1)S(1)} %add_convert_fusion.3.q_ref, bf16[1024,768]{1,0:T(8,128)(2,1)S(1)} %convolution_convert_fusion.k_ref, bf16[1024,768]{1,0:T(8,128)(2,1)S(1)} %add_convert_fusion.1.v_ref), custom_call_target="tpu_custom_call" | custom-call | flops 12884901888 | bytes 15728640 | tf_op jit(solution)/shard_map/attend/pallas_call | solution.py:167
  176.9 10.8 %collective-permute-done.2 = bf16[1024,768]{1,0:T(8,128)(2,1)S(1)} collective-permute-done((bf16[1024,768]{1,0:T(8,128)(2,1)S(1)}, bf16[1024,768]{1,0:T(8,128)(2,1)S(1)}, u32[]{:S(2)}, u32[]{:S(2)}) %collective-permute-start.2) | collective-permute-done | bytes 1572896 | tf_op jit(solution)/shard_map/ppermute | solution.py:649
  190.6 22.4 %attend_more.1 = (f32[1024,768]{1,0:T(8,128)}, f32[6,2,1024]{2,1,0:T(2,128)S(1)}) custom-call(s32[2]{0:T(128)S(1)} %pad_add_fusion.where_ref, bf16[1024,768]{1,0:T(8,128)(2,1)S(1)} %add_convert_fusion.3.q_ref, bf16[1024,768]{1,0:T(8,128)(2,1)S(1)} %convolution_convert_fusion.1.k_ref, bf16[1024,768]{1,0:T(8,128)(2,1)S(1)} %add_convert_fusion.2.v_ref, ...), custom_call_target="tpu_custom_call" | custom-call | flops 12884901888 | bytes 15728640 | tf_op jit(solution)/shard_map/attend_more/pallas_call | solution.py:167
  213.7 37.3 %middle.1 = (bf16[1024,768]{1,0:T(8,128)(2,1)}, bf16[1024,768]{1,0:T(8,128)(2,1)}, bf16[1024,768]{1,0:T(8,128)(2,1)}, bf16[1024,3072]{1,0:T(8,128)(2,1)}, bf16[1...) custom-call(f32[1024,768]{1,0:T(8,128)} %get-tuple-element.217.ctx_r, ...), custom_call_target="tpu_custom_call" | custom-call | flops 43486543872 | bytes 34603008 | tf_op jit(solution)/shard_map/middle/pallas_call | solution.py:375
  250.9 13.9 %weight_sums.2 = bf16[3456,768]{1,0:T(8,128)(2,1)} custom-call(s32[1]{0:T(128)} %bitcast.18.half_ref, bf16[1024,3072]{1,0:T(8,128)(2,1)} %get-tuple-element.225.act_ref, bf16[1024,768]{1,0:T(8,128)(2,1)} %get-tuple-element.226.gffn_ref, bf16[1024,3072]{1,0:T(8,128)(2,1)} %get-tuple-element.227.gpre_ref, bf16[1024,768]{1,0:T(8,128)(2,1)} %get-tuple-element.228.norm_ref, ...), custom_call_target="tpu_custom_call" | custom-call | flops 5435817984 | bytes 12386304 | tf_op jit(solution)/shard_map/weight_sums/pallas_call | solution.py:438
  264.8 13.8 %weight_sums.3 = bf16[3456,768]{1,0:T(8,128)(2,1)} custom-call(s32[1]{0:T(128)} %bitcast.17.half_ref.core_ref, bf16[1024,3072]{1,0:T(8,128)(2,1)} %get-tuple-element.225.act_ref, bf16[1024,768]{1,0:T(8,128)(2,1)} %get-tuple-element.226.gffn_ref, bf16[1024,3072]{1,0:T(8,128)(2,1)} %get-tuple-element.227.gpre_ref, ...), custom_call_target="tpu_custom_call" | custom-call | flops 5435817984 | bytes 12386304 | tf_op jit(solution)/shard_map/weight_sums/pallas_call | solution.py:438
  287.9 26.6 %attend_back0.1 = (f32[1024,768]{1,0:T(8,128)}, bf16[1024,768]{1,0:T(8,128)(2,1)}, bf16[1024,768]{1,0:T(8,128)(2,1)}) custom-call(s32[2]{0:T(128)} %copy-done.2, bf16[1024,768]{1,0:T(8,128)(2,1)} %copy-done.5, bf16[1024,768]{1,0:T(8,128)(2,1)} %get-tuple-element.294.g_ref, f32[1024,768]{1,0:T(8,128)} %get-tuple-element.217.ctx_ref.o_ref, ...), custom_call_target="tpu_custom_call" | custom-call | flops 21474836480 | bytes 12582912 | tf_op jit(solution)/shard_map/attend_back0/pallas_call | solution.py:247
  322.3 14.9 %attend_back4.1 = (f32[1024,768]{1,0:T(8,128)}, bf16[1024,768]{1,0:T(8,128)(2,1)}, bf16[1024,768]{1,0:T(8,128)(2,1)}) custom-call(s32[2]{0:T(128)} %copy-done.2, bf16[1024,768]{1,0:T(8,128)(2,1)} %copy-done.5, bf16[1024,768]{1,0:T(8,128)(2,1)} %get-tuple-element.294.g_ref, ...), custom_call_target="tpu_custom_call", output_to_operand_aliasing={{0}: (7, {}), {1}: (8, {}), {2}: (9, {})} | custom-call | flops 10737418240 | bytes 6291456 | tf_op jit(solution)/shard_map/attend_back4/pallas_call | solution.py:247
  346.4 15.1 %attend_back_more0.1 = (bf16[1024,768]{1,0:T(8,128)(2,1)}, bf16[1024,768]{1,0:T(8,128)(2,1)}, bf16[1024,768]{1,0:T(8,128)(2,1)}) custom-call(s32[2]{0:T(128)} %copy-done.1, bf16[1024,768]{1,0:T(8,128)(2,1)} %copy-done.5, bf16[1024,768]{1,0:T(8,128)(2,1)} %get-tuple-element.294.g_ref, f32[1024,768]{1,0:T(8,128)} %get-tuple-element.217.ctx_ref.o_ref, ...), custom_call_target="tpu_custom_call" | custom-call | flops 10737418240 | bytes 6291456 | tf_op jit(solution)/shard_map/attend_back_more0/pallas_call | solution.py:247
  363.7 14.9 %attend_back_more2.1 = (bf16[1024,768]{1,0:T(8,128)(2,1)}, bf16[1024,768]{1,0:T(8,128)(2,1)}, bf16[1024,768]{1,0:T(8,128)(2,1)}) custom-call(s32[2]{0:T(128)} %copy-done.1, bf16[1024,768]{1,0:T(8,128)(2,1)} %copy-done.5, bf16[1024,768]{1,0:T(8,128)(2,1)} %get-tuple-element.294.g_ref, ...), custom_call_target="tpu_custom_call", output_to_operand_aliasing={{0}: (8, {}), {1}: (9, {}), {2}: (10, {})} | custom-call | flops 10737418240 | bytes 6291456 | tf_op jit(solution)/shard_map/attend_back_more2/pallas_call | solution.py:247
  379.7 15.5 %attend_back_more4.1 = (bf16[1024,768]{1,0:T(8,128)(2,1)}, bf16[1024,768]{1,0:T(8,128)(2,1)}, bf16[1024,768]{1,0:T(8,128)(2,1)}) custom-call(s32[2]{0:T(128)} %copy-done.1, bf16[1024,768]{1,0:T(8,128)(2,1)} %copy-done.5, bf16[1024,768]{1,0:T(8,128)(2,1)} %get-tuple-element.294.g_ref, ...), custom_call_target="tpu_custom_call", output_to_operand_aliasing={{0}: (8, {}), {1}: (9, {}), {2}: (10, {})} | custom-call | flops 10737418240 | bytes 6291456 | tf_op jit(solution)/shard_map/attend_back_more4/pallas_call | solution.py:247
  413.9 10.9 %fusion.17 = bf16[4096,768]{1,0:T(8,128)(2,1)} fusion(bf16[1024,768]{1,0:T(8,128)(2,1)S(1)} %get-tuple-element.316, s32[1024]{0:T(1024)S(1)} %copy-done.45, s32[1024]{0:T(1024)S(1)} %copy-done.43), kind=kOutput, calls=%fused_computation.20 | convolution fusion | flops 6458179584 | bytes 7872512 | tf_op jit(solution)/shard_map/dot_general | solution.py:24
  473.1 55.2 %collective-permute-done.18 = bf16[320,768]{1,0:T(8,128)(2,1)} collective-permute-done((bf16[320,768]{1,0:T(8,128)(2,1)S(1)}, bf16[320,768]{1,0:T(8,128)(2,1)}, u32[]{:S(2)}, u32[]{:S(2)}) %collective-permute-start.18) | collective-permute-done | bytes 491552 | tf_op jit(solution)/shard_map/ppermute | solution.py:525
  543.1 8.1 %fusion.7 = f32[576,768]{1,0:T(8,128)} fusion(bf16[4096,768]{1,0:T(8,128)(2,1)} %bitcast.20, s32[4096]{0:T(1024)S(1)} %copy-done.41, s32[576]{0:T(1024)S(1)} %copy-done.58), kind=kOutput, calls=%fused_computation.9 | convolution fusion | flops 3626237952 | bytes 8079616 | tf_op jit(solution)/shard_map/dot_general | solution.py:24
  560.2 21.0 %collective-permute-done.23 = bf16[864,768]{1,0:T(8,128)(2,1)S(1)} collective-permute-done((bf16[864,768]{1,0:T(8,128)(2,1)S(1)}, bf16[864,768]{1,0:T(8,128)(2,1)S(1)}, u32[]{:S(2)}, u32[]{:S(2)}) %collective-permute-start.23) | collective-permute-done | bytes 1327136 | tf_op jit(solution)/shard_map/ppermute | solution.py:525
  584.6 9.1 %collective-permute-done.25 = bf16[80,768]{1,0:T(8,128)(2,1)S(1)} collective-permute-done((bf16[80,768]{1,0:T(8,128)(2,1)S(1)}, bf16[80,768]{1,0:T(8,128)(2,1)S(1)}, u32[]{:S(2)}, u32[]{:S(2)}) %collective-permute-start.25) | collective-permute-done | bytes 122912 | tf_op jit(solution)/shard_map/ppermute | solution.py:525
  593.8 7.9 %collective-permute-done.26 = bf16[160,768]{1,0:T(8,128)(2,1)S(1)} collective-permute-done((bf16[160,768]{1,0:T(8,128)(2,1)S(1)}, bf16[160,768]{1,0:T(8,128)(2,1)S(1)}, u32[]{:S(2)}, u32[]{:S(2)}) %collective-permute-start.26) | collective-permute-done | bytes 245792 | tf_op jit(solution)/shard_map/ppermute | solution.py:525
  607.3 7.9 %unpack0.1 = f32[3072,768]{1,0:T(8,128)} custom-call(s32[1]{0:T(128)} %bitcast.17.half_ref.core_ref, bf16[3456,768]{1,0:T(8,128)(2,1)} %copy-done.9, bf16[3456,768]{1,0:T(8,128)(2,1)} %copy-done.10), custom_call_target="tpu_custom_call" | custom-call | flops 2359296 | bytes 14155776 | tf_op jit(solution)/shard_map/unpack0/pallas_call | solution.py:469
  615.4 13.0 %collective-permute-done.30 = bf16[288,768]{1,0:T(8,128)(2,1)S(1)} collective-permute-done((bf16[288,768]{1,0:T(8,128)(2,1)S(1)}, bf16[288,768]{1,0:T(8,128)(2,1)S(1)}, u32[]{:S(2)}, u32[]{:S(2)}) %collective-permute-start.30) | collective-permute-done | bytes 442400 | tf_op jit(solution)/shard_map/ppermute | solution.py:525
  630.2 8.5 %unpack8.1 = f32[768,3072]{1,0:T(8,128)} custom-call(s32[1]{0:T(128)} %bitcast.17.half_ref.core_ref, bf16[3456,768]{1,0:T(8,128)(2,1)} %copy-done.9, bf16[3456,768]{1,0:T(8,128)(2,1)} %copy-done.10), custom_call_target="tpu_custom_call" | custom-call | flops 2359296 | bytes 14155776 | tf_op jit(solution)/shard_map/unpack8/pallas_call | solution.py:469
  (342 shorter events, 213.8 us)
Async XLA Ops:
  0.7 26.0 %collective-permute-start = (bf16[288,768]{1,0:T(8,128)(2,1)}, bf16[288,768]{1,0:T(8,128)(2,1)}, u32[]{:S(2)}, u32[]{:S(2)}) collective-permute-start(bf16[288,768]{1,0:T(8,128)(2,1)} %param.31), channel_id=1, source_target_pairs={{0,16},{16,0},{1,17},{17,1},{2,18},{18,2},{3,19},{19,3},{4,20},{20... | collective-permute-start | bytes 1327112 | tf_op jit(solution)/shard_map/ppermute | solution.py:614
  11.0 15.7 %all-to-all-start = ((s32[16,1,256]{2,1,0:T(1,128)}), s32[16,1,256]{2,1,0:T(1,128)S(1)}, u32[]{:S(2)}, u32[]{:S(2)}) async-start(s32[16,1,256]{2,1,0:T(1,128)} %bitcast.6), calls=%async_computation | async-start | bytes 32768 | tf_op jit(solution)/shard_map/all_to_all | solution.py:611
  35.0 81.8 %all-to-all-start.1 = ((bf16[16,192,768]{2,1,0:T(8,128)(2,1)}), bf16[16,192,768]{2,1,0:T(8,128)(2,1)}, u32[]{:S(2)}, u32[]{:S(2)}) async-start(bf16[16,192,768]{2,1,0:T(8,128)(2,1)} %bitcast.71), calls=%async_computation.1 | async-start | bytes 9437184 | tf_op jit(solution)/shard_map/all_to_all | solution.py:611
  39.6 75.0 %collective-permute-start.1 = (bf16[288,768]{1,0:T(8,128)(2,1)S(1)}, bf16[288,768]{1,0:T(8,128)(2,1)S(1)}, u32[]{:S(2)}, u32[]{:S(2)}) collective-permute-start(bf16[288,768]{1,0:T(8,128)(2,1)S(1)} %reduce_sum.75), channel_id=1, source_target_pairs={{0,16},{16,0},{1,17},{17,1},{2,18},{18,2},{3,19},{19,3},{4,20},{20... | collective-permute-start | bytes 1327112 | tf_op jit(solution)/shard_map/ppermute | solution.py:622
  116.8 28.1 %all-to-all-start.2 = ((bf16[16,64,768]{2,1,0:T(8,128)(2,1)}), bf16[16,64,768]{2,1,0:T(8,128)(2,1)}, u32[]{:S(2)}, u32[]{:S(2)}) async-start(bf16[16,64,768]{2,1,0:T(8,128)(2,1)} %bitcast.72), calls=%async_computation.2 | async-start | bytes 3145728 | tf_op jit(solution)/shard_map/all_to_all | solution.py:611
  128.7 48.2 %collective-permute-start.3 = (s32[576]{0:T(1024)S(1)}, s32[576]{0:T(1024)S(1)}, u32[]{:S(2)}, u32[]{:S(2)}) collective-permute-start(s32[576]{0:T(1024)S(1)} %get-tuple-element.395), channel_id=1, source_target_pairs={{0,16},{16,0},{1,17},{17,1},{2,18},{18,2},{3,19},{19,3},{4,20},{20... | collective-permute-start | bytes 6920 | tf_op jit(solution)/shard_map/ppermute | solution.py:658
  150.9 36.9 %collective-permute-start.2 = (bf16[1024,768]{1,0:T(8,128)(2,1)S(1)}, bf16[1024,768]{1,0:T(8,128)(2,1)S(1)}, u32[]{:S(2)}, u32[]{:S(2)}) collective-permute-start(bf16[1024,768]{1,0:T(8,128)(2,1)S(1)} %get-tuple-element.450), channel_id=1, source_target_pairs={{0,1},{1,0},{2,3},{3,2},{4,5},{5,4},{6,7},{7,6},{8,9},{9,8},{10,11... | collective-permute-start | bytes 4718600 | tf_op jit(solution)/shard_map/ppermute | solution.py:649
  284.7 32.1 %collective-permute-start.5 = (bf16[864,768]{1,0:T(8,128)(2,1)S(1)}, bf16[864,768]{1,0:T(8,128)(2,1)S(1)}, u32[]{:S(2)}, u32[]{:S(2)}) collective-permute-start(bf16[864,768]{1,0:T(8,128)(2,1)S(1)} %get-tuple-element.237), channel_id=1, source_target_pairs={{0,4},{4,0},{1,5},{5,1},{2,6},{6,2},{3,7},{7,3},{8,12},{12,8},{9,1... | collective-permute-start | bytes 3981320 | tf_op jit(solution)/shard_map/ppermute | solution.py:525
  287.2 31.8 %collective-permute-start.6 = (bf16[864,768]{1,0:T(8,128)(2,1)S(1)}, bf16[864,768]{1,0:T(8,128)(2,1)}, u32[]{:S(2)}, u32[]{:S(2)}) collective-permute-start(bf16[864,768]{1,0:T(8,128)(2,1)S(1)} %get-tuple-element.238), channel_id=1, source_target_pairs={{0,1},{1,0},{2,3},{3,2},{4,5},{5,4},{6,7},{7,6},{8,9},{9,8},{10,11... | collective-permute-start | bytes 3981320 | tf_op jit(solution)/shard_map/ppermute | solution.py:525
  321.2 16.7 %collective-permute-start.7 = (bf16[432,768]{1,0:T(8,128)(2,1)S(1)}, bf16[432,768]{1,0:T(8,128)(2,1)S(1)}, u32[]{:S(2)}, u32[]{:S(2)}) collective-permute-start(bf16[432,768]{1,0:T(8,128)(2,1)S(1)} %get-tuple-element.251), channel_id=1, source_target_pairs={{0,1},{1,0},{2,3},{3,2},{4,5},{5,4},{6,7},{7,6},{8,9},{9,8},{10,11... | collective-permute-start | bytes 1990664 | tf_op jit(solution)/shard_map/ppermute | solution.py:525
  321.9 16.3 %collective-permute-start.8 = (bf16[432,768]{1,0:T(8,128)(2,1)S(1)}, bf16[432,768]{1,0:T(8,128)(2,1)S(1)}, u32[]{:S(2)}, u32[]{:S(2)}) collective-permute-start(bf16[432,768]{1,0:T(8,128)(2,1)S(1)} %get-tuple-element.252), channel_id=1, source_target_pairs={{0,4},{4,0},{1,5},{5,1},{2,6},{6,2},{3,7},{7,3},{8,12},{12,8},{9,1... | collective-permute-start | bytes 1990664 | tf_op jit(solution)/shard_map/ppermute | solution.py:525
  344.9 16.5 %collective-permute-start.9 = (bf16[432,768]{1,0:T(8,128)(2,1)S(1)}, bf16[432,768]{1,0:T(8,128)(2,1)S(1)}, u32[]{:S(2)}, u32[]{:S(2)}) collective-permute-start(bf16[432,768]{1,0:T(8,128)(2,1)S(1)} %get-tuple-element.268), channel_id=1, source_target_pairs={{0,8},{8,0},{1,9},{9,1},{2,10},{10,2},{3,11},{11,3},{4,12},{12,4},... | collective-permute-start | bytes 1990664 | tf_op jit(solution)/shard_map/ppermute | solution.py:525
  345.0 50.4 %collective-permute-start.12 = (bf16[1024,768]{1,0:T(8,128)(2,1)S(1)}, bf16[1024,768]{1,0:T(8,128)(2,1)S(1)}, u32[]{:S(2)}, u32[]{:S(2)}) collective-permute-start(bf16[1024,768]{1,0:T(8,128)(2,1)S(1)} %add_convert_fusion), channel_id=1, source_target_pairs={{0,1},{1,0},{2,3},{3,2},{4,5},{5,4},{6,7},{7,6},{8,9},{9,8},{10,11... | collective-permute-start | bytes 4718600 | tf_op jit(solution)/shard_map/ppermute | solution.py:525
  361.7 16.9 %collective-permute-start.10 = (bf16[216,768]{1,0:T(8,128)(2,1)S(1)}, bf16[216,768]{1,0:T(8,128)(2,1)S(1)}, u32[]{:S(2)}, u32[]{:S(2)}) collective-permute-start(bf16[216,768]{1,0:T(8,128)(2,1)S(1)} %get-tuple-element.279), channel_id=1, source_target_pairs={{0,16},{16,0},{1,17},{17,1},{2,18},{18,2},{3,19},{19,3},{4,20},{20... | collective-permute-start | bytes 995336 | tf_op jit(solution)/shard_map/ppermute | solution.py:525
  378.7 16.5 %collective-permute-start.11 = (bf16[216,768]{1,0:T(8,128)(2,1)S(1)}, bf16[216,768]{1,0:T(8,128)(2,1)S(1)}, u32[]{:S(2)}, u32[]{:S(2)}) collective-permute-start(bf16[216,768]{1,0:T(8,128)(2,1)S(1)} %add.253), channel_id=1, source_target_pairs={{0,16},{16,0},{1,17},{17,1},{2,18},{18,2},{3,19},{19,3},{4,20},{20... | collective-permute-start | bytes 995336 | tf_op jit(solution)/shard_map/ppermute | solution.py:525
  395.4 16.5 %collective-permute-start.13 = (bf16[432,768]{1,0:T(8,128)(2,1)S(1)}, bf16[432,768]{1,0:T(8,128)(2,1)S(1)}, u32[]{:S(2)}, u32[]{:S(2)}) collective-permute-start(bf16[432,768]{1,0:T(8,128)(2,1)S(1)} %pad_maximum_fusion.4), channel_id=1, source_target_pairs={{0,8},{8,0},{1,9},{9,1},{2,10},{10,2},{3,11},{11,3},{4,12},{12,4},... | collective-permute-start | bytes 1990664 | tf_op jit(solution)/shard_map/ppermute | solution.py:525
  429.3 99.9 %all-to-all-start.3 = ((bf16[16,256,768]{2,1,0:T(8,128)(2,1)}), bf16[16,256,768]{2,1,0:T(8,128)(2,1)}, u32[]{:S(2)}, u32[]{:S(2)}) async-start(bf16[16,256,768]{2,1,0:T(8,128)(2,1)} %bitcast.70), calls=%async_computation.3 | async-start | bytes 12582912 | tf_op jit(solution)/shard_map/all_to_all | solution.py:611
  467.6 60.6 %collective-permute-start.18 = (bf16[320,768]{1,0:T(8,128)(2,1)S(1)}, bf16[320,768]{1,0:T(8,128)(2,1)}, u32[]{:S(2)}, u32[]{:S(2)}) collective-permute-start(bf16[320,768]{1,0:T(8,128)(2,1)S(1)} %get-tuple-element.428), channel_id=1, source_target_pairs={{0,1},{1,0},{2,3},{3,2},{4,5},{5,4},{6,7},{7,6},{8,9},{9,8},{10,11... | collective-permute-start | bytes 1474568 | tf_op jit(solution)/shard_map/ppermute | solution.py:525
  470.2 59.0 %collective-permute-start.17 = (bf16[320,768]{1,0:T(8,128)(2,1)S(1)}, bf16[320,768]{1,0:T(8,128)(2,1)}, u32[]{:S(2)}, u32[]{:S(2)}) collective-permute-start(bf16[320,768]{1,0:T(8,128)(2,1)S(1)} %get-tuple-element.430), channel_id=1, source_target_pairs={{0,4},{4,0},{1,5},{5,1},{2,6},{6,2},{3,7},{7,3},{8,12},{12,8},{9,1... | collective-permute-start | bytes 1474568 | tf_op jit(solution)/shard_map/ppermute | solution.py:525
  551.2 29.9 %collective-permute-start.23 = (bf16[864,768]{1,0:T(8,128)(2,1)S(1)}, bf16[864,768]{1,0:T(8,128)(2,1)S(1)}, u32[]{:S(2)}, u32[]{:S(2)}) collective-permute-start(bf16[864,768]{1,0:T(8,128)(2,1)S(1)} %pad_maximum_fusion.2), channel_id=1, source_target_pairs={{0,4},{4,0},{1,5},{5,1},{2,6},{6,2},{3,7},{7,3},{8,12},{12,8},{9,1... | collective-permute-start | bytes 3981320 | tf_op jit(solution)/shard_map/ppermute | solution.py:525
  551.5 29.7 %collective-permute-start.24 = (bf16[864,768]{1,0:T(8,128)(2,1)S(1)}, bf16[864,768]{1,0:T(8,128)(2,1)S(1)}, u32[]{:S(2)}, u32[]{:S(2)}) collective-permute-start(bf16[864,768]{1,0:T(8,128)(2,1)S(1)} %copy-done.13), channel_id=1, source_target_pairs={{0,1},{1,0},{2,3},{3,2},{4,5},{5,4},{6,7},{7,6},{8,9},{9,8},{10,11... | collective-permute-start | bytes 3981320 | tf_op jit(solution)/shard_map/ppermute | solution.py:525
  584.5 17.2 %collective-permute-start.27 = (bf16[3456,768]{1,0:T(8,128)(2,1)S(1)}, bf16[3456,768]{1,0:T(8,128)(2,1)S(1)}, u32[]{:S(2)}, u32[]{:S(2)}) collective-permute-start(bf16[3456,768]{1,0:T(8,128)(2,1)S(1)} %pad_maximum_fusion.own_ref), channel_id=1, source_target_pairs={{0,2},{2,0},{1,3},{3,1},{4,6},{6,4},{5,7},{7,5},{8,10},{10,8},{9,1... | collective-permute-start | bytes 15925256 | tf_op jit(solution)/shard_map/ppermute | solution.py:525
  607.2 21.2 %collective-permute-start.30 = (bf16[288,768]{1,0:T(8,128)(2,1)S(1)}, bf16[288,768]{1,0:T(8,128)(2,1)S(1)}, u32[]{:S(2)}, u32[]{:S(2)}) collective-permute-start(bf16[288,768]{1,0:T(8,128)(2,1)S(1)} %get-tuple-element.433), channel_id=1, source_target_pairs={{0,16},{16,0},{1,17},{17,1},{2,18},{18,2},{3,19},{19,3},{4,20},{20... | collective-permute-start | bytes 1327112 | tf_op jit(solution)/shard_map/ppermute | solution.py:525
  630.2 18.7 %collective-permute-start.33 = (bf16[288,768]{1,0:T(8,128)(2,1)S(1)}, bf16[288,768]{1,0:T(8,128)(2,1)S(1)}, u32[]{:S(2)}, u32[]{:S(2)}) collective-permute-start(bf16[288,768]{1,0:T(8,128)(2,1)S(1)} %get-tuple-element.432), channel_id=1, source_target_pairs={{0,16},{16,0},{1,17},{17,1},{2,18},{18,2},{3,19},{19,3},{4,20},{20... | collective-permute-start | bytes 1327112 | tf_op jit(solution)/shard_map/ppermute | solution.py:525
  (89 other events, 949.1 us)

commit v11 on v10

--- a/solution.py
+++ b/solution.py
@@ -768,43 +768,44 @@
     returned, keeps, came, early = lax.optimization_barrier((returned, keeps, came, early))
     late = end(keeps, came, stages[0])
     last = len(stages) - 1
+    spread = 4
+    early_keeps, early_sends = begin(early, stages[done])
+    early_came = []
     early_parts = []
-    early_step = begin(early, stages[done])
     for at, stage in enumerate(stages[1:], start=1):
         keeps, sends = begin(late, stage)
-        if at == 1:
-            keeps, sends, early_step = lax.optimization_barrier((keeps, sends, early_step))
-            early_came = travel(early_step[1], stages[done])
-        if at == 4:
-            keeps, sends, early_came = lax.optimization_barrier((keeps, sends, early_came))
-            early = end(early_step[0], early_came, stages[done])
-            early = jnp.concatenate(run_stages(early, stages[done + 1 :]), axis=0)
-            early_step = (early, swap(early, core))
         if at == last - 1:
-            keeps, sends, early_step, for_other = lax.optimization_barrier(
-                (keeps, sends, early_step, for_other)
-            )
+            keeps, sends, for_other = lax.optimization_barrier((keeps, sends, for_other))
             from_other = [swap(part, top_axis) for part in jnp.split(for_other, 2, axis=0)]
         if at == last:
             keeps, sends, from_other[0] = lax.optimization_barrier((keeps, sends, from_other[0]))
         came = travel(sends, stage)
+        if 2 <= at < 2 + spread:
+            rows = early_sends[0].shape[0] // spread
+            some = [p[(at - 2) * rows : (at - 1) * rows] for p in early_sends]
+            some, came = lax.optimization_barrier((travel(some, stages[done]), came))
+            early_came.append(some)
         if at == 2:
             table_own = mm(owned[0].astype(BF16), returned)
             came, table_own = lax.optimization_barrier((came, table_own))
         if at == 3:
             for_other = mm(owned[1].astype(BF16), returned).astype(BF16)
             came, for_other = lax.optimization_barrier((came, for_other))
-        if at >= last - 1:
-            part = at - last + 1
-            early_parts.append(
-                unpack(my_core, *early_step, part * wide, wide, part == 1)
+        if at == last - 1:
+            early_came = [jnp.concatenate(parts, axis=0) for parts in zip(*early_came)]
+            early = end(early_keeps, early_came, stages[done])
+            early = jnp.concatenate(run_stages(early, stages[done + 1 :]), axis=0)
+            came, early = lax.optimization_barrier((came, early))
+            early_step = (early, swap(early, core))
+        if at == last:
+            early_parts.append(unpack(my_core, *early_step, 0, wide, False))
+            came, early_parts, from_other[1] = lax.optimization_barrier(
+                (came, early_parts, from_other[1])
             )
-            came, early_parts = lax.optimization_barrier((came, early_parts))
-        if at == last:
-            came, from_other[1] = lax.optimization_barrier((came, from_other[1]))
         late = end(keeps, came, stage)
     late = jnp.concatenate(late, axis=0)
     late_other = swap(late, core)
+    early_parts.append(unpack(my_core, *early_step, wide, wide, True))
     early_parts.append(unpack(my_core, *early_step, 2 * wide, width, False))
     late_other, early_parts, from_other = lax.optimization_barrier(
         (late_other, early_parts, from_other)

time: 673 us -> 669 us (level)
  starting transfers between devices: 53.2 us -> 66 us
  waiting for transfers between devices: 242 us -> 231 us
    ppermute x31 -> x37, starting transfers between devices: 24.7 us -> 37.5 us  [swap(): return lax.ppermute(value, axis, SWAP)]
    ppermute x31 -> x37, waiting for transfers between devices: 144 us -> 133 us  [swap(): return lax.ppermute(value, axis, SWAP)]
  transfers between devices with their start and end apart: 39 -> 45, of which waited for: 25 -> 23; matrix products, arithmetic and copies ran while one was open for 14% -> 15% of each run, Pallas kernels for 22% -> 22%
where the time goes in v11:
time: 669 us; the launch traced here: 661 us
  waiting for transfers between devices  231 us (35%)
  Pallas kernels  224 us (33%)
  matrix products  82.2 us (12%)
  starting transfers between devices  66 us (10%)
  other arithmetic  35.9 us (5%)
  local copies, waits for them, and re-layouts  18.4 us (3%)
    ppermute x37, waiting for transfers between devices, swap(): return lax.ppermute(value, axis, SWAP)  133 us
    pallas_call x5, Pallas kernels, attend_back(): pl.pallas_call(functools.partial(attend_back_kernel, add, len(into)), gri...  86.9 us
    dot_general x25, matrix products, mm(): return lax.dot_general(left, right, dims, preferred_element_type=F32)  82.2 us
    ppermute x1, waiting for transfers between devices, local(): know_other = lax.ppermute(know_sum, top_axis, SWAP)  73.8 us
    pallas_call x2, Pallas kernels, attend(): pl.pallas_call(functools.partial(attend_kernel, merge), grid_spec=pltpu.P...  43.5 us
    ppermute x37, starting transfers between devices, swap(): return lax.ppermute(value, axis, SWAP)  37.5 us
    pallas_call x1, Pallas kernels, middle(): pl.pallas_call(middle_kernel, grid=(tokens // block,), in_specs=[rows(wid...  37.2 us
    pallas_call x2, Pallas kernels, weight_sums(): pl.pallas_call(functools.partial(weight_sums_kernel, counts), grid_spec=p...  27.6 us
  transfers between devices with their start and end apart: 45, of which 23 were waited for; matrix products, arithmetic and copies ran while one was open for 15% of the time, Pallas kernels for 22%

profile of v11, /device:TPU:0, one launch (start us, length us, event | category | flops | bytes accessed | tf_op | source)
XLA Modules:
  0.0 660.9 jit_solution(3325349209035845188)
XLA Ops:
  18.0 8.7 %all-to-all-done = s32[16,1,256]{2,1,0:T(1,128)S(1)} async-done(((s32[16,1,256]{2,1,0:T(1,128)}), s32[16,1,256]{2,1,0:T(1,128)S(1)}, u32[]{:S(2)}, u32[]{:S(2)}) %all-to-all-start) | async-done | bytes 16416 | tf_op jit(solution)/shard_map/all_to_all | solution.py:611
  26.8 8.2 %fusion.25 = bf16[3072,768]{1,0:T(8,128)(2,1)} fusion(s32[864]{0:T(1024)S(1)} %iota_add_fusion.2, s32[3072]{0:T(1024)S(1)} %eq.199, bf16[288,768]{1,0:T(8,128)(2,1)} %collective-permute-done, bf16[288,768]{1,0:T(8,128)(2,1)S(1)} %reduce_sum.75, bf16[288,768]{1,0:T(8,128)(2,1)S(1)} %copy-done.65), kind=kOutput, calls=%fused_computation.27 | convolution fusion | flops 4085858304 | bytes 6061440 | tf_op jit(solution)/shard_map/dot_general | solution.py:24
  40.8 73.8 %collective-permute-done.1 = bf16[288,768]{1,0:T(8,128)(2,1)S(1)} collective-permute-done((bf16[288,768]{1,0:T(8,128)(2,1)S(1)}, bf16[288,768]{1,0:T(8,128)(2,1)S(1)}, u32[]{:S(2)}, u32[]{:S(2)}) %collective-permute-start.1) | collective-permute-done | bytes 442400 | tf_op jit(solution)/shard_map/ppermute | solution.py:622
  130.8 9.5 %fusion.3 = f32[1024,768]{1,0:T(8,128)} fusion(bf16[3072,768]{1,0:T(8,128)(2,1)} %bitcast.9, s32[3072]{0:T(1024)S(1)} %eq.189, s32[1024]{0:T(1024)S(1)} %reduce.3, s32[1024]{0:T(1024)S(1)} %reduce.2), kind=kOutput, calls=%fused_computation.4 | convolution fusion | flops 4841275392 | bytes 7884800 | tf_op jit(solution)/shard_map/dot_general | solution.py:24
  155.8 21.1 %attend.1 = (f32[768,1024]{1,0:T(8,128)}, f32[6,2,1024]{2,1,0:T(2,128)S(1)}) custom-call(s32[2]{0:T(128)S(1)} %pad_add_fusion.1.where_ref, bf16[1024,768]{1,0:T(8,128)(2,1)S(1)} %add_convert_fusion.3.q_ref, bf16[1024,768]{1,0:T(8,128)(2,1)S(1)} %convolution_convert_fusion.k_ref, bf16[1024,768]{1,0:T(8,128)(2,1)S(1)} %add_convert_fusion.1.v_ref), custom_call_target="tpu_custom_call" | custom-call | flops 12884901888 | bytes 15728640 | tf_op jit(solution)/shard_map/attend/pallas_call | solution.py:167
  176.9 10.8 %collective-permute-done.2 = bf16[1024,768]{1,0:T(8,128)(2,1)S(1)} collective-permute-done((bf16[1024,768]{1,0:T(8,128)(2,1)S(1)}, bf16[1024,768]{1,0:T(8,128)(2,1)S(1)}, u32[]{:S(2)}, u32[]{:S(2)}) %collective-permute-start.2) | collective-permute-done | bytes 1572896 | tf_op jit(solution)/shard_map/ppermute | solution.py:649
  190.6 22.4 %attend_more.1 = (f32[1024,768]{1,0:T(8,128)}, f32[6,2,1024]{2,1,0:T(2,128)S(1)}) custom-call(s32[2]{0:T(128)S(1)} %pad_add_fusion.where_ref, bf16[1024,768]{1,0:T(8,128)(2,1)S(1)} %add_convert_fusion.3.q_ref, bf16[1024,768]{1,0:T(8,128)(2,1)S(1)} %convolution_convert_fusion.1.k_ref, bf16[1024,768]{1,0:T(8,128)(2,1)S(1)} %add_convert_fusion.2.v_ref, ...), custom_call_target="tpu_custom_call" | custom-call | flops 12884901888 | bytes 15728640 | tf_op jit(solution)/shard_map/attend_more/pallas_call | solution.py:167
  213.6 37.2 %middle.1 = (bf16[1024,768]{1,0:T(8,128)(2,1)}, bf16[1024,768]{1,0:T(8,128)(2,1)}, bf16[1024,768]{1,0:T(8,128)(2,1)}, bf16[1024,3072]{1,0:T(8,128)(2,1)}, bf16[1...) custom-call(f32[1024,768]{1,0:T(8,128)} %get-tuple-element.212.ctx_r, ...), custom_call_target="tpu_custom_call" | custom-call | flops 43486543872 | bytes 34603008 | tf_op jit(solution)/shard_map/middle/pallas_call | solution.py:375
  250.8 13.8 %weight_sums.2 = bf16[3456,768]{1,0:T(8,128)(2,1)} custom-call(s32[1]{0:T(128)} %bitcast.18.half_ref, bf16[1024,3072]{1,0:T(8,128)(2,1)} %get-tuple-element.220.act_ref, bf16[1024,768]{1,0:T(8,128)(2,1)} %get-tuple-element.221.gffn_ref, bf16[1024,3072]{1,0:T(8,128)(2,1)} %get-tuple-element.222.gpre_ref, bf16[1024,768]{1,0:T(8,128)(2,1)} %get-tuple-element.223.norm_ref, ...), custom_call_target="tpu_custom_call" | custom-call | flops 5435817984 | bytes 12386304 | tf_op jit(solution)/shard_map/weight_sums/pallas_call | solution.py:438
  264.7 13.8 %weight_sums.3 = bf16[3456,768]{1,0:T(8,128)(2,1)} custom-call(s32[1]{0:T(128)} %bitcast.17.half_ref.core_ref, bf16[1024,3072]{1,0:T(8,128)(2,1)} %get-tuple-element.220.act_ref, bf16[1024,768]{1,0:T(8,128)(2,1)} %get-tuple-element.221.gffn_ref, bf16[1024,3072]{1,0:T(8,128)(2,1)} %get-tuple-element.222.gpre_ref, ...), custom_call_target="tpu_custom_call" | custom-call | flops 5435817984 | bytes 12386304 | tf_op jit(solution)/shard_map/weight_sums/pallas_call | solution.py:438
  287.8 26.5 %attend_back0.1 = (f32[1024,768]{1,0:T(8,128)}, bf16[1024,768]{1,0:T(8,128)(2,1)}, bf16[1024,768]{1,0:T(8,128)(2,1)}) custom-call(s32[2]{0:T(128)} %copy-done.2, bf16[1024,768]{1,0:T(8,128)(2,1)} %copy-done.5, bf16[1024,768]{1,0:T(8,128)(2,1)} %get-tuple-element.289.g_ref, f32[1024,768]{1,0:T(8,128)} %get-tuple-element.212.ctx_ref.o_ref, ...), custom_call_target="tpu_custom_call" | custom-call | flops 21474836480 | bytes 12582912 | tf_op jit(solution)/shard_map/attend_back0/pallas_call | solution.py:247
  322.2 14.9 %attend_back4.1 = (f32[1024,768]{1,0:T(8,128)}, bf16[1024,768]{1,0:T(8,128)(2,1)}, bf16[1024,768]{1,0:T(8,128)(2,1)}) custom-call(s32[2]{0:T(128)} %copy-done.2, bf16[1024,768]{1,0:T(8,128)(2,1)} %copy-done.5, bf16[1024,768]{1,0:T(8,128)(2,1)} %get-tuple-element.289.g_ref, ...), custom_call_target="tpu_custom_call", output_to_operand_aliasing={{0}: (7, {}), {1}: (8, {}), {2}: (9, {})} | custom-call | flops 10737418240 | bytes 6291456 | tf_op jit(solution)/shard_map/attend_back4/pallas_call | solution.py:247
  346.2 15.2 %attend_back_more0.1 = (bf16[1024,768]{1,0:T(8,128)(2,1)}, bf16[1024,768]{1,0:T(8,128)(2,1)}, bf16[1024,768]{1,0:T(8,128)(2,1)}) custom-call(s32[2]{0:T(128)} %copy-done.1, bf16[1024,768]{1,0:T(8,128)(2,1)} %copy-done.5, bf16[1024,768]{1,0:T(8,128)(2,1)} %get-tuple-element.289.g_ref, f32[1024,768]{1,0:T(8,128)} %get-tuple-element.212.ctx_ref.o_ref, ...), custom_call_target="tpu_custom_call" | custom-call | flops 10737418240 | bytes 6291456 | tf_op jit(solution)/shard_map/attend_back_more0/pallas_call | solution.py:247
  363.7 14.8 %attend_back_more2.1 = (bf16[1024,768]{1,0:T(8,128)(2,1)}, bf16[1024,768]{1,0:T(8,128)(2,1)}, bf16[1024,768]{1,0:T(8,128)(2,1)}) custom-call(s32[2]{0:T(128)} %copy-done.1, bf16[1024,768]{1,0:T(8,128)(2,1)} %copy-done.5, bf16[1024,768]{1,0:T(8,128)(2,1)} %get-tuple-element.289.g_ref, ...), custom_call_target="tpu_custom_call", output_to_operand_aliasing={{0}: (8, {}), {1}: (9, {}), {2}: (10, {})} | custom-call | flops 10737418240 | bytes 6291456 | tf_op jit(solution)/shard_map/attend_back_more2/pallas_call | solution.py:247
  379.7 15.4 %attend_back_more4.1 = (bf16[1024,768]{1,0:T(8,128)(2,1)}, bf16[1024,768]{1,0:T(8,128)(2,1)}, bf16[1024,768]{1,0:T(8,128)(2,1)}) custom-call(s32[2]{0:T(128)} %copy-done.1, bf16[1024,768]{1,0:T(8,128)(2,1)} %copy-done.5, bf16[1024,768]{1,0:T(8,128)(2,1)} %get-tuple-element.289.g_ref, ...), custom_call_target="tpu_custom_call", output_to_operand_aliasing={{0}: (8, {}), {1}: (9, {}), {2}: (10, {})} | custom-call | flops 10737418240 | bytes 6291456 | tf_op jit(solution)/shard_map/attend_back_more4/pallas_call | solution.py:247
  405.1 6.7 %collective-permute-done.13 = bf16[432,768]{1,0:T(8,128)(2,1)S(1)} collective-permute-done((bf16[432,768]{1,0:T(8,128)(2,1)S(1)}, bf16[432,768]{1,0:T(8,128)(2,1)S(1)}, u32[]{:S(2)}, u32[]{:S(2)}) %collective-permute-start.13) | collective-permute-done | bytes 663584 | tf_op jit(solution)/shard_map/ppermute | solution.py:525
  413.8 10.9 %fusion.17 = bf16[4096,768]{1,0:T(8,128)(2,1)} fusion(bf16[1024,768]{1,0:T(8,128)(2,1)S(1)} %get-tuple-element.311, s32[1024]{0:T(1024)S(1)} %copy-done.44, s32[1024]{0:T(1024)S(1)} %copy-done.42), kind=kOutput, calls=%fused_computation.20 | convolution fusion | flops 6458179584 | bytes 7872512 | tf_op jit(solution)/shard_map/dot_general | solution.py:24
  473.0 55.2 %collective-permute-done.18 = bf16[320,768]{1,0:T(8,128)(2,1)} collective-permute-done((bf16[320,768]{1,0:T(8,128)(2,1)S(1)}, bf16[320,768]{1,0:T(8,128)(2,1)}, u32[]{:S(2)}, u32[]{:S(2)}) %collective-permute-start.18) | collective-permute-done | bytes 491552 | tf_op jit(solution)/shard_map/ppermute | solution.py:525
  543.4 7.9 %fusion.7 = f32[576,768]{1,0:T(8,128)} fusion(bf16[4096,768]{1,0:T(8,128)(2,1)} %bitcast.20, s32[4096]{0:T(1024)S(1)} %copy-done.40, s32[576]{0:T(1024)S(1)} %copy-done.57), kind=kOutput, calls=%fused_computation.9 | convolution fusion | flops 3626237952 | bytes 8079616 | tf_op jit(solution)/shard_map/dot_general | solution.py:24
  566.4 6.9 %collective-permute-done.27 = bf16[216,768]{1,0:T(8,128)(2,1)S(1)} collective-permute-done((bf16[216,768]{1,0:T(8,128)(2,1)S(1)}, bf16[216,768]{1,0:T(8,128)(2,1)S(1)}, u32[]{:S(2)}, u32[]{:S(2)}) %collective-permute-start.27) | collective-permute-done | bytes 331808 | tf_op jit(solution)/shard_map/ppermute | solution.py:525
  591.9 19.9 %collective-permute-done.35 = bf16[288,768]{1,0:T(8,128)(2,1)S(1)} collective-permute-done((bf16[288,768]{1,0:T(8,128)(2,1)S(1)}, bf16[288,768]{1,0:T(8,128)(2,1)S(1)}, u32[]{:S(2)}, u32[]{:S(2)}) %collective-permute-start.35) | collective-permute-done | bytes 442400 | tf_op jit(solution)/shard_map/ppermute | solution.py:525
  614.6 7.9 %unpack0.1 = f32[3072,768]{1,0:T(8,128)} custom-call(s32[1]{0:T(128)} %bitcast.17.half_ref.core_ref, bf16[3456,768]{1,0:T(8,128)(2,1)} %copy-done.9, bf16[3456,768]{1,0:T(8,128)(2,1)} %collective-permute-done.38.other_ref), custom_call_target="tpu_custom_call" | custom-call | flops 2359296 | bytes 14155776 | tf_op jit(solution)/shard_map/unpack0/pallas_call | solution.py:469
  622.5 13.7 %collective-permute-done.39 = bf16[288,768]{1,0:T(8,128)(2,1)S(1)} collective-permute-done((bf16[288,768]{1,0:T(8,128)(2,1)S(1)}, bf16[288,768]{1,0:T(8,128)(2,1)S(1)}, u32[]{:S(2)}, u32[]{:S(2)}) %collective-permute-start.39) | collective-permute-done | bytes 442400 | tf_op jit(solution)/shard_map/ppermute | solution.py:525
  641.1 8.5 %unpack8.1 = f32[768,3072]{1,0:T(8,128)} custom-call(s32[1]{0:T(128)} %bitcast.17.half_ref.core_ref, bf16[3456,768]{1,0:T(8,128)(2,1)} %copy-done.9, bf16[3456,768]{1,0:T(8,128)(2,1)} %collective-permute-done.38.other_ref), custom_call_target="tpu_custom_call" | custom-call | flops 2359296 | bytes 14155776 | tf_op jit(solution)/shard_map/unpack8/pallas_call | solution.py:469
  (362 shorter events, 213.5 us)
Async XLA Ops:
  0.7 26.0 %collective-permute-start = (bf16[288,768]{1,0:T(8,128)(2,1)}, bf16[288,768]{1,0:T(8,128)(2,1)}, u32[]{:S(2)}, u32[]{:S(2)}) collective-permute-start(bf16[288,768]{1,0:T(8,128)(2,1)} %param.31), channel_id=1, source_target_pairs={{0,16},{16,0},{1,17},{17,1},{2,18},{18,2},{3,19},{19,3},{4,20},{20... | collective-permute-start | bytes 1327112 | tf_op jit(solution)/shard_map/ppermute | solution.py:614
  35.0 81.8 %all-to-all-start.1 = ((bf16[16,192,768]{2,1,0:T(8,128)(2,1)}), bf16[16,192,768]{2,1,0:T(8,128)(2,1)}, u32[]{:S(2)}, u32[]{:S(2)}) async-start(bf16[16,192,768]{2,1,0:T(8,128)(2,1)} %bitcast.71), calls=%async_computation.1 | async-start | bytes 9437184 | tf_op jit(solution)/shard_map/all_to_all | solution.py:611
  39.6 75.0 %collective-permute-start.1 = (bf16[288,768]{1,0:T(8,128)(2,1)S(1)}, bf16[288,768]{1,0:T(8,128)(2,1)S(1)}, u32[]{:S(2)}, u32[]{:S(2)}) collective-permute-start(bf16[288,768]{1,0:T(8,128)(2,1)S(1)} %reduce_sum.75), channel_id=1, source_target_pairs={{0,16},{16,0},{1,17},{17,1},{2,18},{18,2},{3,19},{19,3},{4,20},{20... | collective-permute-start | bytes 1327112 | tf_op jit(solution)/shard_map/ppermute | solution.py:622
  116.8 28.1 %all-to-all-start.2 = ((bf16[16,64,768]{2,1,0:T(8,128)(2,1)}), bf16[16,64,768]{2,1,0:T(8,128)(2,1)}, u32[]{:S(2)}, u32[]{:S(2)}) async-start(bf16[16,64,768]{2,1,0:T(8,128)(2,1)} %bitcast.72), calls=%async_computation.2 | async-start | bytes 3145728 | tf_op jit(solution)/shard_map/all_to_all | solution.py:611
  128.7 48.2 %collective-permute-start.3 = (s32[576]{0:T(1024)S(1)}, s32[576]{0:T(1024)S(1)}, u32[]{:S(2)}, u32[]{:S(2)}) collective-permute-start(s32[576]{0:T(1024)S(1)} %get-tuple-element.385), channel_id=1, source_target_pairs={{0,16},{16,0},{1,17},{17,1},{2,18},{18,2},{3,19},{19,3},{4,20},{20... | collective-permute-start | bytes 6920 | tf_op jit(solution)/shard_map/ppermute | solution.py:658
  150.9 36.9 %collective-permute-start.2 = (bf16[1024,768]{1,0:T(8,128)(2,1)S(1)}, bf16[1024,768]{1,0:T(8,128)(2,1)S(1)}, u32[]{:S(2)}, u32[]{:S(2)}) collective-permute-start(bf16[1024,768]{1,0:T(8,128)(2,1)S(1)} %get-tuple-element.444), channel_id=1, source_target_pairs={{0,1},{1,0},{2,3},{3,2},{4,5},{5,4},{6,7},{7,6},{8,9},{9,8},{10,11... | collective-permute-start | bytes 4718600 | tf_op jit(solution)/shard_map/ppermute | solution.py:649
  284.6 32.1 %collective-permute-start.5 = (bf16[864,768]{1,0:T(8,128)(2,1)S(1)}, bf16[864,768]{1,0:T(8,128)(2,1)S(1)}, u32[]{:S(2)}, u32[]{:S(2)}) collective-permute-start(bf16[864,768]{1,0:T(8,128)(2,1)S(1)} %get-tuple-element.232), channel_id=1, source_target_pairs={{0,4},{4,0},{1,5},{5,1},{2,6},{6,2},{3,7},{7,3},{8,12},{12,8},{9,1... | collective-permute-start | bytes 3981320 | tf_op jit(solution)/shard_map/ppermute | solution.py:525
  287.1 31.8 %collective-permute-start.6 = (bf16[864,768]{1,0:T(8,128)(2,1)S(1)}, bf16[864,768]{1,0:T(8,128)(2,1)}, u32[]{:S(2)}, u32[]{:S(2)}) collective-permute-start(bf16[864,768]{1,0:T(8,128)(2,1)S(1)} %get-tuple-element.233), channel_id=1, source_target_pairs={{0,1},{1,0},{2,3},{3,2},{4,5},{5,4},{6,7},{7,6},{8,9},{9,8},{10,11... | collective-permute-start | bytes 3981320 | tf_op jit(solution)/shard_map/ppermute | solution.py:525
  321.1 16.7 %collective-permute-start.7 = (bf16[432,768]{1,0:T(8,128)(2,1)S(1)}, bf16[432,768]{1,0:T(8,128)(2,1)S(1)}, u32[]{:S(2)}, u32[]{:S(2)}) collective-permute-start(bf16[432,768]{1,0:T(8,128)(2,1)S(1)} %get-tuple-element.246), channel_id=1, source_target_pairs={{0,1},{1,0},{2,3},{3,2},{4,5},{5,4},{6,7},{7,6},{8,9},{9,8},{10,11... | collective-permute-start | bytes 1990664 | tf_op jit(solution)/shard_map/ppermute | solution.py:525
  344.8 16.6 %collective-permute-start.9 = (bf16[432,768]{1,0:T(8,128)(2,1)S(1)}, bf16[432,768]{1,0:T(8,128)(2,1)S(1)}, u32[]{:S(2)}, u32[]{:S(2)}) collective-permute-start(bf16[432,768]{1,0:T(8,128)(2,1)S(1)} %get-tuple-element.263), channel_id=1, source_target_pairs={{0,8},{8,0},{1,9},{9,1},{2,10},{10,2},{3,11},{11,3},{4,12},{12,4},... | collective-permute-start | bytes 1990664 | tf_op jit(solution)/shard_map/ppermute | solution.py:525
  344.9 50.4 %collective-permute-start.12 = (bf16[1024,768]{1,0:T(8,128)(2,1)S(1)}, bf16[1024,768]{1,0:T(8,128)(2,1)S(1)}, u32[]{:S(2)}, u32[]{:S(2)}) collective-permute-start(bf16[1024,768]{1,0:T(8,128)(2,1)S(1)} %add_convert_fusion), channel_id=1, source_target_pairs={{0,1},{1,0},{2,3},{3,2},{4,5},{5,4},{6,7},{7,6},{8,9},{9,8},{10,11... | collective-permute-start | bytes 4718600 | tf_op jit(solution)/shard_map/ppermute | solution.py:525
  361.7 16.9 %collective-permute-start.10 = (bf16[216,768]{1,0:T(8,128)(2,1)S(1)}, bf16[216,768]{1,0:T(8,128)(2,1)S(1)}, u32[]{:S(2)}, u32[]{:S(2)}) collective-permute-start(bf16[216,768]{1,0:T(8,128)(2,1)S(1)} %get-tuple-element.274), channel_id=1, source_target_pairs={{0,16},{16,0},{1,17},{17,1},{2,18},{18,2},{3,19},{19,3},{4,20},{20... | collective-permute-start | bytes 995336 | tf_op jit(solution)/shard_map/ppermute | solution.py:525
  378.6 16.5 %collective-permute-start.11 = (bf16[216,768]{1,0:T(8,128)(2,1)S(1)}, bf16[216,768]{1,0:T(8,128)(2,1)S(1)}, u32[]{:S(2)}, u32[]{:S(2)}) collective-permute-start(bf16[216,768]{1,0:T(8,128)(2,1)S(1)} %add.253), channel_id=1, source_target_pairs={{0,16},{16,0},{1,17},{17,1},{2,18},{18,2},{3,19},{19,3},{4,20},{20... | collective-permute-start | bytes 995336 | tf_op jit(solution)/shard_map/ppermute | solution.py:525
  395.3 16.5 %collective-permute-start.13 = (bf16[432,768]{1,0:T(8,128)(2,1)S(1)}, bf16[432,768]{1,0:T(8,128)(2,1)S(1)}, u32[]{:S(2)}, u32[]{:S(2)}) collective-permute-start(bf16[432,768]{1,0:T(8,128)(2,1)S(1)} %pad_maximum_fusion.4), channel_id=1, source_target_pairs={{0,8},{8,0},{1,9},{9,1},{2,10},{10,2},{3,11},{11,3},{4,12},{12,4},... | collective-permute-start | bytes 1990664 | tf_op jit(solution)/shard_map/ppermute | solution.py:525
  429.2 99.9 %all-to-all-start.3 = ((bf16[16,256,768]{2,1,0:T(8,128)(2,1)}), bf16[16,256,768]{2,1,0:T(8,128)(2,1)}, u32[]{:S(2)}, u32[]{:S(2)}) async-start(bf16[16,256,768]{2,1,0:T(8,128)(2,1)} %bitcast.70), calls=%async_computation.3 | async-start | bytes 12582912 | tf_op jit(solution)/shard_map/all_to_all | solution.py:611
  467.5 60.6 %collective-permute-start.18 = (bf16[320,768]{1,0:T(8,128)(2,1)S(1)}, bf16[320,768]{1,0:T(8,128)(2,1)}, u32[]{:S(2)}, u32[]{:S(2)}) collective-permute-start(bf16[320,768]{1,0:T(8,128)(2,1)S(1)} %get-tuple-element.426), channel_id=1, source_target_pairs={{0,1},{1,0},{2,3},{3,2},{4,5},{5,4},{6,7},{7,6},{8,9},{9,8},{10,11... | collective-permute-start | bytes 1474568 | tf_op jit(solution)/shard_map/ppermute | solution.py:525
  470.1 59.0 %collective-permute-start.17 = (bf16[320,768]{1,0:T(8,128)(2,1)S(1)}, bf16[320,768]{1,0:T(8,128)(2,1)}, u32[]{:S(2)}, u32[]{:S(2)}) collective-permute-start(bf16[320,768]{1,0:T(8,128)(2,1)S(1)} %get-tuple-element.428), channel_id=1, source_target_pairs={{0,4},{4,0},{1,5},{5,1},{2,6},{6,2},{3,7},{7,3},{8,12},{12,8},{9,1... | collective-permute-start | bytes 1474568 | tf_op jit(solution)/shard_map/ppermute | solution.py:525
  533.1 18.9 %collective-permute-start.19 = (bf16[216,768]{1,0:T(8,128)(2,1)S(1)}, bf16[216,768]{1,0:T(8,128)(2,1)S(1)}, u32[]{:S(2)}, u32[]{:S(2)}) collective-permute-start(bf16[216,768]{1,0:T(8,128)(2,1)S(1)} %get-tuple-element.406), channel_id=1, source_target_pairs={{0,4},{4,0},{1,5},{5,1},{2,6},{6,2},{3,7},{7,3},{8,12},{12,8},{9,1... | collective-permute-start | bytes 995336 | tf_op jit(solution)/shard_map/ppermute | solution.py:525
  535.3 16.7 %collective-permute-start.20 = (bf16[216,768]{1,0:T(8,128)(2,1)S(1)}, bf16[216,768]{1,0:T(8,128)(2,1)S(1)}, u32[]{:S(2)}, u32[]{:S(2)}) collective-permute-start(bf16[216,768]{1,0:T(8,128)(2,1)S(1)} %get-tuple-element.402), channel_id=1, source_target_pairs={{0,1},{1,0},{2,3},{3,2},{4,5},{5,4},{6,7},{7,6},{8,9},{9,8},{10,11... | collective-permute-start | bytes 995336 | tf_op jit(solution)/shard_map/ppermute | solution.py:525
  588.9 25.7 %collective-permute-start.38 = (bf16[3456,768]{1,0:T(8,128)(2,1)S(1)}, bf16[3456,768]{1,0:T(8,128)(2,1)}, u32[]{:S(2)}, u32[]{:S(2)}) collective-permute-start(bf16[3456,768]{1,0:T(8,128)(2,1)S(1)} %pad_maximum_fusion.own_ref), channel_id=1, source_target_pairs={{0,2},{2,0},{1,3},{3,1},{4,6},{6,4},{5,7},{7,5},{8,10},{10,8},{9,1... | collective-permute-start | bytes 15925256 | tf_op jit(solution)/shard_map/ppermute | solution.py:525
  589.0 22.8 %collective-permute-start.35 = (bf16[288,768]{1,0:T(8,128)(2,1)S(1)}, bf16[288,768]{1,0:T(8,128)(2,1)S(1)}, u32[]{:S(2)}, u32[]{:S(2)}) collective-permute-start(bf16[288,768]{1,0:T(8,128)(2,1)S(1)} %get-tuple-element.431), channel_id=1, source_target_pairs={{0,16},{16,0},{1,17},{17,1},{2,18},{18,2},{3,19},{19,3},{4,20},{20... | collective-permute-start | bytes 1327112 | tf_op jit(solution)/shard_map/ppermute | solution.py:525
  612.5 23.7 %collective-permute-start.36 = (bf16[320,768]{1,0:T(8,128)(2,1)S(1)}, bf16[320,768]{1,0:T(8,128)(2,1)S(1)}, u32[]{:S(2)}, u32[]{:S(2)}) collective-permute-start(bf16[320,768]{1,0:T(8,128)(2,1)S(1)} %pad_maximum_fusion.5), channel_id=1, source_target_pairs={{0,4},{4,0},{1,5},{5,1},{2,6},{6,2},{3,7},{7,3},{8,12},{12,8},{9,1... | collective-permute-start | bytes 1474568 | tf_op jit(solution)/shard_map/ppermute | solution.py:525
  614.0 22.3 %collective-permute-start.37 = (bf16[320,768]{1,0:T(8,128)(2,1)S(1)}, bf16[320,768]{1,0:T(8,128)(2,1)S(1)}, u32[]{:S(2)}, u32[]{:S(2)}) collective-permute-start(bf16[320,768]{1,0:T(8,128)(2,1)S(1)} %pad_maximum_fusion.6), channel_id=1, source_target_pairs={{0,1},{1,0},{2,3},{3,2},{4,5},{5,4},{6,7},{7,6},{8,9},{9,8},{10,11... | collective-permute-start | bytes 1474568 | tf_op jit(solution)/shard_map/ppermute | solution.py:525
  614.6 21.6 %collective-permute-start.39 = (bf16[288,768]{1,0:T(8,128)(2,1)S(1)}, bf16[288,768]{1,0:T(8,128)(2,1)S(1)}, u32[]{:S(2)}, u32[]{:S(2)}) collective-permute-start(bf16[288,768]{1,0:T(8,128)(2,1)S(1)} %get-tuple-element.430), channel_id=1, source_target_pairs={{0,16},{16,0},{1,17},{17,1},{2,18},{18,2},{3,19},{19,3},{4,20},{20... | collective-permute-start | bytes 1327112 | tf_op jit(solution)/shard_map/ppermute | solution.py:525
  (94 other events, 1020.2 us)

commit v12 on v11

--- a/solution.py
+++ b/solution.py
@@ -768,18 +768,22 @@
     returned, keeps, came, early = lax.optimization_barrier((returned, keeps, came, early))
     late = end(keeps, came, stages[0])
     last = len(stages) - 1
-    spread = 4
+    spread = 3
     early_keeps, early_sends = begin(early, stages[done])
     early_came = []
     early_parts = []
+    from_other = []
     for at, stage in enumerate(stages[1:], start=1):
         keeps, sends = begin(late, stage)
-        if at == last - 1:
+        if at >= last - 1:
             keeps, sends, for_other = lax.optimization_barrier((keeps, sends, for_other))
-            from_other = [swap(part, top_axis) for part in jnp.split(for_other, 2, axis=0)]
         if at == last:
-            keeps, sends, from_other[0] = lax.optimization_barrier((keeps, sends, from_other[0]))
+            keeps, sends, early_step = lax.optimization_barrier((keeps, sends, early_step))
         came = travel(sends, stage)
+        if at >= last - 1:
+            quarter = swap(jnp.split(for_other, 4, axis=0)[len(from_other)], top_axis)
+            came, quarter = lax.optimization_barrier((came, quarter))
+            from_other.append(quarter)
         if 2 <= at < 2 + spread:
             rows = early_sends[0].shape[0] // spread
             some = [p[(at - 2) * rows : (at - 1) * rows] for p in early_sends]
@@ -791,7 +795,7 @@
         if at == 3:
             for_other = mm(owned[1].astype(BF16), returned).astype(BF16)
             came, for_other = lax.optimization_barrier((came, for_other))
-        if at == last - 1:
+        if at == last - 2:
             early_came = [jnp.concatenate(parts, axis=0) for parts in zip(*early_came)]
             early = end(early_keeps, early_came, stages[done])
             early = jnp.concatenate(run_stages(early, stages[done + 1 :]), axis=0)
@@ -799,20 +803,29 @@
             early_step = (early, swap(early, core))
         if at == last:
             early_parts.append(unpack(my_core, *early_step, 0, wide, False))
-            came, early_parts, from_other[1] = lax.optimization_barrier(
-                (came, early_parts, from_other[1])
-            )
+            came, early_parts = lax.optimization_barrier((came, early_parts))
         late = end(keeps, came, stage)
     late = jnp.concatenate(late, axis=0)
+    late, for_other = lax.optimization_barrier((late, for_other))
     late_other = swap(late, core)
+    quarters = jnp.split(for_other, 4, axis=0)
+    from_other.append(swap(quarters[2], top_axis))
     early_parts.append(unpack(my_core, *early_step, wide, wide, True))
     early_parts.append(unpack(my_core, *early_step, 2 * wide, width, False))
-    late_other, early_parts, from_other = lax.optimization_barrier(
-        (late_other, early_parts, from_other)
-    )
+    late_other, early_parts, from_other, quarter = lax.optimization_barrier(
+        (late_other, early_parts, from_other, quarters[3])
+    )
+    from_other.append(swap(quarter, top_axis))
+    rows = block_rows // 4
     gene_grad, know_grad = (
-        table_own[part * rows_dev : (part + 1) * rows_dev] + from_other[part].astype(F32)
-        for part in range(2)
+        jnp.concatenate(
+            [
+                table_own[part * rows : (part + 1) * rows] + from_other[part].astype(F32)
+                for part in parts
+            ],
+            axis=0,
+        )
+        for parts in ((0, 1), (2, 3))
     )
     w_down_grad, w_up_grad, w_out_grad = early_parts
     w_query_grad, w_key_grad, w_value_grad, expr_grad, short = unpack_whole(

time: 669 us -> 657 us (0.982)
  waiting for transfers between devices: 231 us -> 220 us
    ppermute x37, waiting for transfers between devices: 133 us -> 122 us  [swap(): return lax.ppermute(value, axis, SWAP)]
  transfers between devices with their start and end apart: 45 -> 45, of which waited for: 23 -> 24; matrix products, arithmetic and copies ran while one was open for 15% -> 16% of each run, Pallas kernels for 22% -> 23%
where the time goes in v12:
time: 657 us; the launch traced here: 649 us
  Pallas kernels  224 us (34%)
  waiting for transfers between devices  220 us (33%)
  matrix products  82.5 us (13%)
  starting transfers between devices  61.8 us (9%)
  other arithmetic  36.6 us (6%)
  local copies, waits for them, and re-layouts  21 us (3%)
    ppermute x37, waiting for transfers between devices, swap(): return lax.ppermute(value, axis, SWAP)  122 us
    pallas_call x5, Pallas kernels, attend_back(): pl.pallas_call(functools.partial(attend_back_kernel, add, len(into)), gri...  86.9 us
    dot_general x25, matrix products, mm(): return lax.dot_general(left, right, dims, preferred_element_type=F32)  82.5 us
    ppermute x1, waiting for transfers between devices, local(): know_other = lax.ppermute(know_sum, top_axis, SWAP)  73.8 us
    pallas_call x2, Pallas kernels, attend(): pl.pallas_call(functools.partial(attend_kernel, merge), grid_spec=pltpu.P...  43.5 us
    pallas_call x1, Pallas kernels, middle(): pl.pallas_call(middle_kernel, grid=(tokens // block,), in_specs=[rows(wid...  37.3 us
    ppermute x37, starting transfers between devices, swap(): return lax.ppermute(value, axis, SWAP)  33.3 us
    pallas_call x2, Pallas kernels, weight_sums(): pl.pallas_call(functools.partial(weight_sums_kernel, counts), grid_spec=p...  27.6 us
  transfers between devices with their start and end apart: 45, of which 24 were waited for; matrix products, arithmetic and copies ran while one was open for 16% of the time, Pallas kernels for 23%

profile of v12, /device:TPU:0, one launch (start us, length us, event | category | flops | bytes accessed | tf_op | source)
XLA Modules:
  0.0 649.3 jit_solution(2164407764777679446)
XLA Ops:
  18.0 8.7 %all-to-all-done = s32[16,1,256]{2,1,0:T(1,128)S(1)} async-done(((s32[16,1,256]{2,1,0:T(1,128)}), s32[16,1,256]{2,1,0:T(1,128)S(1)}, u32[]{:S(2)}, u32[]{:S(2)}) %all-to-all-start) | async-done | bytes 16416 | tf_op jit(solution)/shard_map/all_to_all | solution.py:611
  26.8 8.2 %fusion.25 = bf16[3072,768]{1,0:T(8,128)(2,1)} fusion(s32[864]{0:T(1024)S(1)} %iota_add_fusion.2, s32[3072]{0:T(1024)S(1)} %eq.199, bf16[288,768]{1,0:T(8,128)(2,1)} %collective-permute-done, bf16[288,768]{1,0:T(8,128)(2,1)S(1)} %reduce_sum.75, bf16[288,768]{1,0:T(8,128)(2,1)S(1)} %copy-done.67), kind=kOutput, calls=%fused_computation.27 | convolution fusion | flops 4085858304 | bytes 6061440 | tf_op jit(solution)/shard_map/dot_general | solution.py:24
  40.8 73.8 %collective-permute-done.1 = bf16[288,768]{1,0:T(8,128)(2,1)S(1)} collective-permute-done((bf16[288,768]{1,0:T(8,128)(2,1)S(1)}, bf16[288,768]{1,0:T(8,128)(2,1)S(1)}, u32[]{:S(2)}, u32[]{:S(2)}) %collective-permute-start.1) | collective-permute-done | bytes 442400 | tf_op jit(solution)/shard_map/ppermute | solution.py:622
  130.8 9.5 %fusion.3 = f32[1024,768]{1,0:T(8,128)} fusion(bf16[3072,768]{1,0:T(8,128)(2,1)} %bitcast.9, s32[3072]{0:T(1024)S(1)} %eq.189, s32[1024]{0:T(1024)S(1)} %reduce.3, s32[1024]{0:T(1024)S(1)} %reduce.2), kind=kOutput, calls=%fused_computation.4 | convolution fusion | flops 4841275392 | bytes 7884800 | tf_op jit(solution)/shard_map/dot_general | solution.py:24
  155.8 21.1 %attend.1 = (f32[768,1024]{1,0:T(8,128)}, f32[6,2,1024]{2,1,0:T(2,128)S(1)}) custom-call(s32[2]{0:T(128)S(1)} %pad_add_fusion.1.where_ref, bf16[1024,768]{1,0:T(8,128)(2,1)S(1)} %add_convert_fusion.3.q_ref, bf16[1024,768]{1,0:T(8,128)(2,1)S(1)} %convolution_convert_fusion.k_ref, bf16[1024,768]{1,0:T(8,128)(2,1)S(1)} %add_convert_fusion.1.v_ref), custom_call_target="tpu_custom_call" | custom-call | flops 12884901888 | bytes 15728640 | tf_op jit(solution)/shard_map/attend/pallas_call | solution.py:167
  176.9 10.8 %collective-permute-done.2 = bf16[1024,768]{1,0:T(8,128)(2,1)S(1)} collective-permute-done((bf16[1024,768]{1,0:T(8,128)(2,1)S(1)}, bf16[1024,768]{1,0:T(8,128)(2,1)S(1)}, u32[]{:S(2)}, u32[]{:S(2)}) %collective-permute-start.2) | collective-permute-done | bytes 1572896 | tf_op jit(solution)/shard_map/ppermute | solution.py:649
  190.6 22.4 %attend_more.1 = (f32[1024,768]{1,0:T(8,128)}, f32[6,2,1024]{2,1,0:T(2,128)S(1)}) custom-call(s32[2]{0:T(128)S(1)} %pad_add_fusion.where_ref, bf16[1024,768]{1,0:T(8,128)(2,1)S(1)} %add_convert_fusion.3.q_ref, bf16[1024,768]{1,0:T(8,128)(2,1)S(1)} %convolution_convert_fusion.1.k_ref, bf16[1024,768]{1,0:T(8,128)(2,1)S(1)} %add_convert_fusion.2.v_ref, ...), custom_call_target="tpu_custom_call" | custom-call | flops 12884901888 | bytes 15728640 | tf_op jit(solution)/shard_map/attend_more/pallas_call | solution.py:167
  213.6 37.3 %middle.1 = (bf16[1024,768]{1,0:T(8,128)(2,1)}, bf16[1024,768]{1,0:T(8,128)(2,1)}, bf16[1024,768]{1,0:T(8,128)(2,1)}, bf16[1024,3072]{1,0:T(8,128)(2,1)}, bf16[1...) custom-call(f32[1024,768]{1,0:T(8,128)} %get-tuple-element.223.ctx_r, ...), custom_call_target="tpu_custom_call" | custom-call | flops 43486543872 | bytes 34603008 | tf_op jit(solution)/shard_map/middle/pallas_call | solution.py:375
  250.8 13.8 %weight_sums.2 = bf16[3456,768]{1,0:T(8,128)(2,1)} custom-call(s32[1]{0:T(128)} %bitcast.18.half_ref, bf16[1024,3072]{1,0:T(8,128)(2,1)} %get-tuple-element.231.act_ref, bf16[1024,768]{1,0:T(8,128)(2,1)} %get-tuple-element.232.gffn_ref, bf16[1024,3072]{1,0:T(8,128)(2,1)} %get-tuple-element.233.gpre_ref, bf16[1024,768]{1,0:T(8,128)(2,1)} %get-tuple-element.234.norm_ref, ...), custom_call_target="tpu_custom_call" | custom-call | flops 5435817984 | bytes 12386304 | tf_op jit(solution)/shard_map/weight_sums/pallas_call | solution.py:438
  264.7 13.7 %weight_sums.3 = bf16[3456,768]{1,0:T(8,128)(2,1)} custom-call(s32[1]{0:T(128)} %bitcast.17.half_ref.core_ref, bf16[1024,3072]{1,0:T(8,128)(2,1)} %get-tuple-element.231.act_ref, bf16[1024,768]{1,0:T(8,128)(2,1)} %get-tuple-element.232.gffn_ref, bf16[1024,3072]{1,0:T(8,128)(2,1)} %get-tuple-element.233.gpre_ref, ...), custom_call_target="tpu_custom_call" | custom-call | flops 5435817984 | bytes 12386304 | tf_op jit(solution)/shard_map/weight_sums/pallas_call | solution.py:438
  287.8 26.5 %attend_back0.1 = (f32[1024,768]{1,0:T(8,128)}, bf16[1024,768]{1,0:T(8,128)(2,1)}, bf16[1024,768]{1,0:T(8,128)(2,1)}) custom-call(s32[2]{0:T(128)} %copy-done.2, bf16[1024,768]{1,0:T(8,128)(2,1)} %copy-done.5, bf16[1024,768]{1,0:T(8,128)(2,1)} %get-tuple-element.300.g_ref, f32[1024,768]{1,0:T(8,128)} %get-tuple-element.223.ctx_ref.o_ref, ...), custom_call_target="tpu_custom_call" | custom-call | flops 21474836480 | bytes 12582912 | tf_op jit(solution)/shard_map/attend_back0/pallas_call | solution.py:247
  322.2 14.9 %attend_back4.1 = (f32[1024,768]{1,0:T(8,128)}, bf16[1024,768]{1,0:T(8,128)(2,1)}, bf16[1024,768]{1,0:T(8,128)(2,1)}) custom-call(s32[2]{0:T(128)} %copy-done.2, bf16[1024,768]{1,0:T(8,128)(2,1)} %copy-done.5, bf16[1024,768]{1,0:T(8,128)(2,1)} %get-tuple-element.300.g_ref, ...), custom_call_target="tpu_custom_call", output_to_operand_aliasing={{0}: (7, {}), {1}: (8, {}), {2}: (9, {})} | custom-call | flops 10737418240 | bytes 6291456 | tf_op jit(solution)/shard_map/attend_back4/pallas_call | solution.py:247
  346.2 15.1 %attend_back_more0.1 = (bf16[1024,768]{1,0:T(8,128)(2,1)}, bf16[1024,768]{1,0:T(8,128)(2,1)}, bf16[1024,768]{1,0:T(8,128)(2,1)}) custom-call(s32[2]{0:T(128)} %copy-done.1, bf16[1024,768]{1,0:T(8,128)(2,1)} %copy-done.5, bf16[1024,768]{1,0:T(8,128)(2,1)} %get-tuple-element.300.g_ref, f32[1024,768]{1,0:T(8,128)} %get-tuple-element.223.ctx_ref.o_ref, ...), custom_call_target="tpu_custom_call" | custom-call | flops 10737418240 | bytes 6291456 | tf_op jit(solution)/shard_map/attend_back_more0/pallas_call | solution.py:247
  363.6 14.9 %attend_back_more2.1 = (bf16[1024,768]{1,0:T(8,128)(2,1)}, bf16[1024,768]{1,0:T(8,128)(2,1)}, bf16[1024,768]{1,0:T(8,128)(2,1)}) custom-call(s32[2]{0:T(128)} %copy-done.1, bf16[1024,768]{1,0:T(8,128)(2,1)} %copy-done.5, bf16[1024,768]{1,0:T(8,128)(2,1)} %get-tuple-element.300.g_ref, ...), custom_call_target="tpu_custom_call", output_to_operand_aliasing={{0}: (8, {}), {1}: (9, {}), {2}: (10, {})} | custom-call | flops 10737418240 | bytes 6291456 | tf_op jit(solution)/shard_map/attend_back_more2/pallas_call | solution.py:247
  379.7 15.4 %attend_back_more4.1 = (bf16[1024,768]{1,0:T(8,128)(2,1)}, bf16[1024,768]{1,0:T(8,128)(2,1)}, bf16[1024,768]{1,0:T(8,128)(2,1)}) custom-call(s32[2]{0:T(128)} %copy-done.1, bf16[1024,768]{1,0:T(8,128)(2,1)} %copy-done.5, bf16[1024,768]{1,0:T(8,128)(2,1)} %get-tuple-element.300.g_ref, ...), custom_call_target="tpu_custom_call", output_to_operand_aliasing={{0}: (8, {}), {1}: (9, {}), {2}: (10, {})} | custom-call | flops 10737418240 | bytes 6291456 | tf_op jit(solution)/shard_map/attend_back_more4/pallas_call | solution.py:247
  413.7 10.9 %fusion.17 = bf16[4096,768]{1,0:T(8,128)(2,1)} fusion(bf16[1024,768]{1,0:T(8,128)(2,1)S(1)} %get-tuple-element.322, s32[1024]{0:T(1024)S(1)} %copy-done.46, s32[1024]{0:T(1024)S(1)} %copy-done.44), kind=kOutput, calls=%fused_computation.20 | convolution fusion | flops 6458179584 | bytes 7872512 | tf_op jit(solution)/shard_map/dot_general | solution.py:24
  472.8 55.2 %collective-permute-done.18 = bf16[320,768]{1,0:T(8,128)(2,1)} collective-permute-done((bf16[320,768]{1,0:T(8,128)(2,1)S(1)}, bf16[320,768]{1,0:T(8,128)(2,1)}, u32[]{:S(2)}, u32[]{:S(2)}) %collective-permute-start.18) | collective-permute-done | bytes 491552 | tf_op jit(solution)/shard_map/ppermute | solution.py:525
  532.9 6.9 %fusion.44 = bf16[576,768]{1,0:T(8,128)(2,1)S(1)} fusion(bf16[4096,768]{1,0:T(8,128)(2,1)} %bitcast.20, s32[4096]{0:T(1024)S(1)} %copy-done.42, s32[576]{0:T(1024)S(1)} %copy-done.59), kind=kOutput, calls=%fused_computation.65 | convolution fusion | flops 3626680320 | bytes 7194880 | tf_op jit(solution)/shard_map/dot_general | solution.py:24
  544.2 7.9 %fusion.7 = f32[576,768]{1,0:T(8,128)} fusion(bf16[4096,768]{1,0:T(8,128)(2,1)} %bitcast.20, s32[4096]{0:T(1024)S(1)} %copy-done.42, s32[576]{0:T(1024)S(1)} %copy-done.57), kind=kOutput, calls=%fused_computation.9 | convolution fusion | flops 3626237952 | bytes 8079616 | tf_op jit(solution)/shard_map/dot_general | solution.py:24
  556.6 15.7 %collective-permute-done.24 = bf16[288,768]{1,0:T(8,128)(2,1)S(1)} collective-permute-done((bf16[288,768]{1,0:T(8,128)(2,1)S(1)}, bf16[288,768]{1,0:T(8,128)(2,1)S(1)}, u32[]{:S(2)}, u32[]{:S(2)}) %collective-permute-start.24) | collective-permute-done | bytes 442400 | tf_op jit(solution)/shard_map/ppermute | solution.py:525
  574.0 7.1 %collective-permute-done.29 = bf16[80,768]{1,0:T(8,128)(2,1)S(1)} collective-permute-done((bf16[80,768]{1,0:T(8,128)(2,1)S(1)}, bf16[80,768]{1,0:T(8,128)(2,1)S(1)}, u32[]{:S(2)}, u32[]{:S(2)}) %collective-permute-start.29) | collective-permute-done | bytes 122912 | tf_op jit(solution)/shard_map/ppermute | solution.py:525
  590.4 12.4 %collective-permute-done.33 = bf16[144,768]{1,0:T(8,128)(2,1)S(1)} collective-permute-done((bf16[144,768]{1,0:T(8,128)(2,1)S(1)}, bf16[144,768]{1,0:T(8,128)(2,1)S(1)}, u32[]{:S(2)}, u32[]{:S(2)}) %collective-permute-start.33) | collective-permute-done | bytes 221216 | tf_op jit(solution)/shard_map/ppermute | solution.py:525
  608.0 7.9 %unpack0.1 = f32[3072,768]{1,0:T(8,128)} custom-call(s32[1]{0:T(128)} %bitcast.17.half_ref.core_ref, bf16[3456,768]{1,0:T(8,128)(2,1)} %copy-done.9, bf16[3456,768]{1,0:T(8,128)(2,1)} %copy-done.10), custom_call_target="tpu_custom_call" | custom-call | flops 2359296 | bytes 14155776 | tf_op jit(solution)/shard_map/unpack0/pallas_call | solution.py:469
  623.7 8.6 %unpack8.1 = f32[768,3072]{1,0:T(8,128)} custom-call(s32[1]{0:T(128)} %bitcast.17.half_ref.core_ref, bf16[3456,768]{1,0:T(8,128)(2,1)} %copy-done.9, bf16[3456,768]{1,0:T(8,128)(2,1)} %copy-done.10), custom_call_target="tpu_custom_call" | custom-call | flops 2359296 | bytes 14155776 | tf_op jit(solution)/shard_map/unpack8/pallas_call | solution.py:469
  (368 shorter events, 206.9 us)
Async XLA Ops:
  0.7 26.0 %collective-permute-start = (bf16[288,768]{1,0:T(8,128)(2,1)}, bf16[288,768]{1,0:T(8,128)(2,1)}, u32[]{:S(2)}, u32[]{:S(2)}) collective-permute-start(bf16[288,768]{1,0:T(8,128)(2,1)} %param.31), channel_id=1, source_target_pairs={{0,16},{16,0},{1,17},{17,1},{2,18},{18,2},{3,19},{19,3},{4,20},{20... | collective-permute-start | bytes 1327112 | tf_op jit(solution)/shard_map/ppermute | solution.py:614
  35.0 81.8 %all-to-all-start.1 = ((bf16[16,192,768]{2,1,0:T(8,128)(2,1)}), bf16[16,192,768]{2,1,0:T(8,128)(2,1)}, u32[]{:S(2)}, u32[]{:S(2)}) async-start(bf16[16,192,768]{2,1,0:T(8,128)(2,1)} %bitcast.71), calls=%async_computation.1 | async-start | bytes 9437184 | tf_op jit(solution)/shard_map/all_to_all | solution.py:611
  39.6 75.0 %collective-permute-start.1 = (bf16[288,768]{1,0:T(8,128)(2,1)S(1)}, bf16[288,768]{1,0:T(8,128)(2,1)S(1)}, u32[]{:S(2)}, u32[]{:S(2)}) collective-permute-start(bf16[288,768]{1,0:T(8,128)(2,1)S(1)} %reduce_sum.75), channel_id=1, source_target_pairs={{0,16},{16,0},{1,17},{17,1},{2,18},{18,2},{3,19},{19,3},{4,20},{20... | collective-permute-start | bytes 1327112 | tf_op jit(solution)/shard_map/ppermute | solution.py:622
  116.8 28.1 %all-to-all-start.2 = ((bf16[16,64,768]{2,1,0:T(8,128)(2,1)}), bf16[16,64,768]{2,1,0:T(8,128)(2,1)}, u32[]{:S(2)}, u32[]{:S(2)}) async-start(bf16[16,64,768]{2,1,0:T(8,128)(2,1)} %bitcast.72), calls=%async_computation.2 | async-start | bytes 3145728 | tf_op jit(solution)/shard_map/all_to_all | solution.py:611
  128.7 48.2 %collective-permute-start.3 = (s32[576]{0:T(1024)S(1)}, s32[576]{0:T(1024)S(1)}, u32[]{:S(2)}, u32[]{:S(2)}) collective-permute-start(s32[576]{0:T(1024)S(1)} %get-tuple-element.407), channel_id=1, source_target_pairs={{0,16},{16,0},{1,17},{17,1},{2,18},{18,2},{3,19},{19,3},{4,20},{20... | collective-permute-start | bytes 6920 | tf_op jit(solution)/shard_map/ppermute | solution.py:658
  150.9 36.9 %collective-permute-start.2 = (bf16[1024,768]{1,0:T(8,128)(2,1)S(1)}, bf16[1024,768]{1,0:T(8,128)(2,1)S(1)}, u32[]{:S(2)}, u32[]{:S(2)}) collective-permute-start(bf16[1024,768]{1,0:T(8,128)(2,1)S(1)} %get-tuple-element.466), channel_id=1, source_target_pairs={{0,1},{1,0},{2,3},{3,2},{4,5},{5,4},{6,7},{7,6},{8,9},{9,8},{10,11... | collective-permute-start | bytes 4718600 | tf_op jit(solution)/shard_map/ppermute | solution.py:649
  284.6 32.2 %collective-permute-start.5 = (bf16[864,768]{1,0:T(8,128)(2,1)S(1)}, bf16[864,768]{1,0:T(8,128)(2,1)S(1)}, u32[]{:S(2)}, u32[]{:S(2)}) collective-permute-start(bf16[864,768]{1,0:T(8,128)(2,1)S(1)} %get-tuple-element.243), channel_id=1, source_target_pairs={{0,4},{4,0},{1,5},{5,1},{2,6},{6,2},{3,7},{7,3},{8,12},{12,8},{9,1... | collective-permute-start | bytes 3981320 | tf_op jit(solution)/shard_map/ppermute | solution.py:525
  287.1 31.8 %collective-permute-start.6 = (bf16[864,768]{1,0:T(8,128)(2,1)S(1)}, bf16[864,768]{1,0:T(8,128)(2,1)}, u32[]{:S(2)}, u32[]{:S(2)}) collective-permute-start(bf16[864,768]{1,0:T(8,128)(2,1)S(1)} %get-tuple-element.244), channel_id=1, source_target_pairs={{0,1},{1,0},{2,3},{3,2},{4,5},{5,4},{6,7},{7,6},{8,9},{9,8},{10,11... | collective-permute-start | bytes 3981320 | tf_op jit(solution)/shard_map/ppermute | solution.py:525
  321.0 16.7 %collective-permute-start.7 = (bf16[432,768]{1,0:T(8,128)(2,1)S(1)}, bf16[432,768]{1,0:T(8,128)(2,1)S(1)}, u32[]{:S(2)}, u32[]{:S(2)}) collective-permute-start(bf16[432,768]{1,0:T(8,128)(2,1)S(1)} %get-tuple-element.257), channel_id=1, source_target_pairs={{0,1},{1,0},{2,3},{3,2},{4,5},{5,4},{6,7},{7,6},{8,9},{9,8},{10,11... | collective-permute-start | bytes 1990664 | tf_op jit(solution)/shard_map/ppermute | solution.py:525
  321.8 16.3 %collective-permute-start.8 = (bf16[432,768]{1,0:T(8,128)(2,1)S(1)}, bf16[432,768]{1,0:T(8,128)(2,1)S(1)}, u32[]{:S(2)}, u32[]{:S(2)}) collective-permute-start(bf16[432,768]{1,0:T(8,128)(2,1)S(1)} %get-tuple-element.258), channel_id=1, source_target_pairs={{0,4},{4,0},{1,5},{5,1},{2,6},{6,2},{3,7},{7,3},{8,12},{12,8},{9,1... | collective-permute-start | bytes 1990664 | tf_op jit(solution)/shard_map/ppermute | solution.py:525
  344.8 16.6 %collective-permute-start.9 = (bf16[432,768]{1,0:T(8,128)(2,1)S(1)}, bf16[432,768]{1,0:T(8,128)(2,1)S(1)}, u32[]{:S(2)}, u32[]{:S(2)}) collective-permute-start(bf16[432,768]{1,0:T(8,128)(2,1)S(1)} %get-tuple-element.274), channel_id=1, source_target_pairs={{0,8},{8,0},{1,9},{9,1},{2,10},{10,2},{3,11},{11,3},{4,12},{12,4},... | collective-permute-start | bytes 1990664 | tf_op jit(solution)/shard_map/ppermute | solution.py:525
  344.9 50.4 %collective-permute-start.12 = (bf16[1024,768]{1,0:T(8,128)(2,1)S(1)}, bf16[1024,768]{1,0:T(8,128)(2,1)S(1)}, u32[]{:S(2)}, u32[]{:S(2)}) collective-permute-start(bf16[1024,768]{1,0:T(8,128)(2,1)S(1)} %add_convert_fusion), channel_id=1, source_target_pairs={{0,1},{1,0},{2,3},{3,2},{4,5},{5,4},{6,7},{7,6},{8,9},{9,8},{10,11... | collective-permute-start | bytes 4718600 | tf_op jit(solution)/shard_map/ppermute | solution.py:525
  361.6 17.0 %collective-permute-start.10 = (bf16[216,768]{1,0:T(8,128)(2,1)S(1)}, bf16[216,768]{1,0:T(8,128)(2,1)S(1)}, u32[]{:S(2)}, u32[]{:S(2)}) collective-permute-start(bf16[216,768]{1,0:T(8,128)(2,1)S(1)} %get-tuple-element.285), channel_id=1, source_target_pairs={{0,16},{16,0},{1,17},{17,1},{2,18},{18,2},{3,19},{19,3},{4,20},{20... | collective-permute-start | bytes 995336 | tf_op jit(solution)/shard_map/ppermute | solution.py:525
  378.7 16.5 %collective-permute-start.11 = (bf16[216,768]{1,0:T(8,128)(2,1)S(1)}, bf16[216,768]{1,0:T(8,128)(2,1)S(1)}, u32[]{:S(2)}, u32[]{:S(2)}) collective-permute-start(bf16[216,768]{1,0:T(8,128)(2,1)S(1)} %add.259), channel_id=1, source_target_pairs={{0,16},{16,0},{1,17},{17,1},{2,18},{18,2},{3,19},{19,3},{4,20},{20... | collective-permute-start | bytes 995336 | tf_op jit(solution)/shard_map/ppermute | solution.py:525
  395.3 16.5 %collective-permute-start.13 = (bf16[432,768]{1,0:T(8,128)(2,1)S(1)}, bf16[432,768]{1,0:T(8,128)(2,1)S(1)}, u32[]{:S(2)}, u32[]{:S(2)}) collective-permute-start(bf16[432,768]{1,0:T(8,128)(2,1)S(1)} %pad_maximum_fusion.6), channel_id=1, source_target_pairs={{0,8},{8,0},{1,9},{9,1},{2,10},{10,2},{3,11},{11,3},{4,12},{12,4},... | collective-permute-start | bytes 1990664 | tf_op jit(solution)/shard_map/ppermute | solution.py:525
  429.1 99.9 %all-to-all-start.3 = ((bf16[16,256,768]{2,1,0:T(8,128)(2,1)}), bf16[16,256,768]{2,1,0:T(8,128)(2,1)}, u32[]{:S(2)}, u32[]{:S(2)}) async-start(bf16[16,256,768]{2,1,0:T(8,128)(2,1)} %bitcast.70), calls=%async_computation.3 | async-start | bytes 12582912 | tf_op jit(solution)/shard_map/all_to_all | solution.py:611
  467.4 60.6 %collective-permute-start.18 = (bf16[320,768]{1,0:T(8,128)(2,1)S(1)}, bf16[320,768]{1,0:T(8,128)(2,1)}, u32[]{:S(2)}, u32[]{:S(2)}) collective-permute-start(bf16[320,768]{1,0:T(8,128)(2,1)S(1)} %get-tuple-element.448), channel_id=1, source_target_pairs={{0,1},{1,0},{2,3},{3,2},{4,5},{5,4},{6,7},{7,6},{8,9},{9,8},{10,11... | collective-permute-start | bytes 1474568 | tf_op jit(solution)/shard_map/ppermute | solution.py:525
  470.0 59.0 %collective-permute-start.17 = (bf16[320,768]{1,0:T(8,128)(2,1)S(1)}, bf16[320,768]{1,0:T(8,128)(2,1)}, u32[]{:S(2)}, u32[]{:S(2)}) collective-permute-start(bf16[320,768]{1,0:T(8,128)(2,1)S(1)} %get-tuple-element.450), channel_id=1, source_target_pairs={{0,4},{4,0},{1,5},{5,1},{2,6},{6,2},{3,7},{7,3},{8,12},{12,8},{9,1... | collective-permute-start | bytes 1474568 | tf_op jit(solution)/shard_map/ppermute | solution.py:525
  552.1 21.9 %collective-permute-start.27 = (bf16[288,768]{1,0:T(8,128)(2,1)S(1)}, bf16[288,768]{1,0:T(8,128)(2,1)S(1)}, u32[]{:S(2)}, u32[]{:S(2)}) collective-permute-start(bf16[288,768]{1,0:T(8,128)(2,1)S(1)} %get-tuple-element.430), channel_id=1, source_target_pairs={{0,4},{4,0},{1,5},{5,1},{2,6},{6,2},{3,7},{7,3},{8,12},{12,8},{9,1... | collective-permute-start | bytes 1327112 | tf_op jit(solution)/shard_map/ppermute | solution.py:525
  553.2 19.1 %collective-permute-start.24 = (bf16[288,768]{1,0:T(8,128)(2,1)S(1)}, bf16[288,768]{1,0:T(8,128)(2,1)S(1)}, u32[]{:S(2)}, u32[]{:S(2)}) collective-permute-start(bf16[288,768]{1,0:T(8,128)(2,1)S(1)} %get-tuple-element.431), channel_id=1, source_target_pairs={{0,4},{4,0},{1,5},{5,1},{2,6},{6,2},{3,7},{7,3},{8,12},{12,8},{9,1... | collective-permute-start | bytes 1327112 | tf_op jit(solution)/shard_map/ppermute | solution.py:525
  554.1 19.9 %collective-permute-start.28 = (bf16[288,768]{1,0:T(8,128)(2,1)S(1)}, bf16[288,768]{1,0:T(8,128)(2,1)S(1)}, u32[]{:S(2)}, u32[]{:S(2)}) collective-permute-start(bf16[288,768]{1,0:T(8,128)(2,1)S(1)} %get-tuple-element.427), channel_id=1, source_target_pairs={{0,1},{1,0},{2,3},{3,2},{4,5},{5,4},{6,7},{7,6},{8,9},{9,8},{10,11... | collective-permute-start | bytes 1327112 | tf_op jit(solution)/shard_map/ppermute | solution.py:525
  555.5 18.3 %collective-permute-start.25 = (bf16[288,768]{1,0:T(8,128)(2,1)S(1)}, bf16[288,768]{1,0:T(8,128)(2,1)S(1)}, u32[]{:S(2)}, u32[]{:S(2)}) collective-permute-start(bf16[288,768]{1,0:T(8,128)(2,1)S(1)} %get-tuple-element.428), channel_id=1, source_target_pairs={{0,1},{1,0},{2,3},{3,2},{4,5},{5,4},{6,7},{7,6},{8,9},{9,8},{10,11... | collective-permute-start | bytes 1327112 | tf_op jit(solution)/shard_map/ppermute | solution.py:525
  556.4 17.4 %collective-permute-start.26 = (bf16[80,768]{1,0:T(8,128)(2,1)S(1)}, bf16[80,768]{1,0:T(8,128)(2,1)S(1)}, u32[]{:S(2)}, u32[]{:S(2)}) collective-permute-start(bf16[80,768]{1,0:T(8,128)(2,1)S(1)} %constant_dynamic-slice_fusion), channel_id=1, source_target_pairs={{0,16},{16,0},{1,17},{17,1},{2,18},{18,2},{3,19},{19,3},{4,20},{20... | collective-permute-start | bytes 368648 | tf_op jit(solution)/shard_map/ppermute | solution.py:525
  587.4 16.2 %collective-permute-start.34 = (bf16[3456,768]{1,0:T(8,128)(2,1)S(1)}, bf16[3456,768]{1,0:T(8,128)(2,1)S(1)}, u32[]{:S(2)}, u32[]{:S(2)}) collective-permute-start(bf16[3456,768]{1,0:T(8,128)(2,1)S(1)} %pad_maximum_fusion.own_ref), channel_id=1, source_target_pairs={{0,2},{2,0},{1,3},{3,1},{4,6},{6,4},{5,7},{7,5},{8,10},{10,8},{9,1... | collective-permute-start | bytes 15925256 | tf_op jit(solution)/shard_map/ppermute | solution.py:525
  (96 other events, 1057.9 us)

commit v13 on v12

--- a/solution.py
+++ b/solution.py
@@ -365,7 +365,7 @@
     gctx_ref[...] = mm(gattn, w_out_ref[...], NT).astype(BF16)
 
 
-def middle(ctx, embedded, cotangent, w_out, w_up, w_down, small, b_up, block=256):
+def middle(ctx, embedded, cotangent, w_out, w_up, w_down, small, b_up, block=512):
     tokens, width = embedded.shape
     wide = w_up.shape[1]
     whole = lambda a: pl.BlockSpec(a.shape, lambda i: (0, 0), pipeline_mode=pl.Buffered(1))
@@ -779,6 +779,8 @@
             keeps, sends, for_other = lax.optimization_barrier((keeps, sends, for_other))
         if at == last:
             keeps, sends, early_step = lax.optimization_barrier((keeps, sends, early_step))
+        if at == 4:
+            keeps, sends, rows_then = lax.optimization_barrier((keeps, sends, returned))
         came = travel(sends, stage)
         if at >= last - 1:
             quarter = swap(jnp.split(for_other, 4, axis=0)[len(from_other)], top_axis)
@@ -792,8 +794,8 @@
         if at == 2:
             table_own = mm(owned[0].astype(BF16), returned)
             came, table_own = lax.optimization_barrier((came, table_own))
-        if at == 3:
-            for_other = mm(owned[1].astype(BF16), returned).astype(BF16)
+        if at == 4:
+            for_other = mm(owned[1].astype(BF16), rows_then).astype(BF16)
             came, for_other = lax.optimization_barrier((came, for_other))
         if at == last - 2:
             early_came = [jnp.concatenate(parts, axis=0) for parts in zip(*early_came)]
@@ -803,6 +805,7 @@
             early_step = (early, swap(early, core))
         if at == last:
             early_parts.append(unpack(my_core, *early_step, 0, wide, False))
+            early_parts.append(unpack(my_core, *early_step, 2 * wide, width, False))
             came, early_parts = lax.optimization_barrier((came, early_parts))
         late = end(keeps, came, stage)
     late = jnp.concatenate(late, axis=0)
@@ -811,7 +814,6 @@
     quarters = jnp.split(for_other, 4, axis=0)
     from_other.append(swap(quarters[2], top_axis))
     early_parts.append(unpack(my_core, *early_step, wide, wide, True))
-    early_parts.append(unpack(my_core, *early_step, 2 * wide, width, False))
     late_other, early_parts, from_other, quarter = lax.optimization_barrier(
         (late_other, early_parts, from_other, quarters[3])
     )
@@ -827,7 +829,7 @@
         )
         for parts in ((0, 1), (2, 3))
     )
-    w_down_grad, w_up_grad, w_out_grad = early_parts
+    w_down_grad, w_out_grad, w_up_grad = early_parts
     w_query_grad, w_key_grad, w_value_grad, expr_grad, short = unpack_whole(
         my_core, late, late_other, heights
     )

time: 657 us -> 655 us (level)
  transfers between devices with their start and end apart: 45 -> 45, of which waited for: 24 -> 25; matrix products, arithmetic and copies ran while one was open for 16% -> 15% of each run, Pallas kernels for 23% -> 23%
where the time goes in v13:
time: 655 us; the launch traced here: 647 us
  Pallas kernels  223 us (34%)
  waiting for transfers between devices  216 us (33%)
  matrix products  82.2 us (13%)
  starting transfers between devices  64.2 us (10%)
  other arithmetic  36.8 us (6%)
  local copies, waits for them, and re-layouts  21.6 us (3%)
    ppermute x37, waiting for transfers between devices, swap(): return lax.ppermute(value, axis, SWAP)  118 us
    pallas_call x5, Pallas kernels, attend_back(): pl.pallas_call(functools.partial(attend_back_kernel, add, len(into)), gri...  86.9 us
    dot_general x25, matrix products, mm(): return lax.dot_general(left, right, dims, preferred_element_type=F32)  82.2 us
    ppermute x1, waiting for transfers between devices, local(): know_other = lax.ppermute(know_sum, top_axis, SWAP)  73.8 us
    pallas_call x2, Pallas kernels, attend(): pl.pallas_call(functools.partial(attend_kernel, merge), grid_spec=pltpu.P...  43.5 us
    pallas_call x1, Pallas kernels, middle(): pl.pallas_call(middle_kernel, grid=(tokens // block,), in_specs=[rows(wid...  36.9 us
    ppermute x37, starting transfers between devices, swap(): return lax.ppermute(value, axis, SWAP)  35.7 us
    pallas_call x2, Pallas kernels, weight_sums(): pl.pallas_call(functools.partial(weight_sums_kernel, counts), grid_spec=p...  27.2 us
  transfers between devices with their start and end apart: 45, of which 25 were waited for; matrix products, arithmetic and copies ran while one was open for 15% of the time, Pallas kernels for 23%

profile of v13, /device:TPU:0, one launch (start us, length us, event | category | flops | bytes accessed | tf_op | source)
XLA Modules:
  0.0 647.5 jit_solution(7454959417049143066)
XLA Ops:
  18.0 8.7 %all-to-all-done = s32[16,1,256]{2,1,0:T(1,128)S(1)} async-done(((s32[16,1,256]{2,1,0:T(1,128)}), s32[16,1,256]{2,1,0:T(1,128)S(1)}, u32[]{:S(2)}, u32[]{:S(2)}) %all-to-all-start) | async-done | bytes 16416 | tf_op jit(solution)/shard_map/all_to_all | solution.py:611
  26.8 8.2 %fusion.25 = bf16[3072,768]{1,0:T(8,128)(2,1)} fusion(s32[864]{0:T(1024)S(1)} %iota_add_fusion.2, s32[3072]{0:T(1024)S(1)} %eq.199, bf16[288,768]{1,0:T(8,128)(2,1)} %collective-permute-done, bf16[288,768]{1,0:T(8,128)(2,1)S(1)} %reduce_sum.75, bf16[288,768]{1,0:T(8,128)(2,1)S(1)} %copy-done.67), kind=kOutput, calls=%fused_computation.27 | convolution fusion | flops 4085858304 | bytes 6061440 | tf_op jit(solution)/shard_map/dot_general | solution.py:24
  40.8 73.8 %collective-permute-done.1 = bf16[288,768]{1,0:T(8,128)(2,1)S(1)} collective-permute-done((bf16[288,768]{1,0:T(8,128)(2,1)S(1)}, bf16[288,768]{1,0:T(8,128)(2,1)S(1)}, u32[]{:S(2)}, u32[]{:S(2)}) %collective-permute-start.1) | collective-permute-done | bytes 442400 | tf_op jit(solution)/shard_map/ppermute | solution.py:622
  130.8 9.5 %fusion.3 = f32[1024,768]{1,0:T(8,128)} fusion(bf16[3072,768]{1,0:T(8,128)(2,1)} %bitcast.9, s32[3072]{0:T(1024)S(1)} %eq.189, s32[1024]{0:T(1024)S(1)} %reduce.3, s32[1024]{0:T(1024)S(1)} %reduce.2), kind=kOutput, calls=%fused_computation.4 | convolution fusion | flops 4841275392 | bytes 7884800 | tf_op jit(solution)/shard_map/dot_general | solution.py:24
  155.8 21.1 %attend.1 = (f32[768,1024]{1,0:T(8,128)}, f32[6,2,1024]{2,1,0:T(2,128)S(1)}) custom-call(s32[2]{0:T(128)S(1)} %pad_add_fusion.1.where_ref, bf16[1024,768]{1,0:T(8,128)(2,1)S(1)} %add_convert_fusion.3.q_ref, bf16[1024,768]{1,0:T(8,128)(2,1)S(1)} %convolution_convert_fusion.k_ref, bf16[1024,768]{1,0:T(8,128)(2,1)S(1)} %add_convert_fusion.1.v_ref), custom_call_target="tpu_custom_call" | custom-call | flops 12884901888 | bytes 15728640 | tf_op jit(solution)/shard_map/attend/pallas_call | solution.py:167
  176.9 10.8 %collective-permute-done.2 = bf16[1024,768]{1,0:T(8,128)(2,1)S(1)} collective-permute-done((bf16[1024,768]{1,0:T(8,128)(2,1)S(1)}, bf16[1024,768]{1,0:T(8,128)(2,1)S(1)}, u32[]{:S(2)}, u32[]{:S(2)}) %collective-permute-start.2) | collective-permute-done | bytes 1572896 | tf_op jit(solution)/shard_map/ppermute | solution.py:649
  190.6 22.4 %attend_more.1 = (f32[1024,768]{1,0:T(8,128)}, f32[6,2,1024]{2,1,0:T(2,128)S(1)}) custom-call(s32[2]{0:T(128)S(1)} %pad_add_fusion.where_ref, bf16[1024,768]{1,0:T(8,128)(2,1)S(1)} %add_convert_fusion.3.q_ref, bf16[1024,768]{1,0:T(8,128)(2,1)S(1)} %convolution_convert_fusion.1.k_ref, bf16[1024,768]{1,0:T(8,128)(2,1)S(1)} %add_convert_fusion.2.v_ref, ...), custom_call_target="tpu_custom_call" | custom-call | flops 12884901888 | bytes 15728640 | tf_op jit(solution)/shard_map/attend_more/pallas_call | solution.py:167
  213.6 36.9 %middle.1 = (bf16[1024,768]{1,0:T(8,128)(2,1)}, bf16[1024,768]{1,0:T(8,128)(2,1)}, bf16[1024,768]{1,0:T(8,128)(2,1)}, bf16[1024,3072]{1,0:T(8,128)(2,1)}, bf16[1...) custom-call(f32[1024,768]{1,0:T(8,128)} %get-tuple-element.227.ctx_r, ...), custom_call_target="tpu_custom_call" | custom-call | flops 43486543872 | bytes 34603008 | tf_op jit(solution)/shard_map/middle/pallas_call | solution.py:375
  250.5 13.8 %weight_sums.2 = bf16[3456,768]{1,0:T(8,128)(2,1)} custom-call(s32[1]{0:T(128)} %bitcast.18.half_ref, bf16[1024,3072]{1,0:T(8,128)(2,1)} %get-tuple-element.235.act_ref, bf16[1024,768]{1,0:T(8,128)(2,1)} %get-tuple-element.236.gffn_ref, bf16[1024,3072]{1,0:T(8,128)(2,1)} %get-tuple-element.237.gpre_ref, bf16[1024,768]{1,0:T(8,128)(2,1)} %get-tuple-element.238.norm_ref, ...), custom_call_target="tpu_custom_call" | custom-call | flops 5435817984 | bytes 12386304 | tf_op jit(solution)/shard_map/weight_sums/pallas_call | solution.py:438
  264.4 13.4 %weight_sums.3 = bf16[3456,768]{1,0:T(8,128)(2,1)} custom-call(s32[1]{0:T(128)} %bitcast.17.half_ref.core_ref, bf16[1024,3072]{1,0:T(8,128)(2,1)} %get-tuple-element.235.act_ref, bf16[1024,768]{1,0:T(8,128)(2,1)} %get-tuple-element.236.gffn_ref, bf16[1024,3072]{1,0:T(8,128)(2,1)} %get-tuple-element.237.gpre_ref, ...), custom_call_target="tpu_custom_call" | custom-call | flops 5435817984 | bytes 12386304 | tf_op jit(solution)/shard_map/weight_sums/pallas_call | solution.py:438
  287.0 26.7 %attend_back0.1 = (f32[1024,768]{1,0:T(8,128)}, bf16[1024,768]{1,0:T(8,128)(2,1)}, bf16[1024,768]{1,0:T(8,128)(2,1)}) custom-call(s32[2]{0:T(128)} %copy-done.2, bf16[1024,768]{1,0:T(8,128)(2,1)} %copy-done.5, bf16[1024,768]{1,0:T(8,128)(2,1)} %get-tuple-element.304.g_ref, f32[1024,768]{1,0:T(8,128)} %get-tuple-element.227.ctx_ref.o_ref, ...), custom_call_target="tpu_custom_call" | custom-call | flops 21474836480 | bytes 12582912 | tf_op jit(solution)/shard_map/attend_back0/pallas_call | solution.py:247
  321.5 14.7 %attend_back4.1 = (f32[1024,768]{1,0:T(8,128)}, bf16[1024,768]{1,0:T(8,128)(2,1)}, bf16[1024,768]{1,0:T(8,128)(2,1)}) custom-call(s32[2]{0:T(128)} %copy-done.2, bf16[1024,768]{1,0:T(8,128)(2,1)} %copy-done.5, bf16[1024,768]{1,0:T(8,128)(2,1)} %get-tuple-element.304.g_ref, ...), custom_call_target="tpu_custom_call", output_to_operand_aliasing={{0}: (7, {}), {1}: (8, {}), {2}: (9, {})} | custom-call | flops 10737418240 | bytes 6291456 | tf_op jit(solution)/shard_map/attend_back4/pallas_call | solution.py:247
  345.5 15.1 %attend_back_more0.1 = (bf16[1024,768]{1,0:T(8,128)(2,1)}, bf16[1024,768]{1,0:T(8,128)(2,1)}, bf16[1024,768]{1,0:T(8,128)(2,1)}) custom-call(s32[2]{0:T(128)} %copy-done.1, bf16[1024,768]{1,0:T(8,128)(2,1)} %copy-done.5, bf16[1024,768]{1,0:T(8,128)(2,1)} %get-tuple-element.304.g_ref, f32[1024,768]{1,0:T(8,128)} %get-tuple-element.227.ctx_ref.o_ref, ...), custom_call_target="tpu_custom_call" | custom-call | flops 10737418240 | bytes 6291456 | tf_op jit(solution)/shard_map/attend_back_more0/pallas_call | solution.py:247
  362.9 14.9 %attend_back_more2.1 = (bf16[1024,768]{1,0:T(8,128)(2,1)}, bf16[1024,768]{1,0:T(8,128)(2,1)}, bf16[1024,768]{1,0:T(8,128)(2,1)}) custom-call(s32[2]{0:T(128)} %copy-done.1, bf16[1024,768]{1,0:T(8,128)(2,1)} %copy-done.5, bf16[1024,768]{1,0:T(8,128)(2,1)} %get-tuple-element.304.g_ref, ...), custom_call_target="tpu_custom_call", output_to_operand_aliasing={{0}: (8, {}), {1}: (9, {}), {2}: (10, {})} | custom-call | flops 10737418240 | bytes 6291456 | tf_op jit(solution)/shard_map/attend_back_more2/pallas_call | solution.py:247
  379.0 15.4 %attend_back_more4.1 = (bf16[1024,768]{1,0:T(8,128)(2,1)}, bf16[1024,768]{1,0:T(8,128)(2,1)}, bf16[1024,768]{1,0:T(8,128)(2,1)}) custom-call(s32[2]{0:T(128)} %copy-done.1, bf16[1024,768]{1,0:T(8,128)(2,1)} %copy-done.5, bf16[1024,768]{1,0:T(8,128)(2,1)} %get-tuple-element.304.g_ref, ...), custom_call_target="tpu_custom_call", output_to_operand_aliasing={{0}: (8, {}), {1}: (9, {}), {2}: (10, {})} | custom-call | flops 10737418240 | bytes 6291456 | tf_op jit(solution)/shard_map/attend_back_more4/pallas_call | solution.py:247
  404.4 6.6 %collective-permute-done.13 = bf16[432,768]{1,0:T(8,128)(2,1)S(1)} collective-permute-done((bf16[432,768]{1,0:T(8,128)(2,1)S(1)}, bf16[432,768]{1,0:T(8,128)(2,1)S(1)}, u32[]{:S(2)}, u32[]{:S(2)}) %collective-permute-start.13) | collective-permute-done | bytes 663584 | tf_op jit(solution)/shard_map/ppermute | solution.py:525
  412.8 10.9 %fusion.17 = bf16[4096,768]{1,0:T(8,128)(2,1)} fusion(bf16[1024,768]{1,0:T(8,128)(2,1)S(1)} %get-tuple-element.326, s32[1024]{0:T(1024)S(1)} %copy-done.46, s32[1024]{0:T(1024)S(1)} %copy-done.44), kind=kOutput, calls=%fused_computation.20 | convolution fusion | flops 6458179584 | bytes 7872512 | tf_op jit(solution)/shard_map/dot_general | solution.py:24
  472.1 55.2 %collective-permute-done.18 = bf16[320,768]{1,0:T(8,128)(2,1)} collective-permute-done((bf16[320,768]{1,0:T(8,128)(2,1)S(1)}, bf16[320,768]{1,0:T(8,128)(2,1)}, u32[]{:S(2)}, u32[]{:S(2)}) %collective-permute-start.18) | collective-permute-done | bytes 491552 | tf_op jit(solution)/shard_map/ppermute | solution.py:525
  542.5 7.9 %fusion.7 = f32[576,768]{1,0:T(8,128)} fusion(bf16[4096,768]{1,0:T(8,128)(2,1)} %bitcast.20, s32[4096]{0:T(1024)S(1)} %copy-done.42, s32[576]{0:T(1024)S(1)} %copy-done.59), kind=kOutput, calls=%fused_computation.9 | convolution fusion | flops 3626237952 | bytes 8079616 | tf_op jit(solution)/shard_map/dot_general | solution.py:24
  553.0 14.8 %collective-permute-done.24 = bf16[288,768]{1,0:T(8,128)(2,1)S(1)} collective-permute-done((bf16[288,768]{1,0:T(8,128)(2,1)S(1)}, bf16[288,768]{1,0:T(8,128)(2,1)S(1)}, u32[]{:S(2)}, u32[]{:S(2)}) %collective-permute-start.24) | collective-permute-done | bytes 442400 | tf_op jit(solution)/shard_map/ppermute | solution.py:525
  569.5 6.7 %fusion.44 = bf16[576,768]{1,0:T(8,128)(2,1)S(1)} fusion(bf16[4096,768]{1,0:T(8,128)(2,1)} %bitcast.20, s32[4096]{0:T(1024)S(1)} %copy-done.42, s32[576]{0:T(1024)S(1)} %copy-done.57), kind=kOutput, calls=%fused_computation.65 | convolution fusion | flops 3626680320 | bytes 7194880 | tf_op jit(solution)/shard_map/dot_general | solution.py:24
  587.5 10.3 %collective-permute-done.33 = bf16[144,768]{1,0:T(8,128)(2,1)S(1)} collective-permute-done((bf16[144,768]{1,0:T(8,128)(2,1)S(1)}, bf16[144,768]{1,0:T(8,128)(2,1)S(1)}, u32[]{:S(2)}, u32[]{:S(2)}) %collective-permute-start.33) | collective-permute-done | bytes 221216 | tf_op jit(solution)/shard_map/ppermute | solution.py:525
  607.2 7.9 %unpack0.1 = f32[3072,768]{1,0:T(8,128)} custom-call(s32[1]{0:T(128)} %bitcast.17.half_ref.core_ref, bf16[3456,768]{1,0:T(8,128)(2,1)} %copy-done.9, bf16[3456,768]{1,0:T(8,128)(2,1)} %copy-done.10), custom_call_target="tpu_custom_call" | custom-call | flops 2359296 | bytes 14155776 | tf_op jit(solution)/shard_map/unpack0/pallas_call | solution.py:469
  619.3 8.5 %unpack8.1 = f32[768,3072]{1,0:T(8,128)} custom-call(s32[1]{0:T(128)} %bitcast.17.half_ref.core_ref, bf16[3456,768]{1,0:T(8,128)(2,1)} %copy-done.9, bf16[3456,768]{1,0:T(8,128)(2,1)} %copy-done.10), custom_call_target="tpu_custom_call" | custom-call | flops 2359296 | bytes 14155776 | tf_op jit(solution)/shard_map/unpack8/pallas_call | solution.py:469
  (368 shorter events, 209.6 us)
Async XLA Ops:
  0.7 26.0 %collective-permute-start = (bf16[288,768]{1,0:T(8,128)(2,1)}, bf16[288,768]{1,0:T(8,128)(2,1)}, u32[]{:S(2)}, u32[]{:S(2)}) collective-permute-start(bf16[288,768]{1,0:T(8,128)(2,1)} %param.31), channel_id=1, source_target_pairs={{0,16},{16,0},{1,17},{17,1},{2,18},{18,2},{3,19},{19,3},{4,20},{20... | collective-permute-start | bytes 1327112 | tf_op jit(solution)/shard_map/ppermute | solution.py:614
  35.0 81.8 %all-to-all-start.1 = ((bf16[16,192,768]{2,1,0:T(8,128)(2,1)}), bf16[16,192,768]{2,1,0:T(8,128)(2,1)}, u32[]{:S(2)}, u32[]{:S(2)}) async-start(bf16[16,192,768]{2,1,0:T(8,128)(2,1)} %bitcast.71), calls=%async_computation.1 | async-start | bytes 9437184 | tf_op jit(solution)/shard_map/all_to_all | solution.py:611
  39.6 75.0 %collective-permute-start.1 = (bf16[288,768]{1,0:T(8,128)(2,1)S(1)}, bf16[288,768]{1,0:T(8,128)(2,1)S(1)}, u32[]{:S(2)}, u32[]{:S(2)}) collective-permute-start(bf16[288,768]{1,0:T(8,128)(2,1)S(1)} %reduce_sum.75), channel_id=1, source_target_pairs={{0,16},{16,0},{1,17},{17,1},{2,18},{18,2},{3,19},{19,3},{4,20},{20... | collective-permute-start | bytes 1327112 | tf_op jit(solution)/shard_map/ppermute | solution.py:622
  116.8 28.1 %all-to-all-start.2 = ((bf16[16,64,768]{2,1,0:T(8,128)(2,1)}), bf16[16,64,768]{2,1,0:T(8,128)(2,1)}, u32[]{:S(2)}, u32[]{:S(2)}) async-start(bf16[16,64,768]{2,1,0:T(8,128)(2,1)} %bitcast.72), calls=%async_computation.2 | async-start | bytes 3145728 | tf_op jit(solution)/shard_map/all_to_all | solution.py:611
  128.7 48.2 %collective-permute-start.3 = (s32[576]{0:T(1024)S(1)}, s32[576]{0:T(1024)S(1)}, u32[]{:S(2)}, u32[]{:S(2)}) collective-permute-start(s32[576]{0:T(1024)S(1)} %get-tuple-element.415), channel_id=1, source_target_pairs={{0,16},{16,0},{1,17},{17,1},{2,18},{18,2},{3,19},{19,3},{4,20},{20... | collective-permute-start | bytes 6920 | tf_op jit(solution)/shard_map/ppermute | solution.py:658
  150.9 36.9 %collective-permute-start.2 = (bf16[1024,768]{1,0:T(8,128)(2,1)S(1)}, bf16[1024,768]{1,0:T(8,128)(2,1)S(1)}, u32[]{:S(2)}, u32[]{:S(2)}) collective-permute-start(bf16[1024,768]{1,0:T(8,128)(2,1)S(1)} %get-tuple-element.474), channel_id=1, source_target_pairs={{0,1},{1,0},{2,3},{3,2},{4,5},{5,4},{6,7},{7,6},{8,9},{9,8},{10,11... | collective-permute-start | bytes 4718600 | tf_op jit(solution)/shard_map/ppermute | solution.py:649
  283.9 32.2 %collective-permute-start.5 = (bf16[864,768]{1,0:T(8,128)(2,1)S(1)}, bf16[864,768]{1,0:T(8,128)(2,1)S(1)}, u32[]{:S(2)}, u32[]{:S(2)}) collective-permute-start(bf16[864,768]{1,0:T(8,128)(2,1)S(1)} %get-tuple-element.247), channel_id=1, source_target_pairs={{0,4},{4,0},{1,5},{5,1},{2,6},{6,2},{3,7},{7,3},{8,12},{12,8},{9,1... | collective-permute-start | bytes 3981320 | tf_op jit(solution)/shard_map/ppermute | solution.py:525
  286.3 31.8 %collective-permute-start.6 = (bf16[864,768]{1,0:T(8,128)(2,1)S(1)}, bf16[864,768]{1,0:T(8,128)(2,1)}, u32[]{:S(2)}, u32[]{:S(2)}) collective-permute-start(bf16[864,768]{1,0:T(8,128)(2,1)S(1)} %get-tuple-element.248), channel_id=1, source_target_pairs={{0,1},{1,0},{2,3},{3,2},{4,5},{5,4},{6,7},{7,6},{8,9},{9,8},{10,11... | collective-permute-start | bytes 3981320 | tf_op jit(solution)/shard_map/ppermute | solution.py:525
  320.3 16.7 %collective-permute-start.7 = (bf16[432,768]{1,0:T(8,128)(2,1)S(1)}, bf16[432,768]{1,0:T(8,128)(2,1)S(1)}, u32[]{:S(2)}, u32[]{:S(2)}) collective-permute-start(bf16[432,768]{1,0:T(8,128)(2,1)S(1)} %get-tuple-element.261), channel_id=1, source_target_pairs={{0,1},{1,0},{2,3},{3,2},{4,5},{5,4},{6,7},{7,6},{8,9},{9,8},{10,11... | collective-permute-start | bytes 1990664 | tf_op jit(solution)/shard_map/ppermute | solution.py:525
  321.1 16.3 %collective-permute-start.8 = (bf16[432,768]{1,0:T(8,128)(2,1)S(1)}, bf16[432,768]{1,0:T(8,128)(2,1)S(1)}, u32[]{:S(2)}, u32[]{:S(2)}) collective-permute-start(bf16[432,768]{1,0:T(8,128)(2,1)S(1)} %get-tuple-element.262), channel_id=1, source_target_pairs={{0,4},{4,0},{1,5},{5,1},{2,6},{6,2},{3,7},{7,3},{8,12},{12,8},{9,1... | collective-permute-start | bytes 1990664 | tf_op jit(solution)/shard_map/ppermute | solution.py:525
  344.1 16.6 %collective-permute-start.9 = (bf16[432,768]{1,0:T(8,128)(2,1)S(1)}, bf16[432,768]{1,0:T(8,128)(2,1)S(1)}, u32[]{:S(2)}, u32[]{:S(2)}) collective-permute-start(bf16[432,768]{1,0:T(8,128)(2,1)S(1)} %get-tuple-element.278), channel_id=1, source_target_pairs={{0,8},{8,0},{1,9},{9,1},{2,10},{10,2},{3,11},{11,3},{4,12},{12,4},... | collective-permute-start | bytes 1990664 | tf_op jit(solution)/shard_map/ppermute | solution.py:525
  344.1 50.4 %collective-permute-start.12 = (bf16[1024,768]{1,0:T(8,128)(2,1)S(1)}, bf16[1024,768]{1,0:T(8,128)(2,1)S(1)}, u32[]{:S(2)}, u32[]{:S(2)}) collective-permute-start(bf16[1024,768]{1,0:T(8,128)(2,1)S(1)} %add_convert_fusion), channel_id=1, source_target_pairs={{0,1},{1,0},{2,3},{3,2},{4,5},{5,4},{6,7},{7,6},{8,9},{9,8},{10,11... | collective-permute-start | bytes 4718600 | tf_op jit(solution)/shard_map/ppermute | solution.py:525
  360.9 17.0 %collective-permute-start.10 = (bf16[216,768]{1,0:T(8,128)(2,1)S(1)}, bf16[216,768]{1,0:T(8,128)(2,1)S(1)}, u32[]{:S(2)}, u32[]{:S(2)}) collective-permute-start(bf16[216,768]{1,0:T(8,128)(2,1)S(1)} %get-tuple-element.289), channel_id=1, source_target_pairs={{0,16},{16,0},{1,17},{17,1},{2,18},{18,2},{3,19},{19,3},{4,20},{20... | collective-permute-start | bytes 995336 | tf_op jit(solution)/shard_map/ppermute | solution.py:525
  377.9 16.5 %collective-permute-start.11 = (bf16[216,768]{1,0:T(8,128)(2,1)S(1)}, bf16[216,768]{1,0:T(8,128)(2,1)S(1)}, u32[]{:S(2)}, u32[]{:S(2)}) collective-permute-start(bf16[216,768]{1,0:T(8,128)(2,1)S(1)} %add.259), channel_id=1, source_target_pairs={{0,16},{16,0},{1,17},{17,1},{2,18},{18,2},{3,19},{19,3},{4,20},{20... | collective-permute-start | bytes 995336 | tf_op jit(solution)/shard_map/ppermute | solution.py:525
  394.5 16.5 %collective-permute-start.13 = (bf16[432,768]{1,0:T(8,128)(2,1)S(1)}, bf16[432,768]{1,0:T(8,128)(2,1)S(1)}, u32[]{:S(2)}, u32[]{:S(2)}) collective-permute-start(bf16[432,768]{1,0:T(8,128)(2,1)S(1)} %pad_maximum_fusion.6), channel_id=1, source_target_pairs={{0,8},{8,0},{1,9},{9,1},{2,10},{10,2},{3,11},{11,3},{4,12},{12,4},... | collective-permute-start | bytes 1990664 | tf_op jit(solution)/shard_map/ppermute | solution.py:525
  428.3 99.9 %all-to-all-start.3 = ((bf16[16,256,768]{2,1,0:T(8,128)(2,1)}), bf16[16,256,768]{2,1,0:T(8,128)(2,1)}, u32[]{:S(2)}, u32[]{:S(2)}) async-start(bf16[16,256,768]{2,1,0:T(8,128)(2,1)} %bitcast.70), calls=%async_computation.3 | async-start | bytes 12582912 | tf_op jit(solution)/shard_map/all_to_all | solution.py:611
  466.7 60.6 %collective-permute-start.18 = (bf16[320,768]{1,0:T(8,128)(2,1)S(1)}, bf16[320,768]{1,0:T(8,128)(2,1)}, u32[]{:S(2)}, u32[]{:S(2)}) collective-permute-start(bf16[320,768]{1,0:T(8,128)(2,1)S(1)} %get-tuple-element.456), channel_id=1, source_target_pairs={{0,1},{1,0},{2,3},{3,2},{4,5},{5,4},{6,7},{7,6},{8,9},{9,8},{10,11... | collective-permute-start | bytes 1474568 | tf_op jit(solution)/shard_map/ppermute | solution.py:525
  469.2 59.0 %collective-permute-start.17 = (bf16[320,768]{1,0:T(8,128)(2,1)S(1)}, bf16[320,768]{1,0:T(8,128)(2,1)}, u32[]{:S(2)}, u32[]{:S(2)}) collective-permute-start(bf16[320,768]{1,0:T(8,128)(2,1)S(1)} %get-tuple-element.458), channel_id=1, source_target_pairs={{0,4},{4,0},{1,5},{5,1},{2,6},{6,2},{3,7},{7,3},{8,12},{12,8},{9,1... | collective-permute-start | bytes 1474568 | tf_op jit(solution)/shard_map/ppermute | solution.py:525
  532.3 18.3 %collective-permute-start.19 = (bf16[288,768]{1,0:T(8,128)(2,1)S(1)}, bf16[288,768]{1,0:T(8,128)(2,1)S(1)}, u32[]{:S(2)}, u32[]{:S(2)}) collective-permute-start(bf16[288,768]{1,0:T(8,128)(2,1)S(1)} %get-tuple-element.437), channel_id=1, source_target_pairs={{0,4},{4,0},{1,5},{5,1},{2,6},{6,2},{3,7},{7,3},{8,12},{12,8},{9,1... | collective-permute-start | bytes 1327112 | tf_op jit(solution)/shard_map/ppermute | solution.py:525
  534.3 41.9 %collective-permute-start.27 = (bf16[288,768]{1,0:T(8,128)(2,1)S(1)}, bf16[288,768]{1,0:T(8,128)(2,1)S(1)}, u32[]{:S(2)}, u32[]{:S(2)}) collective-permute-start(bf16[288,768]{1,0:T(8,128)(2,1)S(1)} %get-tuple-element.438), channel_id=1, source_target_pairs={{0,4},{4,0},{1,5},{5,1},{2,6},{6,2},{3,7},{7,3},{8,12},{12,8},{9,1... | collective-permute-start | bytes 1327112 | tf_op jit(solution)/shard_map/ppermute | solution.py:525
  534.4 33.4 %collective-permute-start.24 = (bf16[288,768]{1,0:T(8,128)(2,1)S(1)}, bf16[288,768]{1,0:T(8,128)(2,1)S(1)}, u32[]{:S(2)}, u32[]{:S(2)}) collective-permute-start(bf16[288,768]{1,0:T(8,128)(2,1)S(1)} %get-tuple-element.439), channel_id=1, source_target_pairs={{0,4},{4,0},{1,5},{5,1},{2,6},{6,2},{3,7},{7,3},{8,12},{12,8},{9,1... | collective-permute-start | bytes 1327112 | tf_op jit(solution)/shard_map/ppermute | solution.py:525
  550.5 25.7 %collective-permute-start.28 = (bf16[288,768]{1,0:T(8,128)(2,1)S(1)}, bf16[288,768]{1,0:T(8,128)(2,1)S(1)}, u32[]{:S(2)}, u32[]{:S(2)}) collective-permute-start(bf16[288,768]{1,0:T(8,128)(2,1)S(1)} %get-tuple-element.435), channel_id=1, source_target_pairs={{0,1},{1,0},{2,3},{3,2},{4,5},{5,4},{6,7},{7,6},{8,9},{9,8},{10,11... | collective-permute-start | bytes 1327112 | tf_op jit(solution)/shard_map/ppermute | solution.py:525
  551.1 18.2 %collective-permute-start.25 = (bf16[288,768]{1,0:T(8,128)(2,1)S(1)}, bf16[288,768]{1,0:T(8,128)(2,1)S(1)}, u32[]{:S(2)}, u32[]{:S(2)}) collective-permute-start(bf16[288,768]{1,0:T(8,128)(2,1)S(1)} %get-tuple-element.436), channel_id=1, source_target_pairs={{0,1},{1,0},{2,3},{3,2},{4,5},{5,4},{6,7},{7,6},{8,9},{9,8},{10,11... | collective-permute-start | bytes 1327112 | tf_op jit(solution)/shard_map/ppermute | solution.py:525
  552.8 16.6 %collective-permute-start.26 = (bf16[80,768]{1,0:T(8,128)(2,1)S(1)}, bf16[80,768]{1,0:T(8,128)(2,1)S(1)}, u32[]{:S(2)}, u32[]{:S(2)}) collective-permute-start(bf16[80,768]{1,0:T(8,128)(2,1)S(1)} %constant_dynamic-slice_fusion), channel_id=1, source_target_pairs={{0,16},{16,0},{1,17},{17,1},{2,18},{18,2},{3,19},{19,3},{4,20},{20... | collective-permute-start | bytes 368648 | tf_op jit(solution)/shard_map/ppermute | solution.py:525
  (96 other events, 1100.4 us)

commit v14 on v13

--- a/solution.py
+++ b/solution.py
@@ -777,18 +777,21 @@
         keeps, sends = begin(late, stage)
         if at >= last - 1:
             keeps, sends, for_other = lax.optimization_barrier((keeps, sends, for_other))
+        early_then = early_sends
+        if 2 < at < 2 + spread:
+            keeps, sends, early_then = lax.optimization_barrier((keeps, sends, early_sends))
         if at == last:
             keeps, sends, early_step = lax.optimization_barrier((keeps, sends, early_step))
         if at == 4:
             keeps, sends, rows_then = lax.optimization_barrier((keeps, sends, returned))
         came = travel(sends, stage)
         if at >= last - 1:
-            quarter = swap(jnp.split(for_other, 4, axis=0)[len(from_other)], top_axis)
-            came, quarter = lax.optimization_barrier((came, quarter))
-            from_other.append(quarter)
+            third = swap(jnp.split(for_other, 3, axis=0)[len(from_other)], top_axis)
+            came, third = lax.optimization_barrier((came, third))
+            from_other.append(third)
         if 2 <= at < 2 + spread:
             rows = early_sends[0].shape[0] // spread
-            some = [p[(at - 2) * rows : (at - 1) * rows] for p in early_sends]
+            some = [p[(at - 2) * rows : (at - 1) * rows] for p in early_then]
             some, came = lax.optimization_barrier((travel(some, stages[done]), came))
             early_came.append(some)
         if at == 2:
@@ -811,24 +814,12 @@
     late = jnp.concatenate(late, axis=0)
     late, for_other = lax.optimization_barrier((late, for_other))
     late_other = swap(late, core)
-    quarters = jnp.split(for_other, 4, axis=0)
-    from_other.append(swap(quarters[2], top_axis))
+    from_other.append(swap(jnp.split(for_other, 3, axis=0)[2], top_axis))
     early_parts.append(unpack(my_core, *early_step, wide, wide, True))
-    late_other, early_parts, from_other, quarter = lax.optimization_barrier(
-        (late_other, early_parts, from_other, quarters[3])
-    )
-    from_other.append(swap(quarter, top_axis))
-    rows = block_rows // 4
-    gene_grad, know_grad = (
-        jnp.concatenate(
-            [
-                table_own[part * rows : (part + 1) * rows] + from_other[part].astype(F32)
-                for part in parts
-            ],
-            axis=0,
-        )
-        for parts in ((0, 1), (2, 3))
-    )
+    late_other, early_parts, from_other = lax.optimization_barrier(
+        (late_other, early_parts, from_other)
+    )
+    table_grads = table_own + jnp.concatenate(from_other, axis=0).astype(F32)
     w_down_grad, w_out_grad, w_up_grad = early_parts
     w_query_grad, w_key_grad, w_value_grad, expr_grad, short = unpack_whole(
         my_core, late, late_other, heights
@@ -840,8 +831,8 @@
     b_query_grad, b_value_grad = short[6 + wide // width], short[7 + wide // width]
     return (
         layer_output.reshape(1, tokens, width),
-        gene_grad,
-        know_grad,
+        table_grads[:rows_dev],
+        table_grads[rows_dev:],
         expr_grad,
         w_query_grad,
         b_query_grad,

time: 655 us -> 656 us (level)
    ppermute x37 -> x36, starting transfers between devices: 35.7 us -> 29.6 us  [swap(): return lax.ppermute(value, axis, SWAP)]
    ppermute x37 -> x36, waiting for transfers between devices: 118 us -> 120 us  [swap(): return lax.ppermute(value, axis, SWAP)]
  transfers between devices with their start and end apart: 45 -> 44, of which waited for: 25 -> 25; matrix products, arithmetic and copies ran while one was open for 15% -> 16% of each run, Pallas kernels for 23% -> 22%
where the time goes in v14:
time: 656 us; the launch traced here: 648 us
  Pallas kernels  223 us (34%)
  waiting for transfers between devices  218 us (33%)
  matrix products  82.2 us (13%)
  starting transfers between devices  58 us (9%)
  other arithmetic  36.6 us (6%)
  local copies, waits for them, and re-layouts  26.7 us (4%)
    ppermute x36, waiting for transfers between devices, swap(): return lax.ppermute(value, axis, SWAP)  120 us
    pallas_call x5, Pallas kernels, attend_back(): pl.pallas_call(functools.partial(attend_back_kernel, add, len(into)), gri...  86.9 us
    dot_general x25, matrix products, mm(): return lax.dot_general(left, right, dims, preferred_element_type=F32)  82.2 us
    ppermute x1, waiting for transfers between devices, local(): know_other = lax.ppermute(know_sum, top_axis, SWAP)  73.8 us
    pallas_call x2, Pallas kernels, attend(): pl.pallas_call(functools.partial(attend_kernel, merge), grid_spec=pltpu.P...  43.5 us
    pallas_call x1, Pallas kernels, middle(): pl.pallas_call(middle_kernel, grid=(tokens // block,), in_specs=[rows(wid...  36.9 us
    ppermute x36, starting transfers between devices, swap(): return lax.ppermute(value, axis, SWAP)  29.6 us
    pallas_call x2, Pallas kernels, weight_sums(): pl.pallas_call(functools.partial(weight_sums_kernel, counts), grid_spec=p...  27.2 us
  transfers between devices with their start and end apart: 44, of which 25 were waited for; matrix products, arithmetic and copies ran while one was open for 16% of the time, Pallas kernels for 22%

profile of v14, /device:TPU:0, one launch (start us, length us, event | category | flops | bytes accessed | tf_op | source)
XLA Modules:
  0.0 648.1 jit_solution(1491718976497153770)
XLA Ops:
  18.0 8.7 %all-to-all-done = s32[16,1,256]{2,1,0:T(1,128)S(1)} async-done(((s32[16,1,256]{2,1,0:T(1,128)}), s32[16,1,256]{2,1,0:T(1,128)S(1)}, u32[]{:S(2)}, u32[]{:S(2)}) %all-to-all-start) | async-done | bytes 16416 | tf_op jit(solution)/shard_map/all_to_all | solution.py:611
  26.8 8.2 %fusion.25 = bf16[3072,768]{1,0:T(8,128)(2,1)} fusion(s32[864]{0:T(1024)S(1)} %iota_add_fusion.2, s32[3072]{0:T(1024)S(1)} %eq.199, bf16[288,768]{1,0:T(8,128)(2,1)} %collective-permute-done, bf16[288,768]{1,0:T(8,128)(2,1)S(1)} %reduce_sum.75, bf16[288,768]{1,0:T(8,128)(2,1)S(1)} %copy-done.64), kind=kOutput, calls=%fused_computation.27 | convolution fusion | flops 4085858304 | bytes 6061440 | tf_op jit(solution)/shard_map/dot_general | solution.py:24
  40.8 73.8 %collective-permute-done.1 = bf16[288,768]{1,0:T(8,128)(2,1)S(1)} collective-permute-done((bf16[288,768]{1,0:T(8,128)(2,1)S(1)}, bf16[288,768]{1,0:T(8,128)(2,1)S(1)}, u32[]{:S(2)}, u32[]{:S(2)}) %collective-permute-start.1) | collective-permute-done | bytes 442400 | tf_op jit(solution)/shard_map/ppermute | solution.py:622
  130.8 9.5 %fusion.3 = f32[1024,768]{1,0:T(8,128)} fusion(bf16[3072,768]{1,0:T(8,128)(2,1)} %bitcast.9, s32[3072]{0:T(1024)S(1)} %eq.189, s32[1024]{0:T(1024)S(1)} %reduce.3, s32[1024]{0:T(1024)S(1)} %reduce.2), kind=kOutput, calls=%fused_computation.4 | convolution fusion | flops 4841275392 | bytes 7884800 | tf_op jit(solution)/shard_map/dot_general | solution.py:24
  155.8 21.1 %attend.1 = (f32[768,1024]{1,0:T(8,128)}, f32[6,2,1024]{2,1,0:T(2,128)S(1)}) custom-call(s32[2]{0:T(128)S(1)} %pad_add_fusion.1.where_ref, bf16[1024,768]{1,0:T(8,128)(2,1)S(1)} %add_convert_fusion.3.q_ref, bf16[1024,768]{1,0:T(8,128)(2,1)S(1)} %convolution_convert_fusion.k_ref, bf16[1024,768]{1,0:T(8,128)(2,1)S(1)} %add_convert_fusion.1.v_ref), custom_call_target="tpu_custom_call" | custom-call | flops 12884901888 | bytes 15728640 | tf_op jit(solution)/shard_map/attend/pallas_call | solution.py:167
  176.9 10.8 %collective-permute-done.2 = bf16[1024,768]{1,0:T(8,128)(2,1)S(1)} collective-permute-done((bf16[1024,768]{1,0:T(8,128)(2,1)S(1)}, bf16[1024,768]{1,0:T(8,128)(2,1)S(1)}, u32[]{:S(2)}, u32[]{:S(2)}) %collective-permute-start.2) | collective-permute-done | bytes 1572896 | tf_op jit(solution)/shard_map/ppermute | solution.py:649
  190.6 22.4 %attend_more.1 = (f32[1024,768]{1,0:T(8,128)}, f32[6,2,1024]{2,1,0:T(2,128)S(1)}) custom-call(s32[2]{0:T(128)S(1)} %pad_add_fusion.where_ref, bf16[1024,768]{1,0:T(8,128)(2,1)S(1)} %add_convert_fusion.3.q_ref, bf16[1024,768]{1,0:T(8,128)(2,1)S(1)} %convolution_convert_fusion.1.k_ref, bf16[1024,768]{1,0:T(8,128)(2,1)S(1)} %add_convert_fusion.2.v_ref, ...), custom_call_target="tpu_custom_call" | custom-call | flops 12884901888 | bytes 15728640 | tf_op jit(solution)/shard_map/attend_more/pallas_call | solution.py:167
  213.6 36.9 %middle.1 = (bf16[1024,768]{1,0:T(8,128)(2,1)}, bf16[1024,768]{1,0:T(8,128)(2,1)}, bf16[1024,768]{1,0:T(8,128)(2,1)}, bf16[1024,3072]{1,0:T(8,128)(2,1)}, bf16[1...) custom-call(f32[1024,768]{1,0:T(8,128)} %get-tuple-element.234.ctx_r, ...), custom_call_target="tpu_custom_call" | custom-call | flops 43486543872 | bytes 34603008 | tf_op jit(solution)/shard_map/middle/pallas_call | solution.py:375
  250.5 13.9 %weight_sums.2 = bf16[3456,768]{1,0:T(8,128)(2,1)} custom-call(s32[1]{0:T(128)} %bitcast.18.half_ref, bf16[1024,3072]{1,0:T(8,128)(2,1)} %get-tuple-element.242.act_ref, bf16[1024,768]{1,0:T(8,128)(2,1)} %get-tuple-element.243.gffn_ref, bf16[1024,3072]{1,0:T(8,128)(2,1)} %get-tuple-element.244.gpre_ref, bf16[1024,768]{1,0:T(8,128)(2,1)} %get-tuple-element.245.norm_ref, ...), custom_call_target="tpu_custom_call" | custom-call | flops 5435817984 | bytes 12386304 | tf_op jit(solution)/shard_map/weight_sums/pallas_call | solution.py:438
  264.4 13.4 %weight_sums.3 = bf16[3456,768]{1,0:T(8,128)(2,1)} custom-call(s32[1]{0:T(128)} %bitcast.17.half_ref.core_ref, bf16[1024,3072]{1,0:T(8,128)(2,1)} %get-tuple-element.242.act_ref, bf16[1024,768]{1,0:T(8,128)(2,1)} %get-tuple-element.243.gffn_ref, bf16[1024,3072]{1,0:T(8,128)(2,1)} %get-tuple-element.244.gpre_ref, ...), custom_call_target="tpu_custom_call" | custom-call | flops 5435817984 | bytes 12386304 | tf_op jit(solution)/shard_map/weight_sums/pallas_call | solution.py:438
  287.0 26.7 %attend_back0.1 = (f32[1024,768]{1,0:T(8,128)}, bf16[1024,768]{1,0:T(8,128)(2,1)}, bf16[1024,768]{1,0:T(8,128)(2,1)}) custom-call(s32[2]{0:T(128)} %copy-done.2, bf16[1024,768]{1,0:T(8,128)(2,1)} %copy-done.5, bf16[1024,768]{1,0:T(8,128)(2,1)} %get-tuple-element.311.g_ref, f32[1024,768]{1,0:T(8,128)} %get-tuple-element.234.ctx_ref.o_ref, ...), custom_call_target="tpu_custom_call" | custom-call | flops 21474836480 | bytes 12582912 | tf_op jit(solution)/shard_map/attend_back0/pallas_call | solution.py:247
  321.4 14.7 %attend_back4.1 = (f32[1024,768]{1,0:T(8,128)}, bf16[1024,768]{1,0:T(8,128)(2,1)}, bf16[1024,768]{1,0:T(8,128)(2,1)}) custom-call(s32[2]{0:T(128)} %copy-done.2, bf16[1024,768]{1,0:T(8,128)(2,1)} %copy-done.5, bf16[1024,768]{1,0:T(8,128)(2,1)} %get-tuple-element.311.g_ref, ...), custom_call_target="tpu_custom_call", output_to_operand_aliasing={{0}: (7, {}), {1}: (8, {}), {2}: (9, {})} | custom-call | flops 10737418240 | bytes 6291456 | tf_op jit(solution)/shard_map/attend_back4/pallas_call | solution.py:247
  345.6 15.1 %attend_back_more0.1 = (bf16[1024,768]{1,0:T(8,128)(2,1)}, bf16[1024,768]{1,0:T(8,128)(2,1)}, bf16[1024,768]{1,0:T(8,128)(2,1)}) custom-call(s32[2]{0:T(128)} %copy-done.1, bf16[1024,768]{1,0:T(8,128)(2,1)} %copy-done.5, bf16[1024,768]{1,0:T(8,128)(2,1)} %get-tuple-element.311.g_ref, f32[1024,768]{1,0:T(8,128)} %get-tuple-element.234.ctx_ref.o_ref, ...), custom_call_target="tpu_custom_call" | custom-call | flops 10737418240 | bytes 6291456 | tf_op jit(solution)/shard_map/attend_back_more0/pallas_call | solution.py:247
  362.9 14.9 %attend_back_more2.1 = (bf16[1024,768]{1,0:T(8,128)(2,1)}, bf16[1024,768]{1,0:T(8,128)(2,1)}, bf16[1024,768]{1,0:T(8,128)(2,1)}) custom-call(s32[2]{0:T(128)} %copy-done.1, bf16[1024,768]{1,0:T(8,128)(2,1)} %copy-done.5, bf16[1024,768]{1,0:T(8,128)(2,1)} %get-tuple-element.311.g_ref, ...), custom_call_target="tpu_custom_call", output_to_operand_aliasing={{0}: (8, {}), {1}: (9, {}), {2}: (10, {})} | custom-call | flops 10737418240 | bytes 6291456 | tf_op jit(solution)/shard_map/attend_back_more2/pallas_call | solution.py:247
  379.0 15.4 %attend_back_more4.1 = (bf16[1024,768]{1,0:T(8,128)(2,1)}, bf16[1024,768]{1,0:T(8,128)(2,1)}, bf16[1024,768]{1,0:T(8,128)(2,1)}) custom-call(s32[2]{0:T(128)} %copy-done.1, bf16[1024,768]{1,0:T(8,128)(2,1)} %copy-done.5, bf16[1024,768]{1,0:T(8,128)(2,1)} %get-tuple-element.311.g_ref, ...), custom_call_target="tpu_custom_call", output_to_operand_aliasing={{0}: (8, {}), {1}: (9, {}), {2}: (10, {})} | custom-call | flops 10737418240 | bytes 6291456 | tf_op jit(solution)/shard_map/attend_back_more4/pallas_call | solution.py:247
  404.4 6.6 %collective-permute-done.13 = bf16[432,768]{1,0:T(8,128)(2,1)S(1)} collective-permute-done((bf16[432,768]{1,0:T(8,128)(2,1)S(1)}, bf16[432,768]{1,0:T(8,128)(2,1)S(1)}, u32[]{:S(2)}, u32[]{:S(2)}) %collective-permute-start.13) | collective-permute-done | bytes 663584 | tf_op jit(solution)/shard_map/ppermute | solution.py:525
  412.9 10.9 %fusion.17 = bf16[4096,768]{1,0:T(8,128)(2,1)} fusion(bf16[1024,768]{1,0:T(8,128)(2,1)S(1)} %get-tuple-element.333, s32[1024]{0:T(1024)S(1)} %copy-done.43, s32[1024]{0:T(1024)S(1)} %copy-done.41), kind=kOutput, calls=%fused_computation.20 | convolution fusion | flops 6458179584 | bytes 7872512 | tf_op jit(solution)/shard_map/dot_general | solution.py:24
  472.1 55.2 %collective-permute-done.18 = bf16[320,768]{1,0:T(8,128)(2,1)} collective-permute-done((bf16[320,768]{1,0:T(8,128)(2,1)S(1)}, bf16[320,768]{1,0:T(8,128)(2,1)}, u32[]{:S(2)}, u32[]{:S(2)}) %collective-permute-start.18) | collective-permute-done | bytes 491552 | tf_op jit(solution)/shard_map/ppermute | solution.py:525
  545.1 7.9 %fusion.7 = f32[576,768]{1,0:T(8,128)} fusion(bf16[4096,768]{1,0:T(8,128)(2,1)} %bitcast.20, s32[4096]{0:T(1024)S(1)} %copy-done.39, s32[576]{0:T(1024)S(1)} %copy-done.56), kind=kOutput, calls=%fused_computation.9 | convolution fusion | flops 3626237952 | bytes 8079616 | tf_op jit(solution)/shard_map/dot_general | solution.py:24
  555.2 7.0 %collective-permute-done.26 = bf16[80,768]{1,0:T(8,128)(2,1)S(1)} collective-permute-done((bf16[80,768]{1,0:T(8,128)(2,1)S(1)}, bf16[80,768]{1,0:T(8,128)(2,1)S(1)}, u32[]{:S(2)}, u32[]{:S(2)}) %collective-permute-start.26) | collective-permute-done | bytes 122912 | tf_op jit(solution)/shard_map/ppermute | solution.py:525
  566.5 6.7 %fusion.44 = bf16[576,768]{1,0:T(8,128)(2,1)S(1)} fusion(bf16[4096,768]{1,0:T(8,128)(2,1)} %bitcast.20, s32[4096]{0:T(1024)S(1)} %copy-done.39, s32[576]{0:T(1024)S(1)} %copy-done.54), kind=kOutput, calls=%fused_computation.66 | convolution fusion | flops 3626680320 | bytes 7194880 | tf_op jit(solution)/shard_map/dot_general | solution.py:24
  585.5 7.3 %collective-permute-done.31 = bf16[160,768]{1,0:T(8,128)(2,1)S(1)} collective-permute-done((bf16[160,768]{1,0:T(8,128)(2,1)S(1)}, bf16[160,768]{1,0:T(8,128)(2,1)S(1)}, u32[]{:S(2)}, u32[]{:S(2)}) %collective-permute-start.31) | collective-permute-done | bytes 245792 | tf_op jit(solution)/shard_map/ppermute | solution.py:525
  605.5 7.9 %unpack0.1 = f32[3072,768]{1,0:T(8,128)} custom-call(s32[1]{0:T(128)} %bitcast.17.half_ref.core_ref, bf16[3456,768]{1,0:T(8,128)(2,1)} %copy-done.9, bf16[3456,768]{1,0:T(8,128)(2,1)} %copy-done.10), custom_call_target="tpu_custom_call" | custom-call | flops 2359296 | bytes 14155776 | tf_op jit(solution)/shard_map/unpack0/pallas_call | solution.py:469
  622.0 8.5 %unpack8.1 = f32[768,3072]{1,0:T(8,128)} custom-call(s32[1]{0:T(128)} %bitcast.17.half_ref.core_ref, bf16[3456,768]{1,0:T(8,128)(2,1)} %copy-done.9, bf16[3456,768]{1,0:T(8,128)(2,1)} %copy-done.10), custom_call_target="tpu_custom_call" | custom-call | flops 2359296 | bytes 14155776 | tf_op jit(solution)/shard_map/unpack8/pallas_call | solution.py:469
  (363 shorter events, 220.9 us)
Async XLA Ops:
  0.7 26.0 %collective-permute-start = (bf16[288,768]{1,0:T(8,128)(2,1)}, bf16[288,768]{1,0:T(8,128)(2,1)}, u32[]{:S(2)}, u32[]{:S(2)}) collective-permute-start(bf16[288,768]{1,0:T(8,128)(2,1)} %param.31), channel_id=1, source_target_pairs={{0,16},{16,0},{1,17},{17,1},{2,18},{18,2},{3,19},{19,3},{4,20},{20... | collective-permute-start | bytes 1327112 | tf_op jit(solution)/shard_map/ppermute | solution.py:614
  35.0 81.8 %all-to-all-start.1 = ((bf16[16,192,768]{2,1,0:T(8,128)(2,1)}), bf16[16,192,768]{2,1,0:T(8,128)(2,1)}, u32[]{:S(2)}, u32[]{:S(2)}) async-start(bf16[16,192,768]{2,1,0:T(8,128)(2,1)} %bitcast.71), calls=%async_computation.1 | async-start | bytes 9437184 | tf_op jit(solution)/shard_map/all_to_all | solution.py:611
  39.6 75.0 %collective-permute-start.1 = (bf16[288,768]{1,0:T(8,128)(2,1)S(1)}, bf16[288,768]{1,0:T(8,128)(2,1)S(1)}, u32[]{:S(2)}, u32[]{:S(2)}) collective-permute-start(bf16[288,768]{1,0:T(8,128)(2,1)S(1)} %reduce_sum.75), channel_id=1, source_target_pairs={{0,16},{16,0},{1,17},{17,1},{2,18},{18,2},{3,19},{19,3},{4,20},{20... | collective-permute-start | bytes 1327112 | tf_op jit(solution)/shard_map/ppermute | solution.py:622
  116.8 28.1 %all-to-all-start.2 = ((bf16[16,64,768]{2,1,0:T(8,128)(2,1)}), bf16[16,64,768]{2,1,0:T(8,128)(2,1)}, u32[]{:S(2)}, u32[]{:S(2)}) async-start(bf16[16,64,768]{2,1,0:T(8,128)(2,1)} %bitcast.72), calls=%async_computation.2 | async-start | bytes 3145728 | tf_op jit(solution)/shard_map/all_to_all | solution.py:611
  128.7 48.2 %collective-permute-start.3 = (s32[576]{0:T(1024)S(1)}, s32[576]{0:T(1024)S(1)}, u32[]{:S(2)}, u32[]{:S(2)}) collective-permute-start(s32[576]{0:T(1024)S(1)} %get-tuple-element.429), channel_id=1, source_target_pairs={{0,16},{16,0},{1,17},{17,1},{2,18},{18,2},{3,19},{19,3},{4,20},{20... | collective-permute-start | bytes 6920 | tf_op jit(solution)/shard_map/ppermute | solution.py:658
  150.9 36.9 %collective-permute-start.2 = (bf16[1024,768]{1,0:T(8,128)(2,1)S(1)}, bf16[1024,768]{1,0:T(8,128)(2,1)S(1)}, u32[]{:S(2)}, u32[]{:S(2)}) collective-permute-start(bf16[1024,768]{1,0:T(8,128)(2,1)S(1)} %get-tuple-element.480), channel_id=1, source_target_pairs={{0,1},{1,0},{2,3},{3,2},{4,5},{5,4},{6,7},{7,6},{8,9},{9,8},{10,11... | collective-permute-start | bytes 4718600 | tf_op jit(solution)/shard_map/ppermute | solution.py:649
  284.0 32.2 %collective-permute-start.5 = (bf16[864,768]{1,0:T(8,128)(2,1)S(1)}, bf16[864,768]{1,0:T(8,128)(2,1)S(1)}, u32[]{:S(2)}, u32[]{:S(2)}) collective-permute-start(bf16[864,768]{1,0:T(8,128)(2,1)S(1)} %get-tuple-element.254), channel_id=1, source_target_pairs={{0,4},{4,0},{1,5},{5,1},{2,6},{6,2},{3,7},{7,3},{8,12},{12,8},{9,1... | collective-permute-start | bytes 3981320 | tf_op jit(solution)/shard_map/ppermute | solution.py:525
  286.4 31.8 %collective-permute-start.6 = (bf16[864,768]{1,0:T(8,128)(2,1)S(1)}, bf16[864,768]{1,0:T(8,128)(2,1)}, u32[]{:S(2)}, u32[]{:S(2)}) collective-permute-start(bf16[864,768]{1,0:T(8,128)(2,1)S(1)} %get-tuple-element.255), channel_id=1, source_target_pairs={{0,1},{1,0},{2,3},{3,2},{4,5},{5,4},{6,7},{7,6},{8,9},{9,8},{10,11... | collective-permute-start | bytes 3981320 | tf_op jit(solution)/shard_map/ppermute | solution.py:525
  320.4 16.7 %collective-permute-start.7 = (bf16[432,768]{1,0:T(8,128)(2,1)S(1)}, bf16[432,768]{1,0:T(8,128)(2,1)S(1)}, u32[]{:S(2)}, u32[]{:S(2)}) collective-permute-start(bf16[432,768]{1,0:T(8,128)(2,1)S(1)} %get-tuple-element.268), channel_id=1, source_target_pairs={{0,1},{1,0},{2,3},{3,2},{4,5},{5,4},{6,7},{7,6},{8,9},{9,8},{10,11... | collective-permute-start | bytes 1990664 | tf_op jit(solution)/shard_map/ppermute | solution.py:525
  344.0 16.7 %collective-permute-start.9 = (bf16[432,768]{1,0:T(8,128)(2,1)S(1)}, bf16[432,768]{1,0:T(8,128)(2,1)S(1)}, u32[]{:S(2)}, u32[]{:S(2)}) collective-permute-start(bf16[432,768]{1,0:T(8,128)(2,1)S(1)} %get-tuple-element.285), channel_id=1, source_target_pairs={{0,8},{8,0},{1,9},{9,1},{2,10},{10,2},{3,11},{11,3},{4,12},{12,4},... | collective-permute-start | bytes 1990664 | tf_op jit(solution)/shard_map/ppermute | solution.py:525
  344.1 50.5 %collective-permute-start.12 = (bf16[1024,768]{1,0:T(8,128)(2,1)S(1)}, bf16[1024,768]{1,0:T(8,128)(2,1)S(1)}, u32[]{:S(2)}, u32[]{:S(2)}) collective-permute-start(bf16[1024,768]{1,0:T(8,128)(2,1)S(1)} %add_convert_fusion), channel_id=1, source_target_pairs={{0,1},{1,0},{2,3},{3,2},{4,5},{5,4},{6,7},{7,6},{8,9},{9,8},{10,11... | collective-permute-start | bytes 4718600 | tf_op jit(solution)/shard_map/ppermute | solution.py:525
  360.9 16.9 %collective-permute-start.10 = (bf16[216,768]{1,0:T(8,128)(2,1)S(1)}, bf16[216,768]{1,0:T(8,128)(2,1)S(1)}, u32[]{:S(2)}, u32[]{:S(2)}) collective-permute-start(bf16[216,768]{1,0:T(8,128)(2,1)S(1)} %get-tuple-element.296), channel_id=1, source_target_pairs={{0,16},{16,0},{1,17},{17,1},{2,18},{18,2},{3,19},{19,3},{4,20},{20... | collective-permute-start | bytes 995336 | tf_op jit(solution)/shard_map/ppermute | solution.py:525
  377.9 16.5 %collective-permute-start.11 = (bf16[216,768]{1,0:T(8,128)(2,1)S(1)}, bf16[216,768]{1,0:T(8,128)(2,1)S(1)}, u32[]{:S(2)}, u32[]{:S(2)}) collective-permute-start(bf16[216,768]{1,0:T(8,128)(2,1)S(1)} %add.250), channel_id=1, source_target_pairs={{0,16},{16,0},{1,17},{17,1},{2,18},{18,2},{3,19},{19,3},{4,20},{20... | collective-permute-start | bytes 995336 | tf_op jit(solution)/shard_map/ppermute | solution.py:525
  394.6 16.4 %collective-permute-start.13 = (bf16[432,768]{1,0:T(8,128)(2,1)S(1)}, bf16[432,768]{1,0:T(8,128)(2,1)S(1)}, u32[]{:S(2)}, u32[]{:S(2)}) collective-permute-start(bf16[432,768]{1,0:T(8,128)(2,1)S(1)} %pad_maximum_fusion.4), channel_id=1, source_target_pairs={{0,8},{8,0},{1,9},{9,1},{2,10},{10,2},{3,11},{11,3},{4,12},{12,4},... | collective-permute-start | bytes 1990664 | tf_op jit(solution)/shard_map/ppermute | solution.py:525
  428.3 99.9 %all-to-all-start.3 = ((bf16[16,256,768]{2,1,0:T(8,128)(2,1)}), bf16[16,256,768]{2,1,0:T(8,128)(2,1)}, u32[]{:S(2)}, u32[]{:S(2)}) async-start(bf16[16,256,768]{2,1,0:T(8,128)(2,1)} %bitcast.70), calls=%async_computation.3 | async-start | bytes 12582912 | tf_op jit(solution)/shard_map/all_to_all | solution.py:611
  466.7 60.6 %collective-permute-start.18 = (bf16[320,768]{1,0:T(8,128)(2,1)S(1)}, bf16[320,768]{1,0:T(8,128)(2,1)}, u32[]{:S(2)}, u32[]{:S(2)}) collective-permute-start(bf16[320,768]{1,0:T(8,128)(2,1)S(1)} %get-tuple-element.462), channel_id=1, source_target_pairs={{0,1},{1,0},{2,3},{3,2},{4,5},{5,4},{6,7},{7,6},{8,9},{9,8},{10,11... | collective-permute-start | bytes 1474568 | tf_op jit(solution)/shard_map/ppermute | solution.py:525
  469.2 59.0 %collective-permute-start.17 = (bf16[320,768]{1,0:T(8,128)(2,1)S(1)}, bf16[320,768]{1,0:T(8,128)(2,1)}, u32[]{:S(2)}, u32[]{:S(2)}) collective-permute-start(bf16[320,768]{1,0:T(8,128)(2,1)S(1)} %get-tuple-element.464), channel_id=1, source_target_pairs={{0,4},{4,0},{1,5},{5,1},{2,6},{6,2},{3,7},{7,3},{8,12},{12,8},{9,1... | collective-permute-start | bytes 1474568 | tf_op jit(solution)/shard_map/ppermute | solution.py:525
  534.6 18.4 %collective-permute-start.20 = (bf16[288,768]{1,0:T(8,128)(2,1)S(1)}, bf16[288,768]{1,0:T(8,128)(2,1)S(1)}, u32[]{:S(2)}, u32[]{:S(2)}) collective-permute-start(bf16[288,768]{1,0:T(8,128)(2,1)S(1)} %slice.87), channel_id=1, source_target_pairs={{0,1},{1,0},{2,3},{3,2},{4,5},{5,4},{6,7},{7,6},{8,9},{9,8},{10,11... | collective-permute-start | bytes 1327112 | tf_op jit(solution)/shard_map/ppermute | solution.py:525
  535.3 17.7 %collective-permute-start.19 = (bf16[288,768]{1,0:T(8,128)(2,1)S(1)}, bf16[288,768]{1,0:T(8,128)(2,1)S(1)}, u32[]{:S(2)}, u32[]{:S(2)}) collective-permute-start(bf16[288,768]{1,0:T(8,128)(2,1)S(1)} %slice.86), channel_id=1, source_target_pairs={{0,4},{4,0},{1,5},{5,1},{2,6},{6,2},{3,7},{7,3},{8,12},{12,8},{9,1... | collective-permute-start | bytes 1327112 | tf_op jit(solution)/shard_map/ppermute | solution.py:525
  581.6 17.3 %collective-permute-start.34 = (bf16[3456,768]{1,0:T(8,128)(2,1)S(1)}, bf16[3456,768]{1,0:T(8,128)(2,1)S(1)}, u32[]{:S(2)}, u32[]{:S(2)}) collective-permute-start(bf16[3456,768]{1,0:T(8,128)(2,1)S(1)} %pad_maximum_fusion.own_ref), channel_id=1, source_target_pairs={{0,2},{2,0},{1,3},{3,1},{4,6},{6,4},{5,7},{7,5},{8,10},{10,8},{9,1... | collective-permute-start | bytes 15925256 | tf_op jit(solution)/shard_map/ppermute | solution.py:525
  581.7 17.0 %collective-permute-start.33 = (bf16[192,768]{1,0:T(8,128)(2,1)S(1)}, bf16[192,768]{1,0:T(8,128)(2,1)S(1)}, u32[]{:S(2)}, u32[]{:S(2)}) collective-permute-start(bf16[192,768]{1,0:T(8,128)(2,1)S(1)} %split.25), channel_id=1, source_target_pairs={{0,16},{16,0},{1,17},{17,1},{2,18},{18,2},{3,19},{19,3},{4,20},{20... | collective-permute-start | bytes 884744 | tf_op jit(solution)/shard_map/ppermute | solution.py:525
  601.2 17.2 %collective-permute-start.35 = (bf16[320,768]{1,0:T(8,128)(2,1)S(1)}, bf16[320,768]{1,0:T(8,128)(2,1)S(1)}, u32[]{:S(2)}, u32[]{:S(2)}) collective-permute-start(bf16[320,768]{1,0:T(8,128)(2,1)S(1)} %pad_maximum_fusion.5), channel_id=1, source_target_pairs={{0,4},{4,0},{1,5},{5,1},{2,6},{6,2},{3,7},{7,3},{8,12},{12,8},{9,1... | collective-permute-start | bytes 1474568 | tf_op jit(solution)/shard_map/ppermute | solution.py:525
  601.7 16.7 %collective-permute-start.36 = (bf16[320,768]{1,0:T(8,128)(2,1)S(1)}, bf16[320,768]{1,0:T(8,128)(2,1)S(1)}, u32[]{:S(2)}, u32[]{:S(2)}) collective-permute-start(bf16[320,768]{1,0:T(8,128)(2,1)S(1)} %pad_maximum_fusion.6), channel_id=1, source_target_pairs={{0,1},{1,0},{2,3},{3,2},{4,5},{5,4},{6,7},{7,6},{8,9},{9,8},{10,11... | collective-permute-start | bytes 1474568 | tf_op jit(solution)/shard_map/ppermute | solution.py:525
  619.3 17.4 %collective-permute-start.38 = (bf16[1280,768]{1,0:T(8,128)(2,1)S(1)}, bf16[1280,768]{1,0:T(8,128)(2,1)}, u32[]{:S(2)}, u32[]{:S(2)}) collective-permute-start(bf16[1280,768]{1,0:T(8,128)(2,1)S(1)} %pad_maximum_fusion.1.own_ref), channel_id=1, source_target_pairs={{0,2},{2,0},{1,3},{3,1},{4,6},{6,4},{5,7},{7,5},{8,10},{10,8},{9,1... | collective-permute-start | bytes 5898248 | tf_op jit(solution)/shard_map/ppermute | solution.py:525
  (92 other events, 975.6 us)
